TPU v7x, 32 devices: a whole 2x2x4 slice. The times are simulated.
32 devices in a mesh: group: 4 (over x, core), ctx: 8 (over z, y).
Axes of the slice: x: 2, y: 2, z: 4, core: 2. Of those that a mesh axis runs over, the one named last changes fastest.
Arguments:
- tokens_in: bfloat16 [16, 2048, 768], P('group', 'ctx'), may hold values from -6 to 6
- seq_lengths: int32 [16], P('group'), may hold values from 512 to 2048, as said below
- norm_gain: float32 [768], replicated, may hold values from 0.5 to 1.5
- w_zx: bfloat16 [768, 3328], P('group'), may hold values from -0.21875 to 0.21875
- w_delta: bfloat16 [768, 24], P('group'), may hold values from -0.21875 to 0.21875
- w_out: bfloat16 [1536, 768], P('group'), may hold values from -0.15625 to 0.15625
- conv_weight: float32 [4, 1792], replicated, may hold values from -3 to 3
- conv_bias: float32 [1792], replicated, may hold values from -1.8 to 1.8
- delta_bias: float32 [24], replicated, may hold values from -2 to 0
- decay_log: float32 [24], replicated, may hold values from -11 to -2
- skip_gain: float32 [24], replicated, may hold values from 0.5 to 1.5
- gated_gain: float32 [1536], replicated, may hold values from 0.5 to 1.5
- cotangent: bfloat16 [16, 2048, 768], P('group', 'ctx'), may hold values from -6 to 6
Outputs:
- mixed_out: bfloat16 [16, 2048, 768], P('group', 'ctx')
- grad_tokens: bfloat16 [16, 2048, 768], P('group', 'ctx')
- grad_norm_gain: float32 [768], replicated
- grad_w_zx: float32 [768, 3328], P('group')
- grad_w_delta: float32 [768, 24], P('group')
- grad_w_out: float32 [1536, 768], P('group')
- grad_conv_weight: float32 [4, 1792], replicated
- grad_conv_bias: float32 [1792], replicated
- grad_delta_bias: float32 [24], replicated
- grad_decay_log: float32 [24], replicated
- grad_skip_gain: float32 [24], replicated
- grad_gated_gain: float32 [1536], replicated
Inputs may be any that keep to these rules, and one draw needn't show every extreme that they name: `seq_lengths`: valid slots of each sequence, counted from its start; some sequence is full and some has 512.
All inputs are finite; a program needn't handle non-finite values.
Results may differ from a plain program's by a relative error of at most 0.015.
Values may be sent and summed in bfloat16 or wider, within the bound.
A program may use at most 192 MiB of HBM per device.

v0:
```python
import jax
import jax.numpy as jnp
from jax import lax
from jax.sharding import PartitionSpec as P

D = 768
HEADS = 24
HEADDIM = 64
NSTATE = 128
KCONV = 4
SPAN = 256
DIN = 1536
ZXW = 3328


epsilon = 1e-05


def passed_along(value, axis, steps):
    count = lax.axis_size(axis)
    leading, last = (max(0, -steps), min(count, count - steps))
    return lax.ppermute(value, axis, [(source, source + steps) for source in range(leading, last)])


def input_norm(values, scale_row):
    return (
        values * lax.rsqrt(jnp.mean(values * values, axis=-1, keepdims=True) + epsilon) * scale_row
    )


def prepare(conv_rows, delta_raw, before_rows, conv_weight, conv_bias, delta_bias, decay_log):
    row_count = conv_rows.shape[0]
    extended = jnp.concatenate([before_rows, conv_rows], axis=0)
    conv_out = conv_bias[None, :]
    for offset in range(KCONV):
        conv_out = conv_out + conv_weight[offset][None, :] * extended[offset : offset + row_count]
    activated = jax.nn.silu(conv_out)
    seq_inputs = activated[:, :DIN].reshape(row_count, HEADS, HEADDIM)
    write_b = activated[:, DIN : DIN + NSTATE]
    read_c = activated[:, DIN + NSTATE :]
    step_size = jax.nn.softplus(delta_raw + delta_bias[None, :])
    log_decay = -jnp.exp(decay_log)[None, :] * step_size
    cumulative = jnp.cumsum(log_decay, axis=0)
    return (seq_inputs, write_b, read_c, step_size, cumulative)


def block_states(seq_inputs, write_b, step_size, cumulative):
    to_end = jnp.exp(cumulative[-1][None, :] - cumulative)
    weighted = seq_inputs * (step_size * to_end)[:, :, None]
    local_state = jnp.einsum("qhp,qn->hpn", weighted, write_b, precision=lax.Precision.HIGHEST)
    return (local_state, jnp.exp(cumulative[-1]))


def finish(
    gate_part, seq_inputs, write_b, read_c, step_size, cumulative, state_in, skip_gain, gated_gain
):
    row_count = gate_part.shape[0]
    scores = jnp.dot(read_c, write_b.T, precision=lax.Precision.HIGHEST)
    causal = jnp.arange(row_count)[:, None] >= jnp.arange(row_count)[None, :]
    log_gaps = cumulative.T[:, :, None] - cumulative.T[:, None, :]
    decays = jnp.exp(jnp.where(causal[None], log_gaps, -jnp.inf))
    scaled = seq_inputs * step_size[:, :, None]
    within = jnp.einsum(
        "hts,shp->thp", decays * scores[None], scaled, precision=lax.Precision.HIGHEST
    )
    carried = (
        jnp.einsum("tn,hpn->thp", read_c, state_in, precision=lax.Precision.HIGHEST)
        * jnp.exp(cumulative)[:, :, None]
    )
    outputs = within + carried + skip_gain[None, :, None] * seq_inputs
    flat_rows = outputs.reshape(row_count, HEADS * HEADDIM)
    gated_rows = flat_rows * jax.nn.silu(gate_part)
    return input_norm(gated_rows, gated_gain)


def local(
    tokens_in,
    seq_lengths,
    norm_gain,
    w_zx,
    w_delta,
    w_out,
    conv_weight,
    conv_bias,
    delta_bias,
    decay_log,
    skip_gain,
    gated_gain,
    cotangent,
):
    seq_count = tokens_in.shape[0]
    row_total = seq_count * SPAN
    rim_start = SPAN - KCONV + 1
    contract_rows = (((0,), (0,)), ((), ()))
    contract_cols = (((1,), (1,)), ((), ()))
    full_zx, full_delta, full_out = (
        lax.all_gather(w_zx, "group", axis=0, tiled=True),
        lax.all_gather(w_delta, "group", axis=0, tiled=True),
        lax.all_gather(w_out, "group", axis=0, tiled=True),
    )
    positions = lax.axis_index("ctx") * SPAN + jnp.arange(SPAN, dtype=jnp.int32)
    live_mask = (positions[None, :] < seq_lengths[:, None]).astype(jnp.float32)[:, :, None]
    tokens32 = tokens_in.astype(jnp.float32)
    normed_full, norm_pull = jax.vjp(input_norm, tokens32, norm_gain)
    normed_low = normed_full.astype(jnp.bfloat16).reshape(row_total, D)
    proj_zx = jnp.dot(normed_low, full_zx, preferred_element_type=jnp.float32).reshape(
        seq_count, SPAN, ZXW
    )
    proj_delta = jnp.dot(normed_low, full_delta, preferred_element_type=jnp.float32).reshape(
        seq_count, SPAN, HEADS
    )
    gate_part = proj_zx[:, :, :DIN]
    conv_in = proj_zx[:, :, DIN:]
    before_rows = passed_along(conv_in[:, rim_start:, :], "ctx", 1)

    def front_part(members):
        pieces = prepare(
            members[0], members[1], members[2], conv_weight, conv_bias, delta_bias, decay_log
        )
        return pieces + block_states(pieces[0], pieces[1], pieces[3], pieces[4])

    seq_inputs, write_b, read_c, step_size, cumulative, local_states, totals = lax.map(
        front_part, (conv_in, proj_delta, before_rows)
    )

    def relay_step(counter, carried_in):
        return passed_along(totals[:, :, None, None] * carried_in + local_states, "ctx", 1)

    state_in = lax.fori_loop(0, lax.axis_size("ctx") - 1, relay_step, jnp.zeros_like(local_states))

    def finish_part(members):
        return finish(*members, skip_gain, gated_gain)

    mixer_rows = lax.map(
        finish_part, (gate_part, seq_inputs, write_b, read_c, step_size, cumulative, state_in)
    )
    mixer_low = mixer_rows.astype(jnp.bfloat16).reshape(row_total, DIN)
    out_proj = jnp.dot(mixer_low, full_out, preferred_element_type=jnp.float32).reshape(
        seq_count, SPAN, D
    )
    mixed_out = (live_mask * (tokens32 + out_proj)).astype(jnp.bfloat16)
    cotangent32 = cotangent.astype(jnp.float32)
    drive = (live_mask * cotangent32).astype(jnp.bfloat16).reshape(row_total, D)
    back_zx, back_delta, back_out = (
        lax.all_gather(w_zx, "group", axis=0, tiled=True),
        lax.all_gather(w_delta, "group", axis=0, tiled=True),
        lax.all_gather(w_out, "group", axis=0, tiled=True),
    )
    grad_out_full = lax.dot_general(
        mixer_low, drive, contract_rows, preferred_element_type=jnp.float32
    )
    grad_mixer = lax.dot_general(
        drive, back_out, contract_cols, preferred_element_type=jnp.float32
    ).reshape(seq_count, SPAN, DIN)

    def finish_back(members):
        primal, pullback = jax.vjp(finish, *members[:7], skip_gain, gated_gain)
        return pullback(members[7])

    finish_grads = lax.map(
        finish_back,
        (gate_part, seq_inputs, write_b, read_c, step_size, cumulative, state_in, grad_mixer),
    )
    grad_direct = finish_grads[6]

    def relay_back(counter, carried_in):
        return passed_along(grad_direct + totals[:, :, None, None] * carried_in, "ctx", -1)

    later_grad = lax.fori_loop(0, lax.axis_size("ctx") - 1, relay_back, jnp.zeros_like(grad_direct))
    grad_totals = jnp.sum(later_grad * state_in, axis=(2, 3))

    def front_back(members):
        (
            conv_rows,
            delta_rows,
            rim_rows,
            grad_inputs,
            grad_write,
            grad_read,
            grad_step,
            grad_cumulative,
            grad_local,
            grad_total,
        ) = members
        pieces, prepare_pull = jax.vjp(
            prepare, conv_rows, delta_rows, rim_rows, conv_weight, conv_bias, delta_bias, decay_log
        )
        states_out, states_pull = jax.vjp(block_states, pieces[0], pieces[1], pieces[3], pieces[4])
        state_grads = states_pull((grad_local, grad_total))
        return prepare_pull(
            (
                grad_inputs + state_grads[0],
                grad_write + state_grads[1],
                grad_read,
                grad_step + state_grads[2],
                grad_cumulative + state_grads[3],
            )
        )

    front_grads = lax.map(
        front_back,
        (
            conv_in,
            proj_delta,
            before_rows,
            finish_grads[1],
            finish_grads[2],
            finish_grads[3],
            finish_grads[4],
            finish_grads[5],
            later_grad,
            grad_totals,
        ),
    )
    grad_rim = passed_along(front_grads[2].astype(jnp.bfloat16), "ctx", -1).astype(jnp.float32)
    grad_conv = front_grads[0]
    grad_conv = jnp.concatenate(
        [grad_conv[:, :rim_start, :], grad_conv[:, rim_start:, :] + grad_rim], axis=1
    )
    grad_zx_low = (
        jnp.concatenate([finish_grads[0], grad_conv], axis=2)
        .astype(jnp.bfloat16)
        .reshape(row_total, ZXW)
    )
    grad_delta_low = front_grads[1].astype(jnp.bfloat16).reshape(row_total, HEADS)
    grad_zx_full = lax.dot_general(
        normed_low, grad_zx_low, contract_rows, preferred_element_type=jnp.float32
    )
    grad_delta_full = lax.dot_general(
        normed_low, grad_delta_low, contract_rows, preferred_element_type=jnp.float32
    )
    grad_normed = lax.dot_general(
        grad_zx_low, back_zx, contract_cols, preferred_element_type=jnp.float32
    )
    grad_normed = grad_normed + lax.dot_general(
        grad_delta_low, back_delta, contract_cols, preferred_element_type=jnp.float32
    )
    grad_tokens_part, grad_gain = norm_pull(grad_normed.reshape(seq_count, SPAN, D))
    grad_tokens = (live_mask * cotangent32 + grad_tokens_part).astype(jnp.bfloat16)
    scattered = (
        lax.psum_scatter(
            grad_zx_full.astype(jnp.bfloat16), "group", scatter_dimension=0, tiled=True
        ).astype(jnp.float32),
        lax.psum_scatter(
            grad_delta_full.astype(jnp.bfloat16), "group", scatter_dimension=0, tiled=True
        ).astype(jnp.float32),
        lax.psum_scatter(
            grad_out_full.astype(jnp.bfloat16), "group", scatter_dimension=0, tiled=True
        ).astype(jnp.float32),
    )
    summed = (
        lax.psum(scattered[0].astype(jnp.bfloat16), "ctx").astype(jnp.float32),
        lax.psum(scattered[1].astype(jnp.bfloat16), "ctx").astype(jnp.float32),
        lax.psum(scattered[2].astype(jnp.bfloat16), "ctx").astype(jnp.float32),
    )
    small_sums = lax.psum(
        (
            grad_gain,
            jnp.sum(front_grads[3], 0),
            jnp.sum(front_grads[4], 0),
            jnp.sum(front_grads[5], 0),
            jnp.sum(front_grads[6], 0),
            jnp.sum(finish_grads[7], 0),
            jnp.sum(finish_grads[8], 0),
        ),
        ("group", "ctx"),
    )
    return (
        mixed_out,
        grad_tokens,
        small_sums[0],
        summed[0],
        summed[1],
        summed[2],
        small_sums[1],
        small_sums[2],
        small_sums[3],
        small_sums[4],
        small_sums[5],
        small_sums[6],
    )


def solution(mesh):
    in_specs = (
        P("group", "ctx", None),
        P("group"),
        P(),
        P("group", None),
        P("group", None),
        P("group", None),
        P(),
        P(),
        P(),
        P(),
        P(),
        P(),
        P("group", "ctx", None),
    )
    out_specs = (
        P("group", "ctx", None),
        P("group", "ctx", None),
        P(),
        P("group", None),
        P("group", None),
        P("group", None),
        P(),
        P(),
        P(),
        P(),
        P(),
        P(),
    )
    return jax.shard_map(local, mesh=mesh, in_specs=in_specs, out_specs=out_specs, check_vma=False)
```

profile of v0, /device:TPU:0, one launch (start us, length us, event | category | flops | bytes accessed | tf_op | source)
XLA Modules:
  0.0 1951.9 jit_solution(10326079172951933625)
XLA Ops:
  17.5 34.6 %all-gather.4.cloned.1.call-done = bf16[768,3328]{1,0:T(8,128)(2,1)} async-done(((bf16[192,3328]{1,0:T(8,128)(2,1)}), bf16[768,3328]{1,0:T(8,128)(2,1)}) %all-gather.4.cloned.1.call-update) | async-done | bytes 5111824 | tf_op jit(solution)/shard_map/all_gather | solution.py:97
  108.5 77.5 %while.105 = (s32[]{:T(128)}, f32[4,256,24,64]{1,3,2,0:T(8,128)}, f32[4,256,128]{2,1,0:T(8,128)}, f32[4,256,128]{2,1,0:T(8,128)}, f32[4,256,24]{1,2,0:T(8,128)},...) while((s32[]{:T(128)}, f32[4,256,24,64]{1,3,2,0:T(8,128)}, ...), condition=%wide.region_4.5_spmd, body=%wide.region_1.4_spmd.sunk | while | flops 612200512 | bytes 20300856 | solution.py:122
  186.8 517.6 %while.106 = (s32[]{:T(128)}, f32[4,24,64,128]{3,2,1,0:T(8,128)S(1)}, f32[4,24]{1,0:T(4,128)S(1)}, f32[4,24,64,128]{3,2,1,0:T(8,128)}, s32[]{:T(128)}) while((s32[]{:T(128)}, f32[4,24,64,128]{3,2,1,0:T(8,128)S(1)}, f32[4,24]{1,0:T(4,128)S(1)}, f32[4,24,64,128]{3,2,1,0:T(8,128)}, s32[]{:T(128)}) %tuple.255), condition=%wide.region_6.7_spmd, body=%wide.region_5.6_spmd.sunk | while | flops 1572866 | bytes 22020580 | solution.py:129
  194.2 67.9 %collective-permute-done = f32[4,24,64,128]{3,2,1,0:T(8,128)S(1)} collective-permute-done((f32[4,24,64,128]{3,2,1,0:T(8,128)}, f32[4,24,64,128]{3,2,1,0:T(8,128)S(1)}, u32[]{:S(2)}, u32[]{:S(2)}) %collective-permute-start) | collective-permute-done | bytes 3145760 | tf_op jit(solution)/shard_map/while/body/eval_jaxpr/ppermute | solution.py:22
  270.5 67.1 %collective-permute-done = f32[4,24,64,128]{3,2,1,0:T(8,128)S(1)} collective-permute-done((f32[4,24,64,128]{3,2,1,0:T(8,128)}, f32[4,24,64,128]{3,2,1,0:T(8,128)S(1)}, u32[]{:S(2)}, u32[]{:S(2)}) %collective-permute-start) | collective-permute-done | bytes 3145760 | tf_op jit(solution)/shard_map/while/body/eval_jaxpr/ppermute | solution.py:22
  345.9 66.1 %collective-permute-done = f32[4,24,64,128]{3,2,1,0:T(8,128)S(1)} collective-permute-done((f32[4,24,64,128]{3,2,1,0:T(8,128)}, f32[4,24,64,128]{3,2,1,0:T(8,128)S(1)}, u32[]{:S(2)}, u32[]{:S(2)}) %collective-permute-start) | collective-permute-done | bytes 3145760 | tf_op jit(solution)/shard_map/while/body/eval_jaxpr/ppermute | solution.py:22
  421.3 65.2 %collective-permute-done = f32[4,24,64,128]{3,2,1,0:T(8,128)S(1)} collective-permute-done((f32[4,24,64,128]{3,2,1,0:T(8,128)}, f32[4,24,64,128]{3,2,1,0:T(8,128)S(1)}, u32[]{:S(2)}, u32[]{:S(2)}) %collective-permute-start) | collective-permute-done | bytes 3145760 | tf_op jit(solution)/shard_map/while/body/eval_jaxpr/ppermute | solution.py:22
  495.8 64.3 %collective-permute-done = f32[4,24,64,128]{3,2,1,0:T(8,128)S(1)} collective-permute-done((f32[4,24,64,128]{3,2,1,0:T(8,128)}, f32[4,24,64,128]{3,2,1,0:T(8,128)S(1)}, u32[]{:S(2)}, u32[]{:S(2)}) %collective-permute-start) | collective-permute-done | bytes 3145760 | tf_op jit(solution)/shard_map/while/body/eval_jaxpr/ppermute | solution.py:22
  569.3 63.4 %collective-permute-done = f32[4,24,64,128]{3,2,1,0:T(8,128)S(1)} collective-permute-done((f32[4,24,64,128]{3,2,1,0:T(8,128)}, f32[4,24,64,128]{3,2,1,0:T(8,128)S(1)}, u32[]{:S(2)}, u32[]{:S(2)}) %collective-permute-start) | collective-permute-done | bytes 3145760 | tf_op jit(solution)/shard_map/while/body/eval_jaxpr/ppermute | solution.py:22
  642.0 62.4 %collective-permute-done = f32[4,24,64,128]{3,2,1,0:T(8,128)S(1)} collective-permute-done((f32[4,24,64,128]{3,2,1,0:T(8,128)}, f32[4,24,64,128]{3,2,1,0:T(8,128)S(1)}, u32[]{:S(2)}, u32[]{:S(2)}) %collective-permute-start) | collective-permute-done | bytes 3145760 | tf_op jit(solution)/shard_map/while/body/eval_jaxpr/ppermute | solution.py:22
  713.4 258.0 %while.108 = (s32[]{:T(128)}, bf16[4,256,1536]{2,1,0:T(8,128)(2,1)}, f32[4,256,24,64]{1,3,2,0:T(8,128)}, f32[4,256,128]{2,1,0:T(8,128)}, f32[4,256,128]{2,1,0:T(...) while((s32[]{:T(128)}, bf16[4,256,1536]{2,1,0:T(8,128)(2,1)}, ...), condition=%wide.region_20.21_spmd, body=%wide.region_10.20_spmd.sunk | while | flops 5786598912 | bytes 129713048 | solution.py:160
  726.5 10.0 multiply_reduce_fusion.16
  790.7 10.1 multiply_reduce_fusion.16
  809.9 8.9 fusion.298
  855.2 10.2 multiply_reduce_fusion.16
  874.5 8.9 fusion.298
  919.6 9.9 multiply_reduce_fusion.16
  973.8 482.4 %while.109 = (s32[]{:T(128)}, f32[4,24,64,128]{3,2,1,0:T(8,128)S(1)}, f32[4,24]{1,0:T(4,128)S(1)}, f32[4,24,64,128]{3,2,1,0:T(8,128)}, s32[]{:T(128)}) while((s32[]{:T(128)}, f32[4,24,64,128]{3,2,1,0:T(8,128)S(1)}, f32[4,24]{1,0:T(4,128)S(1)}, f32[4,24,64,128]{3,2,1,0:T(8,128)}, s32[]{:T(128)}) %tuple.256), condition=%wide.region_22.23_spmd, body=%wide.region_21.22_spmd.sunk | while | flops 1572866 | bytes 22020580 | solution.py:169
  979.0 66.2 %collective-permute-done.1 = f32[4,24,64,128]{3,2,1,0:T(8,128)S(1)} collective-permute-done((f32[4,24,64,128]{3,2,1,0:T(8,128)}, f32[4,24,64,128]{3,2,1,0:T(8,128)S(1)}, u32[]{:S(2)}, u32[]{:S(2)}) %collective-permute-start.1) | collective-permute-done | bytes 3145760 | tf_op jit(solution)/shard_map/while/body/eval_jaxpr/ppermute | solution.py:22
  1050.6 65.6 %collective-permute-done.1 = f32[4,24,64,128]{3,2,1,0:T(8,128)S(1)} collective-permute-done((f32[4,24,64,128]{3,2,1,0:T(8,128)}, f32[4,24,64,128]{3,2,1,0:T(8,128)S(1)}, u32[]{:S(2)}, u32[]{:S(2)}) %collective-permute-start.1) | collective-permute-done | bytes 3145760 | tf_op jit(solution)/shard_map/while/body/eval_jaxpr/ppermute | solution.py:22
  1121.4 64.0 %collective-permute-done.1 = f32[4,24,64,128]{3,2,1,0:T(8,128)S(1)} collective-permute-done((f32[4,24,64,128]{3,2,1,0:T(8,128)}, f32[4,24,64,128]{3,2,1,0:T(8,128)S(1)}, u32[]{:S(2)}, u32[]{:S(2)}) %collective-permute-start.1) | collective-permute-done | bytes 3145760 | tf_op jit(solution)/shard_map/while/body/eval_jaxpr/ppermute | solution.py:22
  1190.7 63.1 %collective-permute-done.1 = f32[4,24,64,128]{3,2,1,0:T(8,128)S(1)} collective-permute-done((f32[4,24,64,128]{3,2,1,0:T(8,128)}, f32[4,24,64,128]{3,2,1,0:T(8,128)S(1)}, u32[]{:S(2)}, u32[]{:S(2)}) %collective-permute-start.1) | collective-permute-done | bytes 3145760 | tf_op jit(solution)/shard_map/while/body/eval_jaxpr/ppermute | solution.py:22
  1259.1 63.0 %collective-permute-done.1 = f32[4,24,64,128]{3,2,1,0:T(8,128)S(1)} collective-permute-done((f32[4,24,64,128]{3,2,1,0:T(8,128)}, f32[4,24,64,128]{3,2,1,0:T(8,128)S(1)}, u32[]{:S(2)}, u32[]{:S(2)}) %collective-permute-start.1) | collective-permute-done | bytes 3145760 | tf_op jit(solution)/shard_map/while/body/eval_jaxpr/ppermute | solution.py:22
  1327.4 63.0 %collective-permute-done.1 = f32[4,24,64,128]{3,2,1,0:T(8,128)S(1)} collective-permute-done((f32[4,24,64,128]{3,2,1,0:T(8,128)}, f32[4,24,64,128]{3,2,1,0:T(8,128)S(1)}, u32[]{:S(2)}, u32[]{:S(2)}) %collective-permute-start.1) | collective-permute-done | bytes 3145760 | tf_op jit(solution)/shard_map/while/body/eval_jaxpr/ppermute | solution.py:22
  1395.7 60.5 %collective-permute-done.1 = f32[4,24,64,128]{3,2,1,0:T(8,128)S(1)} collective-permute-done((f32[4,24,64,128]{3,2,1,0:T(8,128)}, f32[4,24,64,128]{3,2,1,0:T(8,128)S(1)}, u32[]{:S(2)}, u32[]{:S(2)}) %collective-permute-start.1) | collective-permute-done | bytes 3145760 | tf_op jit(solution)/shard_map/while/body/eval_jaxpr/ppermute | solution.py:22
  1458.5 63.7 %while.107 = (s32[]{:T(128)}, bf16[4,256,1536]{1,2,0:T(8,128)(2,1)}, f32[4,256,24,64]{1,3,2,0:T(8,128)}, f32[4,256,24]{1,2,0:T(8,128)}, f32[4,256,24]{1,2,0:T(8,...) while((s32[]{:T(128)}, bf16[4,256,1536]{1,2,0:T(8,128)(2,1)}, ...), condition=%wide.region_9.10_spmd, body=%wide.region_7.9_spmd.sunk | while | flops 1925251328 | bytes 43775740 | solution.py:134
  1529.9 215.9 %while.110 = (s32[]{:T(128)}, f32[4,256,1792]{2,1,0:T(8,128)}, bf16[4,256,24]{1,2,0:T(8,128)(2,1)}, bf16[4,3,1792]{2,1,0:T(4,128)(2,1)}, f32[4,4,1792]{2,1,0:T(4...) while((s32[]{:T(128)}, f32[4,256,1792]{2,1,0:T(8,128)}, ...), condition=%wide.region_38.39_spmd, body=%wide.region_24.38_spmd.sunk | while | flops 1232564224 | bytes 144974240 | solution.py:200
  1777.4 39.5 %reduce-scatter.6.cloned.1.call-done = bf16[192,3328]{1,0:T(8,128)(2,1)} async-done(((bf16[768,3328]{1,0:T(8,128)(2,1)}), bf16[192,3328]{1,0:T(8,128)(2,1)}) %reduce-scatter.6.cloned.1.call-update) | async-done | bytes 1277968 | tf_op jit(solution)/shard_map/reduce_scatter | solution.py:241
  1817.0 9.8 fusion.188
  1827.9 42.3 %all-reduce.13 = (f32[768]{0:T(1024)}, f32[4,1792]{1,0:T(4,128)}, f32[1792]{0:T(1024)}, f32[24]{0:T(128)}, f32[24]{0:T(128)}, /*index=5*/f32[24]{0:T(128)}, f32[1536]{0:T(1024)}) all-reduce(f32[768]{0:T(1024)S(1)} %get-tuple-element.1013, f32[4,1792]{1,0:T(4,128)S(1)} %reduce_sum.344, ...), channel_id=1, replica_groups=mesh['group'=4,'ctx'=8] {'group','ctx'}, use_global_device_ids=true, to_apply=%region_41.42 | all-reduce | flops 11336 | bytes 90688 | tf_op jit(solution)/shard_map/psum | solution.py:256
  1874.5 36.5 %psum.72 = bf16[192,24]{0,1:T(8,128)(2,1)S(1)} all-reduce(bf16[192,24]{0,1:T(8,128)(2,1)S(1)} %copy.132), channel_id=1, replica_groups=mesh['group'=4,'ctx'=8] {'ctx'}, use_global_device_ids=true, to_apply=%region_45.46 | all-reduce | flops 4608 | bytes 18432 | tf_op jit(solution)/shard_map/psum | solution.py:253
  1911.6 28.8 %all-reduce.17.cloned.1.call-done = (bf16[192,3328]{1,0:T(8,128)(2,1)}, bf16[384,768]{1,0:T(8,128)(2,1)}) async-done(((bf16[192,3328]{1,0:T(8,128)(2,1)}, bf16[384,768]{1,0:T(8,128)(2,1)}), (bf16[192,3328]{1,0:T(8,128)(2,1)}, bf16[384,768]{1,0:T(8,128)(2,1)})) %all-reduce.17.cloned.1.call-update) | async-done | bytes 1867792 | tf_op jit(solution)/shard_map/psum | solution.py:252
  (975 shorter events, 781.9 us)
Async XLA Ops:
  7.2 44.8 %all-gather.4.cloned.1.call-start = ((), (), s32[]{:S(2)}) async-start(), calls=%async_computation.3 | async-start | bytes 6389760 | tf_op jit(solution)/shard_map/all_gather | solution.py:97
  8.0 69.7 %all-gather.6.cloned.1.call-start = ((), (), s32[]{:S(2)}) async-start(), calls=%async_computation.4 | async-start | bytes 2949120 | tf_op jit(solution)/shard_map/all_gather | solution.py:99
  8.7 1768.7 %reduce-scatter.8.cloned.1.call-start = ((), (), s32[]{:S(2)}) async-start(), calls=%async_computation.6 | async-start | bytes 2949120 | tf_op jit(solution)/shard_map/reduce_scatter | solution.py:247
  16.9 60.8 %copy-start.66 = (f32[4,256]{1,0:T(4,128)}, f32[4,256]{1,0:T(4,128)S(1)}, u32[]{:S(2)}) copy-start(f32[4,256]{1,0:T(4,128)S(1)} %compare_convert_fusion) | copy-start | bytes 12292
  16.9 35.2 %copy-start.58 = (f32[4,256]{1,0:T(4,128)}, f32[4,256]{1,0:T(4,128)S(1)}, u32[]{:S(2)}) copy-start(f32[4,256]{1,0:T(4,128)S(1)} %fusion.206) | copy-start | bytes 12292
  17.5 60.2 %copy-start.39 = (bf16[4,256,768]{2,1,0:T(8,128)(2,1)S(1)}, bf16[4,256,768]{2,1,0:T(8,128)(2,1)}, u32[]{:S(2)}) copy-start(bf16[4,256,768]{2,1,0:T(8,128)(2,1)} %param.37) | copy-start | bytes 4718596
  65.1 34.3 %collective-permute-start.2 = (f32[4,3,1792]{2,1,0:T(4,128)S(1)}, f32[4,3,1792]{2,1,0:T(4,128)}, u32[]{:S(2)}, u32[]{:S(2)}) collective-permute-start(f32[4,3,1792]{2,1,0:T(4,128)S(1)} %slice.190), channel_id=1, source_target_pairs={{0,1},{1,2},{2,3},{3,4},{4,5},{5,6},{6,7},{8,9},{9,10},{10,11},{11... | collective-permute-start | bytes 258056 | tf_op jit(solution)/shard_map/ppermute | solution.py:22
  190.7 71.4 %collective-permute-start = (f32[4,24,64,128]{3,2,1,0:T(8,128)}, f32[4,24,64,128]{3,2,1,0:T(8,128)S(1)}, u32[]{:S(2)}, u32[]{:S(2)}) collective-permute-start(f32[4,24,64,128]{3,2,1,0:T(8,128)} %multiply_add_fusion.8), channel_id=1, source_target_pairs={{0,1},{1,2},{2,3},{3,4},{4,5},{5,6},{6,7},{8,9},{9,10},{10,11},{11... | collective-permute-start | bytes 9437192 | tf_op jit(solution)/shard_map/while/body/eval_jaxpr/ppermute | solution.py:22
  266.0 71.5 %collective-permute-start = (f32[4,24,64,128]{3,2,1,0:T(8,128)}, f32[4,24,64,128]{3,2,1,0:T(8,128)S(1)}, u32[]{:S(2)}, u32[]{:S(2)}) collective-permute-start(f32[4,24,64,128]{3,2,1,0:T(8,128)} %multiply_add_fusion.8), channel_id=1, source_target_pairs={{0,1},{1,2},{2,3},{3,4},{4,5},{5,6},{6,7},{8,9},{9,10},{10,11},{11... | collective-permute-start | bytes 9437192 | tf_op jit(solution)/shard_map/while/body/eval_jaxpr/ppermute | solution.py:22
  341.4 70.6 %collective-permute-start = (f32[4,24,64,128]{3,2,1,0:T(8,128)}, f32[4,24,64,128]{3,2,1,0:T(8,128)S(1)}, u32[]{:S(2)}, u32[]{:S(2)}) collective-permute-start(f32[4,24,64,128]{3,2,1,0:T(8,128)} %multiply_add_fusion.8), channel_id=1, source_target_pairs={{0,1},{1,2},{2,3},{3,4},{4,5},{5,6},{6,7},{8,9},{9,10},{10,11},{11... | collective-permute-start | bytes 9437192 | tf_op jit(solution)/shard_map/while/body/eval_jaxpr/ppermute | solution.py:22
  415.9 70.6 %collective-permute-start = (f32[4,24,64,128]{3,2,1,0:T(8,128)}, f32[4,24,64,128]{3,2,1,0:T(8,128)S(1)}, u32[]{:S(2)}, u32[]{:S(2)}) collective-permute-start(f32[4,24,64,128]{3,2,1,0:T(8,128)} %multiply_add_fusion.8), channel_id=1, source_target_pairs={{0,1},{1,2},{2,3},{3,4},{4,5},{5,6},{6,7},{8,9},{9,10},{10,11},{11... | collective-permute-start | bytes 9437192 | tf_op jit(solution)/shard_map/while/body/eval_jaxpr/ppermute | solution.py:22
  490.4 69.7 %collective-permute-start = (f32[4,24,64,128]{3,2,1,0:T(8,128)}, f32[4,24,64,128]{3,2,1,0:T(8,128)S(1)}, u32[]{:S(2)}, u32[]{:S(2)}) collective-permute-start(f32[4,24,64,128]{3,2,1,0:T(8,128)} %multiply_add_fusion.8), channel_id=1, source_target_pairs={{0,1},{1,2},{2,3},{3,4},{4,5},{5,6},{6,7},{8,9},{9,10},{10,11},{11... | collective-permute-start | bytes 9437192 | tf_op jit(solution)/shard_map/while/body/eval_jaxpr/ppermute | solution.py:22
  563.9 68.7 %collective-permute-start = (f32[4,24,64,128]{3,2,1,0:T(8,128)}, f32[4,24,64,128]{3,2,1,0:T(8,128)S(1)}, u32[]{:S(2)}, u32[]{:S(2)}) collective-permute-start(f32[4,24,64,128]{3,2,1,0:T(8,128)} %multiply_add_fusion.8), channel_id=1, source_target_pairs={{0,1},{1,2},{2,3},{3,4},{4,5},{5,6},{6,7},{8,9},{9,10},{10,11},{11... | collective-permute-start | bytes 9437192 | tf_op jit(solution)/shard_map/while/body/eval_jaxpr/ppermute | solution.py:22
  636.6 67.8 %collective-permute-start = (f32[4,24,64,128]{3,2,1,0:T(8,128)}, f32[4,24,64,128]{3,2,1,0:T(8,128)S(1)}, u32[]{:S(2)}, u32[]{:S(2)}) collective-permute-start(f32[4,24,64,128]{3,2,1,0:T(8,128)} %multiply_add_fusion.8), channel_id=1, source_target_pairs={{0,1},{1,2},{2,3},{3,4},{4,5},{5,6},{6,7},{8,9},{9,10},{10,11},{11... | collective-permute-start | bytes 9437192 | tf_op jit(solution)/shard_map/while/body/eval_jaxpr/ppermute | solution.py:22
  713.9 12.6 copy-start.6
  715.5 21.7 %copy-start.23 = (f32[256,256]{1,0:T(8,128)}, f32[256,256]{1,0:T(8,128)S(1)}, u32[]{:S(2)}) copy-start(f32[256,256]{1,0:T(8,128)S(1)} %fusion.294) | copy-start | bytes 786436 | tf_op jit(solution)/shard_map/while
  779.8 21.8 %copy-start.23 = (f32[256,256]{1,0:T(8,128)}, f32[256,256]{1,0:T(8,128)S(1)}, u32[]{:S(2)}) copy-start(f32[256,256]{1,0:T(8,128)S(1)} %fusion.294) | copy-start | bytes 786436 | tf_op jit(solution)/shard_map/while
  844.2 21.9 %copy-start.23 = (f32[256,256]{1,0:T(8,128)}, f32[256,256]{1,0:T(8,128)S(1)}, u32[]{:S(2)}) copy-start(f32[256,256]{1,0:T(8,128)S(1)} %fusion.294) | copy-start | bytes 786436 | tf_op jit(solution)/shard_map/while
  908.7 21.6 %copy-start.23 = (f32[256,256]{1,0:T(8,128)}, f32[256,256]{1,0:T(8,128)S(1)}, u32[]{:S(2)}) copy-start(f32[256,256]{1,0:T(8,128)S(1)} %fusion.294) | copy-start | bytes 786436 | tf_op jit(solution)/shard_map/while
  977.7 67.5 %collective-permute-start.1 = (f32[4,24,64,128]{3,2,1,0:T(8,128)}, f32[4,24,64,128]{3,2,1,0:T(8,128)S(1)}, u32[]{:S(2)}, u32[]{:S(2)}) collective-permute-start(f32[4,24,64,128]{3,2,1,0:T(8,128)} %multiply_add_fusion.9), channel_id=1, source_target_pairs={{1,0},{2,1},{3,2},{4,3},{5,4},{6,5},{7,6},{9,8},{10,9},{11,10},{12... | collective-permute-start | bytes 9437192 | tf_op jit(solution)/shard_map/while/body/eval_jaxpr/ppermute | solution.py:22
  1049.3 66.9 %collective-permute-start.1 = (f32[4,24,64,128]{3,2,1,0:T(8,128)}, f32[4,24,64,128]{3,2,1,0:T(8,128)S(1)}, u32[]{:S(2)}, u32[]{:S(2)}) collective-permute-start(f32[4,24,64,128]{3,2,1,0:T(8,128)} %multiply_add_fusion.9), channel_id=1, source_target_pairs={{1,0},{2,1},{3,2},{4,3},{5,4},{6,5},{7,6},{9,8},{10,9},{11,10},{12... | collective-permute-start | bytes 9437192 | tf_op jit(solution)/shard_map/while/body/eval_jaxpr/ppermute | solution.py:22
  1120.1 65.3 %collective-permute-start.1 = (f32[4,24,64,128]{3,2,1,0:T(8,128)}, f32[4,24,64,128]{3,2,1,0:T(8,128)S(1)}, u32[]{:S(2)}, u32[]{:S(2)}) collective-permute-start(f32[4,24,64,128]{3,2,1,0:T(8,128)} %multiply_add_fusion.9), channel_id=1, source_target_pairs={{1,0},{2,1},{3,2},{4,3},{5,4},{6,5},{7,6},{9,8},{10,9},{11,10},{12... | collective-permute-start | bytes 9437192 | tf_op jit(solution)/shard_map/while/body/eval_jaxpr/ppermute | solution.py:22
  1189.4 64.4 %collective-permute-start.1 = (f32[4,24,64,128]{3,2,1,0:T(8,128)}, f32[4,24,64,128]{3,2,1,0:T(8,128)S(1)}, u32[]{:S(2)}, u32[]{:S(2)}) collective-permute-start(f32[4,24,64,128]{3,2,1,0:T(8,128)} %multiply_add_fusion.9), channel_id=1, source_target_pairs={{1,0},{2,1},{3,2},{4,3},{5,4},{6,5},{7,6},{9,8},{10,9},{11,10},{12... | collective-permute-start | bytes 9437192 | tf_op jit(solution)/shard_map/while/body/eval_jaxpr/ppermute | solution.py:22
  1257.8 64.3 %collective-permute-start.1 = (f32[4,24,64,128]{3,2,1,0:T(8,128)}, f32[4,24,64,128]{3,2,1,0:T(8,128)S(1)}, u32[]{:S(2)}, u32[]{:S(2)}) collective-permute-start(f32[4,24,64,128]{3,2,1,0:T(8,128)} %multiply_add_fusion.9), channel_id=1, source_target_pairs={{1,0},{2,1},{3,2},{4,3},{5,4},{6,5},{7,6},{9,8},{10,9},{11,10},{12... | collective-permute-start | bytes 9437192 | tf_op jit(solution)/shard_map/while/body/eval_jaxpr/ppermute | solution.py:22
  1326.1 64.3 %collective-permute-start.1 = (f32[4,24,64,128]{3,2,1,0:T(8,128)}, f32[4,24,64,128]{3,2,1,0:T(8,128)S(1)}, u32[]{:S(2)}, u32[]{:S(2)}) collective-permute-start(f32[4,24,64,128]{3,2,1,0:T(8,128)} %multiply_add_fusion.9), channel_id=1, source_target_pairs={{1,0},{2,1},{3,2},{4,3},{5,4},{6,5},{7,6},{9,8},{10,9},{11,10},{12... | collective-permute-start | bytes 9437192 | tf_op jit(solution)/shard_map/while/body/eval_jaxpr/ppermute | solution.py:22
  1394.4 61.8 %collective-permute-start.1 = (f32[4,24,64,128]{3,2,1,0:T(8,128)}, f32[4,24,64,128]{3,2,1,0:T(8,128)S(1)}, u32[]{:S(2)}, u32[]{:S(2)}) collective-permute-start(f32[4,24,64,128]{3,2,1,0:T(8,128)} %multiply_add_fusion.9), channel_id=1, source_target_pairs={{1,0},{2,1},{3,2},{4,3},{5,4},{6,5},{7,6},{9,8},{10,9},{11,10},{12... | collective-permute-start | bytes 9437192 | tf_op jit(solution)/shard_map/while/body/eval_jaxpr/ppermute | solution.py:22
  1458.4 63.7 %copy-start.67 = (f32[4,256]{1,0:T(4,128)S(1)}, f32[4,256]{1,0:T(4,128)}, u32[]{:S(2)}) copy-start(f32[4,256]{1,0:T(4,128)} %copy-done.66) | copy-start | bytes 12292
  1528.7 288.2 %reduce-scatter.6.cloned.1.call-start = ((), (), s32[]{:S(2)}) async-start(), calls=%async_computation.5 | async-start | bytes 6389760 | tf_op jit(solution)/shard_map/reduce_scatter | solution.py:241
  1745.8 7.1 collective-permute-start.3
  1766.0 107.7 %reduce-scatter.10.cloned.1.call-start = ((), (), s32[]{:S(2)}) async-start(), calls=%async_computation.7 | async-start | bytes 245760
  1768.2 172.2 %all-reduce.17.cloned.1.call-start = ((), (), s32[]{:S(2)}) async-start(), calls=%async_computation.8 | async-start | bytes 3735552 | tf_op jit(solution)/shard_map/psum | solution.py:252
  1826.8 43.4 %copy-start.61 = (f32[4,256]{1,0:T(4,128)S(1)}, f32[4,256]{1,0:T(4,128)}, u32[]{:S(2)}) copy-start(f32[4,256]{1,0:T(4,128)} %copy-done.60) | copy-start | bytes 12292
  (216 other events, 933.7 us)
Sparse Core Ops, SparseCore 0:
  9.6 42.3 all-gather.3
  53.6 24.0 all-gather.5
  1528.8 33.2 reduce-scatter.7
  1766.1 50.8 reduce-scatter.5
  1819.8 19.7 reduce-scatter.9
  1843.1 97.3 all-reduce.16
where the time goes:
time: 1960 us; the launch traced here: 1950 us
  waiting for transfers between devices  1020 us (52%)
  matrix products  308 us (16%)
  local copies, waits for them, and re-layouts  258 us (13%)
  other arithmetic  217 us (11%)
  blocking collectives  84.9 us (4%)
  starting transfers between devices  49.1 us (3%)
    ppermute x16, waiting for transfers between devices, passed_along(): lax.ppermute(value, axis, [(source, source + steps) for source in range(l...  904 us
    dot_general x16, matrix products, finish(): jnp.einsum('hts,shp->thp', decays * scores[None], scaled, precision=lax.P...  139 us
    dot_general x16, matrix products, finish(): jnp.einsum('tn,hpn->thp', read_c, state_in, precision=lax.Precision.HIGHEST)  53.1 us
    ppermute x16, starting transfers between devices, passed_along(): lax.ppermute(value, axis, [(source, source + steps) for source in range(l...  48.8 us
    psum x1, blocking collectives, local(): lax.psum((grad_gain, jnp.sum(front_grads[3], 0), jnp.sum(front_grads[4],...  42.3 us
    dot_general x12, matrix products, block_states(): jnp.einsum('qhp,qn->hpn', weighted, write_b, precision=lax.Precision.HIGH...  42.1 us
    reduce_scatter x1, waiting for transfers between devices, local(): lax.psum_scatter(grad_zx_full.astype(jnp.bfloat16), 'group', scatter_dime...  39.5 us
  transfers between devices with their start and end apart: 22, of which 19 were waited for; matrix products, arithmetic and copies ran while one was open for 14% of the time, Pallas kernels for 0%

commit v1 on v0

v1 whole, which is shorter than its diff:
```python
import jax
import jax.numpy as jnp
from jax import lax
from jax.experimental import pallas as pl
from jax.experimental.pallas import tpu as pltpu
from jax.sharding import PartitionSpec as P

D = 768
HEADS = 24
HEADDIM = 64
NSTATE = 128
KCONV = 4
SPAN = 256
DIN = 1536
CONVW = 1792
ZXW = 3328
RIM = 16
HALF = 128
TILE = 256
PAIRS = 12
EPS = 1e-05

f32 = jnp.float32
bf16 = jnp.bfloat16
NT = (((1,), (1,)), ((), ()))
TN = (((0,), (0,)), ((), ()))
VMEM_LIMIT = 62 * 1024 * 1024


def mm(a, b):
    return jnp.dot(a, b, preferred_element_type=f32)


def mm_nt(a, b):
    return lax.dot_general(a, b, NT, preferred_element_type=f32)


def mm_tn(a, b):
    return lax.dot_general(a, b, TN, preferred_element_type=f32)


def halves(v):
    high = v.astype(bf16)
    return high, (v - high.astype(f32)).astype(bf16)


def head_map():
    rows = lax.broadcasted_iota(jnp.int32, (2 * HALF, DIN), 0) % HALF
    cols = lax.broadcasted_iota(jnp.int32, (2 * HALF, DIN), 1) // HEADDIM
    return jnp.where(rows == cols, 1.0, 0.0).astype(bf16)


def spread(v, sel):
    return mm(jnp.concatenate(halves(v), axis=1), sel[...])


def gather_heads(v, sel_part):
    high, low = halves(v)
    return mm_nt(high, sel_part) + mm_nt(low, sel_part)


def triangle(size, lower):
    rows = lax.broadcasted_iota(jnp.int32, (size, size), 0)
    cols = lax.broadcasted_iota(jnp.int32, (size, size), 1)
    keep = rows >= cols if lower else rows <= cols
    return jnp.where(keep, 1.0, 0.0).astype(f32)


def exact_mm(a, b):
    return jnp.dot(a, b, precision=lax.Precision.HIGHEST, preferred_element_type=f32)


def softplus(v):
    return jnp.maximum(v, 0.0) + jnp.log1p(jnp.exp(-jnp.abs(v)))


def sigmoid(v):
    return 1.0 / (1.0 + jnp.exp(-v))


def local_decays(cum):
    mid, end = cum[HALF - 1 : HALF], cum[SPAN - 1 : SPAN]
    rows = lax.broadcasted_iota(jnp.int32, (SPAN, 1), 0)
    first = rows < HALF
    start = jnp.where(first, 0.0, mid)
    stop = jnp.where(first, mid, end)
    return jnp.exp(cum - start), jnp.exp(stop - cum), jnp.exp(mid), jnp.exp(end - mid), jnp.exp(end)


def rows_of(v):
    return jnp.broadcast_to(v, (8, v.shape[1]))


def normalized(rows, gain):
    rows = rows.astype(f32)
    inv = lax.rsqrt(jnp.mean(rows * rows, axis=-1, keepdims=True) + EPS)
    return rows, inv, (rows * inv * gain).astype(bf16)


def first_kernel(
    tok, halo, gain, wzx, wdl, cw, cb, db, dl,
    normed, nhalo, cin, act, gate, vout, cumout, st0, loc, tdec,
    sel, ext, fexp,
):
    @pl.when(pl.program_id(0) == 0)
    def _():
        sel[...] = head_map()

    nh = normalized(halo[0], gain[...])[2]
    nm = normalized(tok[0], gain[...])[2]
    ext[0:RIM] = nh
    ext[RIM:] = nm
    nhalo[0] = nh
    normed[0] = nm
    v = mm(nm, wdl[...]) + db[...]
    vout[0] = v
    dt = softplus(v)
    cum = exact_mm(triangle(SPAN, True), -jnp.exp(dl[...]) * dt)
    cumout[0] = cum
    e_in, e_out, tot0, tot1, total = local_decays(cum)
    fexp[...] = spread(dt * e_out, sel)
    tot1x = spread(rows_of(tot1), sel)[0:1]
    tdec[0] = spread(rows_of(total), sel)[0:1]

    def conv_tile(c):
        cols = pl.ds(c, TILE)
        cin[0, :, cols] = mm(ext[...], wzx[:, pl.ds(DIN + c, TILE)])
        o = cb[:, cols]
        for k in range(KCONV):
            o = o + cw[k : k + 1, cols] * cin[0, RIM - KCONV + 1 + k : RIM - KCONV + 1 + k + SPAN, cols]
        a = o * sigmoid(o)
        act[0, :, cols] = a
        return a

    bc = conv_tile(DIN)
    bt = jnp.transpose(bc[:, :NSTATE]).astype(bf16)

    for j in range(DIN // TILE):
        c = j * TILE
        cols = pl.ds(c, TILE)
        a = conv_tile(c)
        xw = (a * fexp[:, cols]).astype(bf16)
        s0 = mm(bt[:, :HALF], xw[:HALF])
        s1 = mm(bt[:, HALF:], xw[HALF:])
        st0[0, :, cols] = s0
        loc[0, :, cols] = (tot1x[:, c : c + TILE] * s0 + s1).astype(bf16)
    for j in range(DIN // TILE):
        gate[0, :, j * TILE : (j + 1) * TILE] = mm(ext[RIM:], wzx[:, j * TILE : (j + 1) * TILE])


def pair_decays(cum, cum_t, p, causal):
    rolled = pltpu.roll(cum, lax.rem(HALF - 2 * p, HALF), 1)
    out = []
    for q in range(2):
        rows = slice(q * HALF, (q + 1) * HALF)
        for a in range(2):
            gaps = rolled[rows, a : a + 1] - cum_t[q, pl.ds(2 * p + a, 1), :]
            out.append(jnp.exp(jnp.where(causal, gaps, -jnp.inf)))
    return out


def second_kernel(
    rel, tok, cot, act, gate, vin, cumin, st0, sin, wout, skip, ggain,
    mixed, mlow, dyout, ggate, wred, dirout, dir1, dcs, gskip, gggain, sin1out,
    sel, cum_t, dtx, einx, ys, gs, ss, s_in, dcacc,
):
    s = pl.program_id(0)

    @pl.when(s == 0)
    def _():
        sel[...] = head_map()
        gskip[...] = jnp.zeros_like(gskip)
        gggain[...] = jnp.zeros_like(gggain)

    causal = lax.broadcasted_iota(jnp.int32, (HALF, HALF), 0) >= lax.broadcasted_iota(jnp.int32, (HALF, HALF), 1)
    low_lanes = lax.broadcasted_iota(jnp.int32, (HALF, HALF), 1) < HEADDIM
    cum = cumin[0]
    dt = softplus(vin[0])
    e_in, e_out, tot0, tot1, total = local_decays(cum)
    cum_t[0] = jnp.transpose(cum[:HALF])
    cum_t[1] = jnp.transpose(cum[HALF:])
    dtx[...] = spread(dt, sel)
    einx[...] = spread(e_in, sel)
    tot0x = spread(rows_of(tot0), sel)[0:1]
    s_in[0] = sin[0]
    s_in[1] = (tot0x * sin[0].astype(f32) + st0[0]).astype(bf16)
    sin1out[0] = s_in[1]
    bb = act[0, :, DIN : DIN + NSTATE].astype(bf16)
    cc = act[0, :, DIN + NSTATE :].astype(bf16)
    scores = [mm_nt(cc[q * HALF : (q + 1) * HALF], bb[q * HALF : (q + 1) * HALF]) for q in range(2)]

    def pair_step(p, _):
        cols = pl.ds(pl.multiple_of(p * HALF, HALF), HALF)
        decays = pair_decays(cum, cum_t, p, causal)
        for q in range(2):
            rows = slice(q * HALF, (q + 1) * HALF)
            m = jnp.concatenate([(decays[2 * q + a] * scores[q]).astype(bf16) for a in range(2)], axis=1)
            x = act[0, rows, cols]
            xs = x * dtx[rows, cols]
            xs = jnp.concatenate([jnp.where(low_lanes, xs, 0.0), jnp.where(low_lanes, 0.0, xs)], axis=0)
            yn = mm(m, xs.astype(bf16)) + einx[rows, cols] * mm(cc[rows], s_in[q, :, cols])
            ys[rows, cols] = yn + skip[:, cols] * x
        return 0

    lax.fori_loop(0, PAIRS, pair_step, 0)

    def gate_step(j, total_sq):
        cols = pl.ds(pl.multiple_of(j * HALF, HALF), HALF)
        g = gate[0, :, cols]
        gated = ys[:, cols] * (g * sigmoid(g))
        gs[:, cols] = gated
        return total_sq + gated * gated

    sq = lax.fori_loop(0, PAIRS, gate_step, jnp.zeros((SPAN, HALF), f32))
    inv = lax.rsqrt(jnp.sum(sq, axis=1, keepdims=True) * (1.0 / DIN) + EPS)

    def low_step(j, _):
        cols = pl.ds(pl.multiple_of(j * HALF, HALF), HALF)
        mlow[0, :, cols] = (gs[:, cols] * inv * ggain[:, cols]).astype(bf16)
        return 0

    lax.fori_loop(0, PAIRS, low_step, 0)
    live = (lax.broadcasted_iota(jnp.int32, (SPAN, 1), 0) < rel[s]).astype(f32)
    for j in range(D // TILE):
        cols = slice(j * TILE, (j + 1) * TILE)
        mixed[0, :, cols] = (live * (tok[0, :, cols].astype(f32) + mm(mlow[0], wout[:, cols]))).astype(bf16)
    drive = (live * cot[0].astype(f32)).astype(bf16)

    def back_step(j, acc):
        cols = pl.ds(pl.multiple_of(j * TILE, TILE), TILE)
        gm = mm_nt(drive, wout[cols, :])
        gated = gs[:, cols]
        gggain[:, cols] += jnp.sum(gm * (gated * inv), axis=0, keepdims=True)
        scaled = gm * ggain[:, cols]
        ss[:, cols] = scaled
        prod = scaled * gated
        return acc + prod[:, :HALF] + prod[:, HALF:]

    dots = lax.fori_loop(0, DIN // TILE, back_step, jnp.zeros((SPAN, HALF), f32))
    dots = jnp.sum(dots, axis=1, keepdims=True) * (1.0 / DIN)
    corr = inv * inv * inv * dots
    cct = jnp.transpose(act[0, :, DIN + NSTATE :]).astype(bf16)
    tot0_rows = tot0x
    dcacc[...] = jnp.zeros_like(dcacc)
    wred[0] = jnp.zeros((SPAN, HALF), f32)
    for j in range(DIN // TILE):
        cols = slice(j * TILE, (j + 1) * TILE)
        g = gate[0, :, cols]
        sg = sigmoid(g)
        sl = g * sg
        grad_gated = inv * ss[:, cols] - gs[:, cols] * corr
        dy = grad_gated * sl
        y = ys[:, cols]
        ggate[0, :, cols] = (grad_gated * y * (sg + sl * (1.0 - sg))).astype(bf16)
        dyout[0, :, cols] = dy.astype(bf16)
        x = act[0, :, cols]
        gskip[:, cols] += jnp.sum(dy * x, axis=0, keepdims=True)
        wred[0] += gather_heads(dy * (y - skip[:, cols] * x), sel[:HALF, cols])
        dye = (dy * einx[:, cols]).astype(bf16)
        d0 = mm(cct[:, :HALF], dye[:HALF])
        d1 = mm(cct[:, HALF:], dye[HALF:])
        dir1[0, :, cols] = d1
        dirout[0, :, cols] = (d0 + tot0_rows[:, cols] * d1).astype(bf16)
        dcacc[:HALF] += mm_nt(dye[:HALF], s_in[0, :, cols])
        dcacc[HALF:] += mm_nt(dye[HALF:], s_in[1, :, cols])
    dcs[0] = dcacc[...]


def third_kernel(
    cin, vin, cumin, dyin, wred, dcs, dir1, later, sin, loc, cw, cb, dl, skip, skip_rows,
    gz, gzh, gdelta, gcw, gcb, gdb, gdl,
    sel, cum_t, dtx, eoutx, xx, sp, dact, xwb, g_s, dg_s, dout, qacc, gp,
):
    s = pl.program_id(0)

    @pl.when(s == 0)
    def _():
        sel[...] = head_map()
        gcw[...] = jnp.zeros_like(gcw)
        gcb[...] = jnp.zeros_like(gcb)
        gdb[...] = jnp.zeros_like(gdb)
        gdl[...] = jnp.zeros_like(gdl)
        gp[0:RIM] = jnp.zeros((RIM, CONVW), f32)
        gp[RIM + SPAN :] = jnp.zeros((8, CONVW), f32)

    causal = lax.broadcasted_iota(jnp.int32, (HALF, HALF), 0) >= lax.broadcasted_iota(jnp.int32, (HALF, HALF), 1)
    low_lanes = lax.broadcasted_iota(jnp.int32, (HALF, HALF), 1) < HEADDIM
    cum = cumin[0]
    v = vin[0]
    dt = softplus(v)
    e_in, e_out, tot0, tot1, total = local_decays(cum)
    cum_t[0] = jnp.transpose(cum[:HALF])
    cum_t[1] = jnp.transpose(cum[HALF:])
    dtx[...] = spread(dt, sel)
    eoutx[...] = spread(e_out, sel)
    tot1x = spread(rows_of(tot1), sel)[0:1]
    totalx = spread(rows_of(total), sel)[0:1]

    def conv_step(j, _):
        cols = pl.ds(pl.multiple_of(j * HALF, HALF), HALF)
        o = cb[:, cols]
        for k in range(KCONV):
            o = o + cw[k : k + 1, cols] * cin[0, RIM - KCONV + 1 + k : RIM - KCONV + 1 + k + SPAN, cols]
        sg = sigmoid(o)
        a = o * sg
        xx[:, cols] = a
        sp[:, cols] = sg + a * (1.0 - sg)
        return 0

    lax.fori_loop(0, CONVW // HALF, conv_step, 0)
    bb = xx[:, DIN : DIN + NSTATE].astype(bf16)
    cc = xx[:, DIN + NSTATE :].astype(bf16)
    for q in range(2):
        rows = slice(q * HALF, (q + 1) * HALF)
        g_s[q] = mm_nt(cc[rows], bb[rows])
    dg_s[...] = jnp.zeros_like(dg_s)
    qacc[...] = jnp.zeros_like(qacc)
    dout[1] = later[0]
    dout[0] = (dir1[0] + tot1x * later[0].astype(f32)).astype(bf16)

    def pair_step(p, _):
        cols = pl.ds(pl.multiple_of(p * HALF, HALF), HALF)
        decays = pair_decays(cum, cum_t, p, causal)
        for q in range(2):
            rows = slice(q * HALF, (q + 1) * HALF)
            x = xx[rows, cols]
            dte = dtx[rows, cols]
            eo = eoutx[rows, cols]
            xs = x * dte
            xsb = xs.astype(bf16)
            dyb = dyin[0, rows, cols]
            dyf = dyb.astype(f32)
            dxs = []
            for a in range(2):
                m = (decays[2 * q + a] * g_s[q]).astype(bf16)
                dxs.append(mm_tn(m, dyb))
                mine = low_lanes if a == 0 else jnp.logical_not(low_lanes)
                dm = mm_nt(jnp.where(mine, dyf, 0.0).astype(bf16), xsb)
                dg_s[q] += dm * decays[2 * q + a]
            dx_s = jnp.where(low_lanes, dxs[0], dxs[1]) + eo * mm(bb[rows], dout[q, :, cols])
            dact[rows, cols] = dte * dx_s + skip[:, cols] * dyf
            qacc[rows] += gather_heads(x * dx_s, sel[:HALF, cols])
            xwb[rows, cols] = (xs * eo).astype(bf16)
        return 0

    lax.fori_loop(0, PAIRS, pair_step, 0)
    for q in range(2):
        rows = slice(q * HALF, (q + 1) * HALF)
        dg = dg_s[q].astype(bf16)
        dact[rows, DIN : DIN + NSTATE] = mm_tn(dg, cc[rows]) + mm_nt(xwb[rows, :], dout[q])
        dact[rows, DIN + NSTATE :] = mm(dg, bb[rows]) + dcs[0, rows]

    ends = jnp.sum(later[0].astype(f32) * (totalx * sin[0].astype(f32) + loc[0].astype(f32)), axis=0, keepdims=True)
    ends = gather_heads(rows_of(ends), sel[:HALF])[0:1]
    at_end = lax.broadcasted_iota(jnp.int32, (SPAN, 1), 0) == SPAN - 1
    dcum = wred[0] - dt * qacc[...] + jnp.where(at_end, ends, 0.0)
    glog = exact_mm(triangle(SPAN, False), dcum)
    rate = jnp.exp(dl[...])
    gpd = (qacc[...] - rate * glog) * sigmoid(v)
    lanes = lax.broadcasted_iota(jnp.int32, (SPAN, HALF), 1) < HEADS
    gpd = jnp.where(lanes, gpd, 0.0)
    gdelta[0] = gpd.astype(bf16)
    gdb[...] += jnp.sum(gpd, axis=0, keepdims=True)
    gdl[...] += -rate * jnp.sum(dt * glog, axis=0, keepdims=True)

    def out_step(j, _):
        cols = pl.ds(pl.multiple_of(j * HALF, HALF), HALF)
        gco = dact[:, cols] * sp[:, cols]
        gp[RIM : RIM + SPAN, cols] = gco
        gcb[:, cols] += jnp.sum(gco, axis=0, keepdims=True)
        for k in range(KCONV):
            gcw[k : k + 1, cols] += jnp.sum(
                gco * cin[0, RIM - KCONV + 1 + k : RIM - KCONV + 1 + k + SPAN, cols], axis=0, keepdims=True
            )
        main = jnp.zeros((SPAN, HALF), f32)
        rim = jnp.zeros((RIM, HALF), f32)
        for k in range(KCONV):
            ahead = KCONV - 1 - k
            main = main + cw[k : k + 1, cols] * gp[RIM + ahead : RIM + ahead + SPAN, cols]
            rim = rim + cw[k : k + 1, cols] * gp[ahead : ahead + RIM, cols]
        gz[0, :, cols] = main.astype(bf16)
        gzh[0, :, cols] = rim.astype(bf16)
        return 0

    lax.fori_loop(0, CONVW // HALF, out_step, 0)


def fourth_kernel(
    rel, tok, halo, cot, gain, ggate, gz, gzh, gdelta, wzx, wdl,
    gtok, gtail, grim, ggain,
):
    s = pl.program_id(0)

    @pl.when(s == 0)
    def _():
        ggain[...] = jnp.zeros_like(ggain)

    def back(rows, grad):
        rows, inv, _ = normalized(rows, gain[...])
        ggain[...] += jnp.sum(grad * rows * inv, axis=0, keepdims=True)
        gained = gain[...] * grad
        mean = jnp.mean(gained * rows, axis=-1, keepdims=True)
        return inv * gained - rows * (inv * inv * inv * mean)

    grad = mm_nt(ggate[0], wzx[:, :DIN]) + mm_nt(gz[0], wzx[:, DIN:]) + mm_nt(gdelta[0], wdl[...])
    live = (lax.broadcasted_iota(jnp.int32, (SPAN, 1), 0) < rel[s]).astype(f32)
    out = live * cot[0].astype(f32) + back(tok[0], grad)
    gtok[0] = out.astype(bf16)
    gtail[0] = out[SPAN - RIM :]
    grim[0] = back(halo[0], mm_nt(gzh[0], wzx[:, DIN:])).astype(bf16)


def whole(shape):
    zeros = (0,) * len(shape)
    return pl.BlockSpec(shape, lambda s: zeros, pipeline_mode=pl.Buffered(1))


def summed(shape):
    zeros = (0,) * len(shape)
    return pl.BlockSpec(shape, lambda s: zeros)


def per_seq(*shape):
    zeros = (0,) * len(shape)
    return pl.BlockSpec((1,) + shape, lambda s: (s,) + zeros)


SMEM = pl.BlockSpec(memory_space=pltpu.SMEM)


def call(kernel, seqs, in_specs, outs, scratch, name, flops=0):
    params = pltpu.CompilerParams(vmem_limit_bytes=VMEM_LIMIT)
    return pl.pallas_call(
        kernel,
        grid=(seqs,),
        in_specs=in_specs,
        out_specs=[o[0] for o in outs],
        out_shape=[jax.ShapeDtypeStruct(o[1], o[2]) for o in outs],
        scratch_shapes=[pltpu.VMEM(*sc) for sc in scratch],
        compiler_params=params,
        name=name,
    )


def state_scan(local, decay, count, reverse):
    seqs = local.shape[0]
    part = NSTATE // count
    moved = local.reshape(seqs, count, part, DIN).transpose(1, 0, 2, 3)
    moved = lax.all_to_all(moved, "ctx", 0, 0, tiled=True)
    decays = lax.all_gather(decay, "ctx", axis=0)
    order = range(count - 1, -1, -1) if reverse else range(count)
    carry = jnp.zeros((seqs, part, DIN), f32)
    found = [None] * count
    for b in order:
        found[b] = carry
        carry = decays[b] * carry + moved[b].astype(f32)
    back = jnp.stack(found).astype(bf16)
    back = lax.all_to_all(back, "ctx", 0, 0, tiled=True)
    return back.transpose(1, 0, 2, 3).reshape(seqs, NSTATE, DIN)


def passed_along(value, axis, steps):
    count = lax.axis_size(axis)
    leading, last = (max(0, -steps), min(count, count - steps))
    return lax.ppermute(value, axis, [(source, source + steps) for source in range(leading, last)])


def lanes_of(v):
    return jnp.pad(v[None, :], ((0, 0), (0, HALF - v.shape[0])))


def local(
    tokens_in, seq_lengths, norm_gain, w_zx, w_delta, w_out, conv_weight, conv_bias,
    delta_bias, decay_log, skip_gain, gated_gain, cotangent,
):
    seqs = tokens_in.shape[0]
    count = lax.axis_size("ctx")
    full_zx = lax.all_gather(w_zx, "group", axis=0, tiled=True)
    full_delta = lax.all_gather(w_delta, "group", axis=0, tiled=True)
    full_out = lax.all_gather(w_out, "group", axis=0, tiled=True)
    full_delta = jnp.pad(full_delta, ((0, 0), (0, HALF - HEADS)))
    rel = seq_lengths - lax.axis_index("ctx") * SPAN
    halo = passed_along(tokens_in[:, SPAN - RIM :, :], "ctx", 1)
    gain = norm_gain[None, :]
    cb = conv_bias[None, :]
    db = lanes_of(delta_bias)
    dl = lanes_of(decay_log)
    skip = jnp.repeat(skip_gain, HEADDIM)[None, :]
    ggain = gated_gain[None, :]

    normed, nhalo, cin, act, gate, vraw, cum, st0, loc, tdec = call(
        first_kernel,
        seqs,
        [per_seq(SPAN, D), per_seq(RIM, D), whole((1, D)), whole((D, ZXW)), whole((D, HALF)), whole((KCONV, CONVW)),
         whole((1, CONVW)), whole((1, HALF)), whole((1, HALF))],
        [
            (per_seq(SPAN, D), (seqs, SPAN, D), bf16),
            (per_seq(RIM, D), (seqs, RIM, D), bf16),
            (per_seq(RIM + SPAN, CONVW), (seqs, RIM + SPAN, CONVW), f32),
            (per_seq(SPAN, CONVW), (seqs, SPAN, CONVW), f32),
            (per_seq(SPAN, DIN), (seqs, SPAN, DIN), f32),
            (per_seq(SPAN, HALF), (seqs, SPAN, HALF), f32),
            (per_seq(SPAN, HALF), (seqs, SPAN, HALF), f32),
            (per_seq(NSTATE, DIN), (seqs, NSTATE, DIN), f32),
            (per_seq(NSTATE, DIN), (seqs, NSTATE, DIN), bf16),
            (per_seq(1, DIN), (seqs, 1, DIN), f32),
        ],
        [((2 * HALF, DIN), bf16), ((RIM + SPAN, D), bf16), ((SPAN, DIN), f32)],
        "first",
    )(tokens_in, halo, gain, full_zx, full_delta, conv_weight, cb, db, dl)

    state_in = state_scan(loc, tdec, count, False)

    mixed_out, mlow, dy, ggate, wred, direct, dir1, dcs, gskip, gggain, sin1 = call(
        second_kernel,
        seqs,
        [SMEM, per_seq(SPAN, D), per_seq(SPAN, D), per_seq(SPAN, CONVW), per_seq(SPAN, DIN), per_seq(SPAN, HALF),
         per_seq(SPAN, HALF), per_seq(NSTATE, DIN), per_seq(NSTATE, DIN), whole((DIN, D)), whole((1, DIN)), whole((1, DIN))],
        [
            (per_seq(SPAN, D), (seqs, SPAN, D), bf16),
            (per_seq(SPAN, DIN), (seqs, SPAN, DIN), bf16),
            (per_seq(SPAN, DIN), (seqs, SPAN, DIN), bf16),
            (per_seq(SPAN, DIN), (seqs, SPAN, DIN), bf16),
            (per_seq(SPAN, HALF), (seqs, SPAN, HALF), f32),
            (per_seq(NSTATE, DIN), (seqs, NSTATE, DIN), bf16),
            (per_seq(NSTATE, DIN), (seqs, NSTATE, DIN), f32),
            (per_seq(SPAN, HALF), (seqs, SPAN, HALF), f32),
            (summed((1, DIN)), (1, DIN), f32),
            (summed((1, DIN)), (1, DIN), f32),
            (per_seq(NSTATE, DIN), (seqs, NSTATE, DIN), bf16),
        ],
        [((2 * HALF, DIN), bf16), ((2, HALF, HALF), f32), ((SPAN, DIN), f32), ((SPAN, DIN), f32), ((SPAN, DIN), f32),
         ((SPAN, DIN), f32), ((SPAN, DIN), f32), ((2, NSTATE, DIN), bf16), ((SPAN, HALF), f32)],
        "second",
    )(rel, tokens_in, cotangent, act, gate, vraw, cum, st0, state_in, full_out, skip, ggain)

    later = state_scan(direct, tdec, count, True)

    gz, gzh, gdelta, gcw, gcb, gdb, gdl = call(
        third_kernel,
        seqs,
        [per_seq(RIM + SPAN, CONVW), per_seq(SPAN, HALF), per_seq(SPAN, HALF), per_seq(SPAN, DIN), per_seq(SPAN, HALF),
         per_seq(SPAN, HALF), per_seq(NSTATE, DIN), per_seq(NSTATE, DIN), per_seq(NSTATE, DIN), per_seq(NSTATE, DIN),
         whole((KCONV, CONVW)), whole((1, CONVW)), whole((1, HALF)), whole((1, DIN)), whole((1, HALF))],
        [
            (per_seq(SPAN, CONVW), (seqs, SPAN, CONVW), bf16),
            (per_seq(RIM, CONVW), (seqs, RIM, CONVW), bf16),
            (per_seq(SPAN, HALF), (seqs, SPAN, HALF), bf16),
            (summed((KCONV, CONVW)), (KCONV, CONVW), f32),
            (summed((1, CONVW)), (1, CONVW), f32),
            (summed((1, HALF)), (1, HALF), f32),
            (summed((1, HALF)), (1, HALF), f32),
        ],
        [((2 * HALF, DIN), bf16), ((2, HALF, HALF), f32), ((SPAN, DIN), f32), ((SPAN, DIN), f32), ((SPAN, CONVW), f32),
         ((SPAN, CONVW), f32), ((SPAN, CONVW), f32), ((SPAN, DIN), bf16), ((2, HALF, HALF), f32), ((2, HALF, HALF), f32),
         ((2, NSTATE, DIN), bf16), ((SPAN, HALF), f32), ((RIM + SPAN + 8, CONVW), f32)],
        "third",
    )(cin, vraw, cum, dy, wred, dcs, dir1, later, state_in, loc, conv_weight, cb, dl, skip, db)

    live = (jnp.arange(SPAN, dtype=jnp.int32)[None, :] < rel[:, None]).astype(f32)[:, :, None]
    drive = (live * cotangent.astype(f32)).astype(bf16)
    flat = lambda v: v.reshape(-1, v.shape[-1])
    g_out = mm_tn(flat(mlow), flat(drive))
    g_gate = mm_tn(flat(normed), flat(ggate))
    g_conv = mm_tn(flat(normed), flat(gz)) + mm_tn(flat(nhalo), flat(gzh))
    g_delta = mm_tn(flat(normed), flat(gdelta))

    gtok, gtail, grim, g_gain = call(
        fourth_kernel,
        seqs,
        [SMEM, per_seq(SPAN, D), per_seq(RIM, D), per_seq(SPAN, D), whole((1, D)), per_seq(SPAN, DIN), per_seq(SPAN, CONVW),
         per_seq(RIM, CONVW), per_seq(SPAN, HALF), whole((D, ZXW)), whole((D, HALF))],
        [
            (per_seq(SPAN, D), (seqs, SPAN, D), bf16),
            (per_seq(RIM, D), (seqs, RIM, D), f32),
            (per_seq(RIM, D), (seqs, RIM, D), bf16),
            (summed((1, D)), (1, D), f32),
        ],
        [],
        "fourth",
    )(rel, tokens_in, halo, cotangent, gain, ggate, gz, gzh, gdelta, full_zx, full_delta)
    grim = passed_along(grim, "ctx", -1)
    gtok = lax.dynamic_update_slice(gtok, (gtail + grim.astype(f32)).astype(bf16), (0, SPAN - RIM, 0))

    def reduced(g):
        part = lax.psum_scatter(g.astype(bf16), "group", scatter_dimension=0, tiled=True)
        return lax.psum(part, "ctx").astype(f32)

    g_zx = jnp.concatenate([reduced(g_gate), reduced(g_conv)], axis=1)
    g_out = reduced(g_out)
    g_delta = reduced(g_delta)[:, :HEADS]
    small = jnp.concatenate(
        [g_gain.reshape(-1), gcw.reshape(-1), gcb.reshape(-1), gdb[0], gdl[0],
         gskip.reshape(-1), gggain.reshape(-1)]
    )
    small = lax.psum(small, ("group", "ctx"))
    at = 0
    pieces = []
    for size in (D, KCONV * CONVW, CONVW, HALF, HALF, DIN, DIN):
        pieces.append(small[at : at + size])
        at += size
    return (
        mixed_out, gtok, pieces[0], g_zx, g_delta, g_out, pieces[1].reshape(KCONV, CONVW), pieces[2],
        pieces[3][:HEADS], pieces[4][:HEADS], pieces[5].reshape(HEADS, HEADDIM).sum(1), pieces[6],
    )


def solution(mesh):
    rows = P("group", "ctx", None)
    own = P("group", None)
    in_specs = (rows, P("group"), P(), own, own, own, P(), P(), P(), P(), P(), P(), rows)
    out_specs = (rows, rows, P(), own, own, own, P(), P(), P(), P(), P(), P())
    return jax.shard_map(local, mesh=mesh, in_specs=in_specs, out_specs=out_specs, check_vma=False)
```

time: 1960 us -> 571 us (0.29)
  waiting for transfers between devices: 1020 us -> 147 us
  matrix products: 308 us -> 20.9 us
  local copies, waits for them, and re-layouts: 258 us -> 18.7 us
  other arithmetic: 217 us -> 12.9 us
  Pallas kernels: 0 us -> 156 us
  blocking collectives: 84.9 us -> 180 us
  starting transfers between devices: 49.1 us -> 19.8 us
    ppermute x16 -> x2, waiting for transfers between devices: 904 us -> 0.01 us  [passed_along(): lax.ppermute(value, axis, [(source, source + steps) for source in range(l...]
    dot_general x69 -> x5, matrix products: 308 us -> 20.9 us  [mm_tn(): return lax.dot_general(a, b, TN, preferred_element_type=f32)]
    pallas_call x0 -> x4, Pallas kernels: none -> 156 us  [the longest x1 64.7 us: local(): call(third_kernel, seqs, [per_seq(RIM + SPAN, CONVW), per_seq(SPAN, HALF)...]
    dynamic_update_slice x52 -> x0, local copies, waits for them, and re-layouts: 69.3 us -> none  [the longest x32 33.8 us: local(): lax.map(front_part, (conv_in, proj_delta, before_rows))]
    all_to_all x0 -> x3, waiting for transfers between devices: none -> 59.9 us  [the longest x1 30.7 us: state_scan(): back = lax.all_to_all(back, 'ctx', 0, 0, tiled=True)]
    add x16 -> x0, other arithmetic: 56.1 us -> none  [the longest x7 27.9 us: relay_back(): grad_direct + totals[:, :, None, None] * carried_in]
    all_gather x1 -> x2, blocking collectives: 6.18 us -> 61.7 us  [the longest x1 56.3 us: state_scan(): decays = lax.all_gather(decay, 'ctx', axis=0)]
    ppermute x16 -> x2, starting transfers between devices: 48.8 us -> 6.16 us  [passed_along(): lax.ppermute(value, axis, [(source, source + steps) for source in range(l...]
  transfers between devices with their start and end apart: 22 -> 12, of which waited for: 19 -> 5; matrix products, arithmetic and copies ran while one was open for 14% -> 7% of each run, Pallas kernels for 0% -> 14%
where the time goes in v1:
time: 571 us; the launch traced here: 570 us
  blocking collectives  180 us (32%)
  Pallas kernels  156 us (27%)
  waiting for transfers between devices  147 us (26%)
  matrix products  20.9 us (4%)
  starting transfers between devices  19.8 us (3%)
  local copies, waits for them, and re-layouts  18.7 us (3%)
  between operations  14.7 us (3%)
  other arithmetic  12.9 us (2%)
    pallas_call x1, Pallas kernels, local(): call(third_kernel, seqs, [per_seq(RIM + SPAN, CONVW), per_seq(SPAN, HALF)...  64.7 us
    all_gather x1, blocking collectives, state_scan(): decays = lax.all_gather(decay, 'ctx', axis=0)  56.3 us
    pallas_call x1, Pallas kernels, local(): call(second_kernel, seqs, [SMEM, per_seq(SPAN, D), per_seq(SPAN, D), per_...  49.4 us
    psum x1, waiting for transfers between devices, reduced(): return lax.psum(part, 'ctx').astype(f32)  41 us
    all_to_all x1, blocking collectives, state_scan(): back = lax.all_to_all(back, 'ctx', 0, 0, tiled=True)  40.3 us
    psum x1, blocking collectives, local(): small = lax.psum(small, ('group', 'ctx'))  40 us
    psum x1, blocking collectives, reduced(): return lax.psum(part, 'ctx').astype(f32)  38.3 us
    all_to_all x1, waiting for transfers between devices, state_scan(): back = lax.all_to_all(back, 'ctx', 0, 0, tiled=True)  30.7 us
  transfers between devices with their start and end apart: 12, of which 5 were waited for; matrix products, arithmetic and copies ran while one was open for 7% of the time, Pallas kernels for 14%

profile of v1, /device:TPU:0, one launch (start us, length us, event | category | flops | bytes accessed | tf_op | source)
XLA Modules:
  0.0 570.2 jit_solution(14816515504694373936)
XLA Ops:
  8.0 0.9 slice.114
  8.9 4.9 collective-permute-start
  13.7 5.4 all-gather.1
  22.3 29.8 %all-gather.5.cloned.1.call-done.wzx = bf16[768,3328]{1,0:T(8,128)(2,1)} async-done(((bf16[192,3328]{1,0:T(8,128)(2,1)}), bf16[768,3328]{1,0:T(8,128)(2,1)}) %all-gather.5.cloned.1.call-update) | async-done | bytes 5111824 | tf_op jit(solution)/shard_map/all_gather | solution.py:478
  52.0 27.3 %first.1 = (bf16[4,256,768]{2,1,0:T(8,128)(2,1)}, bf16[4,16,768]{2,1,0:T(8,128)(2,1)}, f32[4,272,1792]{2,1,0:T(8,128)}, f32[4,256,1792]{2,1,0:T(8,128)}, f32[4,2...) custom-call(bf16[4,256,768]{2,1,0:T(8,128)(2,1)} %tok.5, ...), custom_call_target="tpu_custom_call" | custom-call | tf_op jit(solution)/shard_map/first/pallas_call | solution.py:491
  79.4 2.7 copy.74
  82.1 5.6 all-to-all-start
  89.2 56.3 %all-gather = f32[32,1,1536]{2,1,0:T(1,128)S(1)} all-gather(f32[4,1,1536]{2,1,0:T(1,128)S(1)} %copy-done.11), channel_id=2, replica_groups=mesh['group'=4,'ctx'=8] {'ctx'}, dimensions={0}, use_global_device_ids=true | all-gather | bytes 221184 | tf_op jit(solution)/shard_map/all_gather | solution.py:450
  151.1 3.8 all-to-all-start.1
  156.9 30.7 %all-to-all-done.1 = bf16[8,4,16,1536]{3,2,1,0:T(8,128)(2,1)S(1)} async-done(((bf16[8,4,16,1536]{3,2,1,0:T(8,128)(2,1)}), bf16[8,4,16,1536]{3,2,1,0:T(8,128)(2,1)S(1)}, u32[]{:S(2)}, u32[]{:S(2)}) %all-to-all-start.1) | async-done | bytes 1572896 | tf_op jit(solution)/shard_map/all_to_all | solution.py:458
  187.7 1.3 copy.43
  189.0 49.4 %second.1 = (bf16[4,256,768]{2,1,0:T(8,128)(2,1)}, bf16[4,256,1536]{2,1,0:T(8,128)(2,1)}, bf16[4,256,1536]{2,1,0:T(8,128)(2,1)}, bf16[4,256,1536]{2,1,0:T(8,128)...) custom-call(s32[4]{0:T(128)} %broadcast_subtract_fusion.rel, ...), custom_call_target="tpu_custom_call" | custom-call | tf_op jit(solution)/shard_map/second/pallas_call | solution.py:514
  238.3 5.8 %bitcast_convert_fusion.1 = bf16[768,1536]{1,0:T(8,128)(2,1)} fusion(bf16[4,256,768]{2,1,0:T(8,128)(2,1)S(1)} %copy-done.1, bf16[4,256,1536]{2,1,0:T(8,128)(2,1)} %get-tuple-element.51.ggate), kind=kOutput, calls=%fused_computation.3 | convolution fusion | flops 2417098752 | bytes 7077888 | tf_op jit(solution)/shard_map/dot_general | solution.py:39
  244.1 1.4 copy-done.3
  245.5 1.3 copy.73
  246.9 3.8 all-to-all-start.2
  250.8 6.3 %bitcast_convert_fusion = bf16[1536,768]{1,0:T(8,128)(2,1)} fusion(bf16[4,256,1536]{2,1,0:T(8,128)(2,1)} %get-tuple-element.73, bf16[4,256,768]{2,1,0:T(8,128)(2,1)S(1)} %copy-done, f32[4,256]{1,0:T(4,128)S(1)} %fusion.22), kind=kOutput, calls=%fused_computation.2 | convolution fusion | flops 2419458048 | bytes 7081984 | tf_op jit(solution)/shard_map/dot_general | solution.py:39
  257.1 29.2 %all-to-all-done.2 = bf16[8,4,16,1536]{3,2,1,0:T(8,128)(2,1)S(1)} async-done(((bf16[8,4,16,1536]{3,2,1,0:T(8,128)(2,1)}), bf16[8,4,16,1536]{3,2,1,0:T(8,128)(2,1)S(1)}, u32[]{:S(2)}, u32[]{:S(2)}) %all-to-all-start.2) | async-done | bytes 1572896 | tf_op jit(solution)/shard_map/all_to_all | solution.py:449
  287.2 40.3 %all_to_all.20 = bf16[8,4,16,1536]{3,2,1,0:T(8,128)(2,1)S(1)} all-to-all(bf16[8,4,16,1536]{3,2,1,0:T(8,128)(2,1)S(1)} %broadcast_dynamic-update-slice_fusion), channel_id=1, replica_groups=mesh['group'=4,'ctx'=8] {'ctx'}, dimensions={0} | all-to-all | bytes 3145728 | tf_op jit(solution)/shard_map/all_to_all | solution.py:458
  327.5 1.2 copy.45
  328.7 64.7 %third.1 = (bf16[4,256,1792]{2,1,0:T(8,128)(2,1)}, bf16[4,16,1792]{2,1,0:T(8,128)(2,1)}, bf16[4,256,128]{2,1,0:T(8,128)(2,1)}, f32[4,1792]{1,0:T(4,128)}, f32[1,...) custom-call(f32[4,272,1792]{2,1,0:T(8,128)} %get-tuple-element.52.cin, f32[4,256,128]{2,1,0:T(8,128)} %get-tuple-element.45.vin, ...), custom_call_target="tpu_custom_call" | custom-call | tf_op jit(solution)/shard_map/third/pallas_call | solution.py:539
  393.4 5.2 fusion.25
  398.6 2.4 fusion
  402.0 1.3 fusion.2
  403.5 14.8 %fourth.1 = (bf16[4,256,768]{2,1,0:T(8,128)(2,1)}, f32[4,16,768]{2,1,0:T(8,128)}, bf16[4,16,768]{2,1,0:T(8,128)(2,1)}, f32[1,768]{1,0:T(1,128)}) custom-call(s32[4]{0:T(128)} %broadcast_subtract_fusion.rel, bf16[4,256,768]{2,1,0:T(8,128)(2,1)} %tok.5, bf16[4,16,768]{2,1,0:T(8,128)(2,1)} %copy-done.7, bf16[4,256,768]{2,1,0:T(8,128)(2,1)} %cot.3, ...), custom_call_target="tpu_custom_call" | custom-call | tf_op jit(solution)/shard_map/fourth/pallas_call | solution.py:568
  419.1 1.3 collective-permute-start.1
  420.4 14.5 %reduce-scatter.7.cloned.1.call-done = bf16[192,1792]{1,0:T(8,128)(2,1)} async-done(((bf16[768,1792]{1,0:T(8,128)(2,1)}), bf16[192,1792]{1,0:T(8,128)(2,1)}) %reduce-scatter.7.cloned.1.call-update) | async-done | bytes 688144 | tf_op jit(solution)/shard_map/reduce_scatter | solution.py:586
  435.1 40.0 %psum.35 = f32[13056]{0:T(1024)S(1)} all-reduce(f32[13056]{0:T(1024)S(1)} %constant_dynamic-update-slice_fusion.1), channel_id=1, replica_groups=mesh['group'=4,'ctx'=8] {'group','ctx'}, use_global_device_ids=true, to_apply=%region_0.1 | all-reduce | flops 13056 | bytes 104448 | tf_op jit(solution)/shard_map/psum | solution.py:596
  479.4 38.3 %psum.38 = bf16[192,128]{1,0:T(8,128)(2,1)S(1)} all-reduce(bf16[192,128]{1,0:T(8,128)(2,1)} %reduce-scatter.9.cloned.1.call-done), channel_id=1, replica_groups=mesh['group'=4,'ctx'=8] {'ctx'}, use_global_device_ids=true, to_apply=%region_6.7 | all-reduce | flops 24576 | bytes 98304 | tf_op jit(solution)/shard_map/psum | solution.py:587
  518.4 41.0 %all-reduce.6.cloned.1.call-done = (bf16[192,1792]{1,0:T(8,128)(2,1)}, bf16[192,1536]{1,0:T(8,128)(2,1)}, bf16[384,768]{1,0:T(8,128)(2,1)}) async-done(((bf16[192,1792]{1,0:T(8,128)(2,1)}, bf16[192,1536]{1,0:T(8,128)(2,1)}, bf16[384,768]{1,0:T(8,128)(2,1)}), (bf16[192,1792]{1,0:T(8,128)(2,1)}, bf16[192,1536]{1,0:T(8,128)(2,1)}, bf16[384,768]{1,0:T(8,128)(2,1)})) %all-reduce.6.cloned.1.call-update) | async-done | bytes 1867792 | tf_op jit(solution)/shard_map/psum | solution.py:587
  559.4 2.3 convert_element_type.165
  561.7 1.6 maximum_convert_fusion
  (129 shorter events, 20.9 us)
Async XLA Ops:
  7.2 12.2 %copy-start.13 = (f32[1792]{0:T(1024)S(1)}, f32[1792]{0:T(1024)}, u32[]{:S(2)}) copy-start(f32[1792]{0:T(1024)} %param.20) | copy-start | bytes 21508
  7.2 12.8 %copy-start.18 = (f32[768]{0:T(1024)S(1)}, f32[768]{0:T(1024)}, u32[]{:S(2)}) copy-start(f32[768]{0:T(1024)} %param.15) | copy-start | bytes 9220
  7.2 13.3 %copy-start.21 = (f32[24]{0:T(128)S(1)}, f32[24]{0:T(128)}, u32[]{:S(2)}) copy-start(f32[24]{0:T(128)} %param.21) | copy-start | bytes 292
  7.2 13.8 %copy-start.22 = (f32[24]{0:T(128)S(1)}, f32[24]{0:T(128)}, u32[]{:S(2)}) copy-start(f32[24]{0:T(128)} %param.22) | copy-start | bytes 292
  7.2 44.8 %all-gather.5.cloned.1.call-start = ((), (), s32[]{:S(2)}) async-start(), calls=%async_computation.8 | async-start | bytes 6389760 | tf_op jit(solution)/shard_map/all_gather | solution.py:478
  8.9 13.4 %collective-permute-start = (bf16[4,16,768]{2,1,0:T(8,128)(2,1)S(1)}, bf16[4,16,768]{2,1,0:T(8,128)(2,1)S(1)}, u32[]{:S(2)}, u32[]{:S(2)}) collective-permute-start(bf16[4,16,768]{2,1,0:T(8,128)(2,1)S(1)} %slice.114), channel_id=1, source_target_pairs={{0,1},{1,2},{2,3},{3,4},{4,5},{5,6},{6,7},{8,9},{9,10},{10,11},{11... | collective-permute-start | bytes 294920 | tf_op jit(solution)/shard_map/ppermute | solution.py:465
  22.3 29.8 %copy-start.7 = (bf16[4,16,768]{2,1,0:T(8,128)(2,1)}, bf16[4,16,768]{2,1,0:T(8,128)(2,1)S(1)}, u32[]{:S(2)}) copy-start(bf16[4,16,768]{2,1,0:T(8,128)(2,1)S(1)} %collective-permute-done.halo) | copy-start | bytes 294916
  82.1 7.1 %copy-start.11 = (f32[4,1,1536]{2,1,0:T(1,128)S(1)}, f32[4,1,1536]{2,1,0:T(1,128)}, u32[]{:S(2)}) copy-start(f32[4,1,1536]{2,1,0:T(1,128)} %get-tuple-element.48) | copy-start | bytes 73732
  82.1 63.5 %all-to-all-start = ((bf16[8,4,16,1536]{3,2,1,0:T(8,128)(2,1)}), bf16[8,4,16,1536]{3,2,1,0:T(8,128)(2,1)S(1)}, u32[]{:S(2)}, u32[]{:S(2)}) async-start(bf16[8,4,16,1536]{3,2,1,0:T(8,128)(2,1)} %bitcast.58), calls=%async_computation | async-start | bytes 3145728 | tf_op jit(solution)/shard_map/all_to_all | solution.py:449
  87.7 101.3 %all-gather.7.cloned.1.call-start = ((), (), s32[]{:S(2)}) async-start(), calls=%async_computation.9 | async-start | bytes 2949120 | tf_op jit(solution)/shard_map/all_gather | solution.py:480
  151.1 4.0 copy-start.19
  151.1 4.8 copy-start.12
  151.1 5.4 copy-start.23
  151.1 36.6 %all-to-all-start.1 = ((bf16[8,4,16,1536]{3,2,1,0:T(8,128)(2,1)}), bf16[8,4,16,1536]{3,2,1,0:T(8,128)(2,1)S(1)}, u32[]{:S(2)}, u32[]{:S(2)}) async-start(bf16[8,4,16,1536]{3,2,1,0:T(8,128)(2,1)} %fusion.18), calls=%async_computation.1 | async-start | bytes 3145728 | tf_op jit(solution)/shard_map/all_to_all | solution.py:458
  154.8 265.5 %reduce-scatter.5.cloned.1.call-start = ((), (), s32[]{:S(2)}) async-start(), calls=%async_computation.10 | async-start | bytes 2949120 | tf_op jit(solution)/shard_map/reduce_scatter | solution.py:586
  189.0 49.4 %copy-start.1 = (bf16[4,256,768]{2,1,0:T(8,128)(2,1)S(1)}, bf16[4,256,768]{2,1,0:T(8,128)(2,1)}, u32[]{:S(2)}) copy-start(bf16[4,256,768]{2,1,0:T(8,128)(2,1)} %get-tuple-element.71) | copy-start | bytes 4718596
  246.9 3.9 copy-start.17
  246.9 3.9 copy-start
  246.9 39.4 %all-to-all-start.2 = ((bf16[8,4,16,1536]{3,2,1,0:T(8,128)(2,1)}), bf16[8,4,16,1536]{3,2,1,0:T(8,128)(2,1)S(1)}, u32[]{:S(2)}, u32[]{:S(2)}) async-start(bf16[8,4,16,1536]{3,2,1,0:T(8,128)(2,1)} %bitcast.65), calls=%async_computation.2 | async-start | bytes 3145728 | tf_op jit(solution)/shard_map/all_to_all | solution.py:449
  250.7 169.7 %reduce-scatter.11.cloned.1.call-start = ((), (), s32[]{:S(2)}) async-start(), calls=%async_computation.13 | async-start | bytes 2949120 | tf_op jit(solution)/shard_map/reduce_scatter | solution.py:586
  257.1 177.8 %reduce-scatter.7.cloned.1.call-start = ((), (), s32[]{:S(2)}) async-start(), calls=%async_computation.11 | async-start | bytes 3440640 | tf_op jit(solution)/shard_map/reduce_scatter | solution.py:586
  328.7 64.7 %copy-start.2 = (bf16[4,256,768]{2,1,0:T(8,128)(2,1)S(1)}, bf16[4,256,768]{2,1,0:T(8,128)(2,1)}, u32[]{:S(2)}) copy-start(bf16[4,256,768]{2,1,0:T(8,128)(2,1)} %get-tuple-element.71) | copy-start | bytes 4718596
  393.4 5.2 copy-start.8
  393.4 5.2 copy-start.20
  401.1 78.3 %reduce-scatter.9.cloned.1.call-start = ((), (), s32[]{:S(2)}) async-start(), calls=%async_computation.12 | async-start | bytes 245760 | tf_op jit(solution)/shard_map/reduce_scatter | solution.py:586
  403.3 156.1 %all-reduce.6.cloned.1.call-start = ((), (), s32[]{:S(2)}) async-start(), calls=%async_computation.14 | async-start | bytes 3735552 | tf_op jit(solution)/shard_map/psum | solution.py:587
  403.5 15.6 %copy-start.14 = (f32[1,1792]{1,0:T(1,128)S(1)}, f32[1,1792]{1,0:T(1,128)}, u32[]{:S(2)}) copy-start(f32[1,1792]{1,0:T(1,128)} %get-tuple-element.66) | copy-start | bytes 21508
  418.2 16.7 %copy-start.10 = (f32[4,1792]{1,0:T(4,128)S(1)}, f32[4,1792]{1,0:T(4,128)}, u32[]{:S(2)}) copy-start(f32[4,1792]{1,0:T(4,128)} %get-tuple-element.65) | copy-start | bytes 86020
  418.2 16.8 %copy-start.25 = (f32[1,128]{1,0:T(1,128)S(1)}, f32[1,128]{1,0:T(1,128)}, u32[]{:S(2)}) copy-start(f32[1,128]{1,0:T(1,128)} %get-tuple-element.67) | copy-start | bytes 1540
  418.3 16.8 %copy-start.24 = (f32[1,128]{1,0:T(1,128)S(1)}, f32[1,128]{1,0:T(1,128)}, u32[]{:S(2)}) copy-start(f32[1,128]{1,0:T(1,128)} %get-tuple-element.68) | copy-start | bytes 1540
  418.3 60.5 %copy-start.9 = (f32[4,16,768]{2,1,0:T(8,128)S(1)}, f32[4,16,768]{2,1,0:T(8,128)}, u32[]{:S(2)}) copy-start(f32[4,16,768]{2,1,0:T(8,128)} %get-tuple-element.62) | copy-start | bytes 589828
  419.1 59.7 %collective-permute-start.1 = (bf16[4,16,768]{2,1,0:T(8,128)(2,1)}, bf16[4,16,768]{2,1,0:T(8,128)(2,1)S(1)}, u32[]{:S(2)}, u32[]{:S(2)}) collective-permute-start(bf16[4,16,768]{2,1,0:T(8,128)(2,1)} %get-tuple-element.63), channel_id=1, source_target_pairs={{1,0},{2,1},{3,2},{4,3},{5,4},{6,5},{7,6},{9,8},{10,9},{11,10},{12... | collective-permute-start | bytes 294920 | tf_op jit(solution)/shard_map/ppermute | solution.py:465
  (6 other events, 11.5 us)
Sparse Core Ops, SparseCore 0:
  9.6 42.3 all-gather.4
  90.1 24.5 all-gather.6
  244.3 30.9 reduce-scatter.4
  277.8 33.0 reduce-scatter.10
  401.2 33.6 reduce-scatter.6
  437.4 19.7 reduce-scatter.8
  461.5 97.8 all-reduce.5

commit v2 on v1

v2 whole, which is shorter than its diff:
```python
import jax
import jax.numpy as jnp
from jax import lax
from jax.experimental import pallas as pl
from jax.experimental.pallas import tpu as pltpu
from jax.sharding import PartitionSpec as P

D = 768
HEADS = 24
HEADDIM = 64
NSTATE = 128
KCONV = 4
SPAN = 256
DIN = 1536
CONVW = 1792
ZXW = 3328
RIM = 16
HALF = 128
TILE = 256
PAIRS = 12
EPS = 1e-05

f32 = jnp.float32
bf16 = jnp.bfloat16
NT = (((1,), (1,)), ((), ()))
TN = (((0,), (0,)), ((), ()))
VMEM_LIMIT = 62 * 1024 * 1024


def mm(a, b):
    return jnp.dot(a, b, preferred_element_type=f32)


def mm_nt(a, b):
    return lax.dot_general(a, b, NT, preferred_element_type=f32)


def mm_tn(a, b):
    return lax.dot_general(a, b, TN, preferred_element_type=f32)


def halves(v):
    high = v.astype(bf16)
    return high, (v - high.astype(f32)).astype(bf16)


def head_map():
    rows = lax.broadcasted_iota(jnp.int32, (2 * HALF, DIN), 0) % HALF
    cols = lax.broadcasted_iota(jnp.int32, (2 * HALF, DIN), 1) // HEADDIM
    return jnp.where(rows == cols, 1.0, 0.0).astype(bf16)


def spread(v, sel):
    return mm(jnp.concatenate(halves(v), axis=1), sel[...])


def gather_heads(v, sel_part):
    high, low = halves(v)
    return mm_nt(high, sel_part) + mm_nt(low, sel_part)


def triangle(size, lower):
    rows = lax.broadcasted_iota(jnp.int32, (size, size), 0)
    cols = lax.broadcasted_iota(jnp.int32, (size, size), 1)
    keep = rows >= cols if lower else rows <= cols
    return jnp.where(keep, 1.0, 0.0).astype(f32)


def exact_mm(a, b):
    return jnp.dot(a, b, precision=lax.Precision.HIGHEST, preferred_element_type=f32)


def softplus(v):
    return jnp.maximum(v, 0.0) + jnp.log1p(jnp.exp(-jnp.abs(v)))


def sigmoid(v):
    return 1.0 / (1.0 + jnp.exp(-v))


def local_decays(cum):
    mid, end = cum[HALF - 1 : HALF], cum[SPAN - 1 : SPAN]
    rows = lax.broadcasted_iota(jnp.int32, (SPAN, 1), 0)
    first = rows < HALF
    start = jnp.where(first, 0.0, mid)
    stop = jnp.where(first, mid, end)
    return jnp.exp(cum - start), jnp.exp(stop - cum), jnp.exp(mid), jnp.exp(end - mid), jnp.exp(end)


def rows_of(v):
    return jnp.broadcast_to(v, (8, v.shape[1]))


def normalized(rows, gain):
    rows = rows.astype(f32)
    inv = lax.rsqrt(jnp.mean(rows * rows, axis=-1, keepdims=True) + EPS)
    return rows, inv, (rows * inv * gain).astype(bf16)


def remote(src, dst, send_sem, recv_sem, **where):
    return pltpu.make_async_remote_copy(
        src_ref=src, dst_ref=dst, send_sem=send_sem, recv_sem=recv_sem,
        device_id=where, device_id_type=pl.DeviceIdType.MESH,
    )


def loop(start, stop, body):
    def step(i, c):
        body(i)
        return c

    lax.fori_loop(start, stop, step, 0)


def meet(axes):
    barrier = pltpu.get_barrier_semaphore()
    total = 0
    for axis in axes:
        size = lax.axis_size(axis)
        me = lax.axis_index(axis)

        def greet(d):
            pl.semaphore_signal(
                barrier, inc=1, device_id={axis: lax.rem(me + d, size)}, device_id_type=pl.DeviceIdType.MESH
            )

        loop(1, size, greet)
        total += size - 1
    pl.semaphore_wait(barrier, total)


class Exchange:
    def __init__(self, count, buf, recv, back, out, sends, recvs, back_sends, back_recvs, own_sem):
        self.count = count
        self.parts = min(count, 8)
        self.stride = count // self.parts
        self.rows = NSTATE // self.parts
        self.me = lax.axis_index("ctx")
        self.mine = self.me // self.stride
        self.buf, self.recv, self.back, self.out = buf, recv, back, out
        self.sends, self.recvs, self.back_sends, self.back_recvs, self.own_sem = (
            sends, recvs, back_sends, back_recvs, own_sem,
        )

    def part(self, j):
        return pl.ds(pl.multiple_of(j * self.rows, self.rows), self.rows)

    def owners(self, body):
        if self.stride == 1:
            loop(1, self.parts, lambda d: body(lax.rem(self.mine + d, self.parts)))
        else:
            def step(d):
                j = lax.rem(self.mine + d, self.parts)
                pl.when(j * self.stride != self.me)(lambda: body(j))

            loop(0, self.parts, step)

    def if_owner(self, body):
        if self.stride == 1:
            body()
        else:
            pl.when(self.mine * self.stride == self.me)(body)

    def others(self, body):
        loop(1, self.count, lambda d: body(lax.rem(self.me + d, self.count)))

    def to_owner(self, s, j, sender):
        return remote(
            self.buf.at[s, self.part(j)], self.recv.at[s, sender], self.sends.at[s, j], self.recvs.at[s, sender],
            ctx=j * self.stride,
        )

    def to_block(self, s, b, j):
        return remote(
            self.back.at[s, b], self.out.at[s, self.part(j)], self.back_sends.at[s, b], self.back_recvs.at[s, j], ctx=b
        )

    def keep(self, s):
        return pltpu.make_async_copy(self.back.at[s, self.me], self.out.at[s, self.part(self.mine)], self.own_sem.at[s])

    def start(self, s):
        self.owners(lambda j: self.to_owner(s, j, self.me).start())

        def own():
            self.recv[s, self.me] = self.buf[s, self.part(self.mine), :]

        self.if_owner(own)

    def scan(self, s, decx, reverse):
        def run():
            self.others(lambda b: self.to_owner(s, self.mine, b).wait_recv())

            def block(k, carry):
                b = self.count - 1 - k if reverse else k
                self.back[s, b] = carry.astype(bf16)
                return decx[pl.ds(pl.multiple_of(b * 8, 8), 8), :][0:1] * carry + self.recv[s, b].astype(f32)

            lax.fori_loop(0, self.count, block, jnp.zeros((self.rows, DIN), f32))
            self.others(lambda b: self.to_block(s, b, self.mine).start())
            self.keep(s).start()

        self.if_owner(run)

    def finish(self, s):
        self.owners(lambda j: self.to_block(s, self.me, j).wait_recv())
        self.owners(lambda j: self.to_owner(s, j, self.me).wait_send())

        def own():
            self.others(lambda b: self.to_block(s, b, self.mine).wait_send())
            self.keep(s).wait()

        self.if_owner(own)


class Spread:
    def __init__(self, index, shard, full, cols, sems):
        self.index, self.shard, self.full, self.cols = index, shard, full, cols
        self.x_send, self.x_recv, self.m_send, self.m_recv, self.own = sems
        self.size = lax.axis_size("group")
        self.cores = 2 if self.size % 2 == 0 else 1
        self.chips = self.size // self.cores
        self.me = lax.axis_index("group")
        self.core = lax.rem(self.me, self.cores)
        self.chip = self.me // self.cores
        self.rows = shard.shape[0]

    def place(self, member):
        return self.full.at[pl.ds(pl.multiple_of(member * self.rows, 64), self.rows), self.cols]

    def source(self):
        return self.shard.at[:, self.cols]

    def across(self, d):
        peer = lax.rem(self.chip + d, self.chips) * self.cores + self.core
        return remote(
            self.source(), self.place(self.me), self.x_send.at[self.index, d], self.x_recv.at[self.index, d], group=peer
        )

    def mate(self, d):
        member = lax.rem(self.chip + self.chips - d, self.chips) * self.cores + self.core
        src = self.source() if d == 0 else self.place(member)
        return remote(
            src, self.place(member), self.m_send.at[self.index, d], self.m_recv.at[self.index, d],
            group=self.me + 1 - 2 * self.core,
        )

    def keep(self):
        return pltpu.make_async_copy(self.source(), self.place(self.me), self.own.at[self.index])

    def start(self):
        for d in range(1, self.chips):
            self.across(d).start()
        if self.cores == 2:
            self.mate(0).start()
        self.keep().start()

    def forward(self):
        for d in range(1, self.chips):
            self.across(d).wait_recv()
            if self.cores == 2:
                self.mate(d).start()

    def finish(self):
        self.keep().wait()
        if self.cores == 2:
            for d in range(self.chips):
                self.mate(d).wait_recv()

    def drain(self):
        for d in range(1, self.chips):
            self.across(d).wait_send()
        if self.cores == 2:
            for d in range(self.chips):
                self.mate(d).wait_send()


def masks():
    rows = lax.broadcasted_iota(jnp.int32, (HALF, HALF), 0)
    cols = lax.broadcasted_iota(jnp.int32, (HALF, HALF), 1)
    return rows >= cols, cols < HEADDIM


def both(q):
    return slice(q * HALF, (q + 1) * HALF)


def pair_decays(cum, cum_t, p, causal):
    rolled = pltpu.roll(cum, lax.rem(HALF - 2 * p, HALF), 1)
    out = []
    for q in range(2):
        for a in range(2):
            gaps = rolled[both(q), a : a + 1] - cum_t[q, pl.ds(2 * p + a, 1), :]
            out.append(jnp.exp(jnp.where(causal, gaps, -jnp.inf)))
    return out


def front_kernel(
    tok, tok_all, wcat, wout, gain, cw, cb, db, dl,
    normed, nhalo, cin, xb, vout, cumout, st0, loc, ylocal, gate, decs_out, wfull, wofull, sin,
    sel, halo, ext, ns, xs_s, cum_s, dt_s, cum_t, wv, wg, fexp, decs, decx, buf, recv, back,
    halo_sem, x_send, x_recv, m_send, m_recv, w_own, w_load, sends, recvs, back_sends, back_recvs, own_sem,
    dec_send, dec_recv,
):
    i = pl.program_id(0)
    seqs = tok_all.shape[0]
    count = lax.axis_size("ctx")
    me = lax.axis_index("ctx")
    ex = Exchange(count, buf, recv, back, sin, sends, recvs, back_sends, back_recvs, own_sem)
    sems = (x_send, x_recv, m_send, m_recv, w_own)
    conv_cols, gate_cols = pl.ds(DIN, CONVW + HALF), pl.ds(0, DIN)
    spreads = [
        Spread(0, wcat, wfull, conv_cols, sems),
        Spread(1, wcat, wfull, gate_cols, sems),
        Spread(2, wout, wofull, pl.ds(0, D), sems),
    ]
    halo_copy = remote(
        tok_all.at[:, pl.ds(SPAN - RIM, RIM), :], halo, halo_sem.at[0], halo_sem.at[1], ctx=lax.rem(me + 1, count)
    )
    load_v = pltpu.make_async_copy(wfull.at[:, conv_cols], wv, w_load.at[0])
    load_g = pltpu.make_async_copy(wfull.at[:, gate_cols], wg, w_load.at[1])

    def dec_copy(s, j, sender):
        rows = pl.ds(pl.multiple_of(sender * 8, 8), 8)
        return remote(
            decs.at[s, rows, :], decs.at[s, rows, :], dec_send.at[s, j], dec_recv.at[s, sender], ctx=j * ex.stride
        )

    @pl.when(i == 0)
    def _():
        meet(("ctx", "group"))
        pl.when(me < count - 1)(lambda: halo_copy.start())
        for sp in spreads:
            sp.start()
        sel[...] = head_map()

        @pl.when(me == 0)
        def _():
            halo[...] = jnp.zeros_like(halo)

        @pl.when(me > 0)
        def _():
            halo_copy.wait_recv()

        spreads[0].forward()
        spreads[0].finish()
        load_v.start()
        load_v.wait()

    @pl.when(i == 1)
    def _():
        spreads[1].forward()
        spreads[2].forward()

    @pl.when(i == seqs - 1)
    def _():
        spreads[1].finish()
        load_g.start()

    @pl.when(i < seqs)
    def _():
        s = i
        nh = normalized(halo[s], gain[...])[2]
        nm = normalized(tok[0], gain[...])[2]
        ext[0:RIM] = nh
        ext[RIM:] = nm
        ns[s] = nm
        nhalo[0] = nh
        normed[0] = nm
        v = mm(nm, wv[:, CONVW:]) + db[...]
        vout[0] = v
        dt = softplus(v)
        cum = exact_mm(triangle(SPAN, True), -jnp.exp(dl[...]) * dt)
        cumout[0] = cum
        cum_s[s] = cum
        dt_s[s] = dt
        e_in, e_out, tot0, tot1, total = local_decays(cum)
        decs[s, pl.ds(pl.multiple_of(me * 8, 8), 8), :] = rows_of(total)
        ex.owners(lambda j: dec_copy(s, j, me).start())
        fexp[...] = spread(dt * e_out, sel)
        tot1x = spread(rows_of(tot1), sel)[0:1]

        def conv_tile(c):
            cols = slice(c, c + TILE)
            cin[0, :, cols] = mm(ext[...], wv[:, cols])
            o = cb[:, cols]
            for k in range(KCONV):
                o = o + cw[k : k + 1, cols] * cin[0, RIM - KCONV + 1 + k : RIM - KCONV + 1 + k + SPAN, cols]
            a = o * sigmoid(o)
            low = a.astype(bf16)
            xb[0, :, cols] = low
            xs_s[s, :, cols] = low
            return a

        bc = conv_tile(DIN)
        bt = jnp.transpose(bc[:, :NSTATE]).astype(bf16)
        for j in range(DIN // TILE):
            c = j * TILE
            cols = slice(c, c + TILE)
            a = conv_tile(c)
            xw = (a * fexp[:, cols]).astype(bf16)
            s0 = mm(bt[:, :HALF], xw[:HALF])
            s1 = mm(bt[:, HALF:], xw[HALF:])
            st0[0, :, cols] = s0
            low = (tot1x[:, cols] * s0 + s1).astype(bf16)
            loc[0, :, cols] = low
            buf[s, :, cols] = low
        ex.start(s)

    def scan(s):
        ex.if_owner(lambda: ex.others(lambda b: dec_copy(s, ex.mine, b).wait_recv()))
        decx[...] = spread(decs[s], sel)
        ex.scan(s, decx, False)

    @pl.when(i == seqs)
    def _():
        load_g.wait()
        for s in range(seqs - 1):
            scan(s)

    @pl.when(i == seqs + 1)
    def _():
        scan(seqs - 1)

    @pl.when(i >= seqs)
    def _():
        s = i - seqs
        causal, low_lanes = masks()
        cum = cum_s[s]
        for q in range(2):
            cum_t[q] = jnp.transpose(cum[both(q)])
        fexp[...] = spread(dt_s[s], sel)
        bb = xs_s[s, :, DIN : DIN + NSTATE]
        cc = xs_s[s, :, DIN + NSTATE :]
        scores = [mm_nt(cc[both(q)], bb[both(q)]) for q in range(2)]

        def pair_step(p):
            cols = pl.ds(pl.multiple_of(p * HALF, HALF), HALF)
            decays = pair_decays(cum, cum_t, p, causal)
            for q in range(2):
                rows = both(q)
                m = jnp.concatenate([(decays[2 * q + a] * scores[q]).astype(bf16) for a in range(2)], axis=1)
                x = xs_s[s, rows, cols].astype(f32) * fexp[rows, cols]
                x = jnp.concatenate([jnp.where(low_lanes, x, 0.0), jnp.where(low_lanes, 0.0, x)], axis=0)
                ylocal[0, rows, cols] = mm(m, x.astype(bf16))

        loop(0, PAIRS, pair_step)
        for j in range(DIN // TILE):
            cols = slice(j * TILE, (j + 1) * TILE)
            gate[0, :, cols] = mm(ns[s], wg[:, cols])

    @pl.when(i == 2 * seqs - 1)
    def _():
        decs_out[...] = decs[...]
        for s in range(seqs):
            ex.finish(s)
            ex.owners(lambda j: dec_copy(s, j, me).wait_send())
        for sp in spreads[1:]:
            if sp.index == 2:
                sp.finish()
        for sp in spreads:
            sp.drain()
        pl.when(me < count - 1)(lambda: halo_copy.wait_send())


def middle_kernel(
    rel, tok, cot, ylocal, gate, xb, vin, cumin, st0, sin, decs, wout, skip, ggain,
    mixed, mlow, dyout, ggate, wred, dir1, gskip, gggain, dxs, dbc, later,
    sel, cum_t, einx, ys, gs, ss, s_in, dcs, dy_s, ml_s, g_s, dg_s, decx, buf, recv, back,
    sends, recvs, back_sends, back_recvs, own_sem,
):
    i = pl.program_id(0)
    seqs = dy_s.shape[0]
    count = lax.axis_size("ctx")
    ex = Exchange(count, buf, recv, back, later, sends, recvs, back_sends, back_recvs, own_sem)

    @pl.when(i == 0)
    def _():
        meet(("ctx",))
        sel[...] = head_map()
        gskip[...] = jnp.zeros_like(gskip)
        gggain[...] = jnp.zeros_like(gggain)

    @pl.when(i < seqs)
    def _():
        s = i
        cum = cumin[0]
        e_in, e_out, tot0, tot1, total = local_decays(cum)
        einx[...] = spread(e_in, sel)
        tot0x = spread(rows_of(tot0), sel)[0:1]
        s_in[0] = sin[0]
        s_in[1] = (tot0x * sin[0].astype(f32) + st0[0]).astype(bf16)
        cc = xb[0, :, DIN + NSTATE :]

        def gate_step(j, total_sq):
            cols = pl.ds(pl.multiple_of(j * TILE, TILE), TILE)
            for q in range(2):
                rows = both(q)
                ys[rows, cols] = ylocal[0, rows, cols] + einx[rows, cols] * mm(cc[rows], s_in[q, :, cols])
            y = ys[:, cols] + skip[:, cols] * xb[0, :, cols].astype(f32)
            g = gate[0, :, cols]
            gated = y * (g * sigmoid(g))
            gs[:, cols] = gated
            sq = gated * gated
            return total_sq + sq[:, :HALF] + sq[:, HALF:]

        sq = lax.fori_loop(0, DIN // TILE, gate_step, jnp.zeros((SPAN, HALF), f32))
        inv = lax.rsqrt(jnp.sum(sq, axis=1, keepdims=True) * (1.0 / DIN) + EPS)
        live = (lax.broadcasted_iota(jnp.int32, (SPAN, 1), 0) < rel[s]).astype(f32)
        drive = (live * cot[0].astype(f32)).astype(bf16)

        def back_step(j, acc):
            cols = pl.ds(pl.multiple_of(j * TILE, TILE), TILE)
            gm = mm_nt(drive, wout[cols, :])
            gated = gs[:, cols]
            unit = gated * inv
            low = (unit * ggain[:, cols]).astype(bf16)
            mlow[0, :, cols] = low
            ml_s[s, :, cols] = low
            gggain[:, cols] += jnp.sum(gm * unit, axis=0, keepdims=True)
            scaled = gm * ggain[:, cols]
            ss[:, cols] = scaled
            prod = scaled * gated
            return acc + prod[:, :HALF] + prod[:, HALF:]

        dots = lax.fori_loop(0, DIN // TILE, back_step, jnp.zeros((SPAN, HALF), f32))
        dots = jnp.sum(dots, axis=1, keepdims=True) * (1.0 / DIN)
        corr = inv * inv * inv * dots
        cct = jnp.transpose(cc.astype(f32)).astype(bf16)
        acc = jnp.zeros((SPAN, HALF), f32)
        dc = [jnp.zeros((HALF, HALF), f32) for _ in range(2)]
        for j in range(DIN // TILE):
            cols = slice(j * TILE, (j + 1) * TILE)
            g = gate[0, :, cols]
            sg = sigmoid(g)
            sl = g * sg
            grad_gated = inv * ss[:, cols] - gs[:, cols] * corr
            dy = grad_gated * sl
            yn = ys[:, cols]
            x = xb[0, :, cols].astype(f32)
            y = yn + skip[:, cols] * x
            ggate[0, :, cols] = (grad_gated * y * (sg + sl * (1.0 - sg))).astype(bf16)
            dyb = dy.astype(bf16)
            dyout[0, :, cols] = dyb
            dy_s[s, :, cols] = dyb
            gskip[:, cols] += jnp.sum(dy * x, axis=0, keepdims=True)
            acc = acc + gather_heads(dy * yn, sel[:HALF, cols])
            dye = (dy * einx[:, cols]).astype(bf16)
            d0 = mm(cct[:, :HALF], dye[:HALF])
            d1 = mm(cct[:, HALF:], dye[HALF:])
            dir1[0, :, cols] = d1
            buf[s, :, cols] = (d0 + tot0x[:, cols] * d1).astype(bf16)
            for q in range(2):
                dc[q] = dc[q] + mm_nt(dye[both(q)], s_in[q, :, cols])
        wred[0] = acc
        for q in range(2):
            dcs[s, both(q)] = dc[q]
        ex.start(s)

    def scan(s):
        decx[...] = spread(decs[s], sel)
        ex.scan(s, decx, True)

    @pl.when(i == seqs)
    def _():
        for s in range(seqs - 1):
            scan(s)

    @pl.when(i == seqs + 1)
    def _():
        scan(seqs - 1)

    @pl.when(i >= seqs)
    def _():
        s = i - seqs
        causal, low_lanes = masks()
        cum = cumin[0]
        for q in range(2):
            cum_t[q] = jnp.transpose(cum[both(q)])
        einx[...] = spread(softplus(vin[0]), sel)
        bb = xb[0, :, DIN : DIN + NSTATE]
        cc = xb[0, :, DIN + NSTATE :]
        for q in range(2):
            g_s[q] = mm_nt(cc[both(q)], bb[both(q)])
        dg_s[...] = jnp.zeros_like(dg_s)

        def pair_step(p):
            cols = pl.ds(pl.multiple_of(p * HALF, HALF), HALF)
            decays = pair_decays(cum, cum_t, p, causal)
            for q in range(2):
                rows = both(q)
                xsb = (xb[0, rows, cols].astype(f32) * einx[rows, cols]).astype(bf16)
                dyb = dy_s[s, rows, cols]
                dyf = dyb.astype(f32)
                grads = []
                for a in range(2):
                    m = (decays[2 * q + a] * g_s[q]).astype(bf16)
                    grads.append(mm_tn(m, dyb))
                    mine = low_lanes if a == 0 else jnp.logical_not(low_lanes)
                    dm = mm_nt(jnp.where(mine, dyf, 0.0).astype(bf16), xsb)
                    dg_s[q] += dm * decays[2 * q + a]
                dxs[0, rows, cols] = jnp.where(low_lanes, grads[0], grads[1])

        loop(0, PAIRS, pair_step)
        for q in range(2):
            rows = both(q)
            dg = dg_s[q].astype(bf16)
            dbc[0, rows, :NSTATE] = mm_tn(dg, cc[rows])
            dbc[0, rows, NSTATE:] = mm(dg, bb[rows]) + dcs[s, rows]
        live = (lax.broadcasted_iota(jnp.int32, (SPAN, 1), 0) < rel[s]).astype(f32)
        for j in range(D // TILE):
            cols = slice(j * TILE, (j + 1) * TILE)
            mixed[0, :, cols] = (live * (tok[0, :, cols].astype(f32) + mm(ml_s[s], wout[:, cols]))).astype(bf16)

    @pl.when(i == 2 * seqs - 1)
    def _():
        for s in range(seqs):
            ex.finish(s)


def third_kernel(
    cin, vin, cumin, dyin, wred, dxs, dbc, dir1, later, sin, loc, cw, cb, dl, skip,
    gz, gzh, gdelta, gcw, gcb, gdb, gdl,
    sel, dtx, eoutx, xx, sp, dact, xwb, dout, qacc, gp,
):
    s = pl.program_id(0)

    @pl.when(s == 0)
    def _():
        sel[...] = head_map()
        gcw[...] = jnp.zeros_like(gcw)
        gcb[...] = jnp.zeros_like(gcb)
        gdb[...] = jnp.zeros_like(gdb)
        gdl[...] = jnp.zeros_like(gdl)
        gp[0:RIM] = jnp.zeros((RIM, CONVW), f32)
        gp[RIM + SPAN :] = jnp.zeros((8, CONVW), f32)

    cum = cumin[0]
    v = vin[0]
    dt = softplus(v)
    e_in, e_out, tot0, tot1, total = local_decays(cum)
    dtx[...] = spread(dt, sel)
    eoutx[...] = spread(e_out, sel)
    tot1x = spread(rows_of(tot1), sel)[0:1]
    totalx = spread(rows_of(total), sel)[0:1]

    def conv_step(j):
        cols = pl.ds(pl.multiple_of(j * HALF, HALF), HALF)
        o = cb[:, cols]
        for k in range(KCONV):
            o = o + cw[k : k + 1, cols] * cin[0, RIM - KCONV + 1 + k : RIM - KCONV + 1 + k + SPAN, cols]
        sg = sigmoid(o)
        a = o * sg
        xx[:, cols] = a
        sp[:, cols] = sg + a * (1.0 - sg)

    loop(0, CONVW // HALF, conv_step)
    bb = xx[:, DIN : DIN + NSTATE].astype(bf16)
    qacc[...] = jnp.zeros_like(qacc)
    dout[1] = later[0]
    dout[0] = (dir1[0] + tot1x * later[0].astype(f32)).astype(bf16)

    def state_step(j):
        cols = pl.ds(pl.multiple_of(j * TILE, TILE), TILE)
        for q in range(2):
            rows = both(q)
            x = xx[rows, cols]
            dte = dtx[rows, cols]
            eo = eoutx[rows, cols]
            dx_s = dxs[0, rows, cols] + eo * mm(bb[rows], dout[q, :, cols])
            dact[rows, cols] = dte * dx_s + skip[:, cols] * dyin[0, rows, cols].astype(f32)
            qacc[rows] += gather_heads(x * dx_s, sel[:HALF, cols])
            xwb[rows, cols] = (x * dte * eo).astype(bf16)

    loop(0, DIN // TILE, state_step)
    for q in range(2):
        rows = both(q)
        dact[rows, DIN : DIN + NSTATE] = dbc[0, rows, :NSTATE] + mm_nt(xwb[rows, :], dout[q])
        dact[rows, DIN + NSTATE :] = dbc[0, rows, NSTATE:]

    ends = jnp.sum(later[0].astype(f32) * (totalx * sin[0].astype(f32) + loc[0].astype(f32)), axis=0, keepdims=True)
    ends = gather_heads(rows_of(ends), sel[:HALF])[0:1]
    at_end = lax.broadcasted_iota(jnp.int32, (SPAN, 1), 0) == SPAN - 1
    dcum = wred[0] - dt * qacc[...] + jnp.where(at_end, ends, 0.0)
    glog = exact_mm(triangle(SPAN, False), dcum)
    rate = jnp.exp(dl[...])
    gpd = (qacc[...] - rate * glog) * sigmoid(v)
    lanes = lax.broadcasted_iota(jnp.int32, (SPAN, HALF), 1) < HEADS
    gpd = jnp.where(lanes, gpd, 0.0)
    gdelta[0] = gpd.astype(bf16)
    gdb[...] += jnp.sum(gpd, axis=0, keepdims=True)
    gdl[...] += -rate * jnp.sum(dt * glog, axis=0, keepdims=True)

    def out_step(j):
        cols = pl.ds(pl.multiple_of(j * HALF, HALF), HALF)
        gco = dact[:, cols] * sp[:, cols]
        gp[RIM : RIM + SPAN, cols] = gco
        gcb[:, cols] += jnp.sum(gco, axis=0, keepdims=True)
        for k in range(KCONV):
            gcw[k : k + 1, cols] += jnp.sum(
                gco * cin[0, RIM - KCONV + 1 + k : RIM - KCONV + 1 + k + SPAN, cols], axis=0, keepdims=True
            )
        main = jnp.zeros((SPAN, HALF), f32)
        rim = jnp.zeros((RIM, HALF), f32)
        for k in range(KCONV):
            ahead = KCONV - 1 - k
            main = main + cw[k : k + 1, cols] * gp[RIM + ahead : RIM + ahead + SPAN, cols]
            rim = rim + cw[k : k + 1, cols] * gp[ahead : ahead + RIM, cols]
        gz[0, :, cols] = main.astype(bf16)
        gzh[0, :, cols] = rim.astype(bf16)

    loop(0, CONVW // HALF, out_step)


def fourth_kernel(
    rel, tok, halo, cot, gain, ggate, gz, gzh, gdelta, wfull,
    gtok, gtail, grim, ggain,
):
    s = pl.program_id(0)

    @pl.when(s == 0)
    def _():
        ggain[...] = jnp.zeros_like(ggain)

    def back(rows, grad):
        rows, inv, _ = normalized(rows, gain[...])
        ggain[...] += jnp.sum(grad * rows * inv, axis=0, keepdims=True)
        gained = gain[...] * grad
        mean = jnp.mean(gained * rows, axis=-1, keepdims=True)
        return inv * gained - rows * (inv * inv * inv * mean)

    grad = mm_nt(ggate[0], wfull[:, :DIN]) + mm_nt(gz[0], wfull[:, DIN:ZXW]) + mm_nt(gdelta[0], wfull[:, ZXW:])
    live = (lax.broadcasted_iota(jnp.int32, (SPAN, 1), 0) < rel[s]).astype(f32)
    out = live * cot[0].astype(f32) + back(tok[0], grad)
    gtok[0] = out.astype(bf16)
    gtail[0] = out[SPAN - RIM :]
    grim[0] = back(halo[0], mm_nt(gzh[0], wfull[:, DIN:ZXW])).astype(bf16)


def whole(shape):
    zeros = (0,) * len(shape)
    return pl.BlockSpec(shape, lambda s: zeros, pipeline_mode=pl.Buffered(1))


def summed(shape):
    zeros = (0,) * len(shape)
    return pl.BlockSpec(shape, lambda s: zeros)


def per_seq(*shape):
    zeros = (0,) * len(shape)
    return pl.BlockSpec((1,) + shape, lambda s: (s,) + zeros)


SMEM = pl.BlockSpec(memory_space=pltpu.SMEM)
ANY = pl.BlockSpec(memory_space=pl.ANY)


def staged(seqs, phase, *shape):
    zeros = (0,) * len(shape)
    if phase == 0:
        return pl.BlockSpec((1,) + shape, lambda i: (jnp.minimum(i, seqs - 1),) + zeros)
    if phase == 1:
        return pl.BlockSpec((1,) + shape, lambda i: (jnp.maximum(i - seqs, 0),) + zeros)
    return pl.BlockSpec((1,) + shape, lambda i: (lax.rem(i, seqs),) + zeros)


def call(kernel, steps, in_specs, outs, scratch, name, collective=None):
    params = dict(vmem_limit_bytes=VMEM_LIMIT)
    if collective is not None:
        params.update(collective_id=collective, has_side_effects=True)
    return pl.pallas_call(
        kernel,
        grid=(steps,),
        in_specs=in_specs,
        out_specs=[o[0] for o in outs],
        out_shape=[jax.ShapeDtypeStruct(o[1], o[2]) for o in outs],
        scratch_shapes=[pltpu.VMEM(*sc) if isinstance(sc, tuple) else sc for sc in scratch],
        compiler_params=pltpu.CompilerParams(**params),
        name=name,
    )


def exchange_scratch(seqs, count):
    parts = min(count, 8)
    rows = NSTATE // parts
    dma = pltpu.SemaphoreType.DMA
    buffers = [((count * 8, DIN), f32), ((seqs, NSTATE, DIN), bf16), ((seqs, count, rows, DIN), bf16),
               ((seqs, count, rows, DIN), bf16)]
    sems = [dma((seqs, parts)), dma((seqs, count)), dma((seqs, count)), dma((seqs, parts)), dma((seqs,))]
    return buffers, sems


def passed_along(value, axis, steps):
    count = lax.axis_size(axis)
    leading, last = (max(0, -steps), min(count, count - steps))
    return lax.ppermute(value, axis, [(source, source + steps) for source in range(leading, last)])


def lanes_of(v):
    return jnp.pad(v[None, :], ((0, 0), (0, HALF - v.shape[0])))


def local(
    tokens_in, seq_lengths, norm_gain, w_zx, w_delta, w_out, conv_weight, conv_bias,
    delta_bias, decay_log, skip_gain, gated_gain, cotangent,
):
    seqs = tokens_in.shape[0]
    count = lax.axis_size("ctx")
    group = lax.axis_size("group")
    chips = max(group // 2, 1)
    rel = seq_lengths - lax.axis_index("ctx") * SPAN
    gain = norm_gain[None, :]
    cb = conv_bias[None, :]
    db = lanes_of(delta_bias)
    dl = lanes_of(decay_log)
    skip = jnp.repeat(skip_gain, HEADDIM)[None, :]
    ggain = gated_gain[None, :]
    wcat = jnp.concatenate([w_zx, jnp.pad(w_delta, ((0, 0), (0, HALF - HEADS)))], axis=1)
    buffers, sems = exchange_scratch(seqs, count)
    dma = pltpu.SemaphoreType.DMA
    at0 = lambda *shape: staged(seqs, 0, *shape)
    at1 = lambda *shape: staged(seqs, 1, *shape)
    at01 = lambda *shape: staged(seqs, 2, *shape)

    normed, nhalo, cin, xb, vraw, cum, st0, loc, ylocal, gate, decs, wfull, wofull, state_in = call(
        front_kernel,
        2 * seqs,
        [at0(SPAN, D), ANY, ANY, ANY, whole((1, D)), whole((KCONV, CONVW)), whole((1, CONVW)), whole((1, HALF)),
         whole((1, HALF))],
        [
            (at0(SPAN, D), (seqs, SPAN, D), bf16),
            (at0(RIM, D), (seqs, RIM, D), bf16),
            (at0(RIM + SPAN, CONVW), (seqs, RIM + SPAN, CONVW), f32),
            (at0(SPAN, CONVW), (seqs, SPAN, CONVW), bf16),
            (at0(SPAN, HALF), (seqs, SPAN, HALF), f32),
            (at0(SPAN, HALF), (seqs, SPAN, HALF), f32),
            (at0(NSTATE, DIN), (seqs, NSTATE, DIN), f32),
            (at0(NSTATE, DIN), (seqs, NSTATE, DIN), bf16),
            (at1(SPAN, DIN), (seqs, SPAN, DIN), f32),
            (at1(SPAN, DIN), (seqs, SPAN, DIN), f32),
            (summed((seqs, count * 8, HALF)), (seqs, count * 8, HALF), f32),
            (ANY, (D, ZXW + HALF), bf16),
            (ANY, (DIN, D), bf16),
            (ANY, (seqs, NSTATE, DIN), bf16),
        ],
        [((2 * HALF, DIN), bf16), ((seqs, RIM, D), bf16), ((RIM + SPAN, D), bf16), ((seqs, SPAN, D), bf16),
         ((seqs, SPAN, CONVW), bf16), ((seqs, SPAN, HALF), f32), ((seqs, SPAN, HALF), f32), ((2, HALF, HALF), f32),
         ((D, CONVW + HALF), bf16), ((D, DIN), bf16), ((SPAN, DIN), f32), ((seqs, count * 8, HALF), f32)]
        + buffers
        + [dma((2,)), dma((3, chips)), dma((3, chips)), dma((3, chips)), dma((3, chips)), dma((3,)), dma((2,))]
        + sems
        + [dma((seqs, min(count, 8))), dma((seqs, count))],
        "front",
        0,
    )(tokens_in, tokens_in, wcat, w_out, gain, conv_weight, cb, db, dl)

    mixed_out, mlow, dy, ggate, wred, dir1, gskip, gggain, dxs, dbc, later = call(
        middle_kernel,
        2 * seqs,
        [SMEM, at1(SPAN, D), at0(SPAN, D), at0(SPAN, DIN), at0(SPAN, DIN), at01(SPAN, CONVW), at01(SPAN, HALF),
         at01(SPAN, HALF), at0(NSTATE, DIN), at0(NSTATE, DIN), whole((seqs, count * 8, HALF)), whole((DIN, D)),
         whole((1, DIN)), whole((1, DIN))],
        [
            (at1(SPAN, D), (seqs, SPAN, D), bf16),
            (at0(SPAN, DIN), (seqs, SPAN, DIN), bf16),
            (at0(SPAN, DIN), (seqs, SPAN, DIN), bf16),
            (at0(SPAN, DIN), (seqs, SPAN, DIN), bf16),
            (at0(SPAN, HALF), (seqs, SPAN, HALF), f32),
            (at0(NSTATE, DIN), (seqs, NSTATE, DIN), f32),
            (summed((1, DIN)), (1, DIN), f32),
            (summed((1, DIN)), (1, DIN), f32),
            (at1(SPAN, DIN), (seqs, SPAN, DIN), f32),
            (at1(SPAN, 2 * NSTATE), (seqs, SPAN, 2 * NSTATE), f32),
            (ANY, (seqs, NSTATE, DIN), bf16),
        ],
        [((2 * HALF, DIN), bf16), ((2, HALF, HALF), f32), ((SPAN, DIN), f32), ((SPAN, DIN), f32), ((SPAN, DIN), f32),
         ((SPAN, DIN), f32), ((2, NSTATE, DIN), bf16), ((seqs, SPAN, HALF), f32), ((seqs, SPAN, DIN), bf16),
         ((seqs, SPAN, DIN), bf16), ((2, HALF, HALF), f32), ((2, HALF, HALF), f32)]
        + buffers
        + sems,
        "middle",
        1,
    )(rel, tokens_in, cotangent, ylocal, gate, xb, vraw, cum, st0, state_in, decs, wofull, skip, ggain)

    gz, gzh, gdelta, gcw, gcb, gdb, gdl = call(
        third_kernel,
        seqs,
        [per_seq(RIM + SPAN, CONVW), per_seq(SPAN, HALF), per_seq(SPAN, HALF), per_seq(SPAN, DIN), per_seq(SPAN, HALF),
         per_seq(SPAN, DIN), per_seq(SPAN, 2 * NSTATE), per_seq(NSTATE, DIN), per_seq(NSTATE, DIN), per_seq(NSTATE, DIN),
         per_seq(NSTATE, DIN), whole((KCONV, CONVW)), whole((1, CONVW)), whole((1, HALF)), whole((1, DIN))],
        [
            (per_seq(SPAN, CONVW), (seqs, SPAN, CONVW), bf16),
            (per_seq(RIM, CONVW), (seqs, RIM, CONVW), bf16),
            (per_seq(SPAN, HALF), (seqs, SPAN, HALF), bf16),
            (summed((KCONV, CONVW)), (KCONV, CONVW), f32),
            (summed((1, CONVW)), (1, CONVW), f32),
            (summed((1, HALF)), (1, HALF), f32),
            (summed((1, HALF)), (1, HALF), f32),
        ],
        [((2 * HALF, DIN), bf16), ((SPAN, DIN), f32), ((SPAN, DIN), f32), ((SPAN, CONVW), f32), ((SPAN, CONVW), f32),
         ((SPAN, CONVW), f32), ((SPAN, DIN), bf16), ((2, NSTATE, DIN), bf16), ((SPAN, HALF), f32),
         ((RIM + SPAN + 8, CONVW), f32)],
        "third",
    )(cin, vraw, cum, dy, wred, dxs, dbc, dir1, later, state_in, loc, conv_weight, cb, dl, skip)

    live = (jnp.arange(SPAN, dtype=jnp.int32)[None, :] < rel[:, None]).astype(f32)[:, :, None]
    drive = (live * cotangent.astype(f32)).astype(bf16)
    flat = lambda v: v.reshape(-1, v.shape[-1])
    g_out = mm_tn(flat(mlow), flat(drive))
    g_gate = mm_tn(flat(normed), flat(ggate))
    g_conv = mm_tn(flat(normed), flat(gz)) + mm_tn(flat(nhalo), flat(gzh))
    g_delta = mm_tn(flat(normed), flat(gdelta))

    halo = passed_along(tokens_in[:, SPAN - RIM :, :], "ctx", 1)
    gtok, gtail, grim, g_gain = call(
        fourth_kernel,
        seqs,
        [SMEM, per_seq(SPAN, D), per_seq(RIM, D), per_seq(SPAN, D), whole((1, D)), per_seq(SPAN, DIN), per_seq(SPAN, CONVW),
         per_seq(RIM, CONVW), per_seq(SPAN, HALF), whole((D, ZXW + HALF))],
        [
            (per_seq(SPAN, D), (seqs, SPAN, D), bf16),
            (per_seq(RIM, D), (seqs, RIM, D), f32),
            (per_seq(RIM, D), (seqs, RIM, D), bf16),
            (summed((1, D)), (1, D), f32),
        ],
        [],
        "fourth",
    )(rel, tokens_in, halo, cotangent, gain, ggate, gz, gzh, gdelta, wfull)
    grim = passed_along(grim, "ctx", -1)
    gtok = lax.dynamic_update_slice(gtok, (gtail + grim.astype(f32)).astype(bf16), (0, SPAN - RIM, 0))

    def reduced(g):
        part = lax.psum_scatter(g.astype(bf16), "group", scatter_dimension=0, tiled=True)
        return lax.psum(part, "ctx").astype(f32)

    g_zx = jnp.concatenate([reduced(g_gate), reduced(g_conv)], axis=1)
    g_out = reduced(g_out)
    g_delta = reduced(g_delta)[:, :HEADS]
    small = jnp.concatenate(
        [g_gain.reshape(-1), gcw.reshape(-1), gcb.reshape(-1), gdb[0], gdl[0],
         gskip.reshape(-1), gggain.reshape(-1)]
    )
    small = lax.psum(small, ("group", "ctx"))
    at = 0
    pieces = []
    for size in (D, KCONV * CONVW, CONVW, HALF, HALF, DIN, DIN):
        pieces.append(small[at : at + size])
        at += size
    return (
        mixed_out, gtok, pieces[0], g_zx, g_delta, g_out, pieces[1].reshape(KCONV, CONVW), pieces[2],
        pieces[3][:HEADS], pieces[4][:HEADS], pieces[5].reshape(HEADS, HEADDIM).sum(1), pieces[6],
    )


def solution(mesh):
    rows = P("group", "ctx", None)
    own = P("group", None)
    in_specs = (rows, P("group"), P(), own, own, own, P(), P(), P(), P(), P(), P(), rows)
    out_specs = (rows, rows, P(), own, own, own, P(), P(), P(), P(), P(), P())
    return jax.shard_map(local, mesh=mesh, in_specs=in_specs, out_specs=out_specs, check_vma=False)
```

time: 571 us -> 482 us (0.84)
  Pallas kernels: 156 us -> 267 us
  blocking collectives: 180 us -> 78 us
  waiting for transfers between devices: 147 us -> 67.2 us
  starting transfers between devices: 19.8 us -> 6.28 us
    pallas_call x2, Pallas kernels: 76.7 us -> 207 us  [the longest x1 120 us: local(): call(front_kernel, 2 * seqs, [at0(SPAN, D), ANY, ANY, ANY, whole((1, D)),...]
    all_gather x2 -> x0, blocking collectives: 61.7 us -> none  [the longest x1 56.3 us: state_scan(): decays = lax.all_gather(decay, 'ctx', axis=0)]
    all_to_all x3 -> x0, waiting for transfers between devices: 59.9 us -> none  [the longest x1 30.7 us: state_scan(): back = lax.all_to_all(back, 'ctx', 0, 0, tiled=True)]
    all_to_all x1 -> x0, blocking collectives: 40.3 us -> none  [state_scan(): back = lax.all_to_all(back, 'ctx', 0, 0, tiled=True)]
    all_gather x2 -> x0, waiting for transfers between devices: 29.8 us -> none  [the longest x1 29.8 us: local(): full_zx = lax.all_gather(w_zx, 'group', axis=0, tiled=True)]
    pallas_call x1, Pallas kernels: 64.7 us -> 45.7 us  [local(): call(third_kernel, seqs, [per_seq(RIM + SPAN, CONVW), per_seq(SPAN, HALF)...]
    all_to_all x3 -> x0, starting transfers between devices: 13.2 us -> none  [the longest x2 9.44 us: state_scan(): moved = lax.all_to_all(moved, 'ctx', 0, 0, tiled=True)]
    reduce_scatter x4, waiting for transfers between devices: 14.5 us -> 24.8 us  [reduced(): lax.psum_scatter(g.astype(bf16), 'group', scatter_dimension=0, tiled=True)]
  transfers between devices with their start and end apart: 12 -> 7, of which waited for: 5 -> 3; matrix products, arithmetic and copies ran while one was open for 7% -> 5% of each run, Pallas kernels for 14% -> 12%
where the time goes in v2:
time: 482 us; the launch traced here: 481 us
  Pallas kernels  267 us (55%)
  blocking collectives  78 us (16%)
  waiting for transfers between devices  67.2 us (14%)
  matrix products  20.9 us (4%)
  local copies, waits for them, and re-layouts  15.8 us (3%)
  between operations  14.1 us (3%)
  other arithmetic  11.2 us (2%)
  starting transfers between devices  6.28 us (1%)
    pallas_call x1, Pallas kernels, local(): call(front_kernel, 2 * seqs, [at0(SPAN, D), ANY, ANY, ANY, whole((1, D)),...  120 us
    pallas_call x1, Pallas kernels, local(): call(middle_kernel, 2 * seqs, [SMEM, at1(SPAN, D), at0(SPAN, D), at0(SPAN...  87.1 us
    pallas_call x1, Pallas kernels, local(): call(third_kernel, seqs, [per_seq(RIM + SPAN, CONVW), per_seq(SPAN, HALF)...  45.7 us
    psum x1, waiting for transfers between devices, reduced(): return lax.psum(part, 'ctx').astype(f32)  40.3 us
    psum x1, blocking collectives, local(): small = lax.psum(small, ('group', 'ctx'))  39.9 us
    psum x1, blocking collectives, reduced(): return lax.psum(part, 'ctx').astype(f32)  38.1 us
    reduce_scatter x4, waiting for transfers between devices, reduced(): lax.psum_scatter(g.astype(bf16), 'group', scatter_dimension=0, tiled=True)  24.8 us
    dot_general x5, matrix products, mm_tn(): return lax.dot_general(a, b, TN, preferred_element_type=f32)  20.9 us
  transfers between devices with their start and end apart: 7, of which 3 were waited for; matrix products, arithmetic and copies ran while one was open for 5% of the time, Pallas kernels for 12%

profile of v2, /device:TPU:0, one launch (start us, length us, event | category | flops | bytes accessed | tf_op | source)
XLA Modules:
  0.0 480.8 jit_solution(11807895098588779312)
XLA Ops:
  7.2 1.3 broadcast_in_dim.22.cb
  8.5 1.3 broadcast_in_dim.21.gain
  9.8 0.8 copy.31
  10.6 1.2 pad.13.dl
  11.8 1.2 pad.12.db
  13.0 0.7 broadcast_in_dim.25
  14.4 1.3 broadcast_in_dim.26.ggain
  15.7 2.5 fusion.3.wcat
  18.6 120.1 %front.1 = (bf16[4,256,768]{2,1,0:T(8,128)(2,1)}, bf16[4,16,768]{2,1,0:T(8,128)(2,1)}, f32[4,272,1792]{2,1,0:T(8,128)}, bf16[4,256,1792]{2,1,0:T(8,128)(2,1)}, f...) custom-call(bf16[4,256,768]{2,1,0:T(8,128)(2,1)} %tok.5, ...), custom_call_target="tpu_custom_call" | custom-call | tf_op jit(solution)/shard_map/front/pallas_call | solution.py:825
  138.7 87.1 %middle.1 = (bf16[4,256,768]{2,1,0:T(8,128)(2,1)}, bf16[4,256,1536]{2,1,0:T(8,128)(2,1)}, bf16[4,256,1536]{2,1,0:T(8,128)(2,1)}, bf16[4,256,1536]{2,1,0:T(8,128)...) custom-call(s32[4]{0:T(128)} %broadcast_subtract_fusion.rel, ...), custom_call_target="tpu_custom_call" | custom-call | tf_op jit(solution)/shard_map/middle/pallas_call | solution.py:857
  225.9 5.9 %bitcast_convert_fusion.1 = bf16[768,1536]{1,0:T(8,128)(2,1)} fusion(bf16[4,256,768]{2,1,0:T(8,128)(2,1)S(1)} %copy-done.1, bf16[4,256,1536]{2,1,0:T(8,128)(2,1)} %get-tuple-element.58.ggate), kind=kOutput, calls=%fused_computation.3 | convolution fusion | flops 2417098752 | bytes 7077888 | tf_op jit(solution)/shard_map/dot_general | solution.py:39
  232.0 6.1 %bitcast_convert_fusion = bf16[1536,768]{1,0:T(8,128)(2,1)} fusion(bf16[4,256,1536]{2,1,0:T(8,128)(2,1)} %get-tuple-element.83, bf16[4,256,768]{2,1,0:T(8,128)(2,1)S(1)} %copy-done, f32[4,256]{1,0:T(4,128)S(1)} %fusion.6), kind=kOutput, calls=%fused_computation.2 | convolution fusion | flops 2419458048 | bytes 7081984 | tf_op jit(solution)/shard_map/dot_general | solution.py:39
  238.2 45.7 %third.1 = (bf16[4,256,1792]{2,1,0:T(8,128)(2,1)}, bf16[4,16,1792]{2,1,0:T(8,128)(2,1)}, bf16[4,256,128]{2,1,0:T(8,128)(2,1)}, f32[4,1792]{1,0:T(4,128)}, f32[1,...) custom-call(f32[4,272,1792]{2,1,0:T(8,128)} %get-tuple-element.59.cin, f32[4,256,128]{2,1,0:T(8,128)} %get-tuple-element.51.vin, ...), custom_call_target="tpu_custom_call" | custom-call | tf_op jit(solution)/shard_map/third/pallas_call | solution.py:885
  283.9 5.2 %fusion.9 = f32[768,1792,1]{1,0,2:T(8,128)S(1)} fusion(bf16[4,256,768]{2,1,0:T(8,128)(2,1)S(1)} %copy-done.1, bf16[4,256,1792]{2,1,0:T(8,128)(2,1)} %get-tuple-element.67.gz), kind=kOutput, calls=%fused_computation.27 | convolution fusion | flops 2818572288 | bytes 10747904 | tf_op jit(solution)/shard_map/dot_general | solution.py:39
  289.1 2.4 fusion
  291.7 0.9 copy-done.3
  292.5 1.3 fusion.4
  293.9 0.9 slice.42
  294.8 4.8 collective-permute-start
  299.7 2.0 collective-permute-done.halo
  302.4 14.3 %fourth.1 = (bf16[4,256,768]{2,1,0:T(8,128)(2,1)}, f32[4,16,768]{2,1,0:T(8,128)}, bf16[4,16,768]{2,1,0:T(8,128)(2,1)}, f32[1,768]{1,0:T(1,128)}) custom-call(s32[4]{0:T(128)} %broadcast_subtract_fusion.rel, bf16[4,256,768]{2,1,0:T(8,128)(2,1)} %tok.5, bf16[4,16,768]{2,1,0:T(8,128)(2,1)} %copy-done.5, bf16[4,256,768]{2,1,0:T(8,128)(2,1)} %cot.3, ...), custom_call_target="tpu_custom_call" | custom-call | tf_op jit(solution)/shard_map/fourth/pallas_call | solution.py:915
  316.7 0.7 reduce
  317.4 1.3 collective-permute-start.1
  318.8 24.7 %reduce-scatter.7.cloned.1.call-done = bf16[192,1792]{1,0:T(8,128)(2,1)} async-done(((bf16[768,1792]{1,0:T(8,128)(2,1)}), bf16[192,1792]{1,0:T(8,128)(2,1)}) %reduce-scatter.7.cloned.1.call-update) | async-done | bytes 688144 | tf_op jit(solution)/shard_map/reduce_scatter | solution.py:933
  343.7 39.9 %psum.35 = f32[13056]{0:T(1024)S(1)} all-reduce(f32[13056]{0:T(1024)S(1)} %constant_dynamic-update-slice_fusion), channel_id=1, replica_groups=mesh['group'=4,'ctx'=8] {'group','ctx'}, use_global_device_ids=true, to_apply=%region_0.1 | all-reduce | flops 13056 | bytes 104448 | tf_op jit(solution)/shard_map/psum | solution.py:943
  387.3 1.6 fusion.5
  388.9 38.1 %psum.38 = bf16[192,128]{1,0:T(8,128)(2,1)S(1)} all-reduce(bf16[192,128]{1,0:T(8,128)(2,1)} %reduce-scatter.9.cloned.1.call-done), channel_id=1, replica_groups=mesh['group'=4,'ctx'=8] {'ctx'}, use_global_device_ids=true, to_apply=%region_6.7 | all-reduce | flops 24576 | bytes 98304 | tf_op jit(solution)/shard_map/psum | solution.py:934
  426.9 0.7 copy.36
  427.6 40.3 %all-reduce.6.cloned.1.call-done = (bf16[192,1792]{1,0:T(8,128)(2,1)}, bf16[192,1536]{1,0:T(8,128)(2,1)}, bf16[384,768]{1,0:T(8,128)(2,1)}) async-done(((bf16[192,1792]{1,0:T(8,128)(2,1)}, bf16[192,1536]{1,0:T(8,128)(2,1)}, bf16[384,768]{1,0:T(8,128)(2,1)}), (bf16[192,1792]{1,0:T(8,128)(2,1)}, bf16[192,1536]{1,0:T(8,128)(2,1)}, bf16[384,768]{1,0:T(8,128)(2,1)})) %all-reduce.6.cloned.1.call-update) | async-done | bytes 1867792 | tf_op jit(solution)/shard_map/psum | solution.py:934
  467.9 2.3 convert_element_type.51
  470.2 2.9 maximum_convert_fusion
  473.1 1.1 copy.53
  (67 shorter events, 6.1 us)
Async XLA Ops:
  7.2 10.9 %copy-start.12 = (s32[4]{0:T(128)S(1)}, s32[4]{0:T(128)}, u32[]{:S(2)}) copy-start(s32[4]{0:T(128)} %param.14) | copy-start | bytes 52
  7.2 311.6 %reduce-scatter.5.cloned.1.call-start = ((), (), s32[]{:S(2)}) async-start(), calls=%async_computation.4 | async-start | bytes 2949120 | tf_op jit(solution)/shard_map/reduce_scatter | solution.py:933
  138.7 87.2 %copy-start.1 = (bf16[4,256,768]{2,1,0:T(8,128)(2,1)S(1)}, bf16[4,256,768]{2,1,0:T(8,128)(2,1)}, u32[]{:S(2)}) copy-start(bf16[4,256,768]{2,1,0:T(8,128)(2,1)} %get-tuple-element.81) | copy-start | bytes 4718596
  225.9 6.0 %copy-start.10 = (s32[4]{0:T(128)S(1)}, s32[4]{0:T(128)}, u32[]{:S(2)}) copy-start(s32[4]{0:T(128)} %broadcast_subtract_fusion.rel) | copy-start | bytes 52
  225.9 6.1 %copy-start = (bf16[4,256,768]{2,1,0:T(8,128)(2,1)S(1)}, bf16[4,256,768]{2,1,0:T(8,128)(2,1)}, u32[]{:S(2)}) copy-start(bf16[4,256,768]{2,1,0:T(8,128)(2,1)} %cot.3) | copy-start | bytes 4718596
  231.8 87.0 %reduce-scatter.11.cloned.1.call-start = ((), (), s32[]{:S(2)}) async-start(), calls=%async_computation.7 | async-start | bytes 2949120 | tf_op jit(solution)/shard_map/reduce_scatter | solution.py:933
  238.1 105.4 %reduce-scatter.7.cloned.1.call-start = ((), (), s32[]{:S(2)}) async-start(), calls=%async_computation.5 | async-start | bytes 3440640 | tf_op jit(solution)/shard_map/reduce_scatter | solution.py:933
  283.9 5.2 %copy-start.4 = (bf16[4,16,1792]{2,1,0:T(8,128)(2,1)S(1)}, bf16[4,16,1792]{2,1,0:T(8,128)(2,1)}, u32[]{:S(2)}) copy-start(bf16[4,16,1792]{2,1,0:T(8,128)(2,1)} %get-tuple-element.68.gzh) | copy-start | bytes 688132
  283.9 5.2 %copy-start.11 = (bf16[4,16,768]{2,1,0:T(8,128)(2,1)S(1)}, bf16[4,16,768]{2,1,0:T(8,128)(2,1)}, u32[]{:S(2)}) copy-start(bf16[4,16,768]{2,1,0:T(8,128)(2,1)} %get-tuple-element.82) | copy-start | bytes 294916
  291.6 0.9 copy-start.3
  291.6 8.0 %copy-start.6 = (f32[4,1792]{1,0:T(4,128)S(1)}, f32[4,1792]{1,0:T(4,128)}, u32[]{:S(2)}) copy-start(f32[4,1792]{1,0:T(4,128)} %get-tuple-element.75) | copy-start | bytes 86020
  291.6 8.0 %copy-start.7 = (f32[1,1792]{1,0:T(1,128)S(1)}, f32[1,1792]{1,0:T(1,128)}, u32[]{:S(2)}) copy-start(f32[1,1792]{1,0:T(1,128)} %get-tuple-element.76) | copy-start | bytes 21508
  291.6 8.1 %copy-start.9 = (f32[1,1536]{1,0:T(1,128)S(1)}, f32[1,1536]{1,0:T(1,128)}, u32[]{:S(2)}) copy-start(f32[1,1536]{1,0:T(1,128)} %get-tuple-element.79) | copy-start | bytes 18436
  291.6 8.1 %copy-start.8 = (f32[1,1536]{1,0:T(1,128)S(1)}, f32[1,1536]{1,0:T(1,128)}, u32[]{:S(2)}) copy-start(f32[1,1536]{1,0:T(1,128)} %get-tuple-element.80) | copy-start | bytes 18436
  291.6 97.2 %reduce-scatter.9.cloned.1.call-start = ((), (), s32[]{:S(2)}) async-start(), calls=%async_computation.6 | async-start | bytes 245760 | tf_op jit(solution)/shard_map/reduce_scatter | solution.py:933
  293.8 174.1 %all-reduce.6.cloned.1.call-start = ((), (), s32[]{:S(2)}) async-start(), calls=%async_computation.8 | async-start | bytes 3735552 | tf_op jit(solution)/shard_map/psum | solution.py:934
  294.8 7.0 %collective-permute-start = (bf16[4,16,768]{2,1,0:T(8,128)(2,1)S(1)}, bf16[4,16,768]{2,1,0:T(8,128)(2,1)S(1)}, u32[]{:S(2)}, u32[]{:S(2)}) collective-permute-start(bf16[4,16,768]{2,1,0:T(8,128)(2,1)S(1)} %slice.42), channel_id=1, source_target_pairs={{0,1},{1,2},{2,3},{3,4},{4,5},{5,6},{6,7},{8,9},{9,10},{10,11},{11... | collective-permute-start | bytes 294920 | tf_op jit(solution)/shard_map/ppermute | solution.py:796
  301.8 0.6 copy-start.5
  302.4 41.2 %copy-start.14 = (f32[1,128]{1,0:T(1,128)S(1)}, f32[1,128]{1,0:T(1,128)}, u32[]{:S(2)}) copy-start(f32[1,128]{1,0:T(1,128)} %get-tuple-element.77) | copy-start | bytes 1540
  302.4 41.2 %copy-start.13 = (f32[1,128]{1,0:T(1,128)S(1)}, f32[1,128]{1,0:T(1,128)}, u32[]{:S(2)}) copy-start(f32[1,128]{1,0:T(1,128)} %get-tuple-element.78) | copy-start | bytes 1540
  317.4 69.8 %collective-permute-start.1 = (bf16[4,16,768]{2,1,0:T(8,128)(2,1)}, bf16[4,16,768]{2,1,0:T(8,128)(2,1)S(1)}, u32[]{:S(2)}, u32[]{:S(2)}) collective-permute-start(bf16[4,16,768]{2,1,0:T(8,128)(2,1)} %get-tuple-element.73), channel_id=1, source_target_pairs={{1,0},{2,1},{3,2},{4,3},{5,4},{6,5},{7,6},{9,8},{10,9},{11,10},{12... | collective-permute-start | bytes 294920 | tf_op jit(solution)/shard_map/ppermute | solution.py:796
  467.9 5.2 %copy-start.2 = (bf16[4,256,768]{2,1,0:T(8,128)(2,1)S(1)}, bf16[4,256,768]{2,1,0:T(8,128)(2,1)}, u32[]{:S(2)}) copy-start(bf16[4,256,768]{2,1,0:T(8,128)(2,1)} %get-tuple-element.127) | copy-start | bytes 4718596
Sparse Core Ops, SparseCore 0:
  231.9 37.6 reduce-scatter.4
  272.4 33.0 reduce-scatter.10
  308.0 35.4 reduce-scatter.6
  346.0 19.7 reduce-scatter.8
  370.0 97.8 all-reduce.5

commit v3 on v2

--- a/solution.py
+++ b/solution.py
@@ -25,6 +25,10 @@
 NT = (((1,), (1,)), ((), ()))
 TN = (((0,), (0,)), ((), ()))
 VMEM_LIMIT = 62 * 1024 * 1024
+GATE_CHUNK = 512
+OUT_CHUNK = 256
+CONV_CHUNK = 512
+GZW = 2048
 
 
 def mm(a, b):
@@ -274,6 +278,218 @@
                 self.mate(d).wait_send()
 
 
+def owner_count(rows, width, by_rows, outer):
+    fits = lambda n: (rows // 2) % (16 * n) == 0 if by_rows else width % (128 * n) == 0
+    return max(n for n in (1, 2, 4) if outer % n == 0 and fits(n))
+
+
+class Reducer:
+    def __init__(self, part, out, rows, width, by_rows, bufs, sems):
+        self.part, self.out, self.rows, self.width, self.by_rows = part, out, rows, width, by_rows
+        self.m_buf, self.x_src, self.x_buf, self.y_src, self.y_buf, self.z_src, self.z_buf, self.full = bufs
+        self.sems = sems
+        self.chunks = part.shape[1] // width
+        self.group = lax.axis_index("group")
+        self.cores = 2
+        self.chips = lax.axis_size("group") // 2
+        self.core = lax.rem(self.group, 2)
+        self.chip = self.group // 2
+        self.ctx = lax.axis_index("ctx")
+        self.outer = lax.axis_size("ctx") // 2
+        self.owners = owner_count(rows, width, by_rows, self.outer)
+        self.stride = self.outer // self.owners
+        self.inner = lax.rem(self.ctx, 2)
+        self.line = self.ctx // 2
+        self.mine = self.line // self.stride
+        self.half = rows // 2
+
+    def cols(self, k):
+        return pl.ds(pl.multiple_of(k * self.width, self.width), self.width)
+
+    def member(self, chip, core):
+        return pl.ds(pl.multiple_of((chip * 2 + core) * self.rows, 64), self.rows)
+
+    def half_rows(self, inner):
+        return pl.ds(pl.multiple_of(inner * self.half, 16), self.half)
+
+    def piece(self, j, base):
+        if self.by_rows:
+            n = self.half // self.owners
+            return pl.ds(pl.multiple_of(base + j * n, 16), n), pl.ds(0, self.width)
+        n = self.width // self.owners
+        return pl.ds(pl.multiple_of(base, 16), self.half), pl.ds(pl.multiple_of(j * n, 128), n)
+
+    def m_copy(self, k, chip):
+        return remote(
+            self.part.at[self.member(chip, 1 - self.core), self.cols(k)], self.m_buf.at[k, chip],
+            self.sems.at[0, k, chip], self.sems.at[1, k, chip], group=self.group + 1 - 2 * self.core,
+        )
+
+    def x_copy(self, k, chip, sender):
+        return remote(
+            self.x_src.at[k, chip], self.x_buf.at[k, sender], self.sems.at[2, k, chip], self.sems.at[3, k, sender],
+            group=chip * 2 + self.core,
+        )
+
+    def y_copy(self, k):
+        return remote(
+            self.y_src.at[k, self.half_rows(1 - self.inner)], self.y_buf.at[k], self.sems.at[4, k, 0], self.sems.at[5, k, 0],
+            ctx=self.ctx + 1 - 2 * self.inner,
+        )
+
+    def z_copy(self, k, j, sender):
+        rows, cols = self.piece(j, 0)
+        return remote(
+            self.z_src.at[k, rows, cols], self.z_buf.at[k, sender], self.sems.at[6, k, j], self.sems.at[7, k, sender],
+            ctx=j * self.stride * 2 + self.inner,
+        )
+
+    def b_copy(self, k, line, j):
+        rows, cols = self.piece(j, self.inner * self.half)
+        return remote(
+            self.full.at[k, rows, cols], self.full.at[k, rows, cols], self.sems.at[8, k, line], self.sems.at[9, k, j],
+            ctx=line * 2 + self.inner,
+        )
+
+    def f_copy(self, k, inner):
+        rows = self.half_rows(inner)
+        return remote(
+            self.full.at[k, rows], self.full.at[k, rows], self.sems.at[10, k, 0], self.sems.at[11, k, 0],
+            ctx=self.ctx + 1 - 2 * self.inner,
+        )
+
+    def other_chips(self, body):
+        for d in range(1, self.chips):
+            body(lax.rem(self.chip + d, self.chips))
+
+    def other_owners(self, body):
+        if self.stride == 1:
+            for d in range(1, self.owners):
+                body(lax.rem(self.mine + d, self.owners))
+        else:
+            for j in range(self.owners):
+                pl.when(j * self.stride != self.line)(lambda j=j: body(j))
+
+    def other_lines(self, body):
+        loop(1, self.outer, lambda d: body(lax.rem(self.line + d, self.outer)))
+
+    def if_owner(self, body):
+        if self.stride == 1:
+            body()
+        else:
+            pl.when(self.mine * self.stride == self.line)(body)
+
+    def m_start(self, k):
+        for chip in range(self.chips):
+            self.m_copy(k, chip).start()
+
+    def m_done(self, k):
+        for chip in range(self.chips):
+            self.m_copy(k, chip).wait_recv()
+            own = self.part[self.member(chip, self.core), self.cols(k)].astype(f32)
+            self.x_src[k, chip] = (own + self.m_buf[k, chip].astype(f32)).astype(bf16)
+        self.other_chips(lambda chip: self.x_copy(k, chip, self.chip).start())
+
+    def x_done(self, k):
+        total = self.x_src[k, self.chip].astype(f32)
+        for d in range(1, self.chips):
+            chip = lax.rem(self.chip + d, self.chips)
+            self.x_copy(k, chip, chip).wait_recv()
+            total = total + self.x_buf[k, chip].astype(f32)
+        self.y_src[k] = total.astype(bf16)
+        self.y_copy(k).start()
+
+    def y_done(self, k):
+        self.y_copy(k).wait_recv()
+        own = self.y_src[k, self.half_rows(self.inner), :].astype(f32)
+        self.z_src[k] = (own + self.y_buf[k].astype(f32)).astype(bf16)
+        self.other_owners(lambda j: self.z_copy(k, j, self.line).start())
+
+    def z_done(self, k):
+        def run():
+            rows, cols = self.piece(self.mine, 0)
+            self.other_lines(lambda line: self.z_copy(k, self.mine, line).wait_recv())
+            self.z_buf[k, self.line] = self.z_src[k, rows, cols]
+            total = self.z_buf[k, 0].astype(f32)
+            for line in range(1, self.outer):
+                total = total + self.z_buf[k, line].astype(f32)
+            rows, cols = self.piece(self.mine, self.inner * self.half)
+            self.full[k, rows, cols] = total.astype(bf16)
+            self.other_lines(lambda line: self.b_copy(k, line, self.mine).start())
+
+        self.if_owner(run)
+
+    def b_done(self, k):
+        self.other_owners(lambda j: self.b_copy(k, self.line, j).wait_recv())
+        self.f_copy(k, self.inner).start()
+
+    def f_done(self, k):
+        self.f_copy(k, 1 - self.inner).wait_recv()
+        self.out[:, self.cols(k)] = self.full[k]
+
+    def drain(self, k):
+        for chip in range(self.chips):
+            self.m_copy(k, chip).wait_send()
+        self.other_chips(lambda chip: self.x_copy(k, chip, self.chip).wait_send())
+        self.y_copy(k).wait_send()
+        self.other_owners(lambda j: self.z_copy(k, j, self.line).wait_send())
+        self.if_owner(lambda: self.other_lines(lambda line: self.b_copy(k, line, self.mine).wait_send()))
+        self.f_copy(k, self.inner).wait_send()
+
+    def wave(self, t):
+        for lag, act in ((4, self.f_done), (3, self.b_done), (2, self.z_done), (1, self.y_done), (0, self.x_done)):
+            k = t - lag
+            pl.when(jnp.logical_and(k >= 0, k < self.chunks))(lambda k=k, act=act: act(k))
+
+    @staticmethod
+    def scratch(chunks, rows, width, by_rows, group, count):
+        chips, outer = group // 2, count // 2
+        owners = owner_count(rows, width, by_rows, outer)
+        half = rows // 2
+        piece = (half // owners, width) if by_rows else (half, width // owners)
+        bufs = [(chunks, chips, rows, width), (chunks, chips, rows, width), (chunks, chips, rows, width), (chunks, rows, width),
+                (chunks, half, width), (chunks, half, width), (chunks, outer) + piece, (chunks, rows, width)]
+        return [(b, bf16) for b in bufs] + [pltpu.SemaphoreType.DMA((12, chunks, max(chips, outer, 2)))]
+
+
+class Small:
+    def __init__(self, held, got, sends, recvs):
+        self.held, self.got, self.sends, self.recvs = held, got, sends, recvs
+        group, ctx = lax.axis_index("group"), lax.axis_index("ctx")
+        core, chip, inner, line = lax.rem(group, 2), group // 2, lax.rem(ctx, 2), ctx // 2
+        self.hops = [
+            (2, core, lambda j: dict(group=chip * 2 + j)),
+            (lax.axis_size("group") // 2, chip, lambda j: dict(group=j * 2 + core)),
+            (2, inner, lambda j: dict(ctx=line * 2 + j)),
+            (lax.axis_size("ctx") // 2, line, lambda j: dict(ctx=j * 2 + inner)),
+        ]
+
+    def copy(self, h, j, sender):
+        return remote(
+            self.held.at[h], self.got.at[h, sender], self.sends.at[h, j], self.recvs.at[h, sender], **self.hops[h][2](j)
+        )
+
+    def others(self, h, body):
+        size, mine, _ = self.hops[h]
+        loop(1, size, lambda d: body(lax.rem(mine + d, size)))
+
+    def start(self, h):
+        self.others(h, lambda j: self.copy(h, j, self.hops[h][1]).start())
+
+    def done(self, h):
+        size, mine, _ = self.hops[h]
+        self.others(h, lambda j: self.copy(h, j, j).wait_recv())
+        self.got[h, mine] = self.held[h]
+        total = self.got[h, 0]
+        for j in range(1, size):
+            total = total + self.got[h, j]
+        self.held[h + 1] = total
+
+    def drain(self):
+        for h in range(4):
+            self.others(h, lambda j: self.copy(h, j, self.hops[h][1]).wait_send())
+
+
 def masks():
     rows = lax.broadcasted_iota(jnp.int32, (HALF, HALF), 0)
     cols = lax.broadcasted_iota(jnp.int32, (HALF, HALF), 1)
@@ -296,7 +512,7 @@
 
 def front_kernel(
     tok, tok_all, wcat, wout, gain, cw, cb, db, dl,
-    normed, nhalo, cin, xb, vout, cumout, st0, loc, ylocal, gate, decs_out, wfull, wofull, sin,
+    normed, nhalo, rhalo, cin, xb, vout, cumout, st0, loc, ylocal, gate, decs_out, wfull, wofull, sin,
     sel, halo, ext, ns, xs_s, cum_s, dt_s, cum_t, wv, wg, fexp, decs, decx, buf, recv, back,
     halo_sem, x_send, x_recv, m_send, m_recv, w_own, w_load, sends, recvs, back_sends, back_recvs, own_sem,
     dec_send, dec_recv,
@@ -329,8 +545,7 @@
     def _():
         meet(("ctx", "group"))
         pl.when(me < count - 1)(lambda: halo_copy.start())
-        for sp in spreads:
-            sp.start()
+        spreads[0].start()
         sel[...] = head_map()
 
         @pl.when(me == 0)
@@ -344,15 +559,13 @@
         spreads[0].forward()
         spreads[0].finish()
         load_v.start()
+        spreads[1].start()
+        spreads[2].start()
         load_v.wait()
 
-    @pl.when(i == 1)
+    @pl.when(i == seqs - 1)
     def _():
         spreads[1].forward()
-        spreads[2].forward()
-
-    @pl.when(i == seqs - 1)
-    def _():
         spreads[1].finish()
         load_g.start()
 
@@ -365,6 +578,7 @@
         ext[RIM:] = nm
         ns[s] = nm
         nhalo[0] = nh
+        rhalo[0] = halo[s]
         normed[0] = nm
         v = mm(nm, wv[:, CONVW:]) + db[...]
         vout[0] = v
@@ -414,6 +628,7 @@
     @pl.when(i == seqs)
     def _():
         load_g.wait()
+        spreads[2].forward()
         for s in range(seqs - 1):
             scan(s)
 
@@ -618,14 +833,26 @@
 
 
 def third_kernel(
-    cin, vin, cumin, dyin, wred, dxs, dbc, dir1, later, sin, loc, cw, cb, dl, skip,
-    gz, gzh, gdelta, gcw, gcb, gdb, gdl,
-    sel, dtx, eoutx, xx, sp, dact, xwb, dout, qacc, gp,
+    cin, vin, cumin, dyin, wred, dxs, dbc, dir1, later, sin, loc, cw, cb, dl, skip, pgate, pout,
+    gz, gzh, gcw, gcb, gdb, gdl, rgate, rout,
+    sel, dtx, eoutx, xx, sp, dact, xwb, dout, qacc, gp, *comm,
 ):
     s = pl.program_id(0)
+    seqs = pl.num_programs(0)
+    reducers = [
+        Reducer(pgate, rgate, D // lax.axis_size("group"), GATE_CHUNK, False, comm[:8], comm[8]),
+        Reducer(pout, rout, DIN // lax.axis_size("group"), OUT_CHUNK, True, comm[9:17], comm[17]),
+    ]
+
+    def wave(t):
+        reducers[1].wave(t - reducers[0].chunks)
+        reducers[0].wave(t)
 
     @pl.when(s == 0)
     def _():
+        meet(("ctx", "group"))
+        for r in reducers:
+            loop(0, r.chunks, r.m_start)
         sel[...] = head_map()
         gcw[...] = jnp.zeros_like(gcw)
         gcb[...] = jnp.zeros_like(gcb)
@@ -653,7 +880,15 @@
         xx[:, cols] = a
         sp[:, cols] = sg + a * (1.0 - sg)
 
+    wave(3 * s - 2)
     loop(0, CONVW // HALF, conv_step)
+
+    @pl.when(s == 0)
+    def _():
+        for r in reducers:
+            loop(0, r.chunks, r.m_done)
+
+    wave(3 * s - 1)
     bb = xx[:, DIN : DIN + NSTATE].astype(bf16)
     qacc[...] = jnp.zeros_like(qacc)
     dout[1] = later[0]
@@ -686,7 +921,9 @@
     gpd = (qacc[...] - rate * glog) * sigmoid(v)
     lanes = lax.broadcasted_iota(jnp.int32, (SPAN, HALF), 1) < HEADS
     gpd = jnp.where(lanes, gpd, 0.0)
-    gdelta[0] = gpd.astype(bf16)
+    gz[0, :, CONVW : CONVW + HALF] = gpd.astype(bf16)
+    gz[0, :, CONVW + HALF :] = jnp.zeros((SPAN, HALF), bf16)
+    gzh[0, :, CONVW:] = jnp.zeros((RIM, 2 * HALF), bf16)
     gdb[...] += jnp.sum(gpd, axis=0, keepdims=True)
     gdl[...] += -rate * jnp.sum(dt * glog, axis=0, keepdims=True)
 
@@ -708,18 +945,30 @@
         gz[0, :, cols] = main.astype(bf16)
         gzh[0, :, cols] = rim.astype(bf16)
 
+    wave(3 * s)
     loop(0, CONVW // HALF, out_step)
 
-
-def fourth_kernel(
-    rel, tok, halo, cot, gain, ggate, gz, gzh, gdelta, wfull,
-    gtok, gtail, grim, ggain,
+    @pl.when(s == seqs - 1)
+    def _():
+        loop(3 * seqs - 2, reducers[0].chunks + reducers[1].chunks + 4, wave)
+        for r in reducers:
+            loop(0, r.chunks, r.drain)
+
+
+def tail_kernel(
+    rel, tok, halo, cot, gain, ggate, gz, gzh, wfull, pconv, small,
+    gtok, rconv, small_out,
+    ggain, rim_out, rim_in, rim_send, rim_recv, *comm,
 ):
     s = pl.program_id(0)
-
-    @pl.when(s == 0)
-    def _():
-        ggain[...] = jnp.zeros_like(ggain)
+    seqs = pl.num_programs(0)
+    count = lax.axis_size("ctx")
+    me = lax.axis_index("ctx")
+    reducer = Reducer(pconv, rconv, D // lax.axis_size("group"), CONV_CHUNK, False, comm[:8], comm[8])
+    little = Small(*comm[9:13])
+
+    def rim_copy(q):
+        return remote(rim_out.at[q], rim_in.at[q], rim_send.at[q], rim_recv.at[q], ctx=lax.rem(me + count - 1, count))
 
     def back(rows, grad):
         rows, inv, _ = normalized(rows, gain[...])
@@ -728,12 +977,51 @@
         mean = jnp.mean(gained * rows, axis=-1, keepdims=True)
         return inv * gained - rows * (inv * inv * inv * mean)
 
-    grad = mm_nt(ggate[0], wfull[:, :DIN]) + mm_nt(gz[0], wfull[:, DIN:ZXW]) + mm_nt(gdelta[0], wfull[:, ZXW:])
+    @pl.when(s == 0)
+    def _():
+        meet(("ctx", "group"))
+        loop(0, reducer.chunks, reducer.m_start)
+        ggain[...] = jnp.zeros_like(ggain)
+        for q in range(halo.shape[0]):
+            rim_out[q] = back(halo[q], mm_nt(gzh[q, :, :CONVW], wfull[:, DIN:ZXW])).astype(bf16)
+            pl.when(me > 0)(lambda q=q: rim_copy(q).start())
+
+        @pl.when(me == count - 1)
+        def _():
+            rim_in[...] = jnp.zeros_like(rim_in)
+
+        loop(0, reducer.chunks, reducer.m_done)
+
+    @pl.when(s > 0)
+    def _():
+        reducer.wave(s - 1)
+
+    grad = mm_nt(ggate[0], wfull[:, :DIN]) + mm_nt(gz[0, :, : CONVW + HALF], wfull[:, DIN:])
     live = (lax.broadcasted_iota(jnp.int32, (SPAN, 1), 0) < rel[s]).astype(f32)
     out = live * cot[0].astype(f32) + back(tok[0], grad)
-    gtok[0] = out.astype(bf16)
-    gtail[0] = out[SPAN - RIM :]
-    grim[0] = back(halo[0], mm_nt(gzh[0], wfull[:, DIN:ZXW])).astype(bf16)
+    gtok[0, : SPAN - RIM] = out[: SPAN - RIM].astype(bf16)
+    pl.when(me < count - 1)(lambda: rim_copy(s).wait_recv())
+    gtok[0, SPAN - RIM :] = (out[SPAN - RIM :] + rim_in[s].astype(f32)).astype(bf16)
+
+    @pl.when(s == seqs - 1)
+    def _():
+        held = comm[9]
+        held[0] = small[...]
+        for j in range(D // HALF):
+            held[0, j : j + 1, :] = ggain[:, j * HALF : (j + 1) * HALF]
+        little.start(0)
+        first = halo.shape[0] - 1
+        for h in range(4):
+            reducer.wave(first + h)
+            little.done(h)
+            if h < 3:
+                little.start(h + 1)
+        small_out[...] = held[4]
+        loop(first + 4, reducer.chunks + 4, reducer.wave)
+        loop(0, reducer.chunks, reducer.drain)
+        little.drain()
+        for q in range(halo.shape[0]):
+            pl.when(me > 0)(lambda q=q: rim_copy(q).wait_send())
 
 
 def whole(shape):
@@ -788,12 +1076,6 @@
                ((seqs, count, rows, DIN), bf16)]
     sems = [dma((seqs, parts)), dma((seqs, count)), dma((seqs, count)), dma((seqs, parts)), dma((seqs,))]
     return buffers, sems
-
-
-def passed_along(value, axis, steps):
-    count = lax.axis_size(axis)
-    leading, last = (max(0, -steps), min(count, count - steps))
-    return lax.ppermute(value, axis, [(source, source + steps) for source in range(leading, last)])
 
 
 def lanes_of(v):
@@ -822,13 +1104,14 @@
     at1 = lambda *shape: staged(seqs, 1, *shape)
     at01 = lambda *shape: staged(seqs, 2, *shape)
 
-    normed, nhalo, cin, xb, vraw, cum, st0, loc, ylocal, gate, decs, wfull, wofull, state_in = call(
+    normed, nhalo, rhalo, cin, xb, vraw, cum, st0, loc, ylocal, gate, decs, wfull, wofull, state_in = call(
         front_kernel,
         2 * seqs,
         [at0(SPAN, D), ANY, ANY, ANY, whole((1, D)), whole((KCONV, CONVW)), whole((1, CONVW)), whole((1, HALF)),
          whole((1, HALF))],
         [
             (at0(SPAN, D), (seqs, SPAN, D), bf16),
+            (at0(RIM, D), (seqs, RIM, D), bf16),
             (at0(RIM, D), (seqs, RIM, D), bf16),
             (at0(RIM + SPAN, CONVW), (seqs, RIM + SPAN, CONVW), f32),
             (at0(SPAN, CONVW), (seqs, SPAN, CONVW), bf16),
@@ -882,72 +1165,74 @@
         1,
     )(rel, tokens_in, cotangent, ylocal, gate, xb, vraw, cum, st0, state_in, decs, wofull, skip, ggain)
 
-    gz, gzh, gdelta, gcw, gcb, gdb, gdl = call(
+    live = (jnp.arange(SPAN, dtype=jnp.int32)[None, :] < rel[:, None]).astype(f32)[:, :, None]
+    drive = (live * cotangent.astype(f32)).astype(bf16)
+    flat = lambda v: v.reshape(-1, v.shape[-1])
+    p_out = mm_tn(flat(mlow), flat(drive)).astype(bf16)
+    p_gate = mm_tn(flat(normed), flat(ggate)).astype(bf16)
+
+    gz, gzh, gcw, gcb, gdb, gdl, r_gate, r_out = call(
         third_kernel,
         seqs,
         [per_seq(RIM + SPAN, CONVW), per_seq(SPAN, HALF), per_seq(SPAN, HALF), per_seq(SPAN, DIN), per_seq(SPAN, HALF),
          per_seq(SPAN, DIN), per_seq(SPAN, 2 * NSTATE), per_seq(NSTATE, DIN), per_seq(NSTATE, DIN), per_seq(NSTATE, DIN),
-         per_seq(NSTATE, DIN), whole((KCONV, CONVW)), whole((1, CONVW)), whole((1, HALF)), whole((1, DIN))],
+         per_seq(NSTATE, DIN), whole((KCONV, CONVW)), whole((1, CONVW)), whole((1, HALF)), whole((1, DIN)),
+         whole((D, DIN)), whole((DIN, D))],
         [
-            (per_seq(SPAN, CONVW), (seqs, SPAN, CONVW), bf16),
-            (per_seq(RIM, CONVW), (seqs, RIM, CONVW), bf16),
-            (per_seq(SPAN, HALF), (seqs, SPAN, HALF), bf16),
+            (per_seq(SPAN, GZW), (seqs, SPAN, GZW), bf16),
+            (per_seq(RIM, GZW), (seqs, RIM, GZW), bf16),
             (summed((KCONV, CONVW)), (KCONV, CONVW), f32),
             (summed((1, CONVW)), (1, CONVW), f32),
             (summed((1, HALF)), (1, HALF), f32),
             (summed((1, HALF)), (1, HALF), f32),
+            (summed((D // group, DIN)), (D // group, DIN), bf16),
+            (summed((DIN // group, D)), (DIN // group, D), bf16),
         ],
         [((2 * HALF, DIN), bf16), ((SPAN, DIN), f32), ((SPAN, DIN), f32), ((SPAN, CONVW), f32), ((SPAN, CONVW), f32),
          ((SPAN, CONVW), f32), ((SPAN, DIN), bf16), ((2, NSTATE, DIN), bf16), ((SPAN, HALF), f32),
-         ((RIM + SPAN + 8, CONVW), f32)],
+         ((RIM + SPAN + 8, CONVW), f32)]
+        + Reducer.scratch(DIN // GATE_CHUNK, D // group, GATE_CHUNK, False, group, count)
+        + Reducer.scratch(D // OUT_CHUNK, DIN // group, OUT_CHUNK, True, group, count),
         "third",
-    )(cin, vraw, cum, dy, wred, dxs, dbc, dir1, later, state_in, loc, conv_weight, cb, dl, skip)
-
-    live = (jnp.arange(SPAN, dtype=jnp.int32)[None, :] < rel[:, None]).astype(f32)[:, :, None]
-    drive = (live * cotangent.astype(f32)).astype(bf16)
-    flat = lambda v: v.reshape(-1, v.shape[-1])
-    g_out = mm_tn(flat(mlow), flat(drive))
-    g_gate = mm_tn(flat(normed), flat(ggate))
-    g_conv = mm_tn(flat(normed), flat(gz)) + mm_tn(flat(nhalo), flat(gzh))
-    g_delta = mm_tn(flat(normed), flat(gdelta))
-
-    halo = passed_along(tokens_in[:, SPAN - RIM :, :], "ctx", 1)
-    gtok, gtail, grim, g_gain = call(
-        fourth_kernel,
+        2,
+    )(cin, vraw, cum, dy, wred, dxs, dbc, dir1, later, state_in, loc, conv_weight, cb, dl, skip, p_gate, p_out)
+
+    p_conv = (mm_tn(flat(normed), flat(gz)) + mm_tn(flat(nhalo), flat(gzh))).astype(bf16)
+    sizes = (D, KCONV * CONVW, CONVW, HALF, HALF, DIN, DIN)
+    small = jnp.concatenate(
+        [jnp.zeros((D,), f32), gcw.reshape(-1), gcb.reshape(-1), gdb[0], gdl[0], gskip.reshape(-1), gggain.reshape(-1)]
+    ).reshape(-1, HALF)
+    small = jnp.pad(small, ((0, -small.shape[0] % 8), (0, 0)))
+    height = small.shape[0]
+    widest = max(group // 2, count // 2, 2)
+
+    gtok, r_conv, small = call(
+        tail_kernel,
         seqs,
-        [SMEM, per_seq(SPAN, D), per_seq(RIM, D), per_seq(SPAN, D), whole((1, D)), per_seq(SPAN, DIN), per_seq(SPAN, CONVW),
-         per_seq(RIM, CONVW), per_seq(SPAN, HALF), whole((D, ZXW + HALF))],
+        [SMEM, per_seq(SPAN, D), whole((seqs, RIM, D)), per_seq(SPAN, D), whole((1, D)), per_seq(SPAN, DIN),
+         per_seq(SPAN, GZW), whole((seqs, RIM, GZW)), whole((D, ZXW + HALF)), whole((D, GZW)), whole((height, HALF))],
         [
             (per_seq(SPAN, D), (seqs, SPAN, D), bf16),
-            (per_seq(RIM, D), (seqs, RIM, D), f32),
-            (per_seq(RIM, D), (seqs, RIM, D), bf16),
-            (summed((1, D)), (1, D), f32),
+            (summed((D // group, GZW)), (D // group, GZW), bf16),
+            (summed((height, HALF)), (height, HALF), f32),
         ],
-        [],
-        "fourth",
-    )(rel, tokens_in, halo, cotangent, gain, ggate, gz, gzh, gdelta, wfull)
-    grim = passed_along(grim, "ctx", -1)
-    gtok = lax.dynamic_update_slice(gtok, (gtail + grim.astype(f32)).astype(bf16), (0, SPAN - RIM, 0))
-
-    def reduced(g):
-        part = lax.psum_scatter(g.astype(bf16), "group", scatter_dimension=0, tiled=True)
-        return lax.psum(part, "ctx").astype(f32)
-
-    g_zx = jnp.concatenate([reduced(g_gate), reduced(g_conv)], axis=1)
-    g_out = reduced(g_out)
-    g_delta = reduced(g_delta)[:, :HEADS]
-    small = jnp.concatenate(
-        [g_gain.reshape(-1), gcw.reshape(-1), gcb.reshape(-1), gdb[0], gdl[0],
-         gskip.reshape(-1), gggain.reshape(-1)]
-    )
-    small = lax.psum(small, ("group", "ctx"))
+        [((1, D), f32), ((seqs, RIM, D), bf16), ((seqs, RIM, D), bf16), dma((seqs,)), dma((seqs,))]
+        + Reducer.scratch(GZW // CONV_CHUNK, D // group, CONV_CHUNK, False, group, count)
+        + [((5, height, HALF), f32), ((4, widest, height, HALF), f32), dma((4, widest)), dma((4, widest))],
+        "tail",
+        3,
+    )(rel, tokens_in, rhalo, cotangent, gain, ggate, gz, gzh, wfull, p_conv, small)
+
+    g_zx = jnp.concatenate([r_gate, r_conv[:, :CONVW]], axis=1).astype(f32)
+    g_delta = r_conv[:, CONVW : CONVW + HEADS].astype(f32)
+    small = small.reshape(-1)
     at = 0
     pieces = []
-    for size in (D, KCONV * CONVW, CONVW, HALF, HALF, DIN, DIN):
+    for size in sizes:
         pieces.append(small[at : at + size])
         at += size
     return (
-        mixed_out, gtok, pieces[0], g_zx, g_delta, g_out, pieces[1].reshape(KCONV, CONVW), pieces[2],
+        mixed_out, gtok, pieces[0], g_zx, g_delta, r_out.astype(f32), pieces[1].reshape(KCONV, CONVW), pieces[2],
         pieces[3][:HEADS], pieces[4][:HEADS], pieces[5].reshape(HEADS, HEADDIM).sum(1), pieces[6],
     )
 

time: 482 us -> 376 us (0.78)
  blocking collectives: 78 us -> 0 us
  waiting for transfers between devices: 67.2 us -> 0 us
  Pallas kernels: 267 us -> 331 us
  between operations: 14.1 us -> 0.88 us
  starting transfers between devices: 6.28 us -> 0 us
    psum x2 -> x0, blocking collectives: 78 us -> none  [the longest x1 39.9 us: local(): small = lax.psum(small, ('group', 'ctx'))]
    pallas_call x1, Pallas kernels: 14.3 us -> 56.5 us  [local(): call(tail_kernel, seqs, [SMEM, per_seq(SPAN, D), whole((seqs, RIM, D)), p...]
    psum x1 -> x0, waiting for transfers between devices: 40.3 us -> none  [reduced(): return lax.psum(part, 'ctx').astype(f32)]
    pallas_call x1, Pallas kernels: 45.7 us -> 72.1 us  [local(): call(third_kernel, seqs, [per_seq(RIM + SPAN, CONVW), per_seq(SPAN, HALF)...]
    reduce_scatter x4 -> x0, waiting for transfers between devices: 24.8 us -> none  [reduced(): lax.psum_scatter(g.astype(bf16), 'group', scatter_dimension=0, tiled=True)]
    pallas_call x1, Pallas kernels: 120 us -> 112 us  [local(): call(front_kernel, 2 * seqs, [at0(SPAN, D), ANY, ANY, ANY, whole((1, D)),...]
    ppermute x2 -> x0, starting transfers between devices: 6.07 us -> none  [passed_along(): lax.ppermute(value, axis, [(source, source + steps) for source in range(l...]
    dot_general x5 -> x4, matrix products: 20.9 us -> 18.1 us  [mm_tn(): return lax.dot_general(a, b, TN, preferred_element_type=f32)]
  transfers between devices with their start and end apart: 7 -> 0, of which waited for: 3 -> 0; matrix products, arithmetic and copies ran while one was open for 5% -> 0% of each run, Pallas kernels for 12% -> 0%
where the time goes in v3:
time: 376 us; the launch traced here: 375 us
  Pallas kernels  331 us (88%)
  matrix products  18.1 us (5%)
  local copies, waits for them, and re-layouts  16.3 us (4%)
  other arithmetic  9.04 us (2%)
    pallas_call x1, Pallas kernels, local(): call(front_kernel, 2 * seqs, [at0(SPAN, D), ANY, ANY, ANY, whole((1, D)),...  112 us
    pallas_call x1, Pallas kernels, local(): call(middle_kernel, 2 * seqs, [SMEM, at1(SPAN, D), at0(SPAN, D), at0(SPAN...  90.5 us
    pallas_call x1, Pallas kernels, local(): call(third_kernel, seqs, [per_seq(RIM + SPAN, CONVW), per_seq(SPAN, HALF)...  72.1 us
    pallas_call x1, Pallas kernels, local(): call(tail_kernel, seqs, [SMEM, per_seq(SPAN, D), whole((seqs, RIM, D)), p...  56.5 us
    dot_general x4, matrix products, mm_tn(): return lax.dot_general(a, b, TN, preferred_element_type=f32)  18.1 us

profile of v3, /device:TPU:0, one launch (start us, length us, event | category | flops | bytes accessed | tf_op | source)
XLA Modules:
  0.0 375.2 jit_solution(6453624160319459684)
XLA Ops:
  0.7 1.3 broadcast_in_dim.25.cb
  2.0 1.3 broadcast_in_dim.24.gain
  3.2 1.2 pad.17.dl
  4.4 0.8 copy.25
  5.2 2.5 fusion.3.wcat
  8.2 111.7 %front.1 = (bf16[4,256,768]{2,1,0:T(8,128)(2,1)}, bf16[4,16,768]{2,1,0:T(8,128)(2,1)}, bf16[4,16,768]{2,1,0:T(8,128)(2,1)}, f32[4,272,1792]{2,1,0:T(8,128)}, bf1...) custom-call(bf16[4,256,768]{2,1,0:T(8,128)(2,1)} %tok.5, ...), custom_call_target="tpu_custom_call" | custom-call | tf_op jit(solution)/shard_map/front/pallas_call | solution.py:1107
  120.5 0.7 broadcast_in_dim_reshape.3.skip
  121.2 0.6 broadcast_in_dim.29.ggain
  121.8 90.5 %middle.1 = (bf16[4,256,768]{2,1,0:T(8,128)(2,1)}, bf16[4,256,1536]{2,1,0:T(8,128)(2,1)}, bf16[4,256,1536]{2,1,0:T(8,128)(2,1)}, bf16[4,256,1536]{2,1,0:T(8,128)...) custom-call(s32[4]{0:T(128)} %broadcast_subtract_fusion.rel, ...), custom_call_target="tpu_custom_call" | custom-call | tf_op jit(solution)/shard_map/middle/pallas_call | solution.py:1140
  212.4 5.9 %bitcast_convert_fusion.1.pgate = bf16[768,1536]{1,0:T(8,128)(2,1)} fusion(bf16[4,256,768]{2,1,0:T(8,128)(2,1)S(1)} %copy-done.3, bf16[4,256,1536]{2,1,0:T(8,128)(2,1)} %get-tuple-element.60.ggate), kind=kOutput, calls=%fused_computation.3 | convolution fusion | flops 2417098752 | bytes 7077888 | tf_op jit(solution)/shard_map/dot_general | solution.py:43
  218.4 4.2 %bitcast_convert_fusion.pout = bf16[1536,768]{1,0:T(8,128)(2,1)} fusion(bf16[4,256,1536]{2,1,0:T(8,128)(2,1)S(1)} %copy-done.12, bf16[4,256,768]{2,1,0:T(8,128)(2,1)S(1)} %copy-done, f32[4,256]{1,0:T(4,128)S(1)} %fusion.4), kind=kOutput, calls=%fused_computation.2 | convolution fusion | flops 2419458048 | bytes 7081984 | tf_op jit(solution)/shard_map/dot_general | solution.py:43
  222.6 72.1 %third.1 = (bf16[4,256,2048]{2,1,0:T(8,128)(2,1)}, bf16[4,16,2048]{2,1,0:T(8,128)(2,1)}, f32[4,1792]{1,0:T(4,128)}, f32[1,1792]{1,0:T(1,128)}, f32[1,128]{1,0:T(...) custom-call(f32[4,272,1792]{2,1,0:T(8,128)} %get-tuple-element.61.cin, ...), custom_call_target="tpu_custom_call" | custom-call | tf_op jit(solution)/shard_map/third/pallas_call | solution.py:1174
  294.7 0.8 reshape.87
  295.5 0.7 reduce
  296.2 0.7 constant_dynamic-update-slice_fusion.3
  296.9 0.6 constant_dynamic-update-slice_fusion.2
  297.6 0.6 pad.18.small
  298.2 5.3 %fusion.5 = f32[768,2048,1]{1,0,2:T(8,128)S(1)} fusion(bf16[4,256,768]{2,1,0:T(8,128)(2,1)S(1)} %copy-done.3, bf16[4,256,2048]{2,1,0:T(8,128)(2,1)} %get-tuple-element.71.gz), kind=kOutput, calls=%fused_computation.26 | convolution fusion | flops 3221225472 | bytes 12058624 | tf_op jit(solution)/shard_map/dot_general | solution.py:43
  303.6 2.7 fusion.pconv
  306.3 56.5 %tail.1 = (bf16[4,256,768]{2,1,0:T(8,128)(2,1)}, bf16[192,2048]{1,0:T(8,128)(2,1)}, f32[104,128]{1,0:T(8,128)}) custom-call(s32[4]{0:T(128)} %broadcast_subtract_fusion.rel, bf16[4,256,768]{2,1,0:T(8,128)(2,1)} %tok.5, bf16[4,16,768]{2,1,0:T(8,128)(2,1)} %get-tuple-element.59.halo, bf16[4,256,768]{2,1,0:T(8,128)(2,1)} %cot.3, ...), custom_call_target="tpu_custom_call" | custom-call | tf_op jit(solution)/shard_map/tail/pallas_call | solution.py:1209
  362.8 1.2 slice.52
  363.9 1.6 maximum_convert_fusion
  365.6 0.8 slice_convert_fusion
  366.4 0.7 copy.29
  367.1 0.6 reshape.92
  367.7 0.6 slice_bitcast_fusion
  368.4 0.6 reduce_sum.9
  369.0 0.6 slice_bitcast_fusion.1
  369.6 0.6 slice_bitcast_fusion.2
  370.7 2.2 convert_element_type.46
  372.9 1.1 copy.42
  374.0 1.1 copy.43
  (47 shorter events, 1.9 us)
Async XLA Ops:
  0.6 7.0 %copy-start.14 = (f32[24]{0:T(128)S(1)}, f32[24]{0:T(128)}, u32[]{:S(2)}) copy-start(f32[24]{0:T(128)} %param.21) | copy-start | bytes 292
  8.2 111.7 %copy-start.15 = (s32[4]{0:T(128)S(1)}, s32[4]{0:T(128)}, u32[]{:S(2)}) copy-start(s32[4]{0:T(128)} %param.14) | copy-start | bytes 52
  8.2 112.3 %copy-start.11 = (f32[24]{0:T(128)S(1)}, f32[24]{0:T(128)}, u32[]{:S(2)}) copy-start(f32[24]{0:T(128)} %param.23) | copy-start | bytes 292
  8.2 113.0 %copy-start.7 = (f32[1536]{0:T(1024)S(1)}, f32[1536]{0:T(1024)}, u32[]{:S(2)}) copy-start(f32[1536]{0:T(1024)} %param.24) | copy-start | bytes 18436
  121.8 90.5 %copy-start.3 = (bf16[4,256,768]{2,1,0:T(8,128)(2,1)S(1)}, bf16[4,256,768]{2,1,0:T(8,128)(2,1)}, u32[]{:S(2)}) copy-start(bf16[4,256,768]{2,1,0:T(8,128)(2,1)} %get-tuple-element.69) | copy-start | bytes 4718596
  212.3 6.0 %copy-start.10 = (s32[4]{0:T(128)S(1)}, s32[4]{0:T(128)}, u32[]{:S(2)}) copy-start(s32[4]{0:T(128)} %broadcast_subtract_fusion.rel) | copy-start | bytes 52
  212.3 6.0 %copy-start = (bf16[4,256,768]{2,1,0:T(8,128)(2,1)S(1)}, bf16[4,256,768]{2,1,0:T(8,128)(2,1)}, u32[]{:S(2)}) copy-start(bf16[4,256,768]{2,1,0:T(8,128)(2,1)} %cot.3) | copy-start | bytes 4718596
  212.4 6.0 %copy-start.12 = (bf16[4,256,1536]{2,1,0:T(8,128)(2,1)S(1)}, bf16[4,256,1536]{2,1,0:T(8,128)(2,1)}, u32[]{:S(2)}) copy-start(bf16[4,256,1536]{2,1,0:T(8,128)(2,1)} %get-tuple-element.70) | copy-start | bytes 9437188
  222.6 74.9 %copy-start.9 = (f32[1,1536]{1,0:T(1,128)S(1)}, f32[1,1536]{1,0:T(1,128)}, u32[]{:S(2)}) copy-start(f32[1,1536]{1,0:T(1,128)} %get-tuple-element.79) | copy-start | bytes 18436
  222.6 75.0 %copy-start.8 = (f32[1,1536]{1,0:T(1,128)S(1)}, f32[1,1536]{1,0:T(1,128)}, u32[]{:S(2)}) copy-start(f32[1,1536]{1,0:T(1,128)} %get-tuple-element.80) | copy-start | bytes 18436
  298.2 5.3 %copy-start.5 = (bf16[4,16,2048]{2,1,0:T(8,128)(2,1)S(1)}, bf16[4,16,2048]{2,1,0:T(8,128)(2,1)}, u32[]{:S(2)}) copy-start(bf16[4,16,2048]{2,1,0:T(8,128)(2,1)} %get-tuple-element.72.gzh) | copy-start | bytes 786436
  298.2 5.4 %copy-start.13 = (bf16[4,16,768]{2,1,0:T(8,128)(2,1)S(1)}, bf16[4,16,768]{2,1,0:T(8,128)(2,1)}, u32[]{:S(2)}) copy-start(bf16[4,16,768]{2,1,0:T(8,128)(2,1)} %get-tuple-element.74) | copy-start | bytes 294916
  306.3 57.7 %copy-start.4 = (bf16[192,1536]{1,0:T(8,128)(2,1)S(1)}, bf16[192,1536]{1,0:T(8,128)(2,1)}, u32[]{:S(2)}) copy-start(bf16[192,1536]{1,0:T(8,128)(2,1)} %get-tuple-element.83) | copy-start | bytes 1769476
  362.8 4.3 %copy-start.6 = (f32[104,128]{1,0:T(8,128)S(1)}, f32[104,128]{1,0:T(8,128)}, u32[]{:S(2)}) copy-start(f32[104,128]{1,0:T(8,128)} %get-tuple-element.82) | copy-start | bytes 159748
  363.9 8.9 %copy-start.1 = (bf16[4,256,768]{2,1,0:T(8,128)(2,1)S(1)}, bf16[4,256,768]{2,1,0:T(8,128)(2,1)}, u32[]{:S(2)}) copy-start(bf16[4,256,768]{2,1,0:T(8,128)(2,1)} %get-tuple-element.114) | copy-start | bytes 4718596
  367.1 7.0 %copy-start.2 = (bf16[4,256,768]{2,1,0:T(8,128)(2,1)S(1)}, bf16[4,256,768]{2,1,0:T(8,128)(2,1)}, u32[]{:S(2)}) copy-start(bf16[4,256,768]{2,1,0:T(8,128)(2,1)} %get-tuple-element.115) | copy-start | bytes 4718596

commit v4 on v3

--- a/solution.py
+++ b/solution.py
@@ -28,6 +28,9 @@
 GATE_CHUNK = 512
 OUT_CHUNK = 256
 CONV_CHUNK = 512
+MIDDLE_LAG = 2
+SCAN_LAG = 4
+CLOSE_LAG = 6
 GZW = 2048
 
 
@@ -80,6 +83,10 @@
 
 def sigmoid(v):
     return 1.0 / (1.0 + jnp.exp(-v))
+
+
+def gate_of(v):
+    return 0.5 * jnp.tanh(0.5 * v) + 0.5
 
 
 def local_decays(cum):
@@ -134,148 +141,214 @@
 
 
 class Exchange:
-    def __init__(self, count, buf, recv, back, out, sends, recvs, back_sends, back_recvs, own_sem):
-        self.count = count
-        self.parts = min(count, 8)
-        self.stride = count // self.parts
-        self.rows = NSTATE // self.parts
-        self.me = lax.axis_index("ctx")
-        self.mine = self.me // self.stride
-        self.buf, self.recv, self.back, self.out = buf, recv, back, out
-        self.sends, self.recvs, self.back_sends, self.back_recvs, self.own_sem = (
-            sends, recvs, back_sends, back_recvs, own_sem,
-        )
+    def __init__(self, reverse, out_at, bufs, sems):
+        self.reverse, self.out_at, self.sems = reverse, out_at, sems
+        self.buf, self.y_buf, self.z_src, self.z_buf, self.z_back, self.p_buf, self.mine_buf, self.their_buf, self.decx = bufs
+        self.depth = self.buf.shape[1]
+        ctx = lax.axis_index("ctx")
+        self.ctx = ctx
+        self.outer = lax.axis_size("ctx") // 2
+        self.owners = min(self.outer, 4)
+        self.stride = self.outer // self.owners
+        self.inner = lax.rem(ctx, 2)
+        self.line = ctx // 2
+        self.mine = self.line // self.stride
+        self.half = NSTATE // 2
+        self.rows = self.half // self.owners
+
+    def half_rows(self, inner):
+        return pl.ds(pl.multiple_of(inner * self.half, self.half), self.half)
 
     def part(self, j):
         return pl.ds(pl.multiple_of(j * self.rows, self.rows), self.rows)
 
-    def owners(self, body):
+    def other_owners(self, body):
         if self.stride == 1:
-            loop(1, self.parts, lambda d: body(lax.rem(self.mine + d, self.parts)))
+            loop(1, self.owners, lambda d: body(lax.rem(self.mine + d, self.owners)))
         else:
-            def step(d):
-                j = lax.rem(self.mine + d, self.parts)
-                pl.when(j * self.stride != self.me)(lambda: body(j))
-
-            loop(0, self.parts, step)
+            loop(0, self.owners, lambda j: pl.when(j * self.stride != self.line)(lambda: body(j)))
+
+    def other_lines(self, body):
+        loop(1, self.outer, lambda d: body(lax.rem(self.line + d, self.outer)))
 
     def if_owner(self, body):
         if self.stride == 1:
             body()
         else:
-            pl.when(self.mine * self.stride == self.me)(body)
-
-    def others(self, body):
-        loop(1, self.count, lambda d: body(lax.rem(self.me + d, self.count)))
-
-    def to_owner(self, s, j, sender):
+            pl.when(self.mine * self.stride == self.line)(body)
+
+    def y_copy(self, u):
         return remote(
-            self.buf.at[s, self.part(j)], self.recv.at[s, sender], self.sends.at[s, j], self.recvs.at[s, sender],
-            ctx=j * self.stride,
+            self.buf.at[u, :, self.half_rows(1 - self.inner)], self.y_buf.at[u], self.sems.at[0, u, 0], self.sems.at[1, u, 0],
+            ctx=self.ctx + 1 - 2 * self.inner,
         )
 
-    def to_block(self, s, b, j):
+    def z_copy(self, u, j, sender):
         return remote(
-            self.back.at[s, b], self.out.at[s, self.part(j)], self.back_sends.at[s, b], self.back_recvs.at[s, j], ctx=b
+            self.z_src.at[u, :, self.part(j)], self.z_buf.at[u, sender], self.sems.at[2, u, j], self.sems.at[3, u, sender],
+            ctx=j * self.stride * 2 + self.inner,
         )
 
-    def keep(self, s):
-        return pltpu.make_async_copy(self.back.at[s, self.me], self.out.at[s, self.part(self.mine)], self.own_sem.at[s])
-
-    def start(self, s):
-        self.owners(lambda j: self.to_owner(s, j, self.me).start())
-
-        def own():
-            self.recv[s, self.me] = self.buf[s, self.part(self.mine), :]
-
-        self.if_owner(own)
-
-    def scan(self, s, decx, reverse):
+    def b_copy(self, u, line, j):
+        return remote(
+            self.z_back.at[u, line], self.p_buf.at[u, :, self.part(j)], self.sems.at[4, u, line], self.sems.at[5, u, j],
+            ctx=line * 2 + self.inner,
+        )
+
+    def f_copy(self, u, inner):
+        return remote(
+            self.their_buf.at[u], self.out_at(u, self.half_rows(inner)), self.sems.at[6, u, 0], self.sems.at[7, u, 0],
+            ctx=self.ctx + 1 - 2 * self.inner,
+        )
+
+    def keep(self, u):
+        return pltpu.make_async_copy(self.mine_buf.at[u], self.out_at(u, self.half_rows(self.inner)), self.sems.at[8, u, 0])
+
+    def decay(self, a, block):
+        return self.decx[a, pl.ds(pl.multiple_of(block * 8, 8), 8), :][0:1]
+
+    def pair(self, u, a):
+        own = self.buf[u, a, self.half_rows(self.inner), :].astype(f32)
+        other = self.y_buf[u, a].astype(f32)
+        first = self.inner == 0
+        return jnp.where(first, own, other), jnp.where(first, other, own)
+
+    def start(self, u):
+        self.y_copy(u).start()
+
+    def middle(self, u):
+        self.y_copy(u).wait_recv()
+        for a in range(self.depth):
+            s0, s1 = self.pair(u, a)
+            if self.reverse:
+                total = s0 + self.decay(a, 2 * self.line) * s1
+            else:
+                total = self.decay(a, 2 * self.line + 1) * s0 + s1
+            self.z_src[u, a] = total.astype(bf16)
+        self.other_owners(lambda j: self.z_copy(u, j, self.line).start())
+
+    def scan(self, u):
         def run():
-            self.others(lambda b: self.to_owner(s, self.mine, b).wait_recv())
-
-            def block(k, carry):
-                b = self.count - 1 - k if reverse else k
-                self.back[s, b] = carry.astype(bf16)
-                return decx[pl.ds(pl.multiple_of(b * 8, 8), 8), :][0:1] * carry + self.recv[s, b].astype(f32)
-
-            lax.fori_loop(0, self.count, block, jnp.zeros((self.rows, DIN), f32))
-            self.others(lambda b: self.to_block(s, b, self.mine).start())
-            self.keep(s).start()
+            self.other_lines(lambda line: self.z_copy(u, self.mine, line).wait_recv())
+            self.z_buf[u, self.line] = self.z_src[u, :, self.part(self.mine), :]
+            for a in range(self.depth):
+
+                def step(k, carry):
+                    line = self.outer - 1 - k if self.reverse else k
+                    self.z_back[u, line, a] = carry.astype(bf16)
+                    both_decays = self.decay(a, 2 * line) * self.decay(a, 2 * line + 1)
+                    return both_decays * carry + self.z_buf[u, line, a].astype(f32)
+
+                lax.fori_loop(0, self.outer, step, jnp.zeros(self.z_buf.shape[3:], f32))
+            self.other_lines(lambda line: self.b_copy(u, line, self.mine).start())
+            self.p_buf[u, :, self.part(self.mine), :] = self.z_back[u, self.line]
 
         self.if_owner(run)
 
-    def finish(self, s):
-        self.owners(lambda j: self.to_block(s, self.me, j).wait_recv())
-        self.owners(lambda j: self.to_owner(s, j, self.me).wait_send())
-
-        def own():
-            self.others(lambda b: self.to_block(s, b, self.mine).wait_send())
-            self.keep(s).wait()
-
-        self.if_owner(own)
+    def close(self, u):
+        self.other_owners(lambda j: self.b_copy(u, self.line, j).wait_recv())
+        for a in range(self.depth):
+            s0, s1 = self.pair(u, a)
+            near = self.p_buf[u, a].astype(f32)
+            if self.reverse:
+                far = s1 + self.decay(a, 2 * self.line + 1) * near
+            else:
+                far = s0 + self.decay(a, 2 * self.line) * near
+            keeps_near = self.inner == (1 if self.reverse else 0)
+            self.mine_buf[u, a] = jnp.where(keeps_near, near, far).astype(bf16)
+            self.their_buf[u, a] = jnp.where(keeps_near, far, near).astype(bf16)
+        self.f_copy(u, self.inner).start()
+        self.keep(u).start()
+
+    def finish(self, u):
+        self.f_copy(u, 1 - self.inner).wait_recv()
+        self.keep(u).wait()
+        self.y_copy(u).wait_send()
+        self.other_owners(lambda j: self.z_copy(u, j, self.line).wait_send())
+        self.if_owner(lambda: self.other_lines(lambda line: self.b_copy(u, line, self.mine).wait_send()))
+        self.f_copy(u, self.inner).wait_send()
+
+    @staticmethod
+    def scratch(units, depth, lanes, count):
+        outer = count // 2
+        half = NSTATE // 2
+        rows = half // min(outer, 4)
+        bufs = [(units, depth, NSTATE, lanes), (units, depth, half, lanes), (units, depth, half, lanes),
+                (units, outer, depth, rows, lanes), (units, outer, depth, rows, lanes), (units, depth, half, lanes),
+                (units, depth, half, lanes), (units, depth, half, lanes)]
+        return (
+            [(b, bf16) for b in bufs]
+            + [((depth, count * 8, lanes), f32)]
+            + [pltpu.SemaphoreType.DMA((9, units, max(outer, 4)))]
+        )
 
 
 class Spread:
-    def __init__(self, index, shard, full, cols, sems):
-        self.index, self.shard, self.full, self.cols = index, shard, full, cols
+    def __init__(self, shard, full, sems):
+        self.shard, self.full = shard, full
         self.x_send, self.x_recv, self.m_send, self.m_recv, self.own = sems
-        self.size = lax.axis_size("group")
-        self.cores = 2 if self.size % 2 == 0 else 1
-        self.chips = self.size // self.cores
+        size = lax.axis_size("group")
+        self.cores = 2 if size % 2 == 0 else 1
+        self.chips = size // self.cores
         self.me = lax.axis_index("group")
         self.core = lax.rem(self.me, self.cores)
         self.chip = self.me // self.cores
         self.rows = shard.shape[0]
 
-    def place(self, member):
-        return self.full.at[pl.ds(pl.multiple_of(member * self.rows, 64), self.rows), self.cols]
-
-    def source(self):
-        return self.shard.at[:, self.cols]
-
-    def across(self, d):
+    def place(self, member, cols):
+        return self.full.at[pl.ds(pl.multiple_of(member * self.rows, 32), self.rows), cols]
+
+    def across(self, p, cols, d):
         peer = lax.rem(self.chip + d, self.chips) * self.cores + self.core
         return remote(
-            self.source(), self.place(self.me), self.x_send.at[self.index, d], self.x_recv.at[self.index, d], group=peer
+            self.shard.at[:, cols], self.place(self.me, cols), self.x_send.at[p, d], self.x_recv.at[p, d], group=peer
         )
 
-    def mate(self, d):
+    def mate(self, p, cols, d):
         member = lax.rem(self.chip + self.chips - d, self.chips) * self.cores + self.core
-        src = self.source() if d == 0 else self.place(member)
+        src = self.shard.at[:, cols] if d == 0 else self.place(member, cols)
         return remote(
-            src, self.place(member), self.m_send.at[self.index, d], self.m_recv.at[self.index, d],
+            src, self.place(member, cols), self.m_send.at[p, d], self.m_recv.at[p, d],
             group=self.me + 1 - 2 * self.core,
         )
 
-    def keep(self):
-        return pltpu.make_async_copy(self.source(), self.place(self.me), self.own.at[self.index])
-
-    def start(self):
+    def keep(self, p):
+        return pltpu.make_async_copy(self.shard, self.place(self.me, slice(None)), self.own.at[p])
+
+    def start_chip(self, p):
+        if self.cores == 2:
+            self.mate(p, slice(None), 0).start()
+        self.keep(p).start()
+
+    def finish_chip(self, p):
+        if self.cores == 2:
+            self.mate(p, slice(None), 0).wait_recv()
+        self.keep(p).wait()
+
+    def start(self, p, cols):
         for d in range(1, self.chips):
-            self.across(d).start()
+            self.across(p, cols, d).start()
+
+    def forward(self, p, cols):
+        for d in range(1, self.chips):
+            self.across(p, cols, d).wait_recv()
+            if self.cores == 2:
+                self.mate(p, cols, d).start()
+
+    def finish(self, p, cols):
         if self.cores == 2:
-            self.mate(0).start()
-        self.keep().start()
-
-    def forward(self):
+            for d in range(1, self.chips):
+                self.mate(p, cols, d).wait_recv()
+
+    def drain(self, p, cols):
         for d in range(1, self.chips):
-            self.across(d).wait_recv()
+            self.across(p, cols, d).wait_send()
             if self.cores == 2:
-                self.mate(d).start()
-
-    def finish(self):
-        self.keep().wait()
+                self.mate(p, cols, d).wait_send()
+
+    def drain_chip(self, p):
         if self.cores == 2:
-            for d in range(self.chips):
-                self.mate(d).wait_recv()
-
-    def drain(self):
-        for d in range(1, self.chips):
-            self.across(d).wait_send()
-        if self.cores == 2:
-            for d in range(self.chips):
-                self.mate(d).wait_send()
+            self.mate(p, slice(None), 0).wait_send()
 
 
 def owner_count(rows, width, by_rows, outer):
@@ -510,183 +583,246 @@
     return out
 
 
+TILES = DIN // TILE
+PIECES = 2 * TILES + 1
+DT0 = DIN + CONVW - 2 * NSTATE
+
+
 def front_kernel(
-    tok, tok_all, wcat, wout, gain, cw, cb, db, dl,
-    normed, nhalo, rhalo, cin, xb, vout, cumout, st0, loc, ylocal, gate, decs_out, wfull, wofull, sin,
-    sel, halo, ext, ns, xs_s, cum_s, dt_s, cum_t, wv, wg, fexp, decs, decx, buf, recv, back,
-    halo_sem, x_send, x_recv, m_send, m_recv, w_own, w_load, sends, recvs, back_sends, back_recvs, own_sem,
-    dec_send, dec_recv,
+    tok, tok_any, wcat, wout, gain, cw, cb, db, dl,
+    normed, nhalo, rhalo, cin, xb, spb, vout, cumout, st0, loc, ylocal, gate, decs_out, wfull, wofull, sin,
+    sel, halo, ext, w, cin_s, xs_s, bt, scores, out_cat, dt_cat, cum_t, tot1x, decs,
+    halo_sem, x_send, x_recv, m_send, m_recv, w_own, w_store, dec_send, dec_recv, *exchange,
 ):
     i = pl.program_id(0)
-    seqs = tok_all.shape[0]
+    seqs = tok.shape[0]
     count = lax.axis_size("ctx")
     me = lax.axis_index("ctx")
-    ex = Exchange(count, buf, recv, back, sin, sends, recvs, back_sends, back_recvs, own_sem)
     sems = (x_send, x_recv, m_send, m_recv, w_own)
-    conv_cols, gate_cols = pl.ds(DIN, CONVW + HALF), pl.ds(0, DIN)
-    spreads = [
-        Spread(0, wcat, wfull, conv_cols, sems),
-        Spread(1, wcat, wfull, gate_cols, sems),
-        Spread(2, wout, wofull, pl.ds(0, D), sems),
-    ]
+    zx, wo = Spread(wcat, w, sems), Spread(wout, wofull, sems)
+    last = PIECES
+
+    def unit_cols(u):
+        return pl.ds(pl.multiple_of(u * TILE, TILE), TILE)
+
+    def piece(p):
+        at = jnp.where(p <= TILES, DIN + (p - 1) * TILE, (p - 1 - TILES) * TILE)
+        return pl.ds(pl.multiple_of(at, TILE), TILE)
+
+    first_piece = pl.ds(DT0, 2 * NSTATE + HALF)
+    ex = Exchange(False, lambda u, rows: sin.at[:, rows, unit_cols(u)], exchange[:9], exchange[9])
     halo_copy = remote(
-        tok_all.at[:, pl.ds(SPAN - RIM, RIM), :], halo, halo_sem.at[0], halo_sem.at[1], ctx=lax.rem(me + 1, count)
+        tok_any.at[:, pl.ds(SPAN - RIM, RIM), :], halo, halo_sem.at[0], halo_sem.at[1], ctx=lax.rem(me + 1, count)
     )
-    load_v = pltpu.make_async_copy(wfull.at[:, conv_cols], wv, w_load.at[0])
-    load_g = pltpu.make_async_copy(wfull.at[:, gate_cols], wg, w_load.at[1])
-
-    def dec_copy(s, j, sender):
+    keep_w = pltpu.make_async_copy(w, wfull, w_store.at[0])
+
+    def dec_copy(block, sender):
         rows = pl.ds(pl.multiple_of(sender * 8, 8), 8)
-        return remote(
-            decs.at[s, rows, :], decs.at[s, rows, :], dec_send.at[s, j], dec_recv.at[s, sender], ctx=j * ex.stride
-        )
+        return remote(decs.at[:, rows, :], decs.at[:, rows, :], dec_send.at[block], dec_recv.at[sender], ctx=block)
+
+    def other_blocks(body):
+        loop(1, count, lambda d: body(lax.rem(me + d, count)))
+
+    def conv_tile(s, cols_w, cols_c):
+        cin_s[s] = mm(ext[s], w[:, cols_w])
+        cin[s] = cin_s[s].astype(bf16)
+        o = cb[:, cols_c]
+        for k in range(KCONV):
+            o = o + cw[k : k + 1, cols_c] * cin_s[s, RIM - KCONV + 1 + k : RIM - KCONV + 1 + k + SPAN, :]
+        sg = gate_of(o)
+        a = o * sg
+        xb[s] = a.astype(bf16)
+        spb[s] = (sg + a * (1.0 - sg)).astype(bf16)
+        return a
+
+    def unit_decays(u):
+        for s in range(seqs):
+            ex.decx[s] = spread(decs[s], sel.at[:, unit_cols(u)])
 
     @pl.when(i == 0)
     def _():
         meet(("ctx", "group"))
         pl.when(me < count - 1)(lambda: halo_copy.start())
-        spreads[0].start()
+        zx.start(0, first_piece)
+        zx.start_chip(0)
+        zx.start(1, piece(1))
+        zx.start(2, piece(2))
+        wo.start_chip(1)
         sel[...] = head_map()
 
         @pl.when(me == 0)
         def _():
             halo[...] = jnp.zeros_like(halo)
 
+        def norm_main(s):
+            nm = normalized(tok[s], gain[...])[2]
+            ext[s, RIM:] = nm
+            normed[s] = nm
+
+        loop(0, seqs, norm_main)
+
         @pl.when(me > 0)
         def _():
             halo_copy.wait_recv()
 
-        spreads[0].forward()
-        spreads[0].finish()
-        load_v.start()
-        spreads[1].start()
-        spreads[2].start()
-        load_v.wait()
-
-    @pl.when(i == seqs - 1)
-    def _():
-        spreads[1].forward()
-        spreads[1].finish()
-        load_g.start()
-
-    @pl.when(i < seqs)
-    def _():
-        s = i
-        nh = normalized(halo[s], gain[...])[2]
-        nm = normalized(tok[0], gain[...])[2]
-        ext[0:RIM] = nh
-        ext[RIM:] = nm
-        ns[s] = nm
-        nhalo[0] = nh
-        rhalo[0] = halo[s]
-        normed[0] = nm
-        v = mm(nm, wv[:, CONVW:]) + db[...]
-        vout[0] = v
-        dt = softplus(v)
-        cum = exact_mm(triangle(SPAN, True), -jnp.exp(dl[...]) * dt)
-        cumout[0] = cum
-        cum_s[s] = cum
-        dt_s[s] = dt
-        e_in, e_out, tot0, tot1, total = local_decays(cum)
-        decs[s, pl.ds(pl.multiple_of(me * 8, 8), 8), :] = rows_of(total)
-        ex.owners(lambda j: dec_copy(s, j, me).start())
-        fexp[...] = spread(dt * e_out, sel)
-        tot1x = spread(rows_of(tot1), sel)[0:1]
-
-        def conv_tile(c):
-            cols = slice(c, c + TILE)
-            cin[0, :, cols] = mm(ext[...], wv[:, cols])
-            o = cb[:, cols]
-            for k in range(KCONV):
-                o = o + cw[k : k + 1, cols] * cin[0, RIM - KCONV + 1 + k : RIM - KCONV + 1 + k + SPAN, cols]
-            a = o * sigmoid(o)
-            low = a.astype(bf16)
-            xb[0, :, cols] = low
-            xs_s[s, :, cols] = low
-            return a
-
-        bc = conv_tile(DIN)
-        bt = jnp.transpose(bc[:, :NSTATE]).astype(bf16)
-        for j in range(DIN // TILE):
-            c = j * TILE
-            cols = slice(c, c + TILE)
-            a = conv_tile(c)
-            xw = (a * fexp[:, cols]).astype(bf16)
-            s0 = mm(bt[:, :HALF], xw[:HALF])
-            s1 = mm(bt[:, HALF:], xw[HALF:])
-            st0[0, :, cols] = s0
-            low = (tot1x[:, cols] * s0 + s1).astype(bf16)
-            loc[0, :, cols] = low
-            buf[s, :, cols] = low
-        ex.start(s)
-
-    def scan(s):
-        ex.if_owner(lambda: ex.others(lambda b: dec_copy(s, ex.mine, b).wait_recv()))
-        decx[...] = spread(decs[s], sel)
-        ex.scan(s, decx, False)
-
-    @pl.when(i == seqs)
-    def _():
-        load_g.wait()
-        spreads[2].forward()
-        for s in range(seqs - 1):
-            scan(s)
-
-    @pl.when(i == seqs + 1)
-    def _():
-        scan(seqs - 1)
-
-    @pl.when(i >= seqs)
-    def _():
-        s = i - seqs
+        def norm_halo(s):
+            nh = normalized(halo[s], gain[...])[2]
+            ext[s, 0:RIM] = nh
+            nhalo[s] = nh
+            rhalo[s] = halo[s]
+
+        loop(0, seqs, norm_halo)
+        zx.forward(0, first_piece)
+        zx.finish_chip(0)
+
+    @pl.when(i + 1 < PIECES)
+    def _():
+        zx.forward(i + 1, piece(i + 1))
+
+    @pl.when(i + 3 < PIECES)
+    def _():
+        zx.start(i + 3, piece(i + 3))
+
+    @pl.when(i + 3 == PIECES)
+    def _():
+        wo.start(last, slice(None))
+
+    @pl.when(i == 0)
+    def _():
+        zx.finish(0, first_piece)
+
+        def delta(s):
+            a = conv_tile(s, slice(DT0, DT0 + TILE), slice(DIN, DIN + TILE))
+            bb, cc = a[:, :NSTATE].astype(bf16), a[:, NSTATE:].astype(bf16)
+            bt[s] = jnp.transpose(a[:, :NSTATE]).astype(bf16)
+            for q in range(2):
+                scores[s, q] = mm_nt(cc[both(q)], bb[both(q)])
+            v = mm(ext[s, RIM:], w[:, DT0 + TILE :]) + db[...]
+            vout[s] = v
+            dt = softplus(v)
+            cum = exact_mm(triangle(SPAN, True), -jnp.exp(dl[...]) * dt)
+            cumout[s] = cum
+            for q in range(2):
+                cum_t[s, q] = jnp.transpose(cum[both(q)])
+            e_in, e_out, tot0, tot1, total = local_decays(cum)
+            decs[s, pl.ds(pl.multiple_of(me * 8, 8), 8), :] = rows_of(total)
+            out_cat[s] = jnp.concatenate(halves(dt * e_out), axis=1)
+            dt_cat[s] = jnp.concatenate(halves(dt), axis=1)
+            tot1x[s] = spread(rows_of(tot1), sel)
+
+        loop(0, seqs, delta)
+        other_blocks(lambda b: dec_copy(b, me).start())
+
+    @pl.when(jnp.logical_and(i >= 1, i < PIECES))
+    def _():
+        zx.finish(i, piece(i))
+
+    def act_at(lag, act):
+        u = i - 1 - lag
+        pl.when(jnp.logical_and(u >= 0, u < TILES))(lambda: act(u))
+
+    def close(u):
+        unit_decays(u)
+        ex.close(u)
+
+    def scan(u):
+        unit_decays(u)
+        ex.scan(u)
+
+    def middle(u):
+        unit_decays(u)
+        ex.middle(u)
+
+    @pl.when(i == 3)
+    def _():
+        other_blocks(lambda b: dec_copy(b, b).wait_recv())
+
+    act_at(CLOSE_LAG, close)
+    act_at(SCAN_LAG, scan)
+    act_at(MIDDLE_LAG, middle)
+
+    @pl.when(jnp.logical_and(i >= 1, i <= TILES))
+    def _():
+        u = i - 1
+        cols = unit_cols(u)
+
+        def x_tile(s):
+            a = conv_tile(s, piece(i), cols)
+            xs_s[s, :, cols] = a.astype(bf16)
+            xw = (a * mm(out_cat[s], sel[:, cols])).astype(bf16)
+            s0 = mm(bt[s, :, :HALF], xw[:HALF])
+            s1 = mm(bt[s, :, HALF:], xw[HALF:])
+            st0[s] = s0
+            low = (tot1x[s, :, cols][0:1] * s0 + s1).astype(bf16)
+            loc[s] = low
+            ex.buf[u, s] = low
+
+        loop(0, seqs, x_tile)
+        ex.start(u)
+
+    @pl.when(i > TILES)
+    def _():
+        u = i - 1 - TILES
         causal, low_lanes = masks()
-        cum = cum_s[s]
-        for q in range(2):
-            cum_t[q] = jnp.transpose(cum[both(q)])
-        fexp[...] = spread(dt_s[s], sel)
-        bb = xs_s[s, :, DIN : DIN + NSTATE]
-        cc = xs_s[s, :, DIN + NSTATE :]
-        scores = [mm_nt(cc[both(q)], bb[both(q)]) for q in range(2)]
-
-        def pair_step(p):
-            cols = pl.ds(pl.multiple_of(p * HALF, HALF), HALF)
-            decays = pair_decays(cum, cum_t, p, causal)
-            for q in range(2):
-                rows = both(q)
-                m = jnp.concatenate([(decays[2 * q + a] * scores[q]).astype(bf16) for a in range(2)], axis=1)
-                x = xs_s[s, rows, cols].astype(f32) * fexp[rows, cols]
-                x = jnp.concatenate([jnp.where(low_lanes, x, 0.0), jnp.where(low_lanes, 0.0, x)], axis=0)
-                ylocal[0, rows, cols] = mm(m, x.astype(bf16))
-
-        loop(0, PAIRS, pair_step)
-        for j in range(DIN // TILE):
-            cols = slice(j * TILE, (j + 1) * TILE)
-            gate[0, :, cols] = mm(ns[s], wg[:, cols])
-
-    @pl.when(i == 2 * seqs - 1)
-    def _():
+
+        def intra(s):
+            cum = cumout[s]
+            dtx = mm(dt_cat[s], sel[:, unit_cols(u)])
+            for h in range(2):
+                p = 2 * u + h
+                lanes = slice(h * HALF, (h + 1) * HALF)
+                decays = pair_decays(cum, cum_t.at[s], p, causal)
+                for q in range(2):
+                    rows = both(q)
+                    m = jnp.concatenate([(decays[2 * q + a] * scores[s, q]).astype(bf16) for a in range(2)], axis=1)
+                    x = xs_s[s, rows, pl.ds(pl.multiple_of(p * HALF, HALF), HALF)].astype(f32) * dtx[rows, lanes]
+                    x = jnp.concatenate([jnp.where(low_lanes, x, 0.0), jnp.where(low_lanes, 0.0, x)], axis=0)
+                    ylocal[s, rows, lanes] = mm(m, x.astype(bf16))
+            gate[s] = mm(ext[s, RIM:], w[:, piece(i)])
+
+        loop(0, seqs, intra)
+
+    @pl.when(i == PIECES - 1)
+    def _():
+        keep_w.start()
         decs_out[...] = decs[...]
-        for s in range(seqs):
-            ex.finish(s)
-            ex.owners(lambda j: dec_copy(s, j, me).wait_send())
-        for sp in spreads[1:]:
-            if sp.index == 2:
-                sp.finish()
-        for sp in spreads:
-            sp.drain()
+        wo.forward(last, slice(None))
+        loop(TILES + TILES - CLOSE_LAG, TILES, close)
+        loop(0, TILES, ex.finish)
+        wo.finish(last, slice(None))
+        wo.finish_chip(1)
+        zx.drain_chip(0)
+        wo.drain_chip(1)
+        zx.drain(0, first_piece)
+        loop(1, PIECES, lambda p: zx.drain(p, piece(p)))
+        wo.drain(last, slice(None))
+        other_blocks(lambda b: dec_copy(b, me).wait_send())
         pl.when(me < count - 1)(lambda: halo_copy.wait_send())
+        keep_w.wait()
 
 
 def middle_kernel(
     rel, tok, cot, ylocal, gate, xb, vin, cumin, st0, sin, decs, wout, skip, ggain,
     mixed, mlow, dyout, ggate, wred, dir1, gskip, gggain, dxs, dbc, later,
-    sel, cum_t, einx, ys, gs, ss, s_in, dcs, dy_s, ml_s, g_s, dg_s, decx, buf, recv, back,
-    sends, recvs, back_sends, back_recvs, own_sem,
+    sel, cum_t, einx, ys, gs, ss, s_in, dcs, dy_s, ml_s, g_s, dg_s, *exchange,
 ):
     i = pl.program_id(0)
     seqs = dy_s.shape[0]
-    count = lax.axis_size("ctx")
-    ex = Exchange(count, buf, recv, back, later, sends, recvs, back_sends, back_recvs, own_sem)
+    ex = Exchange(True, lambda u, rows: later.at[pl.ds(u, 1), rows, :], exchange[:9], exchange[9])
+
+    def wave(t):
+        def act_at(lag, act):
+            u = lax.div(t - lag, 2)
+
+            def run():
+                ex.decx[0] = spread(decs[u], sel)
+                act(u)
+
+            pl.when(jnp.logical_and(t >= lag, jnp.logical_and(2 * u + lag == t, u < seqs)))(run)
+
+        act_at(6, ex.close)
+        act_at(5, ex.scan)
+        act_at(4, ex.middle)
 
     @pl.when(i == 0)
     def _():
@@ -694,6 +830,8 @@
         sel[...] = head_map()
         gskip[...] = jnp.zeros_like(gskip)
         gggain[...] = jnp.zeros_like(gggain)
+
+    wave(2 * i)
 
     @pl.when(i < seqs)
     def _():
@@ -713,11 +851,12 @@
                 ys[rows, cols] = ylocal[0, rows, cols] + einx[rows, cols] * mm(cc[rows], s_in[q, :, cols])
             y = ys[:, cols] + skip[:, cols] * xb[0, :, cols].astype(f32)
             g = gate[0, :, cols]
-            gated = y * (g * sigmoid(g))
+            gated = y * (g * gate_of(g))
             gs[:, cols] = gated
             sq = gated * gated
             return total_sq + sq[:, :HALF] + sq[:, HALF:]
 
+        wave(2 * i + 1)
         sq = lax.fori_loop(0, DIN // TILE, gate_step, jnp.zeros((SPAN, HALF), f32))
         inv = lax.rsqrt(jnp.sum(sq, axis=1, keepdims=True) * (1.0 / DIN) + EPS)
         live = (lax.broadcasted_iota(jnp.int32, (SPAN, 1), 0) < rel[s]).astype(f32)
@@ -746,7 +885,7 @@
         for j in range(DIN // TILE):
             cols = slice(j * TILE, (j + 1) * TILE)
             g = gate[0, :, cols]
-            sg = sigmoid(g)
+            sg = gate_of(g)
             sl = g * sg
             grad_gated = inv * ss[:, cols] - gs[:, cols] * corr
             dy = grad_gated * sl
@@ -763,26 +902,13 @@
             d0 = mm(cct[:, :HALF], dye[:HALF])
             d1 = mm(cct[:, HALF:], dye[HALF:])
             dir1[0, :, cols] = d1
-            buf[s, :, cols] = (d0 + tot0x[:, cols] * d1).astype(bf16)
+            ex.buf[s, 0, :, cols] = (d0 + tot0x[:, cols] * d1).astype(bf16)
             for q in range(2):
                 dc[q] = dc[q] + mm_nt(dye[both(q)], s_in[q, :, cols])
         wred[0] = acc
         for q in range(2):
             dcs[s, both(q)] = dc[q]
         ex.start(s)
-
-    def scan(s):
-        decx[...] = spread(decs[s], sel)
-        ex.scan(s, decx, True)
-
-    @pl.when(i == seqs)
-    def _():
-        for s in range(seqs - 1):
-            scan(s)
-
-    @pl.when(i == seqs + 1)
-    def _():
-        scan(seqs - 1)
 
     @pl.when(i >= seqs)
     def _():
@@ -815,7 +941,9 @@
                     dg_s[q] += dm * decays[2 * q + a]
                 dxs[0, rows, cols] = jnp.where(low_lanes, grads[0], grads[1])
 
-        loop(0, PAIRS, pair_step)
+        loop(0, PAIRS // 2, pair_step)
+        wave(2 * i + 1)
+        loop(PAIRS // 2, PAIRS, pair_step)
         for q in range(2):
             rows = both(q)
             dg = dg_s[q].astype(bf16)
@@ -828,14 +956,14 @@
 
     @pl.when(i == 2 * seqs - 1)
     def _():
-        for s in range(seqs):
-            ex.finish(s)
+        loop(4 * seqs, 2 * seqs + 5, wave)
+        loop(0, seqs, ex.finish)
 
 
 def third_kernel(
-    cin, vin, cumin, dyin, wred, dxs, dbc, dir1, later, sin, loc, cw, cb, dl, skip, pgate, pout,
+    cin, xb, spb, vin, cumin, dyin, wred, dxs, dbc, dir1, later, sin, loc, cw, dl, skip, pgate, pout,
     gz, gzh, gcw, gcb, gdb, gdl, rgate, rout,
-    sel, dtx, eoutx, xx, sp, dact, xwb, dout, qacc, gp, *comm,
+    sel, dtx, eoutx, dact, xwb, dout, qacc, gp, *comm,
 ):
     s = pl.program_id(0)
     seqs = pl.num_programs(0)
@@ -870,18 +998,7 @@
     tot1x = spread(rows_of(tot1), sel)[0:1]
     totalx = spread(rows_of(total), sel)[0:1]
 
-    def conv_step(j):
-        cols = pl.ds(pl.multiple_of(j * HALF, HALF), HALF)
-        o = cb[:, cols]
-        for k in range(KCONV):
-            o = o + cw[k : k + 1, cols] * cin[0, RIM - KCONV + 1 + k : RIM - KCONV + 1 + k + SPAN, cols]
-        sg = sigmoid(o)
-        a = o * sg
-        xx[:, cols] = a
-        sp[:, cols] = sg + a * (1.0 - sg)
-
     wave(3 * s - 2)
-    loop(0, CONVW // HALF, conv_step)
 
     @pl.when(s == 0)
     def _():
@@ -889,7 +1006,7 @@
             loop(0, r.chunks, r.m_done)
 
     wave(3 * s - 1)
-    bb = xx[:, DIN : DIN + NSTATE].astype(bf16)
+    bb = xb[0, :, DIN : DIN + NSTATE]
     qacc[...] = jnp.zeros_like(qacc)
     dout[1] = later[0]
     dout[0] = (dir1[0] + tot1x * later[0].astype(f32)).astype(bf16)
@@ -898,7 +1015,7 @@
         cols = pl.ds(pl.multiple_of(j * TILE, TILE), TILE)
         for q in range(2):
             rows = both(q)
-            x = xx[rows, cols]
+            x = xb[0, rows, cols].astype(f32)
             dte = dtx[rows, cols]
             eo = eoutx[rows, cols]
             dx_s = dxs[0, rows, cols] + eo * mm(bb[rows], dout[q, :, cols])
@@ -929,19 +1046,22 @@
 
     def out_step(j):
         cols = pl.ds(pl.multiple_of(j * HALF, HALF), HALF)
-        gco = dact[:, cols] * sp[:, cols]
+        gco = dact[:, cols] * spb[0, :, cols].astype(f32)
         gp[RIM : RIM + SPAN, cols] = gco
         gcb[:, cols] += jnp.sum(gco, axis=0, keepdims=True)
-        for k in range(KCONV):
-            gcw[k : k + 1, cols] += jnp.sum(
-                gco * cin[0, RIM - KCONV + 1 + k : RIM - KCONV + 1 + k + SPAN, cols], axis=0, keepdims=True
-            )
+        own = cin[0, RIM:, cols].astype(f32)
+        before = cin[0, :RIM, cols].astype(f32)
         main = jnp.zeros((SPAN, HALF), f32)
         rim = jnp.zeros((RIM, HALF), f32)
         for k in range(KCONV):
             ahead = KCONV - 1 - k
-            main = main + cw[k : k + 1, cols] * gp[RIM + ahead : RIM + ahead + SPAN, cols]
-            rim = rim + cw[k : k + 1, cols] * gp[ahead : ahead + RIM, cols]
+            moved = gp[RIM + ahead : RIM + ahead + SPAN, cols]
+            early = gp[ahead : ahead + RIM, cols]
+            main = main + cw[k : k + 1, cols] * moved
+            rim = rim + cw[k : k + 1, cols] * early
+            gcw[k : k + 1, cols] += jnp.sum(own * moved, axis=0, keepdims=True) + jnp.sum(
+                before * early, axis=0, keepdims=True
+            )
         gz[0, :, cols] = main.astype(bf16)
         gzh[0, :, cols] = rim.astype(bf16)
 
@@ -1068,16 +1188,6 @@
     )
 
 
-def exchange_scratch(seqs, count):
-    parts = min(count, 8)
-    rows = NSTATE // parts
-    dma = pltpu.SemaphoreType.DMA
-    buffers = [((count * 8, DIN), f32), ((seqs, NSTATE, DIN), bf16), ((seqs, count, rows, DIN), bf16),
-               ((seqs, count, rows, DIN), bf16)]
-    sems = [dma((seqs, parts)), dma((seqs, count)), dma((seqs, count)), dma((seqs, parts)), dma((seqs,))]
-    return buffers, sems
-
-
 def lanes_of(v):
     return jnp.pad(v[None, :], ((0, 0), (0, HALF - v.shape[0])))
 
@@ -1098,41 +1208,48 @@
     skip = jnp.repeat(skip_gain, HEADDIM)[None, :]
     ggain = gated_gain[None, :]
     wcat = jnp.concatenate([w_zx, jnp.pad(w_delta, ((0, 0), (0, HALF - HEADS)))], axis=1)
-    buffers, sems = exchange_scratch(seqs, count)
     dma = pltpu.SemaphoreType.DMA
     at0 = lambda *shape: staged(seqs, 0, *shape)
     at1 = lambda *shape: staged(seqs, 1, *shape)
     at01 = lambda *shape: staged(seqs, 2, *shape)
 
-    normed, nhalo, rhalo, cin, xb, vraw, cum, st0, loc, ylocal, gate, decs, wfull, wofull, state_in = call(
+    def tiled(rows, first, lead=None):
+        def index(i):
+            u = jnp.clip(i - first, 0, TILES - 1)
+            return (0, 0, u if lead is None else jnp.where(i == 0, lead, u))
+
+        return pl.BlockSpec((seqs, rows, TILE), index)
+
+    state = (seqs, NSTATE, DIN)
+    normed, nhalo, rhalo, cin, xb, spb, vraw, cum, st0, loc, ylocal, gate, decs, wfull, wofull, state_in = call(
         front_kernel,
-        2 * seqs,
-        [at0(SPAN, D), ANY, ANY, ANY, whole((1, D)), whole((KCONV, CONVW)), whole((1, CONVW)), whole((1, HALF)),
+        PIECES,
+        [whole((seqs, SPAN, D)), ANY, ANY, ANY, whole((1, D)), whole((KCONV, CONVW)), whole((1, CONVW)), whole((1, HALF)),
          whole((1, HALF))],
         [
-            (at0(SPAN, D), (seqs, SPAN, D), bf16),
-            (at0(RIM, D), (seqs, RIM, D), bf16),
-            (at0(RIM, D), (seqs, RIM, D), bf16),
-            (at0(RIM + SPAN, CONVW), (seqs, RIM + SPAN, CONVW), f32),
-            (at0(SPAN, CONVW), (seqs, SPAN, CONVW), bf16),
-            (at0(SPAN, HALF), (seqs, SPAN, HALF), f32),
-            (at0(SPAN, HALF), (seqs, SPAN, HALF), f32),
-            (at0(NSTATE, DIN), (seqs, NSTATE, DIN), f32),
-            (at0(NSTATE, DIN), (seqs, NSTATE, DIN), bf16),
-            (at1(SPAN, DIN), (seqs, SPAN, DIN), f32),
-            (at1(SPAN, DIN), (seqs, SPAN, DIN), f32),
+            (summed((seqs, SPAN, D)), (seqs, SPAN, D), bf16),
+            (summed((seqs, RIM, D)), (seqs, RIM, D), bf16),
+            (summed((seqs, RIM, D)), (seqs, RIM, D), bf16),
+            (tiled(RIM + SPAN, 1, TILES), (seqs, RIM + SPAN, CONVW), bf16),
+            (tiled(SPAN, 1, TILES), (seqs, SPAN, CONVW), bf16),
+            (tiled(SPAN, 1, TILES), (seqs, SPAN, CONVW), bf16),
+            (summed((seqs, SPAN, HALF)), (seqs, SPAN, HALF), f32),
+            (summed((seqs, SPAN, HALF)), (seqs, SPAN, HALF), f32),
+            (tiled(NSTATE, 1), state, f32),
+            (tiled(NSTATE, 1), state, bf16),
+            (tiled(SPAN, TILES + 1), (seqs, SPAN, DIN), f32),
+            (tiled(SPAN, TILES + 1), (seqs, SPAN, DIN), f32),
             (summed((seqs, count * 8, HALF)), (seqs, count * 8, HALF), f32),
             (ANY, (D, ZXW + HALF), bf16),
             (ANY, (DIN, D), bf16),
-            (ANY, (seqs, NSTATE, DIN), bf16),
+            (ANY, state, bf16),
         ],
-        [((2 * HALF, DIN), bf16), ((seqs, RIM, D), bf16), ((RIM + SPAN, D), bf16), ((seqs, SPAN, D), bf16),
-         ((seqs, SPAN, CONVW), bf16), ((seqs, SPAN, HALF), f32), ((seqs, SPAN, HALF), f32), ((2, HALF, HALF), f32),
-         ((D, CONVW + HALF), bf16), ((D, DIN), bf16), ((SPAN, DIN), f32), ((seqs, count * 8, HALF), f32)]
-        + buffers
-        + [dma((2,)), dma((3, chips)), dma((3, chips)), dma((3, chips)), dma((3, chips)), dma((3,)), dma((2,))]
-        + sems
-        + [dma((seqs, min(count, 8))), dma((seqs, count))],
+        [((2 * HALF, DIN), bf16), ((seqs, RIM, D), bf16), ((seqs, RIM + SPAN, D), bf16), ((D, ZXW + HALF), bf16),
+         ((seqs, RIM + SPAN, TILE), f32), ((seqs, SPAN, DIN), bf16), ((seqs, NSTATE, SPAN), bf16),
+         ((seqs, 2, HALF, HALF), f32), ((seqs, SPAN, 2 * HALF), bf16), ((seqs, SPAN, 2 * HALF), bf16),
+         ((seqs, 2, HALF, HALF), f32), ((seqs, 8, DIN), f32), ((seqs, count * 8, HALF), f32)]
+        + [dma((2,))] + [dma((PIECES + 1, chips))] * 4 + [dma((2,)), dma((1,)), dma((count,)), dma((count,))]
+        + Exchange.scratch(TILES, seqs, TILE, count),
         "front",
         0,
     )(tokens_in, tokens_in, wcat, w_out, gain, conv_weight, cb, db, dl)
@@ -1159,8 +1276,7 @@
         [((2 * HALF, DIN), bf16), ((2, HALF, HALF), f32), ((SPAN, DIN), f32), ((SPAN, DIN), f32), ((SPAN, DIN), f32),
          ((SPAN, DIN), f32), ((2, NSTATE, DIN), bf16), ((seqs, SPAN, HALF), f32), ((seqs, SPAN, DIN), bf16),
          ((seqs, SPAN, DIN), bf16), ((2, HALF, HALF), f32), ((2, HALF, HALF), f32)]
-        + buffers
-        + sems,
+        + Exchange.scratch(seqs, 1, DIN, count),
         "middle",
         1,
     )(rel, tokens_in, cotangent, ylocal, gate, xb, vraw, cum, st0, state_in, decs, wofull, skip, ggain)
@@ -1174,10 +1290,10 @@
     gz, gzh, gcw, gcb, gdb, gdl, r_gate, r_out = call(
         third_kernel,
         seqs,
-        [per_seq(RIM + SPAN, CONVW), per_seq(SPAN, HALF), per_seq(SPAN, HALF), per_seq(SPAN, DIN), per_seq(SPAN, HALF),
-         per_seq(SPAN, DIN), per_seq(SPAN, 2 * NSTATE), per_seq(NSTATE, DIN), per_seq(NSTATE, DIN), per_seq(NSTATE, DIN),
-         per_seq(NSTATE, DIN), whole((KCONV, CONVW)), whole((1, CONVW)), whole((1, HALF)), whole((1, DIN)),
-         whole((D, DIN)), whole((DIN, D))],
+        [per_seq(RIM + SPAN, CONVW), per_seq(SPAN, CONVW), per_seq(SPAN, CONVW), per_seq(SPAN, HALF), per_seq(SPAN, HALF),
+         per_seq(SPAN, DIN), per_seq(SPAN, HALF), per_seq(SPAN, DIN), per_seq(SPAN, 2 * NSTATE), per_seq(NSTATE, DIN),
+         per_seq(NSTATE, DIN), per_seq(NSTATE, DIN), per_seq(NSTATE, DIN), whole((KCONV, CONVW)), whole((1, HALF)),
+         whole((1, DIN)), whole((D, DIN)), whole((DIN, D))],
         [
             (per_seq(SPAN, GZW), (seqs, SPAN, GZW), bf16),
             (per_seq(RIM, GZW), (seqs, RIM, GZW), bf16),
@@ -1188,14 +1304,13 @@
             (summed((D // group, DIN)), (D // group, DIN), bf16),
             (summed((DIN // group, D)), (DIN // group, D), bf16),
         ],
-        [((2 * HALF, DIN), bf16), ((SPAN, DIN), f32), ((SPAN, DIN), f32), ((SPAN, CONVW), f32), ((SPAN, CONVW), f32),
-         ((SPAN, CONVW), f32), ((SPAN, DIN), bf16), ((2, NSTATE, DIN), bf16), ((SPAN, HALF), f32),
-         ((RIM + SPAN + 8, CONVW), f32)]
+        [((2 * HALF, DIN), bf16), ((SPAN, DIN), f32), ((SPAN, DIN), f32), ((SPAN, CONVW), f32), ((SPAN, DIN), bf16),
+         ((2, NSTATE, DIN), bf16), ((SPAN, HALF), f32), ((RIM + SPAN + 8, CONVW), f32)]
         + Reducer.scratch(DIN // GATE_CHUNK, D // group, GATE_CHUNK, False, group, count)
         + Reducer.scratch(D // OUT_CHUNK, DIN // group, OUT_CHUNK, True, group, count),
         "third",
         2,
-    )(cin, vraw, cum, dy, wred, dxs, dbc, dir1, later, state_in, loc, conv_weight, cb, dl, skip, p_gate, p_out)
+    )(cin, xb, spb, vraw, cum, dy, wred, dxs, dbc, dir1, later, state_in, loc, conv_weight, dl, skip, p_gate, p_out)
 
     p_conv = (mm_tn(flat(normed), flat(gz)) + mm_tn(flat(nhalo), flat(gzh))).astype(bf16)
     sizes = (D, KCONV * CONVW, CONVW, HALF, HALF, DIN, DIN)

time: 376 us -> 335 us (0.89)
  Pallas kernels: 331 us -> 291 us
    pallas_call x2, Pallas kernels: 184 us -> 150 us  [the longest x1 80.4 us: local(): call(front_kernel, PIECES, [whole((seqs, SPAN, D)), ANY, ANY, ANY, whole(...]
    pallas_call x1, Pallas kernels: 90.5 us -> 85.3 us  [local(): call(middle_kernel, 2 * seqs, [SMEM, at1(SPAN, D), at0(SPAN, D), at0(SPAN...]
where the time goes in v4:
time: 335 us
  Pallas kernels  291 us (87%)
  matrix products  18.3 us (5%)
  local copies, waits for them, and re-layouts  15.6 us (5%)
  other arithmetic  9.04 us (3%)
    pallas_call x1, Pallas kernels, local(): call(middle_kernel, 2 * seqs, [SMEM, at1(SPAN, D), at0(SPAN, D), at0(SPAN...  85.3 us
    pallas_call x1, Pallas kernels, local(): call(front_kernel, PIECES, [whole((seqs, SPAN, D)), ANY, ANY, ANY, whole(...  80.4 us
    pallas_call x1, Pallas kernels, local(): call(third_kernel, seqs, [per_seq(RIM + SPAN, CONVW), per_seq(SPAN, CONVW...  69.3 us
    pallas_call x1, Pallas kernels, local(): call(tail_kernel, seqs, [SMEM, per_seq(SPAN, D), whole((seqs, RIM, D)), p...  55.9 us
    dot_general x4, matrix products, mm_tn(): return lax.dot_general(a, b, TN, preferred_element_type=f32)  18.3 us

profile of v4, /device:TPU:0, one launch (start us, length us, event | category | flops | bytes accessed | tf_op | source)
XLA Modules:
  0.0 334.8 jit_solution(1351616454690369088)
XLA Ops:
  0.7 1.3 broadcast_in_dim.24.gain
  1.9 1.2 pad.17.dl
  3.1 0.8 copy.25
  3.9 2.5 fusion.3.wcat
  6.4 0.6 broadcast_in_dim.25.cb
  7.5 80.4 %front.1 = (bf16[4,256,768]{2,1,0:T(8,128)(2,1)}, bf16[4,16,768]{2,1,0:T(8,128)(2,1)}, bf16[4,16,768]{2,1,0:T(8,128)(2,1)}, bf16[4,272,1792]{2,1,0:T(8,128)(2,1)...) custom-call(bf16[4,256,768]{2,1,0:T(8,128)(2,1)} %tok.5, ...), custom_call_target="tpu_custom_call" | custom-call | tf_op jit(solution)/shard_map/front/pallas_call | solution.py:1224
  88.5 0.7 broadcast_in_dim_reshape.3.skip
  89.2 0.6 broadcast_in_dim.29.ggain
  89.8 85.3 %middle.1 = (bf16[4,256,768]{2,1,0:T(8,128)(2,1)}, bf16[4,256,1536]{2,1,0:T(8,128)(2,1)}, bf16[4,256,1536]{2,1,0:T(8,128)(2,1)}, bf16[4,256,1536]{2,1,0:T(8,128)...) custom-call(s32[4]{0:T(128)} %broadcast_subtract_fusion.rel, ...), custom_call_target="tpu_custom_call" | custom-call | tf_op jit(solution)/shard_map/middle/pallas_call | solution.py:1257
  175.2 6.1 %bitcast_convert_fusion.1.pgate = bf16[768,1536]{1,0:T(8,128)(2,1)} fusion(bf16[4,256,768]{2,1,0:T(8,128)(2,1)S(1)} %copy-done.3, bf16[4,256,1536]{2,1,0:T(8,128)(2,1)} %get-tuple-element.61.ggate), kind=kOutput, calls=%fused_computation.3 | convolution fusion | flops 2417098752 | bytes 7077888 | tf_op jit(solution)/shard_map/dot_general | solution.py:46
  181.4 4.2 %bitcast_convert_fusion.pout = bf16[1536,768]{1,0:T(8,128)(2,1)} fusion(bf16[4,256,1536]{2,1,0:T(8,128)(2,1)S(1)} %copy-done.13, bf16[4,256,768]{2,1,0:T(8,128)(2,1)S(1)} %copy-done, f32[4,256]{1,0:T(4,128)S(1)} %fusion.4), kind=kOutput, calls=%fused_computation.2 | convolution fusion | flops 2419458048 | bytes 7081984 | tf_op jit(solution)/shard_map/dot_general | solution.py:46
  185.6 69.3 %third.1 = (bf16[4,256,2048]{2,1,0:T(8,128)(2,1)}, bf16[4,16,2048]{2,1,0:T(8,128)(2,1)}, f32[4,1792]{1,0:T(4,128)}, f32[1,1792]{1,0:T(1,128)}, f32[1,128]{1,0:T(...) custom-call(bf16[4,272,1792]{2,1,0:T(8,128)(2,1)} %get-tuple-element.62.cin, ...), custom_call_target="tpu_custom_call" | custom-call | tf_op jit(solution)/shard_map/third/pallas_call | solution.py:1290
  254.9 0.8 reshape.87
  255.7 0.7 reduce
  256.5 0.6 constant_dynamic-update-slice_fusion.3
  257.0 0.7 constant_dynamic-update-slice_fusion.2
  257.8 0.6 pad.18.small
  258.5 5.3 %fusion.5 = f32[768,2048,1]{1,0,2:T(8,128)S(1)} fusion(bf16[4,256,768]{2,1,0:T(8,128)(2,1)S(1)} %copy-done.3, bf16[4,256,2048]{2,1,0:T(8,128)(2,1)} %get-tuple-element.73.gz), kind=kOutput, calls=%fused_computation.26 | convolution fusion | flops 3221225472 | bytes 12058624 | tf_op jit(solution)/shard_map/dot_general | solution.py:46
  263.8 2.6 fusion.pconv
  266.4 55.9 %tail.1 = (bf16[4,256,768]{2,1,0:T(8,128)(2,1)}, bf16[192,2048]{1,0:T(8,128)(2,1)}, f32[104,128]{1,0:T(8,128)}) custom-call(s32[4]{0:T(128)} %broadcast_subtract_fusion.rel, bf16[4,256,768]{2,1,0:T(8,128)(2,1)} %tok.5, bf16[4,16,768]{2,1,0:T(8,128)(2,1)} %get-tuple-element.60.halo, bf16[4,256,768]{2,1,0:T(8,128)(2,1)} %cot.3, ...), custom_call_target="tpu_custom_call" | custom-call | tf_op jit(solution)/shard_map/tail/pallas_call | solution.py:1324
  322.4 1.2 slice.52
  323.6 1.6 maximum_convert_fusion
  325.2 0.8 slice_convert_fusion
  326.0 0.7 copy.29
  326.7 0.6 reshape.92
  327.3 0.6 slice_bitcast_fusion
  328.0 0.6 reduce_sum.9
  328.6 0.6 slice_bitcast_fusion.1
  329.2 0.6 slice_bitcast_fusion.2
  330.3 2.2 convert_element_type.46
  332.5 1.1 copy.42
  333.6 1.1 copy.43
  (49 shorter events, 1.9 us)
Async XLA Ops:
  0.6 5.8 %copy-start.8 = (f32[1792]{0:T(1024)S(1)}, f32[1792]{0:T(1024)}, u32[]{:S(2)}) copy-start(f32[1792]{0:T(1024)} %param.20) | copy-start | bytes 21508
  0.7 6.3 %copy-start.15 = (f32[24]{0:T(128)S(1)}, f32[24]{0:T(128)}, u32[]{:S(2)}) copy-start(f32[24]{0:T(128)} %param.21) | copy-start | bytes 292
  7.5 80.4 %copy-start.16 = (s32[4]{0:T(128)S(1)}, s32[4]{0:T(128)}, u32[]{:S(2)}) copy-start(s32[4]{0:T(128)} %param.14) | copy-start | bytes 52
  7.5 81.0 %copy-start.12 = (f32[24]{0:T(128)S(1)}, f32[24]{0:T(128)}, u32[]{:S(2)}) copy-start(f32[24]{0:T(128)} %param.23) | copy-start | bytes 292
  7.5 81.7 %copy-start.7 = (f32[1536]{0:T(1024)S(1)}, f32[1536]{0:T(1024)}, u32[]{:S(2)}) copy-start(f32[1536]{0:T(1024)} %param.24) | copy-start | bytes 18436
  89.8 85.3 %copy-start.3 = (bf16[4,256,768]{2,1,0:T(8,128)(2,1)S(1)}, bf16[4,256,768]{2,1,0:T(8,128)(2,1)}, u32[]{:S(2)}) copy-start(bf16[4,256,768]{2,1,0:T(8,128)(2,1)} %get-tuple-element.71) | copy-start | bytes 4718596
  175.2 6.1 %copy-start.11 = (s32[4]{0:T(128)S(1)}, s32[4]{0:T(128)}, u32[]{:S(2)}) copy-start(s32[4]{0:T(128)} %broadcast_subtract_fusion.rel) | copy-start | bytes 52
  175.2 6.2 %copy-start = (bf16[4,256,768]{2,1,0:T(8,128)(2,1)S(1)}, bf16[4,256,768]{2,1,0:T(8,128)(2,1)}, u32[]{:S(2)}) copy-start(bf16[4,256,768]{2,1,0:T(8,128)(2,1)} %cot.3) | copy-start | bytes 4718596
  175.2 6.2 %copy-start.13 = (bf16[4,256,1536]{2,1,0:T(8,128)(2,1)S(1)}, bf16[4,256,1536]{2,1,0:T(8,128)(2,1)}, u32[]{:S(2)}) copy-start(bf16[4,256,1536]{2,1,0:T(8,128)(2,1)} %get-tuple-element.72) | copy-start | bytes 9437188
  185.6 72.1 %copy-start.10 = (f32[1,1536]{1,0:T(1,128)S(1)}, f32[1,1536]{1,0:T(1,128)}, u32[]{:S(2)}) copy-start(f32[1,1536]{1,0:T(1,128)} %get-tuple-element.81) | copy-start | bytes 18436
  185.6 72.1 %copy-start.9 = (f32[1,1536]{1,0:T(1,128)S(1)}, f32[1,1536]{1,0:T(1,128)}, u32[]{:S(2)}) copy-start(f32[1,1536]{1,0:T(1,128)} %get-tuple-element.82) | copy-start | bytes 18436
  258.5 5.3 %copy-start.5 = (bf16[4,16,2048]{2,1,0:T(8,128)(2,1)S(1)}, bf16[4,16,2048]{2,1,0:T(8,128)(2,1)}, u32[]{:S(2)}) copy-start(bf16[4,16,2048]{2,1,0:T(8,128)(2,1)} %get-tuple-element.74.gzh) | copy-start | bytes 786436
  258.5 5.4 %copy-start.14 = (bf16[4,16,768]{2,1,0:T(8,128)(2,1)S(1)}, bf16[4,16,768]{2,1,0:T(8,128)(2,1)}, u32[]{:S(2)}) copy-start(bf16[4,16,768]{2,1,0:T(8,128)(2,1)} %get-tuple-element.76) | copy-start | bytes 294916
  266.4 57.1 %copy-start.4 = (bf16[192,1536]{1,0:T(8,128)(2,1)S(1)}, bf16[192,1536]{1,0:T(8,128)(2,1)}, u32[]{:S(2)}) copy-start(bf16[192,1536]{1,0:T(8,128)(2,1)} %get-tuple-element.85) | copy-start | bytes 1769476
  322.4 4.3 %copy-start.6 = (f32[104,128]{1,0:T(8,128)S(1)}, f32[104,128]{1,0:T(8,128)}, u32[]{:S(2)}) copy-start(f32[104,128]{1,0:T(8,128)} %get-tuple-element.84) | copy-start | bytes 159748
  323.6 8.9 %copy-start.1 = (bf16[4,256,768]{2,1,0:T(8,128)(2,1)S(1)}, bf16[4,256,768]{2,1,0:T(8,128)(2,1)}, u32[]{:S(2)}) copy-start(bf16[4,256,768]{2,1,0:T(8,128)(2,1)} %get-tuple-element.116) | copy-start | bytes 4718596
  326.7 7.0 %copy-start.2 = (bf16[4,256,768]{2,1,0:T(8,128)(2,1)S(1)}, bf16[4,256,768]{2,1,0:T(8,128)(2,1)}, u32[]{:S(2)}) copy-start(bf16[4,256,768]{2,1,0:T(8,128)(2,1)} %get-tuple-element.117) | copy-start | bytes 4718596

commit v5 on v4

--- a/solution.py
+++ b/solution.py
@@ -30,6 +30,7 @@
 CONV_CHUNK = 512
 MIDDLE_LAG = 2
 SCAN_LAG = 4
+HOPS = ("group", "ctx")
 CLOSE_LAG = 6
 GZW = 2048
 
@@ -359,7 +360,8 @@
 class Reducer:
     def __init__(self, part, out, rows, width, by_rows, bufs, sems):
         self.part, self.out, self.rows, self.width, self.by_rows = part, out, rows, width, by_rows
-        self.m_buf, self.x_src, self.x_buf, self.y_src, self.y_buf, self.z_src, self.z_buf, self.full = bufs
+        self.m_buf, self.x_buf, self.y_src, self.y_buf, self.z_src, self.z_buf, self.full = bufs
+        self.x_src = self.m_buf
         self.sems = sems
         self.chunks = part.shape[1] // width
         self.group = lax.axis_index("group")
@@ -520,7 +522,7 @@
         owners = owner_count(rows, width, by_rows, outer)
         half = rows // 2
         piece = (half // owners, width) if by_rows else (half, width // owners)
-        bufs = [(chunks, chips, rows, width), (chunks, chips, rows, width), (chunks, chips, rows, width), (chunks, rows, width),
+        bufs = [(chunks, chips, rows, width), (chunks, chips, rows, width), (chunks, rows, width),
                 (chunks, half, width), (chunks, half, width), (chunks, outer) + piece, (chunks, rows, width)]
         return [(b, bf16) for b in bufs] + [pltpu.SemaphoreType.DMA((12, chunks, max(chips, outer, 2)))]
 
@@ -528,39 +530,38 @@
 class Small:
     def __init__(self, held, got, sends, recvs):
         self.held, self.got, self.sends, self.recvs = held, got, sends, recvs
-        group, ctx = lax.axis_index("group"), lax.axis_index("ctx")
-        core, chip, inner, line = lax.rem(group, 2), group // 2, lax.rem(ctx, 2), ctx // 2
-        self.hops = [
-            (2, core, lambda j: dict(group=chip * 2 + j)),
-            (lax.axis_size("group") // 2, chip, lambda j: dict(group=j * 2 + core)),
-            (2, inner, lambda j: dict(ctx=line * 2 + j)),
-            (lax.axis_size("ctx") // 2, line, lambda j: dict(ctx=j * 2 + inner)),
-        ]
 
     def copy(self, h, j, sender):
         return remote(
-            self.held.at[h], self.got.at[h, sender], self.sends.at[h, j], self.recvs.at[h, sender], **self.hops[h][2](j)
+            self.held.at[h], self.got.at[h, sender], self.sends.at[h, j], self.recvs.at[h, sender], **{HOPS[h]: j}
         )
 
     def others(self, h, body):
-        size, mine, _ = self.hops[h]
+        size, mine = lax.axis_size(HOPS[h]), lax.axis_index(HOPS[h])
         loop(1, size, lambda d: body(lax.rem(mine + d, size)))
 
     def start(self, h):
-        self.others(h, lambda j: self.copy(h, j, self.hops[h][1]).start())
+        mine = lax.axis_index(HOPS[h])
+        self.others(h, lambda j: self.copy(h, j, mine).start())
 
     def done(self, h):
-        size, mine, _ = self.hops[h]
         self.others(h, lambda j: self.copy(h, j, j).wait_recv())
-        self.got[h, mine] = self.held[h]
+        self.got[h, lax.axis_index(HOPS[h])] = self.held[h]
         total = self.got[h, 0]
-        for j in range(1, size):
+        for j in range(1, lax.axis_size(HOPS[h])):
             total = total + self.got[h, j]
         self.held[h + 1] = total
 
     def drain(self):
-        for h in range(4):
-            self.others(h, lambda j: self.copy(h, j, self.hops[h][1]).wait_send())
+        for h in range(2):
+            mine = lax.axis_index(HOPS[h])
+            self.others(h, lambda j: self.copy(h, j, mine).wait_send())
+
+    @staticmethod
+    def scratch(height, group, count):
+        widest = max(group, count)
+        dma = pltpu.SemaphoreType.DMA
+        return [((3, height, HALF), f32), ((2, widest, height, HALF), f32), dma((2, widest)), dma((2, widest))]
 
 
 def masks():
@@ -590,8 +591,8 @@
 
 def front_kernel(
     tok, tok_any, wcat, wout, gain, cw, cb, db, dl,
-    normed, nhalo, rhalo, cin, xb, spb, vout, cumout, st0, loc, ylocal, gate, decs_out, wfull, wofull, sin,
-    sel, halo, ext, w, cin_s, xs_s, bt, scores, out_cat, dt_cat, cum_t, tot1x, decs,
+    nt, nth, rhalo, cin, xb, spb, vout, cumout, st0, loc, ylocal, gate, decs_out, wfull, wofull, sin,
+    sel, halo, nh_s, ext, w, cin_s, xs_s, bt, scores, out_cat, dt_cat, cum_t, tot1x, decs,
     halo_sem, x_send, x_recv, m_send, m_recv, w_own, w_store, dec_send, dec_recv, *exchange,
 ):
     i = pl.program_id(0)
@@ -657,7 +658,7 @@
         def norm_main(s):
             nm = normalized(tok[s], gain[...])[2]
             ext[s, RIM:] = nm
-            normed[s] = nm
+            nt[:, pl.ds(pl.multiple_of(s * SPAN, SPAN), SPAN)] = jnp.transpose(nm.astype(f32)).astype(bf16)
 
         loop(0, seqs, norm_main)
 
@@ -668,10 +669,11 @@
         def norm_halo(s):
             nh = normalized(halo[s], gain[...])[2]
             ext[s, 0:RIM] = nh
-            nhalo[s] = nh
+            nh_s[pl.ds(pl.multiple_of(s * RIM, RIM), RIM), :] = nh.astype(f32)
             rhalo[s] = halo[s]
 
         loop(0, seqs, norm_halo)
+        nth[...] = jnp.transpose(nh_s[...]).astype(bf16)
         zx.forward(0, first_piece)
         zx.finish_chip(0)
 
@@ -752,7 +754,7 @@
             xw = (a * mm(out_cat[s], sel[:, cols])).astype(bf16)
             s0 = mm(bt[s, :, :HALF], xw[:HALF])
             s1 = mm(bt[s, :, HALF:], xw[HALF:])
-            st0[s] = s0
+            st0[s] = s0.astype(bf16)
             low = (tot1x[s, :, cols][0:1] * s0 + s1).astype(bf16)
             loc[s] = low
             ex.buf[u, s] = low
@@ -777,8 +779,8 @@
                     m = jnp.concatenate([(decays[2 * q + a] * scores[s, q]).astype(bf16) for a in range(2)], axis=1)
                     x = xs_s[s, rows, pl.ds(pl.multiple_of(p * HALF, HALF), HALF)].astype(f32) * dtx[rows, lanes]
                     x = jnp.concatenate([jnp.where(low_lanes, x, 0.0), jnp.where(low_lanes, 0.0, x)], axis=0)
-                    ylocal[s, rows, lanes] = mm(m, x.astype(bf16))
-            gate[s] = mm(ext[s, RIM:], w[:, piece(i)])
+                    ylocal[s, rows, lanes] = mm(m, x.astype(bf16)).astype(bf16)
+            gate[s] = mm(ext[s, RIM:], w[:, piece(i)]).astype(bf16)
 
         loop(0, seqs, intra)
 
@@ -841,16 +843,16 @@
         einx[...] = spread(e_in, sel)
         tot0x = spread(rows_of(tot0), sel)[0:1]
         s_in[0] = sin[0]
-        s_in[1] = (tot0x * sin[0].astype(f32) + st0[0]).astype(bf16)
+        s_in[1] = (tot0x * sin[0].astype(f32) + st0[0].astype(f32)).astype(bf16)
         cc = xb[0, :, DIN + NSTATE :]
 
         def gate_step(j, total_sq):
             cols = pl.ds(pl.multiple_of(j * TILE, TILE), TILE)
             for q in range(2):
                 rows = both(q)
-                ys[rows, cols] = ylocal[0, rows, cols] + einx[rows, cols] * mm(cc[rows], s_in[q, :, cols])
+                ys[rows, cols] = ylocal[0, rows, cols].astype(f32) + einx[rows, cols] * mm(cc[rows], s_in[q, :, cols])
             y = ys[:, cols] + skip[:, cols] * xb[0, :, cols].astype(f32)
-            g = gate[0, :, cols]
+            g = gate[0, :, cols].astype(f32)
             gated = y * (g * gate_of(g))
             gs[:, cols] = gated
             sq = gated * gated
@@ -884,7 +886,7 @@
         dc = [jnp.zeros((HALF, HALF), f32) for _ in range(2)]
         for j in range(DIN // TILE):
             cols = slice(j * TILE, (j + 1) * TILE)
-            g = gate[0, :, cols]
+            g = gate[0, :, cols].astype(f32)
             sg = gate_of(g)
             sl = g * sg
             grad_gated = inv * ss[:, cols] - gs[:, cols] * corr
@@ -901,7 +903,7 @@
             dye = (dy * einx[:, cols]).astype(bf16)
             d0 = mm(cct[:, :HALF], dye[:HALF])
             d1 = mm(cct[:, HALF:], dye[HALF:])
-            dir1[0, :, cols] = d1
+            dir1[0, :, cols] = d1.astype(bf16)
             ex.buf[s, 0, :, cols] = (d0 + tot0x[:, cols] * d1).astype(bf16)
             for q in range(2):
                 dc[q] = dc[q] + mm_nt(dye[both(q)], s_in[q, :, cols])
@@ -939,7 +941,7 @@
                     mine = low_lanes if a == 0 else jnp.logical_not(low_lanes)
                     dm = mm_nt(jnp.where(mine, dyf, 0.0).astype(bf16), xsb)
                     dg_s[q] += dm * decays[2 * q + a]
-                dxs[0, rows, cols] = jnp.where(low_lanes, grads[0], grads[1])
+                dxs[0, rows, cols] = jnp.where(low_lanes, grads[0], grads[1]).astype(bf16)
 
         loop(0, PAIRS // 2, pair_step)
         wave(2 * i + 1)
@@ -960,135 +962,38 @@
         loop(0, seqs, ex.finish)
 
 
-def third_kernel(
-    cin, xb, spb, vin, cumin, dyin, wred, dxs, dbc, dir1, later, sin, loc, cw, dl, skip, pgate, pout,
-    gz, gzh, gcw, gcb, gdb, gdl, rgate, rout,
-    sel, dtx, eoutx, dact, xwb, dout, qacc, gp, *comm,
+def back_kernel(
+    rel, tok, cot, rhalo, gain, ggate, wfull, cin, xb, spb, bc, dy, dxs, dir1, later, sin, loc,
+    vin, cumin, wred, dbc, cw, dl, skip, nt, nth, pgate, pout, gskip, gggain,
+    gtok, rgate, rout, rconv, small_out, ggain_out,
+    sel, dt_cat, eo_cat, tots, db_s, qacc, ends, gp, gz_s, gzh_s, pconv, gcw, gcb, gdb, gdl, ggain,
+    rim_out, rim_in, rim_send, rim_recv, *comm,
 ):
-    s = pl.program_id(0)
-    seqs = pl.num_programs(0)
-    reducers = [
-        Reducer(pgate, rgate, D // lax.axis_size("group"), GATE_CHUNK, False, comm[:8], comm[8]),
-        Reducer(pout, rout, DIN // lax.axis_size("group"), OUT_CHUNK, True, comm[9:17], comm[17]),
-    ]
-
-    def wave(t):
-        reducers[1].wave(t - reducers[0].chunks)
-        reducers[0].wave(t)
-
-    @pl.when(s == 0)
-    def _():
-        meet(("ctx", "group"))
-        for r in reducers:
-            loop(0, r.chunks, r.m_start)
-        sel[...] = head_map()
-        gcw[...] = jnp.zeros_like(gcw)
-        gcb[...] = jnp.zeros_like(gcb)
-        gdb[...] = jnp.zeros_like(gdb)
-        gdl[...] = jnp.zeros_like(gdl)
-        gp[0:RIM] = jnp.zeros((RIM, CONVW), f32)
-        gp[RIM + SPAN :] = jnp.zeros((8, CONVW), f32)
-
-    cum = cumin[0]
-    v = vin[0]
-    dt = softplus(v)
-    e_in, e_out, tot0, tot1, total = local_decays(cum)
-    dtx[...] = spread(dt, sel)
-    eoutx[...] = spread(e_out, sel)
-    tot1x = spread(rows_of(tot1), sel)[0:1]
-    totalx = spread(rows_of(total), sel)[0:1]
-
-    wave(3 * s - 2)
-
-    @pl.when(s == 0)
-    def _():
-        for r in reducers:
-            loop(0, r.chunks, r.m_done)
-
-    wave(3 * s - 1)
-    bb = xb[0, :, DIN : DIN + NSTATE]
-    qacc[...] = jnp.zeros_like(qacc)
-    dout[1] = later[0]
-    dout[0] = (dir1[0] + tot1x * later[0].astype(f32)).astype(bf16)
-
-    def state_step(j):
-        cols = pl.ds(pl.multiple_of(j * TILE, TILE), TILE)
-        for q in range(2):
-            rows = both(q)
-            x = xb[0, rows, cols].astype(f32)
-            dte = dtx[rows, cols]
-            eo = eoutx[rows, cols]
-            dx_s = dxs[0, rows, cols] + eo * mm(bb[rows], dout[q, :, cols])
-            dact[rows, cols] = dte * dx_s + skip[:, cols] * dyin[0, rows, cols].astype(f32)
-            qacc[rows] += gather_heads(x * dx_s, sel[:HALF, cols])
-            xwb[rows, cols] = (x * dte * eo).astype(bf16)
-
-    loop(0, DIN // TILE, state_step)
-    for q in range(2):
-        rows = both(q)
-        dact[rows, DIN : DIN + NSTATE] = dbc[0, rows, :NSTATE] + mm_nt(xwb[rows, :], dout[q])
-        dact[rows, DIN + NSTATE :] = dbc[0, rows, NSTATE:]
-
-    ends = jnp.sum(later[0].astype(f32) * (totalx * sin[0].astype(f32) + loc[0].astype(f32)), axis=0, keepdims=True)
-    ends = gather_heads(rows_of(ends), sel[:HALF])[0:1]
-    at_end = lax.broadcasted_iota(jnp.int32, (SPAN, 1), 0) == SPAN - 1
-    dcum = wred[0] - dt * qacc[...] + jnp.where(at_end, ends, 0.0)
-    glog = exact_mm(triangle(SPAN, False), dcum)
-    rate = jnp.exp(dl[...])
-    gpd = (qacc[...] - rate * glog) * sigmoid(v)
-    lanes = lax.broadcasted_iota(jnp.int32, (SPAN, HALF), 1) < HEADS
-    gpd = jnp.where(lanes, gpd, 0.0)
-    gz[0, :, CONVW : CONVW + HALF] = gpd.astype(bf16)
-    gz[0, :, CONVW + HALF :] = jnp.zeros((SPAN, HALF), bf16)
-    gzh[0, :, CONVW:] = jnp.zeros((RIM, 2 * HALF), bf16)
-    gdb[...] += jnp.sum(gpd, axis=0, keepdims=True)
-    gdl[...] += -rate * jnp.sum(dt * glog, axis=0, keepdims=True)
-
-    def out_step(j):
-        cols = pl.ds(pl.multiple_of(j * HALF, HALF), HALF)
-        gco = dact[:, cols] * spb[0, :, cols].astype(f32)
-        gp[RIM : RIM + SPAN, cols] = gco
-        gcb[:, cols] += jnp.sum(gco, axis=0, keepdims=True)
-        own = cin[0, RIM:, cols].astype(f32)
-        before = cin[0, :RIM, cols].astype(f32)
-        main = jnp.zeros((SPAN, HALF), f32)
-        rim = jnp.zeros((RIM, HALF), f32)
-        for k in range(KCONV):
-            ahead = KCONV - 1 - k
-            moved = gp[RIM + ahead : RIM + ahead + SPAN, cols]
-            early = gp[ahead : ahead + RIM, cols]
-            main = main + cw[k : k + 1, cols] * moved
-            rim = rim + cw[k : k + 1, cols] * early
-            gcw[k : k + 1, cols] += jnp.sum(own * moved, axis=0, keepdims=True) + jnp.sum(
-                before * early, axis=0, keepdims=True
-            )
-        gz[0, :, cols] = main.astype(bf16)
-        gzh[0, :, cols] = rim.astype(bf16)
-
-    wave(3 * s)
-    loop(0, CONVW // HALF, out_step)
-
-    @pl.when(s == seqs - 1)
-    def _():
-        loop(3 * seqs - 2, reducers[0].chunks + reducers[1].chunks + 4, wave)
-        for r in reducers:
-            loop(0, r.chunks, r.drain)
-
-
-def tail_kernel(
-    rel, tok, halo, cot, gain, ggate, gz, gzh, wfull, pconv, small,
-    gtok, rconv, small_out,
-    ggain, rim_out, rim_in, rim_send, rim_recv, *comm,
-):
-    s = pl.program_id(0)
-    seqs = pl.num_programs(0)
+    i = pl.program_id(0)
+    seqs = rhalo.shape[0]
     count = lax.axis_size("ctx")
     me = lax.axis_index("ctx")
-    reducer = Reducer(pconv, rconv, D // lax.axis_size("group"), CONV_CHUNK, False, comm[:8], comm[8])
-    little = Small(*comm[9:13])
+    members = lax.axis_size("group")
+    gates = Reducer(pgate, rgate, D // members, GATE_CHUNK, False, comm[0:7], comm[7])
+    outs = Reducer(pout, rout, DIN // members, OUT_CHUNK, True, comm[8:15], comm[15])
+    convs = Reducer(pconv, rconv, D // members, CONV_CHUNK, False, comm[16:23], comm[23])
+    little, least = Small(*comm[24:28]), Small(*comm[28:32])
+    last_x = TILES - 1
+    bc_step = TILES
+
+    def wave(t):
+        gates.wave(t - 4)
+        outs.wave(t - 4 - gates.chunks)
+        convs.wave(t - 2 * bc_step - 1)
 
     def rim_copy(q):
         return remote(rim_out.at[q], rim_in.at[q], rim_send.at[q], rim_recv.at[q], ctx=lax.rem(me + count - 1, count))
+
+    def span(s):
+        return pl.ds(pl.multiple_of(s * SPAN, SPAN), SPAN)
+
+    def edge(s):
+        return pl.ds(pl.multiple_of(s * RIM, RIM), RIM)
 
     def back(rows, grad):
         rows, inv, _ = normalized(rows, gain[...])
@@ -1097,51 +1002,177 @@
         mean = jnp.mean(gained * rows, axis=-1, keepdims=True)
         return inv * gained - rows * (inv * inv * inv * mean)
 
-    @pl.when(s == 0)
+    @pl.when(i == 0)
     def _():
         meet(("ctx", "group"))
-        loop(0, reducer.chunks, reducer.m_start)
-        ggain[...] = jnp.zeros_like(ggain)
-        for q in range(halo.shape[0]):
-            rim_out[q] = back(halo[q], mm_nt(gzh[q, :, :CONVW], wfull[:, DIN:ZXW])).astype(bf16)
+        for r in (gates, outs):
+            loop(0, r.chunks, r.m_start)
+        sel[...] = head_map()
+        for acc in (db_s, qacc, ends, gcw, gcb, gdb, gdl, ggain):
+            acc[...] = jnp.zeros_like(acc)
+        gp[0:RIM] = jnp.zeros((RIM, TILE), f32)
+        gp[RIM + SPAN :] = jnp.zeros((8, TILE), f32)
+        pconv[:, CONVW + HALF :] = jnp.zeros((D, GZW - CONVW - HALF), bf16)
+
+        def setup(s):
+            dt = softplus(vin[s])
+            _, e_out, _, tot1, total = local_decays(cumin[s])
+            dt_cat[s] = jnp.concatenate(halves(dt), axis=1)
+            eo_cat[s] = jnp.concatenate(halves(e_out), axis=1)
+            both_rows = jnp.concatenate([rows_of(tot1), rows_of(total)], axis=0)
+            tots[s] = spread(both_rows, sel)
+
+        loop(0, seqs, setup)
+
+    def conv_back(s, dact, cols):
+        gco = dact * spb[s].astype(f32)
+        gp[RIM : RIM + SPAN] = gco
+        gcb[:, cols] += jnp.sum(gco, axis=0, keepdims=True)
+        own = cin[s, RIM:].astype(f32)
+        before = cin[s, :RIM].astype(f32)
+        main = jnp.zeros((SPAN, TILE), f32)
+        rim = jnp.zeros((RIM, TILE), f32)
+        for k in range(KCONV):
+            ahead = KCONV - 1 - k
+            moved = gco if ahead == 0 else gp[RIM + ahead : RIM + ahead + SPAN]
+            early = gp[ahead : ahead + RIM]
+            main = main + cw[k : k + 1, cols] * moved
+            rim = rim + cw[k : k + 1, cols] * early
+            gcw[k : k + 1, cols] += jnp.sum(own * moved, axis=0, keepdims=True) + jnp.sum(
+                before * early, axis=0, keepdims=True
+            )
+        gz_s[span(s), cols] = main.astype(bf16)
+        gzh_s[edge(s), cols] = rim.astype(bf16)
+
+    def partial(cols):
+        pconv[:, cols] = (mm(nt[...], gz_s[:, cols]) + mm(nth[...], gzh_s[:, cols])).astype(bf16)
+
+    wave(2 * i)
+
+    @pl.when(jnp.logical_and(lax.rem(i, 2) == 0, jnp.logical_and(i >= 2, i <= bc_step)))
+    def _():
+        convs.m_done(lax.div(i, 2) - 1)
+
+    @pl.when(i == bc_step + 1)
+    def _():
+        convs.m_done(convs.chunks - 1)
+
+    @pl.when(i < bc_step)
+    def _():
+        cols = pl.ds(pl.multiple_of(i * TILE, TILE), TILE)
+
+        def x_tile(s):
+            dte = mm(dt_cat[s], sel[:, cols])
+            eo = mm(eo_cat[s], sel[:, cols])
+            near = later[s]
+            near32 = near.astype(f32)
+            tot = tots[s, :, cols]
+            reach = [(dir1[s].astype(f32) + tot[0:1] * near32).astype(bf16), near]
+            fed = jnp.concatenate(
+                [mm(bc[s, both(q), :NSTATE], reach[q]) for q in range(2)], axis=0
+            )
+            x = xb[s].astype(f32)
+            dx_s = dxs[s].astype(f32) + eo * fed
+            qacc[s] += gather_heads(x * dx_s, sel[:HALF, cols])
+            xw = (x * dte * eo).astype(bf16)
+            for q in range(2):
+                db_s[s, both(q)] += mm_nt(xw[both(q)], reach[q])
+            held = near32 * (tot[8:9] * sin[s].astype(f32) + loc[s].astype(f32))
+            ends[s] += gather_heads(rows_of(jnp.sum(held, axis=0, keepdims=True)), sel[:HALF, cols])
+            conv_back(s, dte * dx_s + skip[:, cols] * dy[s].astype(f32), cols)
+
+        loop(0, seqs // 2, x_tile)
+
+        @pl.when(i == 0)
+        def _():
+            for r in (gates, outs):
+                loop(0, r.chunks, r.m_done)
+
+        wave(2 * i + 1)
+        loop(seqs // 2, seqs, x_tile)
+        partial(cols)
+
+        @pl.when(lax.rem(i, 2) == 1)
+        def _():
+            convs.m_start(lax.div(i, 2))
+
+    @pl.when(i == bc_step)
+    def _():
+        cols = slice(DIN, CONVW)
+
+        def bc_tile(s):
+            conv_back(s, jnp.concatenate([dbc[s, :, :NSTATE] + db_s[s], dbc[s, :, NSTATE:]], axis=1), cols)
+            v = vin[s]
+            dt = softplus(v)
+            q = qacc[s]
+            at_end = lax.broadcasted_iota(jnp.int32, (SPAN, 1), 0) == SPAN - 1
+            dcum = wred[s] - dt * q + jnp.where(at_end, ends[s][0:1], 0.0)
+            glog = exact_mm(triangle(SPAN, False), dcum)
+            rate = jnp.exp(dl[...])
+            gpd = (q - rate * glog) * sigmoid(v)
+            lanes = lax.broadcasted_iota(jnp.int32, (SPAN, HALF), 1) < HEADS
+            gpd = jnp.where(lanes, gpd, 0.0)
+            gz_s[span(s), CONVW : CONVW + HALF] = gpd.astype(bf16)
+            gdb[...] += jnp.sum(gpd, axis=0, keepdims=True)
+            gdl[...] += -rate * jnp.sum(dt * glog, axis=0, keepdims=True)
+
+        loop(0, seqs, bc_tile)
+        wave(2 * i + 1)
+        partial(cols)
+        pconv[:, CONVW : CONVW + HALF] = mm(nt[...], gz_s[:, CONVW : CONVW + HALF]).astype(bf16)
+        convs.m_start(convs.chunks - 1)
+        rows = [gcw[k : k + 1, j * HALF : (j + 1) * HALF] for k in range(KCONV) for j in range(CONVW // HALF)]
+        rows += [gcb[:, j * HALF : (j + 1) * HALF] for j in range(CONVW // HALF)]
+        rows += [gdb[...], gdl[...]]
+        rows += [gskip[:, j * HALF : (j + 1) * HALF] for j in range(PAIRS)]
+        rows += [gggain[:, j * HALF : (j + 1) * HALF] for j in range(PAIRS)]
+        for r, row in enumerate(rows):
+            little.held[0, r : r + 1, :] = row
+        little.start(0)
+        edges = mm_nt(gzh_s[...], wfull[:, DIN:ZXW])
+        for q in range(seqs):
+            rim_out[q] = back(rhalo[q], edges[q * RIM : (q + 1) * RIM]).astype(bf16)
             pl.when(me > 0)(lambda q=q: rim_copy(q).start())
 
         @pl.when(me == count - 1)
         def _():
             rim_in[...] = jnp.zeros_like(rim_in)
 
-        loop(0, reducer.chunks, reducer.m_done)
-
-    @pl.when(s > 0)
-    def _():
-        reducer.wave(s - 1)
-
-    grad = mm_nt(ggate[0], wfull[:, :DIN]) + mm_nt(gz[0, :, : CONVW + HALF], wfull[:, DIN:])
-    live = (lax.broadcasted_iota(jnp.int32, (SPAN, 1), 0) < rel[s]).astype(f32)
-    out = live * cot[0].astype(f32) + back(tok[0], grad)
-    gtok[0, : SPAN - RIM] = out[: SPAN - RIM].astype(bf16)
-    pl.when(me < count - 1)(lambda: rim_copy(s).wait_recv())
-    gtok[0, SPAN - RIM :] = (out[SPAN - RIM :] + rim_in[s].astype(f32)).astype(bf16)
-
-    @pl.when(s == seqs - 1)
-    def _():
-        held = comm[9]
-        held[0] = small[...]
+    @pl.when(i == bc_step + 2)
+    def _():
+        little.done(0)
+        little.start(1)
+
+    @pl.when(i > bc_step)
+    def _():
+        s = i - bc_step - 1
+        grad = mm_nt(gz_s[span(s), :], wfull[:, DIN:]) + mm_nt(ggate[0], wfull[:, :DIN])
+        wave(2 * i + 1)
+        live = (lax.broadcasted_iota(jnp.int32, (SPAN, 1), 0) < rel[s]).astype(f32)
+        out = live * cot[0].astype(f32) + back(tok[0], grad)
+        gtok[0, : SPAN - RIM] = out[: SPAN - RIM].astype(bf16)
+        pl.when(me < count - 1)(lambda: rim_copy(s).wait_recv())
+        gtok[0, SPAN - RIM :] = (out[SPAN - RIM :] + rim_in[s].astype(f32)).astype(bf16)
+
+    @pl.when(i == bc_step + seqs)
+    def _():
+        least.held[0] = jnp.zeros_like(least.held[0])
         for j in range(D // HALF):
-            held[0, j : j + 1, :] = ggain[:, j * HALF : (j + 1) * HALF]
-        little.start(0)
-        first = halo.shape[0] - 1
-        for h in range(4):
-            reducer.wave(first + h)
-            little.done(h)
-            if h < 3:
-                little.start(h + 1)
-        small_out[...] = held[4]
-        loop(first + 4, reducer.chunks + 4, reducer.wave)
-        loop(0, reducer.chunks, reducer.drain)
+            least.held[0, j : j + 1, :] = ggain[:, j * HALF : (j + 1) * HALF]
+        least.start(0)
+        little.done(1)
+        small_out[...] = little.held[2]
+        least.done(0)
+        least.start(1)
+        loop(2 * (bc_step + seqs) + 2, 2 * bc_step + 1 + convs.chunks + 4, wave)
+        for r in (gates, outs, convs):
+            loop(0, r.chunks, r.drain)
         little.drain()
-        for q in range(halo.shape[0]):
+        for q in range(seqs):
             pl.when(me > 0)(lambda q=q: rim_copy(q).wait_send())
+        least.done(1)
+        ggain_out[...] = least.held[2]
+        least.drain()
 
 
 def whole(shape):
@@ -1221,30 +1252,30 @@
         return pl.BlockSpec((seqs, rows, TILE), index)
 
     state = (seqs, NSTATE, DIN)
-    normed, nhalo, rhalo, cin, xb, spb, vraw, cum, st0, loc, ylocal, gate, decs, wfull, wofull, state_in = call(
+    nt, nth, rhalo, cin, xb, spb, vraw, cum, st0, loc, ylocal, gate, decs, wfull, wofull, state_in = call(
         front_kernel,
         PIECES,
         [whole((seqs, SPAN, D)), ANY, ANY, ANY, whole((1, D)), whole((KCONV, CONVW)), whole((1, CONVW)), whole((1, HALF)),
          whole((1, HALF))],
         [
-            (summed((seqs, SPAN, D)), (seqs, SPAN, D), bf16),
-            (summed((seqs, RIM, D)), (seqs, RIM, D), bf16),
+            (summed((D, seqs * SPAN)), (D, seqs * SPAN), bf16),
+            (summed((D, seqs * RIM)), (D, seqs * RIM), bf16),
             (summed((seqs, RIM, D)), (seqs, RIM, D), bf16),
             (tiled(RIM + SPAN, 1, TILES), (seqs, RIM + SPAN, CONVW), bf16),
             (tiled(SPAN, 1, TILES), (seqs, SPAN, CONVW), bf16),
             (tiled(SPAN, 1, TILES), (seqs, SPAN, CONVW), bf16),
             (summed((seqs, SPAN, HALF)), (seqs, SPAN, HALF), f32),
             (summed((seqs, SPAN, HALF)), (seqs, SPAN, HALF), f32),
-            (tiled(NSTATE, 1), state, f32),
             (tiled(NSTATE, 1), state, bf16),
-            (tiled(SPAN, TILES + 1), (seqs, SPAN, DIN), f32),
-            (tiled(SPAN, TILES + 1), (seqs, SPAN, DIN), f32),
+            (tiled(NSTATE, 1), state, bf16),
+            (tiled(SPAN, TILES + 1), (seqs, SPAN, DIN), bf16),
+            (tiled(SPAN, TILES + 1), (seqs, SPAN, DIN), bf16),
             (summed((seqs, count * 8, HALF)), (seqs, count * 8, HALF), f32),
             (ANY, (D, ZXW + HALF), bf16),
             (ANY, (DIN, D), bf16),
             (ANY, state, bf16),
         ],
-        [((2 * HALF, DIN), bf16), ((seqs, RIM, D), bf16), ((seqs, RIM + SPAN, D), bf16), ((D, ZXW + HALF), bf16),
+        [((2 * HALF, DIN), bf16), ((seqs, RIM, D), bf16), ((seqs * RIM, D), f32), ((seqs, RIM + SPAN, D), bf16), ((D, ZXW + HALF), bf16),
          ((seqs, RIM + SPAN, TILE), f32), ((seqs, SPAN, DIN), bf16), ((seqs, NSTATE, SPAN), bf16),
          ((seqs, 2, HALF, HALF), f32), ((seqs, SPAN, 2 * HALF), bf16), ((seqs, SPAN, 2 * HALF), bf16),
          ((seqs, 2, HALF, HALF), f32), ((seqs, 8, DIN), f32), ((seqs, count * 8, HALF), f32)]
@@ -1266,10 +1297,10 @@
             (at0(SPAN, DIN), (seqs, SPAN, DIN), bf16),
             (at0(SPAN, DIN), (seqs, SPAN, DIN), bf16),
             (at0(SPAN, HALF), (seqs, SPAN, HALF), f32),
-            (at0(NSTATE, DIN), (seqs, NSTATE, DIN), f32),
+            (at0(NSTATE, DIN), (seqs, NSTATE, DIN), bf16),
             (summed((1, DIN)), (1, DIN), f32),
             (summed((1, DIN)), (1, DIN), f32),
-            (at1(SPAN, DIN), (seqs, SPAN, DIN), f32),
+            (at1(SPAN, DIN), (seqs, SPAN, DIN), bf16),
             (at1(SPAN, 2 * NSTATE), (seqs, SPAN, 2 * NSTATE), f32),
             (ANY, (seqs, NSTATE, DIN), bf16),
         ],
@@ -1285,58 +1316,49 @@
     drive = (live * cotangent.astype(f32)).astype(bf16)
     flat = lambda v: v.reshape(-1, v.shape[-1])
     p_out = mm_tn(flat(mlow), flat(drive)).astype(bf16)
-    p_gate = mm_tn(flat(normed), flat(ggate)).astype(bf16)
-
-    gz, gzh, gcw, gcb, gdb, gdl, r_gate, r_out = call(
-        third_kernel,
-        seqs,
-        [per_seq(RIM + SPAN, CONVW), per_seq(SPAN, CONVW), per_seq(SPAN, CONVW), per_seq(SPAN, HALF), per_seq(SPAN, HALF),
-         per_seq(SPAN, DIN), per_seq(SPAN, HALF), per_seq(SPAN, DIN), per_seq(SPAN, 2 * NSTATE), per_seq(NSTATE, DIN),
-         per_seq(NSTATE, DIN), per_seq(NSTATE, DIN), per_seq(NSTATE, DIN), whole((KCONV, CONVW)), whole((1, HALF)),
-         whole((1, DIN)), whole((D, DIN)), whole((DIN, D))],
+    p_gate = mm(nt, flat(ggate)).astype(bf16)
+
+    def tile_in(rows, tiles):
+        return pl.BlockSpec((seqs, rows, TILE), lambda i: (0, 0, jnp.minimum(i, tiles - 1)))
+
+    def late(*shape):
+        zeros = (0,) * len(shape)
+        return pl.BlockSpec((1,) + shape, lambda i: (jnp.clip(i - TILES - 1, 0, seqs - 1),) + zeros)
+
+    bc_spec = pl.BlockSpec((seqs, SPAN, TILE), lambda i: (0, 0, TILES), pipeline_mode=pl.Buffered(1))
+    sizes = (KCONV * CONVW, CONVW, HALF, HALF, DIN, DIN)
+    height = sum(sizes) // HALF
+    gtok, r_gate, r_out, r_conv, small, g_gain = call(
+        back_kernel,
+        TILES + 1 + seqs,
+        [SMEM, late(SPAN, D), late(SPAN, D), whole((seqs, RIM, D)), whole((1, D)), late(SPAN, DIN), whole((D, ZXW + HALF)),
+         tile_in(RIM + SPAN, TILES + 1), tile_in(SPAN, TILES + 1), tile_in(SPAN, TILES + 1), bc_spec, tile_in(SPAN, TILES),
+         tile_in(SPAN, TILES), tile_in(NSTATE, TILES), tile_in(NSTATE, TILES), tile_in(NSTATE, TILES), tile_in(NSTATE, TILES),
+         whole((seqs, SPAN, HALF)), whole((seqs, SPAN, HALF)), whole((seqs, SPAN, HALF)), whole((seqs, SPAN, 2 * NSTATE)),
+         whole((KCONV, CONVW)), whole((1, HALF)), whole((1, DIN)), whole((D, seqs * SPAN)), whole((D, seqs * RIM)),
+         whole((D, DIN)), whole((DIN, D)), whole((1, DIN)), whole((1, DIN))],
         [
-            (per_seq(SPAN, GZW), (seqs, SPAN, GZW), bf16),
-            (per_seq(RIM, GZW), (seqs, RIM, GZW), bf16),
-            (summed((KCONV, CONVW)), (KCONV, CONVW), f32),
-            (summed((1, CONVW)), (1, CONVW), f32),
-            (summed((1, HALF)), (1, HALF), f32),
-            (summed((1, HALF)), (1, HALF), f32),
+            (late(SPAN, D), (seqs, SPAN, D), bf16),
             (summed((D // group, DIN)), (D // group, DIN), bf16),
             (summed((DIN // group, D)), (DIN // group, D), bf16),
-        ],
-        [((2 * HALF, DIN), bf16), ((SPAN, DIN), f32), ((SPAN, DIN), f32), ((SPAN, CONVW), f32), ((SPAN, DIN), bf16),
-         ((2, NSTATE, DIN), bf16), ((SPAN, HALF), f32), ((RIM + SPAN + 8, CONVW), f32)]
-        + Reducer.scratch(DIN // GATE_CHUNK, D // group, GATE_CHUNK, False, group, count)
-        + Reducer.scratch(D // OUT_CHUNK, DIN // group, OUT_CHUNK, True, group, count),
-        "third",
-        2,
-    )(cin, xb, spb, vraw, cum, dy, wred, dxs, dbc, dir1, later, state_in, loc, conv_weight, dl, skip, p_gate, p_out)
-
-    p_conv = (mm_tn(flat(normed), flat(gz)) + mm_tn(flat(nhalo), flat(gzh))).astype(bf16)
-    sizes = (D, KCONV * CONVW, CONVW, HALF, HALF, DIN, DIN)
-    small = jnp.concatenate(
-        [jnp.zeros((D,), f32), gcw.reshape(-1), gcb.reshape(-1), gdb[0], gdl[0], gskip.reshape(-1), gggain.reshape(-1)]
-    ).reshape(-1, HALF)
-    small = jnp.pad(small, ((0, -small.shape[0] % 8), (0, 0)))
-    height = small.shape[0]
-    widest = max(group // 2, count // 2, 2)
-
-    gtok, r_conv, small = call(
-        tail_kernel,
-        seqs,
-        [SMEM, per_seq(SPAN, D), whole((seqs, RIM, D)), per_seq(SPAN, D), whole((1, D)), per_seq(SPAN, DIN),
-         per_seq(SPAN, GZW), whole((seqs, RIM, GZW)), whole((D, ZXW + HALF)), whole((D, GZW)), whole((height, HALF))],
-        [
-            (per_seq(SPAN, D), (seqs, SPAN, D), bf16),
             (summed((D // group, GZW)), (D // group, GZW), bf16),
             (summed((height, HALF)), (height, HALF), f32),
+            (summed((8, HALF)), (8, HALF), f32),
         ],
-        [((1, D), f32), ((seqs, RIM, D), bf16), ((seqs, RIM, D), bf16), dma((seqs,)), dma((seqs,))]
+        [((2 * HALF, DIN), bf16), ((seqs, SPAN, 2 * HALF), bf16), ((seqs, SPAN, 2 * HALF), bf16), ((seqs, 16, DIN), f32),
+         ((seqs, SPAN, NSTATE), f32), ((seqs, SPAN, HALF), f32), ((seqs, 8, HALF), f32), ((RIM + SPAN + 8, TILE), f32),
+         ((seqs * SPAN, CONVW + HALF), bf16), ((seqs * RIM, CONVW), bf16), ((D, GZW), bf16), ((KCONV, CONVW), f32),
+         ((1, CONVW), f32), ((1, HALF), f32), ((1, HALF), f32), ((1, D), f32), ((seqs, RIM, D), bf16), ((seqs, RIM, D), bf16),
+         dma((seqs,)), dma((seqs,))]
+        + Reducer.scratch(DIN // GATE_CHUNK, D // group, GATE_CHUNK, False, group, count)
+        + Reducer.scratch(D // OUT_CHUNK, DIN // group, OUT_CHUNK, True, group, count)
         + Reducer.scratch(GZW // CONV_CHUNK, D // group, CONV_CHUNK, False, group, count)
-        + [((5, height, HALF), f32), ((4, widest, height, HALF), f32), dma((4, widest)), dma((4, widest))],
-        "tail",
-        3,
-    )(rel, tokens_in, rhalo, cotangent, gain, ggate, gz, gzh, wfull, p_conv, small)
+        + Small.scratch(height, group, count)
+        + Small.scratch(8, group, count),
+        "back",
+        2,
+    )(rel, tokens_in, cotangent, rhalo, gain, ggate, wfull, cin, xb, spb, xb, dy, dxs, dir1, later, state_in, loc,
+      vraw, cum, wred, dbc, conv_weight, dl, skip, nt, nth, p_gate, p_out, gskip, gggain)
 
     g_zx = jnp.concatenate([r_gate, r_conv[:, :CONVW]], axis=1).astype(f32)
     g_delta = r_conv[:, CONVW : CONVW + HEADS].astype(f32)
@@ -1347,8 +1369,8 @@
         pieces.append(small[at : at + size])
         at += size
     return (
-        mixed_out, gtok, pieces[0], g_zx, g_delta, r_out.astype(f32), pieces[1].reshape(KCONV, CONVW), pieces[2],
-        pieces[3][:HEADS], pieces[4][:HEADS], pieces[5].reshape(HEADS, HEADDIM).sum(1), pieces[6],
+        mixed_out, gtok, g_gain.reshape(-1)[:D], g_zx, g_delta, r_out.astype(f32), pieces[0].reshape(KCONV, CONVW), pieces[1],
+        pieces[2][:HEADS], pieces[3][:HEADS], pieces[4].reshape(HEADS, HEADDIM).sum(1), pieces[5],
     )
 
 

time: 335 us -> 321 us (0.958)
  matrix products: 18.3 us -> 10.3 us
    dot_general x4 -> x1, matrix products: 18.3 us -> 4.24 us  [mm_tn(): return lax.dot_general(a, b, TN, preferred_element_type=f32)]
    dot_general x0 -> x1, matrix products: none -> 6.03 us  [mm(): return jnp.dot(a, b, preferred_element_type=f32)]
    pallas_call x2 -> x1, Pallas kernels: 125 us -> 123 us  [local(): call(back_kernel, TILES + 1 + seqs, [SMEM, late(SPAN, D), late(SPAN, D),...]
where the time goes in v5:
time: 321 us; the launch traced here: 320 us
  Pallas kernels  288 us (90%)
  local copies, waits for them, and re-layouts  13 us (4%)
  matrix products  10.3 us (3%)
  other arithmetic  8.4 us (3%)
    pallas_call x1, Pallas kernels, local(): call(back_kernel, TILES + 1 + seqs, [SMEM, late(SPAN, D), late(SPAN, D),...  123 us
    pallas_call x1, Pallas kernels, local(): call(middle_kernel, 2 * seqs, [SMEM, at1(SPAN, D), at0(SPAN, D), at0(SPAN...  84.5 us
    pallas_call x1, Pallas kernels, local(): call(front_kernel, PIECES, [whole((seqs, SPAN, D)), ANY, ANY, ANY, whole(...  80 us

profile of v5, /device:TPU:0, one launch (start us, length us, event | category | flops | bytes accessed | tf_op | source)
XLA Modules:
  0.0 320.3 jit_solution(3504971565635007869)
XLA Ops:
  0.7 1.3 broadcast_in_dim.21.gain
  1.9 1.2 pad.13.dl
  3.1 0.8 copy.25
  3.9 2.5 fusion.2.wcat
  6.4 0.6 broadcast_in_dim.22.cb
  7.0 0.5 pad.12.db
  7.5 80.0 %front.1 = (bf16[768,1024]{1,0:T(8,128)(2,1)}, bf16[768,64]{1,0:T(8,128)(2,1)}, bf16[4,16,768]{2,1,0:T(8,128)(2,1)}, bf16[4,272,1792]{2,1,0:T(8,128)(2,1)}, bf16...) custom-call(bf16[4,256,768]{2,1,0:T(8,128)(2,1)} %tok.5, ...), custom_call_target="tpu_custom_call" | custom-call | tf_op jit(solution)/shard_map/front/pallas_call | solution.py:1255
  87.6 0.5 broadcast_subtract_fusion.rel
  88.1 0.1 broadcast_in_dim.25
  88.1 0.7 broadcast_in_dim_reshape.3.skip
  88.8 0.6 broadcast_in_dim.26.ggain
  89.4 84.5 %middle.1 = (bf16[4,256,768]{2,1,0:T(8,128)(2,1)}, bf16[4,256,1536]{2,1,0:T(8,128)(2,1)}, bf16[4,256,1536]{2,1,0:T(8,128)(2,1)}, bf16[4,256,1536]{2,1,0:T(8,128)...) custom-call(s32[4]{0:T(128)} %broadcast_subtract_fusion.rel, ...), custom_call_target="tpu_custom_call" | custom-call | tf_op jit(solution)/shard_map/middle/pallas_call | solution.py:1288
  174.0 0.0 copy-start.8
  174.0 0.0 copy-start
  174.0 6.0 %convolution_convert_fusion.pgate = bf16[768,1536]{1,0:T(8,128)(2,1)} fusion(bf16[768,1024]{1,0:T(8,128)(2,1)S(1)} %copy-done.1, bf16[1024,1536]{1,0:T(8,128)(2,1)} %bitcast.18), kind=kOutput, calls=%fused_computation.1 | convolution fusion | flops 2417098752 | bytes 7077888 | tf_op jit(solution)/shard_map/dot_general | solution.py:39
  180.0 0.1 fusion.3
  180.1 4.2 %bitcast_convert_fusion.pout = bf16[1536,768]{1,0:T(8,128)(2,1)} fusion(bf16[4,256,1536]{2,1,0:T(8,128)(2,1)S(1)} %copy-done.11, bf16[4,256,768]{2,1,0:T(8,128)(2,1)S(1)} %copy-done, f32[4,256]{1,0:T(4,128)S(1)} %fusion.3), kind=kOutput, calls=%fused_computation | convolution fusion | flops 2419458048 | bytes 7081984 | tf_op jit(solution)/shard_map/dot_general | solution.py:47
  184.4 123.4 %back.1 = (bf16[4,256,768]{2,1,0:T(8,128)(2,1)}, bf16[192,1536]{1,0:T(8,128)(2,1)}, bf16[384,768]{1,0:T(8,128)(2,1)}, bf16[192,2048]{1,0:T(8,128)(2,1)}, f32[96,128]{1,0:T(8,128)}, /*index=5*/f32[8,128]{1,0:T(8,128)}) custom-call(s32[4]{0:T(128)} %broadcast_subtract_fusion.rel, bf16[4,256,768]{2,1,0:T(8,128)(2,1)} %tok.5, bf16[4,256,768]{2,1,0:T(8,128)(2,1)} %cot.3, ...), custom_call_target="tpu_custom_call" | custom-call | tf_op jit(solution)/shard_map/back/pallas_call | solution.py:1331
  307.8 1.2 slice.52
  309.0 2.8 maximum_convert_fusion
  311.8 1.1 convert_element_type.40
  312.9 0.8 slice_convert_fusion
  313.7 0.7 copy.27
  314.4 0.6 reshape.71
  315.0 0.6 slice_bitcast_fusion
  315.6 0.1 reshape.72
  315.7 0.6 reduce_sum.9
  316.3 0.6 slice_bitcast_fusion.1
  316.9 0.6 slice_bitcast_fusion.2
  317.5 0.5 slice_bitcast_fusion.3
  318.1 1.1 copy.31
  319.2 1.1 copy.32
  (27 shorter events, 0.1 us)
Async XLA Ops:
  0.6 5.8 %copy-start.7 = (f32[1792]{0:T(1024)S(1)}, f32[1792]{0:T(1024)}, u32[]{:S(2)}) copy-start(f32[1792]{0:T(1024)} %param.20) | copy-start | bytes 21508
  0.7 6.3 %copy-start.12 = (f32[24]{0:T(128)S(1)}, f32[24]{0:T(128)}, u32[]{:S(2)}) copy-start(f32[24]{0:T(128)} %param.21) | copy-start | bytes 292
  7.5 80.0 %copy-start.13 = (s32[4]{0:T(128)S(1)}, s32[4]{0:T(128)}, u32[]{:S(2)}) copy-start(s32[4]{0:T(128)} %param.14) | copy-start | bytes 52
  7.5 80.6 %copy-start.10 = (f32[24]{0:T(128)S(1)}, f32[24]{0:T(128)}, u32[]{:S(2)}) copy-start(f32[24]{0:T(128)} %param.23) | copy-start | bytes 292
  7.5 81.3 %copy-start.6 = (f32[1536]{0:T(1024)S(1)}, f32[1536]{0:T(1024)}, u32[]{:S(2)}) copy-start(f32[1536]{0:T(1024)} %param.24) | copy-start | bytes 18436
  89.4 84.5 %copy-start.1 = (bf16[768,1024]{1,0:T(8,128)(2,1)S(1)}, bf16[768,1024]{1,0:T(8,128)(2,1)}, u32[]{:S(2)}) copy-start(bf16[768,1024]{1,0:T(8,128)(2,1)} %get-tuple-element.67.nt) | copy-start | bytes 4718596
  174.0 6.1 %copy-start.8 = (s32[4]{0:T(128)S(1)}, s32[4]{0:T(128)}, u32[]{:S(2)}) copy-start(s32[4]{0:T(128)} %broadcast_subtract_fusion.rel) | copy-start | bytes 52
  174.0 6.1 %copy-start = (bf16[4,256,768]{2,1,0:T(8,128)(2,1)S(1)}, bf16[4,256,768]{2,1,0:T(8,128)(2,1)}, u32[]{:S(2)}) copy-start(bf16[4,256,768]{2,1,0:T(8,128)(2,1)} %cot.3) | copy-start | bytes 4718596
  174.0 6.1 %copy-start.11 = (bf16[4,256,1536]{2,1,0:T(8,128)(2,1)S(1)}, bf16[4,256,1536]{2,1,0:T(8,128)(2,1)}, u32[]{:S(2)}) copy-start(bf16[4,256,1536]{2,1,0:T(8,128)(2,1)} %get-tuple-element.69) | copy-start | bytes 9437188
  307.7 4.1 %copy-start.4 = (bf16[384,768]{1,0:T(8,128)(2,1)S(1)}, bf16[384,768]{1,0:T(8,128)(2,1)}, u32[]{:S(2)}) copy-start(bf16[384,768]{1,0:T(8,128)(2,1)} %get-tuple-element.76) | copy-start | bytes 1769476
  309.0 5.4 %copy-start.5 = (f32[96,128]{1,0:T(8,128)S(1)}, f32[96,128]{1,0:T(8,128)}, u32[]{:S(2)}) copy-start(f32[96,128]{1,0:T(8,128)} %get-tuple-element.77) | copy-start | bytes 147460
  309.0 8.0 %copy-start.9 = (f32[8,128]{1,0:T(8,128)S(1)}, f32[8,128]{1,0:T(8,128)}, u32[]{:S(2)}) copy-start(f32[8,128]{1,0:T(8,128)} %get-tuple-element.73) | copy-start | bytes 12292
  309.0 9.1 %copy-start.2 = (bf16[4,256,768]{2,1,0:T(8,128)(2,1)S(1)}, bf16[4,256,768]{2,1,0:T(8,128)(2,1)}, u32[]{:S(2)}) copy-start(bf16[4,256,768]{2,1,0:T(8,128)(2,1)} %get-tuple-element.106) | copy-start | bytes 4718596
  311.8 7.4 %copy-start.3 = (bf16[4,256,768]{2,1,0:T(8,128)(2,1)S(1)}, bf16[4,256,768]{2,1,0:T(8,128)(2,1)}, u32[]{:S(2)}) copy-start(bf16[4,256,768]{2,1,0:T(8,128)(2,1)} %get-tuple-element.107) | copy-start | bytes 4718596

commit v6 on v5

--- a/solution.py
+++ b/solution.py
@@ -28,6 +28,8 @@
 GATE_CHUNK = 512
 OUT_CHUNK = 256
 CONV_CHUNK = 512
+BACK_LAGS = (5, 7, 9)
+STAGE_LAG = 2
 MIDDLE_LAG = 2
 SCAN_LAG = 4
 HOPS = ("group", "ctx")
@@ -513,7 +515,7 @@
 
     def wave(self, t):
         for lag, act in ((4, self.f_done), (3, self.b_done), (2, self.z_done), (1, self.y_done), (0, self.x_done)):
-            k = t - lag
+            k = t - lag * STAGE_LAG
             pl.when(jnp.logical_and(k >= 0, k < self.chunks))(lambda k=k, act=act: act(k))
 
     @staticmethod
@@ -719,8 +721,8 @@
     def _():
         zx.finish(i, piece(i))
 
-    def act_at(lag, act):
-        u = i - 1 - lag
+    def act_at(t, lag, act):
+        u = t - 1 - lag
         pl.when(jnp.logical_and(u >= 0, u < TILES))(lambda: act(u))
 
     def close(u):
@@ -739,9 +741,12 @@
     def _():
         other_blocks(lambda b: dec_copy(b, b).wait_recv())
 
-    act_at(CLOSE_LAG, close)
-    act_at(SCAN_LAG, scan)
-    act_at(MIDDLE_LAG, middle)
+    def wave(t):
+        act_at(t, CLOSE_LAG, close)
+        act_at(t, SCAN_LAG, scan)
+        act_at(t, MIDDLE_LAG, middle)
+
+    wave(i)
 
     @pl.when(jnp.logical_and(i >= 1, i <= TILES))
     def _():
@@ -789,7 +794,7 @@
         keep_w.start()
         decs_out[...] = decs[...]
         wo.forward(last, slice(None))
-        loop(TILES + TILES - CLOSE_LAG, TILES, close)
+        loop(PIECES, TILES + CLOSE_LAG + 1, wave)
         loop(0, TILES, ex.finish)
         wo.finish(last, slice(None))
         wo.finish_chip(1)
@@ -822,9 +827,9 @@
 
             pl.when(jnp.logical_and(t >= lag, jnp.logical_and(2 * u + lag == t, u < seqs)))(run)
 
-        act_at(6, ex.close)
-        act_at(5, ex.scan)
-        act_at(4, ex.middle)
+        act_at(BACK_LAGS[2], ex.close)
+        act_at(BACK_LAGS[1], ex.scan)
+        act_at(BACK_LAGS[0], ex.middle)
 
     @pl.when(i == 0)
     def _():
@@ -958,7 +963,7 @@
 
     @pl.when(i == 2 * seqs - 1)
     def _():
-        loop(4 * seqs, 2 * seqs + 5, wave)
+        loop(4 * seqs, 2 * seqs + BACK_LAGS[2] - 1, wave)
         loop(0, seqs, ex.finish)
 
 
@@ -1164,7 +1169,7 @@
         small_out[...] = little.held[2]
         least.done(0)
         least.start(1)
-        loop(2 * (bc_step + seqs) + 2, 2 * bc_step + 1 + convs.chunks + 4, wave)
+        loop(2 * (bc_step + seqs) + 2, 2 * bc_step + 1 + convs.chunks + 4 * STAGE_LAG, wave)
         for r in (gates, outs, convs):
             loop(0, r.chunks, r.drain)
         little.drain()

time: 321 us -> 296 us (0.922)
  Pallas kernels: 288 us -> 264 us
    pallas_call x1, Pallas kernels: 123 us -> 109 us  [local(): call(back_kernel, TILES + 1 + seqs, [SMEM, late(SPAN, D), late(SPAN, D),...]
    pallas_call x1, Pallas kernels: 84.5 us -> 74.4 us  [local(): call(middle_kernel, 2 * seqs, [SMEM, at1(SPAN, D), at0(SPAN, D), at0(SPAN...]
where the time goes in v6:
time: 296 us
  Pallas kernels  264 us (89%)
  local copies, waits for them, and re-layouts  13 us (4%)
  matrix products  10.3 us (3%)
  other arithmetic  8.4 us (3%)
    pallas_call x1, Pallas kernels, local(): call(back_kernel, TILES + 1 + seqs, [SMEM, late(SPAN, D), late(SPAN, D),...  109 us
    pallas_call x1, Pallas kernels, local(): call(front_kernel, PIECES, [whole((seqs, SPAN, D)), ANY, ANY, ANY, whole(...  80 us
    pallas_call x1, Pallas kernels, local(): call(middle_kernel, 2 * seqs, [SMEM, at1(SPAN, D), at0(SPAN, D), at0(SPAN...  74.4 us
    dot_general x1, matrix products, mm(): return jnp.dot(a, b, preferred_element_type=f32)  6.03 us

profile of v6, /device:TPU:0, one launch (start us, length us, event | category | flops | bytes accessed | tf_op | source)
XLA Modules:
  0.0 296.0 jit_solution(7336628919960407262)
XLA Ops:
  0.7 1.3 broadcast_in_dim.21.gain
  1.9 1.2 pad.13.dl
  3.1 0.8 copy.25
  3.9 2.5 fusion.2.wcat
  6.4 0.6 broadcast_in_dim.22.cb
  7.0 0.5 pad.12.db
  7.5 80.0 %front.1 = (bf16[768,1024]{1,0:T(8,128)(2,1)}, bf16[768,64]{1,0:T(8,128)(2,1)}, bf16[4,16,768]{2,1,0:T(8,128)(2,1)}, bf16[4,272,1792]{2,1,0:T(8,128)(2,1)}, bf16...) custom-call(bf16[4,256,768]{2,1,0:T(8,128)(2,1)} %tok.5, ...), custom_call_target="tpu_custom_call" | custom-call | tf_op jit(solution)/shard_map/front/pallas_call | solution.py:1260
  87.6 0.5 broadcast_subtract_fusion.rel
  88.1 0.1 broadcast_in_dim.25
  88.1 0.7 broadcast_in_dim_reshape.3.skip
  88.8 0.6 broadcast_in_dim.26.ggain
  89.4 74.4 %middle.1 = (bf16[4,256,768]{2,1,0:T(8,128)(2,1)}, bf16[4,256,1536]{2,1,0:T(8,128)(2,1)}, bf16[4,256,1536]{2,1,0:T(8,128)(2,1)}, bf16[4,256,1536]{2,1,0:T(8,128)...) custom-call(s32[4]{0:T(128)} %broadcast_subtract_fusion.rel, ...), custom_call_target="tpu_custom_call" | custom-call | tf_op jit(solution)/shard_map/middle/pallas_call | solution.py:1293
  163.9 0.0 copy-start.8
  163.9 0.0 copy-start
  163.9 6.0 %convolution_convert_fusion.pgate = bf16[768,1536]{1,0:T(8,128)(2,1)} fusion(bf16[768,1024]{1,0:T(8,128)(2,1)S(1)} %copy-done.1, bf16[1024,1536]{1,0:T(8,128)(2,1)} %bitcast.18), kind=kOutput, calls=%fused_computation.1 | convolution fusion | flops 2417098752 | bytes 7077888 | tf_op jit(solution)/shard_map/dot_general | solution.py:41
  169.9 0.1 fusion.3
  170.0 4.2 %bitcast_convert_fusion.pout = bf16[1536,768]{1,0:T(8,128)(2,1)} fusion(bf16[4,256,1536]{2,1,0:T(8,128)(2,1)S(1)} %copy-done.11, bf16[4,256,768]{2,1,0:T(8,128)(2,1)S(1)} %copy-done, f32[4,256]{1,0:T(4,128)S(1)} %fusion.3), kind=kOutput, calls=%fused_computation | convolution fusion | flops 2419458048 | bytes 7081984 | tf_op jit(solution)/shard_map/dot_general | solution.py:49
  174.2 109.2 %back.1 = (bf16[4,256,768]{2,1,0:T(8,128)(2,1)}, bf16[192,1536]{1,0:T(8,128)(2,1)}, bf16[384,768]{1,0:T(8,128)(2,1)}, bf16[192,2048]{1,0:T(8,128)(2,1)}, f32[96,128]{1,0:T(8,128)}, /*index=5*/f32[8,128]{1,0:T(8,128)}) custom-call(s32[4]{0:T(128)} %broadcast_subtract_fusion.rel, bf16[4,256,768]{2,1,0:T(8,128)(2,1)} %tok.5, bf16[4,256,768]{2,1,0:T(8,128)(2,1)} %cot.3, ...), custom_call_target="tpu_custom_call" | custom-call | tf_op jit(solution)/shard_map/back/pallas_call | solution.py:1336
  283.4 1.2 slice.52
  284.7 2.8 maximum_convert_fusion
  287.5 1.1 convert_element_type.40
  288.6 0.8 slice_convert_fusion
  289.4 0.7 copy.27
  290.1 0.6 reshape.71
  290.7 0.6 slice_bitcast_fusion
  291.3 0.1 reshape.72
  291.4 0.6 reduce_sum.9
  292.0 0.6 slice_bitcast_fusion.1
  292.6 0.6 slice_bitcast_fusion.2
  293.2 0.5 slice_bitcast_fusion.3
  293.7 1.1 copy.31
  294.9 1.1 copy.32
  (27 shorter events, 0.1 us)
Async XLA Ops:
  0.6 5.8 %copy-start.7 = (f32[1792]{0:T(1024)S(1)}, f32[1792]{0:T(1024)}, u32[]{:S(2)}) copy-start(f32[1792]{0:T(1024)} %param.20) | copy-start | bytes 21508
  0.7 6.3 %copy-start.12 = (f32[24]{0:T(128)S(1)}, f32[24]{0:T(128)}, u32[]{:S(2)}) copy-start(f32[24]{0:T(128)} %param.21) | copy-start | bytes 292
  7.5 80.0 %copy-start.13 = (s32[4]{0:T(128)S(1)}, s32[4]{0:T(128)}, u32[]{:S(2)}) copy-start(s32[4]{0:T(128)} %param.14) | copy-start | bytes 52
  7.5 80.6 %copy-start.10 = (f32[24]{0:T(128)S(1)}, f32[24]{0:T(128)}, u32[]{:S(2)}) copy-start(f32[24]{0:T(128)} %param.23) | copy-start | bytes 292
  7.5 81.3 %copy-start.6 = (f32[1536]{0:T(1024)S(1)}, f32[1536]{0:T(1024)}, u32[]{:S(2)}) copy-start(f32[1536]{0:T(1024)} %param.24) | copy-start | bytes 18436
  89.4 74.4 %copy-start.1 = (bf16[768,1024]{1,0:T(8,128)(2,1)S(1)}, bf16[768,1024]{1,0:T(8,128)(2,1)}, u32[]{:S(2)}) copy-start(bf16[768,1024]{1,0:T(8,128)(2,1)} %get-tuple-element.67.nt) | copy-start | bytes 4718596
  163.9 6.1 %copy-start.8 = (s32[4]{0:T(128)S(1)}, s32[4]{0:T(128)}, u32[]{:S(2)}) copy-start(s32[4]{0:T(128)} %broadcast_subtract_fusion.rel) | copy-start | bytes 52
  163.9 6.1 %copy-start = (bf16[4,256,768]{2,1,0:T(8,128)(2,1)S(1)}, bf16[4,256,768]{2,1,0:T(8,128)(2,1)}, u32[]{:S(2)}) copy-start(bf16[4,256,768]{2,1,0:T(8,128)(2,1)} %cot.3) | copy-start | bytes 4718596
  163.9 6.1 %copy-start.11 = (bf16[4,256,1536]{2,1,0:T(8,128)(2,1)S(1)}, bf16[4,256,1536]{2,1,0:T(8,128)(2,1)}, u32[]{:S(2)}) copy-start(bf16[4,256,1536]{2,1,0:T(8,128)(2,1)} %get-tuple-element.69) | copy-start | bytes 9437188
  283.4 4.1 %copy-start.4 = (bf16[384,768]{1,0:T(8,128)(2,1)S(1)}, bf16[384,768]{1,0:T(8,128)(2,1)}, u32[]{:S(2)}) copy-start(bf16[384,768]{1,0:T(8,128)(2,1)} %get-tuple-element.76) | copy-start | bytes 1769476
  284.7 5.4 %copy-start.5 = (f32[96,128]{1,0:T(8,128)S(1)}, f32[96,128]{1,0:T(8,128)}, u32[]{:S(2)}) copy-start(f32[96,128]{1,0:T(8,128)} %get-tuple-element.77) | copy-start | bytes 147460
  284.7 8.0 %copy-start.9 = (f32[8,128]{1,0:T(8,128)S(1)}, f32[8,128]{1,0:T(8,128)}, u32[]{:S(2)}) copy-start(f32[8,128]{1,0:T(8,128)} %get-tuple-element.73) | copy-start | bytes 12292
  284.7 9.1 %copy-start.2 = (bf16[4,256,768]{2,1,0:T(8,128)(2,1)S(1)}, bf16[4,256,768]{2,1,0:T(8,128)(2,1)}, u32[]{:S(2)}) copy-start(bf16[4,256,768]{2,1,0:T(8,128)(2,1)} %get-tuple-element.106) | copy-start | bytes 4718596
  287.5 7.4 %copy-start.3 = (bf16[4,256,768]{2,1,0:T(8,128)(2,1)S(1)}, bf16[4,256,768]{2,1,0:T(8,128)(2,1)}, u32[]{:S(2)}) copy-start(bf16[4,256,768]{2,1,0:T(8,128)(2,1)} %get-tuple-element.107) | copy-start | bytes 4718596

commit v7 on v6

--- a/solution.py
+++ b/solution.py
@@ -24,15 +24,16 @@
 bf16 = jnp.bfloat16
 NT = (((1,), (1,)), ((), ()))
 TN = (((0,), (0,)), ((), ()))
-VMEM_LIMIT = 62 * 1024 * 1024
+VMEM_LIMIT = 63 * 1024 * 1024
 GATE_CHUNK = 512
 OUT_CHUNK = 256
 CONV_CHUNK = 512
 BACK_LAGS = (5, 7, 9)
-STAGE_LAG = 2
+STAGE_LAG = 4
 MIDDLE_LAG = 2
 SCAN_LAG = 4
 HOPS = ("group", "ctx")
+SMALL_ROWS = 88
 CLOSE_LAG = 6
 GZW = 2048
 
@@ -103,6 +104,23 @@
 
 def rows_of(v):
     return jnp.broadcast_to(v, (8, v.shape[1]))
+
+
+def lane_row(ref):
+    lanes = lax.broadcasted_iota(jnp.int32, (1, HALF), 1)
+    row = jnp.zeros((1, HALF), f32)
+    for h in range(HEADS):
+        row = jnp.where(lanes == h, ref[h], row)
+    return row
+
+
+def row_of(ref):
+    return ref[...].reshape(1, ref.shape[0])
+
+
+def live_rows(lengths, s):
+    start = lax.axis_index("ctx") * SPAN
+    return (lax.broadcasted_iota(jnp.int32, (SPAN, 1), 0) + start < lengths[s]).astype(f32)
 
 
 def normalized(rows, gain):
@@ -360,12 +378,17 @@
 
 
 class Reducer:
-    def __init__(self, part, out, rows, width, by_rows, bufs, sems):
+    def __init__(self, part, out, rows, width, by_rows, group_bufs, ctx_bufs):
         self.part, self.out, self.rows, self.width, self.by_rows = part, out, rows, width, by_rows
-        self.m_buf, self.x_buf, self.y_src, self.y_buf, self.z_src, self.z_buf, self.full = bufs
-        self.x_src = self.m_buf
-        self.sems = sems
-        self.chunks = part.shape[1] // width
+        if group_bufs is not None:
+            self.m_buf, self.x_buf, self.g_sems = group_bufs
+        self.ships = ctx_bufs is not None
+        if self.ships:
+            self.y_src, self.y_buf, self.z_src, self.z_buf, self.full, self.c_sems = ctx_bufs
+        else:
+            self.y_src = out
+        self.chunks = self.y_src.shape[0]
+        self.base = 0
         self.group = lax.axis_index("group")
         self.cores = 2
         self.chips = lax.axis_size("group") // 2
@@ -399,39 +422,39 @@
     def m_copy(self, k, chip):
         return remote(
             self.part.at[self.member(chip, 1 - self.core), self.cols(k)], self.m_buf.at[k, chip],
-            self.sems.at[0, k, chip], self.sems.at[1, k, chip], group=self.group + 1 - 2 * self.core,
+            self.g_sems.at[0, k, chip], self.g_sems.at[1, k, chip], group=self.group + 1 - 2 * self.core,
         )
 
     def x_copy(self, k, chip, sender):
         return remote(
-            self.x_src.at[k, chip], self.x_buf.at[k, sender], self.sems.at[2, k, chip], self.sems.at[3, k, sender],
+            self.m_buf.at[k, chip], self.x_buf.at[k, sender], self.g_sems.at[2, k, chip], self.g_sems.at[3, k, sender],
             group=chip * 2 + self.core,
         )
 
     def y_copy(self, k):
         return remote(
-            self.y_src.at[k, self.half_rows(1 - self.inner)], self.y_buf.at[k], self.sems.at[4, k, 0], self.sems.at[5, k, 0],
+            self.y_src.at[k, self.half_rows(1 - self.inner)], self.y_buf.at[k], self.c_sems.at[0, k, 0], self.c_sems.at[1, k, 0],
             ctx=self.ctx + 1 - 2 * self.inner,
         )
 
     def z_copy(self, k, j, sender):
         rows, cols = self.piece(j, 0)
         return remote(
-            self.z_src.at[k, rows, cols], self.z_buf.at[k, sender], self.sems.at[6, k, j], self.sems.at[7, k, sender],
+            self.z_src.at[k, rows, cols], self.z_buf.at[k, sender], self.c_sems.at[2, k, j], self.c_sems.at[3, k, sender],
             ctx=j * self.stride * 2 + self.inner,
         )
 
     def b_copy(self, k, line, j):
         rows, cols = self.piece(j, self.inner * self.half)
         return remote(
-            self.full.at[k, rows, cols], self.full.at[k, rows, cols], self.sems.at[8, k, line], self.sems.at[9, k, j],
+            self.full.at[k, rows, cols], self.full.at[k, rows, cols], self.c_sems.at[4, k, line], self.c_sems.at[5, k, j],
             ctx=line * 2 + self.inner,
         )
 
     def f_copy(self, k, inner):
         rows = self.half_rows(inner)
         return remote(
-            self.full.at[k, rows], self.full.at[k, rows], self.sems.at[10, k, 0], self.sems.at[11, k, 0],
+            self.full.at[k, rows], self.full.at[k, rows], self.c_sems.at[6, k, 0], self.c_sems.at[7, k, 0],
             ctx=self.ctx + 1 - 2 * self.inner,
         )
 
@@ -464,16 +487,20 @@
         for chip in range(self.chips):
             self.m_copy(k, chip).wait_recv()
             own = self.part[self.member(chip, self.core), self.cols(k)].astype(f32)
-            self.x_src[k, chip] = (own + self.m_buf[k, chip].astype(f32)).astype(bf16)
+            self.m_buf[k, chip] = (own + self.m_buf[k, chip].astype(f32)).astype(bf16)
         self.other_chips(lambda chip: self.x_copy(k, chip, self.chip).start())
 
     def x_done(self, k):
-        total = self.x_src[k, self.chip].astype(f32)
+        total = self.m_buf[k, self.chip].astype(f32)
         for d in range(1, self.chips):
             chip = lax.rem(self.chip + d, self.chips)
             self.x_copy(k, chip, chip).wait_recv()
             total = total + self.x_buf[k, chip].astype(f32)
         self.y_src[k] = total.astype(bf16)
+        if self.ships:
+            self.y_start(k)
+
+    def y_start(self, k):
         self.y_copy(k).start()
 
     def y_done(self, k):
@@ -502,31 +529,41 @@
 
     def f_done(self, k):
         self.f_copy(k, 1 - self.inner).wait_recv()
-        self.out[:, self.cols(k)] = self.full[k]
-
-    def drain(self, k):
+        self.out[:, pl.ds(pl.multiple_of(self.base + k * self.width, 128), self.width)] = self.full[k]
+
+    def drain_group(self, k):
         for chip in range(self.chips):
             self.m_copy(k, chip).wait_send()
         self.other_chips(lambda chip: self.x_copy(k, chip, self.chip).wait_send())
+
+    def drain_ctx(self, k):
         self.y_copy(k).wait_send()
         self.other_owners(lambda j: self.z_copy(k, j, self.line).wait_send())
         self.if_owner(lambda: self.other_lines(lambda line: self.b_copy(k, line, self.mine).wait_send()))
         self.f_copy(k, self.inner).wait_send()
 
-    def wave(self, t):
-        for lag, act in ((4, self.f_done), (3, self.b_done), (2, self.z_done), (1, self.y_done), (0, self.x_done)):
-            k = t - lag * STAGE_LAG
-            pl.when(jnp.logical_and(k >= 0, k < self.chunks))(lambda k=k, act=act: act(k))
+    def wave(self, t, acts, chunk_at):
+        for order, act in reversed(list(enumerate(acts))):
+            k, is_due = chunk_at(t - order * STAGE_LAG)
+            pl.when(is_due)(lambda k=k, act=act: act(k))
+
+    def each(self, t):
+        return t, jnp.logical_and(t >= 0, t < self.chunks)
 
     @staticmethod
-    def scratch(chunks, rows, width, by_rows, group, count):
-        chips, outer = group // 2, count // 2
+    def group_scratch(chunks, rows, width, group):
+        chips = group // 2
+        buf = ((chunks, chips, rows, width), bf16)
+        return [buf, buf, pltpu.SemaphoreType.DMA((4, chunks, max(chips, 2)))]
+
+    @staticmethod
+    def ctx_scratch(chunks, rows, width, by_rows, count):
+        outer = count // 2
         owners = owner_count(rows, width, by_rows, outer)
         half = rows // 2
         piece = (half // owners, width) if by_rows else (half, width // owners)
-        bufs = [(chunks, chips, rows, width), (chunks, chips, rows, width), (chunks, rows, width),
-                (chunks, half, width), (chunks, half, width), (chunks, outer) + piece, (chunks, rows, width)]
-        return [(b, bf16) for b in bufs] + [pltpu.SemaphoreType.DMA((12, chunks, max(chips, outer, 2)))]
+        bufs = [(chunks, half, width), (chunks, half, width), (chunks, outer) + piece, (chunks, rows, width)]
+        return [(b, bf16) for b in bufs] + [pltpu.SemaphoreType.DMA((8, chunks, max(outer, 2)))]
 
 
 class Small:
@@ -592,9 +629,9 @@
 
 
 def front_kernel(
-    tok, tok_any, wcat, wout, gain, cw, cb, db, dl,
-    nt, nth, rhalo, cin, xb, spb, vout, cumout, st0, loc, ylocal, gate, decs_out, wfull, wofull, sin,
-    sel, halo, nh_s, ext, w, cin_s, xs_s, bt, scores, out_cat, dt_cat, cum_t, tot1x, decs,
+    tok, tok_any, wzx, wdl, wout, gain, cw, cb_in, db, dl,
+    nt, nth, rhalo, cin, xb, spb, vout, cumout, st0, loc, ylocal, gate, decs_out, wfull, wdfull, wofull, sin,
+    sel, halo, nh_s, ext, w, wd, cb, cin_s, xs_s, bt, scores, out_cat, dt_cat, cum_t, tot1x, decs,
     halo_sem, x_send, x_recv, m_send, m_recv, w_own, w_store, dec_send, dec_recv, *exchange,
 ):
     i = pl.program_id(0)
@@ -602,8 +639,8 @@
     count = lax.axis_size("ctx")
     me = lax.axis_index("ctx")
     sems = (x_send, x_recv, m_send, m_recv, w_own)
-    zx, wo = Spread(wcat, w, sems), Spread(wout, wofull, sems)
-    last = PIECES
+    zx, wo, de = Spread(wzx, w, sems), Spread(wout, wofull, sems), Spread(wdl, wd, sems)
+    last, small_piece = PIECES, PIECES + 1
 
     def unit_cols(u):
         return pl.ds(pl.multiple_of(u * TILE, TILE), TILE)
@@ -612,12 +649,13 @@
         at = jnp.where(p <= TILES, DIN + (p - 1) * TILE, (p - 1 - TILES) * TILE)
         return pl.ds(pl.multiple_of(at, TILE), TILE)
 
-    first_piece = pl.ds(DT0, 2 * NSTATE + HALF)
+    first_piece = pl.ds(DT0, 2 * NSTATE)
     ex = Exchange(False, lambda u, rows: sin.at[:, rows, unit_cols(u)], exchange[:9], exchange[9])
     halo_copy = remote(
         tok_any.at[:, pl.ds(SPAN - RIM, RIM), :], halo, halo_sem.at[0], halo_sem.at[1], ctx=lax.rem(me + 1, count)
     )
     keep_w = pltpu.make_async_copy(w, wfull, w_store.at[0])
+    keep_d = pltpu.make_async_copy(wd, wdfull, w_store.at[1])
 
     def dec_copy(block, sender):
         rows = pl.ds(pl.multiple_of(sender * 8, 8), 8)
@@ -646,8 +684,11 @@
     def _():
         meet(("ctx", "group"))
         pl.when(me < count - 1)(lambda: halo_copy.start())
+        de.start(small_piece, slice(None))
         zx.start(0, first_piece)
+        de.start_chip(2)
         zx.start_chip(0)
+        cb[...] = row_of(cb_in)
         zx.start(1, piece(1))
         zx.start(2, piece(2))
         wo.start_chip(1)
@@ -658,7 +699,7 @@
             halo[...] = jnp.zeros_like(halo)
 
         def norm_main(s):
-            nm = normalized(tok[s], gain[...])[2]
+            nm = normalized(tok[s], row_of(gain))[2]
             ext[s, RIM:] = nm
             nt[:, pl.ds(pl.multiple_of(s * SPAN, SPAN), SPAN)] = jnp.transpose(nm.astype(f32)).astype(bf16)
 
@@ -669,15 +710,17 @@
             halo_copy.wait_recv()
 
         def norm_halo(s):
-            nh = normalized(halo[s], gain[...])[2]
+            nh = normalized(halo[s], row_of(gain))[2]
             ext[s, 0:RIM] = nh
             nh_s[pl.ds(pl.multiple_of(s * RIM, RIM), RIM), :] = nh.astype(f32)
             rhalo[s] = halo[s]
 
         loop(0, seqs, norm_halo)
         nth[...] = jnp.transpose(nh_s[...]).astype(bf16)
+        de.forward(small_piece, slice(None))
         zx.forward(0, first_piece)
         zx.finish_chip(0)
+        de.finish_chip(2)
 
     @pl.when(i + 1 < PIECES)
     def _():
@@ -694,6 +737,8 @@
     @pl.when(i == 0)
     def _():
         zx.finish(0, first_piece)
+        de.finish(small_piece, slice(None))
+        shift, rate = lane_row(db), jnp.exp(lane_row(dl))
 
         def delta(s):
             a = conv_tile(s, slice(DT0, DT0 + TILE), slice(DIN, DIN + TILE))
@@ -701,10 +746,10 @@
             bt[s] = jnp.transpose(a[:, :NSTATE]).astype(bf16)
             for q in range(2):
                 scores[s, q] = mm_nt(cc[both(q)], bb[both(q)])
-            v = mm(ext[s, RIM:], w[:, DT0 + TILE :]) + db[...]
+            v = mm(ext[s, RIM:], wd[...]) + shift
             vout[s] = v
             dt = softplus(v)
-            cum = exact_mm(triangle(SPAN, True), -jnp.exp(dl[...]) * dt)
+            cum = exact_mm(triangle(SPAN, True), -rate * dt)
             cumout[s] = cum
             for q in range(2):
                 cum_t[s, q] = jnp.transpose(cum[both(q)])
@@ -792,6 +837,7 @@
     @pl.when(i == PIECES - 1)
     def _():
         keep_w.start()
+        keep_d.start()
         decs_out[...] = decs[...]
         wo.forward(last, slice(None))
         loop(PIECES, TILES + CLOSE_LAG + 1, wave)
@@ -800,24 +846,39 @@
         wo.finish_chip(1)
         zx.drain_chip(0)
         wo.drain_chip(1)
+        de.drain_chip(2)
+        de.drain(small_piece, slice(None))
         zx.drain(0, first_piece)
         loop(1, PIECES, lambda p: zx.drain(p, piece(p)))
         wo.drain(last, slice(None))
         other_blocks(lambda b: dec_copy(b, me).wait_send())
         pl.when(me < count - 1)(lambda: halo_copy.wait_send())
         keep_w.wait()
+        keep_d.wait()
 
 
 def middle_kernel(
-    rel, tok, cot, ylocal, gate, xb, vin, cumin, st0, sin, decs, wout, skip, ggain,
-    mixed, mlow, dyout, ggate, wred, dir1, gskip, gggain, dxs, dbc, later,
-    sel, cum_t, einx, ys, gs, ss, s_in, dcs, dy_s, ml_s, g_s, dg_s, *exchange,
+    lengths, skip_in, tok, cot, ylocal, gate, xb, vin, cumin, st0, sin, decs, wout, ggain_in, nt,
+    mixed, dyout, ggate, wred, dir1, gskip, gggain, dxs, dbc, xgate, xout, later,
+    sel, skip, ggain, cum_t, einx, ys, gs, ss, s_in, dcs, dy_s, ml_s, gg_s, dr_s, pgate, pout, g_s, dg_s, *exchange,
 ):
     i = pl.program_id(0)
     seqs = dy_s.shape[0]
     ex = Exchange(True, lambda u, rows: later.at[pl.ds(u, 1), rows, :], exchange[:9], exchange[9])
+    members = lax.axis_size("group")
+    gates = Reducer(pgate, xgate, D // members, GATE_CHUNK, False, exchange[10:13], None)
+    outs = Reducer(pout, xout, DIN // members, OUT_CHUNK, True, exchange[13:16], None)
+
+    def span(s):
+        return pl.ds(pl.multiple_of(s * SPAN, SPAN), SPAN)
+
+    def group_wave(t):
+        gates.wave(t - 2 * seqs - 3, [gates.x_done], gates.each)
+        outs.wave(t - 2 * seqs - 3 - gates.chunks, [outs.x_done], outs.each)
 
     def wave(t):
+        group_wave(t)
+
         def act_at(lag, act):
             u = lax.div(t - lag, 2)
 
@@ -833,8 +894,10 @@
 
     @pl.when(i == 0)
     def _():
-        meet(("ctx",))
+        meet(("ctx", "group"))
         sel[...] = head_map()
+        skip[...] = spread(rows_of(lane_row(skip_in)), sel)[0:1]
+        ggain[...] = row_of(ggain_in)
         gskip[...] = jnp.zeros_like(gskip)
         gggain[...] = jnp.zeros_like(gggain)
 
@@ -866,17 +929,16 @@
         wave(2 * i + 1)
         sq = lax.fori_loop(0, DIN // TILE, gate_step, jnp.zeros((SPAN, HALF), f32))
         inv = lax.rsqrt(jnp.sum(sq, axis=1, keepdims=True) * (1.0 / DIN) + EPS)
-        live = (lax.broadcasted_iota(jnp.int32, (SPAN, 1), 0) < rel[s]).astype(f32)
+        live = live_rows(lengths, s)
         drive = (live * cot[0].astype(f32)).astype(bf16)
+        dr_s[span(s), :] = drive
 
         def back_step(j, acc):
             cols = pl.ds(pl.multiple_of(j * TILE, TILE), TILE)
             gm = mm_nt(drive, wout[cols, :])
             gated = gs[:, cols]
             unit = gated * inv
-            low = (unit * ggain[:, cols]).astype(bf16)
-            mlow[0, :, cols] = low
-            ml_s[s, :, cols] = low
+            ml_s[span(s), cols] = (unit * ggain[:, cols]).astype(bf16)
             gggain[:, cols] += jnp.sum(gm * unit, axis=0, keepdims=True)
             scaled = gm * ggain[:, cols]
             ss[:, cols] = scaled
@@ -899,7 +961,9 @@
             yn = ys[:, cols]
             x = xb[0, :, cols].astype(f32)
             y = yn + skip[:, cols] * x
-            ggate[0, :, cols] = (grad_gated * y * (sg + sl * (1.0 - sg))).astype(bf16)
+            low = (grad_gated * y * (sg + sl * (1.0 - sg))).astype(bf16)
+            ggate[0, :, cols] = low
+            gg_s[span(s), cols] = low
             dyb = dy.astype(bf16)
             dyout[0, :, cols] = dyb
             dy_s[s, :, cols] = dyb
@@ -948,30 +1012,55 @@
                     dg_s[q] += dm * decays[2 * q + a]
                 dxs[0, rows, cols] = jnp.where(low_lanes, grads[0], grads[1]).astype(bf16)
 
+        @pl.when(s == 0)
+        def _():
+            for k in range(gates.chunks):
+                cols = slice(k * GATE_CHUNK, (k + 1) * GATE_CHUNK)
+                pgate[:, cols] = mm(nt[...], gg_s[:, cols]).astype(bf16)
+                gates.m_start(k)
+
+        @pl.when(s == 1)
+        def _():
+            loop(0, outs.chunks, outs.m_done)
+
         loop(0, PAIRS // 2, pair_step)
         wave(2 * i + 1)
+
+        @pl.when(s == 0)
+        def _():
+            loop(0, gates.chunks, gates.m_done)
+
+            def out_rows(r):
+                rows = pl.ds(pl.multiple_of(r * TILE, TILE), TILE)
+                pout[rows, :] = mm_tn(ml_s[:, rows], dr_s[...]).astype(bf16)
+
+            loop(0, DIN // TILE, out_rows)
+            loop(0, outs.chunks, outs.m_start)
+
         loop(PAIRS // 2, PAIRS, pair_step)
         for q in range(2):
             rows = both(q)
             dg = dg_s[q].astype(bf16)
             dbc[0, rows, :NSTATE] = mm_tn(dg, cc[rows])
             dbc[0, rows, NSTATE:] = mm(dg, bb[rows]) + dcs[s, rows]
-        live = (lax.broadcasted_iota(jnp.int32, (SPAN, 1), 0) < rel[s]).astype(f32)
+        live = live_rows(lengths, s)
         for j in range(D // TILE):
             cols = slice(j * TILE, (j + 1) * TILE)
-            mixed[0, :, cols] = (live * (tok[0, :, cols].astype(f32) + mm(ml_s[s], wout[:, cols]))).astype(bf16)
+            mixed[0, :, cols] = (live * (tok[0, :, cols].astype(f32) + mm(ml_s[span(s), :], wout[:, cols]))).astype(bf16)
 
     @pl.when(i == 2 * seqs - 1)
     def _():
-        loop(4 * seqs, 2 * seqs + BACK_LAGS[2] - 1, wave)
+        loop(4 * seqs, max(2 * seqs + BACK_LAGS[2] - 1, 2 * seqs + 3 + gates.chunks + outs.chunks), wave)
         loop(0, seqs, ex.finish)
+        for r in (gates, outs):
+            loop(0, r.chunks, r.drain_group)
 
 
 def back_kernel(
-    rel, tok, cot, rhalo, gain, ggate, wfull, cin, xb, spb, bc, dy, dxs, dir1, later, sin, loc,
-    vin, cumin, wred, dbc, cw, dl, skip, nt, nth, pgate, pout, gskip, gggain,
-    gtok, rgate, rout, rconv, small_out, ggain_out,
-    sel, dt_cat, eo_cat, tots, db_s, qacc, ends, gp, gz_s, gzh_s, pconv, gcw, gcb, gdb, gdl, ggain,
+    lengths, dl, skip_in, tok, cot, rhalo, gain, ggate, w_any, wd, cin, xb, spb, bc, dy, dxs, dir1, later, sin, loc,
+    vin, cumin, wred, dbc, cw, nt, nth, xgate, xout, gskip, gggain,
+    gtok, rzx, rout, small_out, ggain_out,
+    sel, skip, wfull, w_sem, dt_cat, eo_cat, tots, db_s, qacc, ends, gp, gz_s, gzh_s, pconv, gcw, gcb, gdb, gdl, ggain,
     rim_out, rim_in, rim_send, rim_recv, *comm,
 ):
     i = pl.program_id(0)
@@ -979,17 +1068,26 @@
     count = lax.axis_size("ctx")
     me = lax.axis_index("ctx")
     members = lax.axis_size("group")
-    gates = Reducer(pgate, rgate, D // members, GATE_CHUNK, False, comm[0:7], comm[7])
-    outs = Reducer(pout, rout, DIN // members, OUT_CHUNK, True, comm[8:15], comm[15])
-    convs = Reducer(pconv, rconv, D // members, CONV_CHUNK, False, comm[16:23], comm[23])
-    little, least = Small(*comm[24:28]), Small(*comm[28:32])
-    last_x = TILES - 1
+    gates = Reducer(None, rzx, D // members, GATE_CHUNK, False, None, (xgate,) + comm[0:5])
+    outs = Reducer(None, rout, DIN // members, OUT_CHUNK, True, None, (xout,) + comm[5:10])
+    convs = Reducer(pconv, rzx, D // members, CONV_CHUNK, False, comm[10:13], comm[13:19])
+    convs.base = DIN
+    load_w = pltpu.make_async_copy(w_any, wfull, w_sem.at[0])
+    little, least = Small(*comm[19:23]), Small(*comm[23:27])
     bc_step = TILES
 
+    last_conv = 2 * bc_step + 5
+
+    def conv_at(t):
+        k = lax.div(t - 7, 4)
+        even = jnp.logical_and(t >= 7, jnp.logical_and(lax.rem(t - 7, 4) == 0, k < convs.chunks - 1))
+        last = t == last_conv
+        return jnp.where(last, convs.chunks - 1, k), jnp.logical_or(even, last)
+
     def wave(t):
-        gates.wave(t - 4)
-        outs.wave(t - 4 - gates.chunks)
-        convs.wave(t - 2 * bc_step - 1)
+        for r, at in ((gates, 2), (outs, 2 + gates.chunks)):
+            r.wave(t - at, [r.y_done, r.z_done, r.b_done, r.f_done], r.each)
+        convs.wave(t, [convs.x_done, convs.y_done, convs.z_done, convs.b_done, convs.f_done], conv_at)
 
     def rim_copy(q):
         return remote(rim_out.at[q], rim_in.at[q], rim_send.at[q], rim_recv.at[q], ctx=lax.rem(me + count - 1, count))
@@ -1001,9 +1099,9 @@
         return pl.ds(pl.multiple_of(s * RIM, RIM), RIM)
 
     def back(rows, grad):
-        rows, inv, _ = normalized(rows, gain[...])
+        rows, inv, _ = normalized(rows, row_of(gain))
         ggain[...] += jnp.sum(grad * rows * inv, axis=0, keepdims=True)
-        gained = gain[...] * grad
+        gained = row_of(gain) * grad
         mean = jnp.mean(gained * rows, axis=-1, keepdims=True)
         return inv * gained - rows * (inv * inv * inv * mean)
 
@@ -1011,8 +1109,10 @@
     def _():
         meet(("ctx", "group"))
         for r in (gates, outs):
-            loop(0, r.chunks, r.m_start)
+            loop(0, r.chunks, r.y_start)
+        load_w.start()
         sel[...] = head_map()
+        skip[...] = spread(rows_of(lane_row(skip_in)), sel)[0:1]
         for acc in (db_s, qacc, ends, gcw, gcb, gdb, gdl, ggain):
             acc[...] = jnp.zeros_like(acc)
         gp[0:RIM] = jnp.zeros((RIM, TILE), f32)
@@ -1054,14 +1154,6 @@
 
     wave(2 * i)
 
-    @pl.when(jnp.logical_and(lax.rem(i, 2) == 0, jnp.logical_and(i >= 2, i <= bc_step)))
-    def _():
-        convs.m_done(lax.div(i, 2) - 1)
-
-    @pl.when(i == bc_step + 1)
-    def _():
-        convs.m_done(convs.chunks - 1)
-
     @pl.when(i < bc_step)
     def _():
         cols = pl.ds(pl.multiple_of(i * TILE, TILE), TILE)
@@ -1088,10 +1180,9 @@
 
         loop(0, seqs // 2, x_tile)
 
-        @pl.when(i == 0)
+        @pl.when(jnp.logical_and(lax.rem(i, 2) == 0, i >= 2))
         def _():
-            for r in (gates, outs):
-                loop(0, r.chunks, r.m_done)
+            convs.m_done(lax.div(i, 2) - 1)
 
         wave(2 * i + 1)
         loop(seqs // 2, seqs, x_tile)
@@ -1104,6 +1195,7 @@
     @pl.when(i == bc_step)
     def _():
         cols = slice(DIN, CONVW)
+        rate = jnp.exp(lane_row(dl))
 
         def bc_tile(s):
             conv_back(s, jnp.concatenate([dbc[s, :, :NSTATE] + db_s[s], dbc[s, :, NSTATE:]], axis=1), cols)
@@ -1113,7 +1205,6 @@
             at_end = lax.broadcasted_iota(jnp.int32, (SPAN, 1), 0) == SPAN - 1
             dcum = wred[s] - dt * q + jnp.where(at_end, ends[s][0:1], 0.0)
             glog = exact_mm(triangle(SPAN, False), dcum)
-            rate = jnp.exp(dl[...])
             gpd = (q - rate * glog) * sigmoid(v)
             lanes = lax.broadcasted_iota(jnp.int32, (SPAN, HALF), 1) < HEADS
             gpd = jnp.where(lanes, gpd, 0.0)
@@ -1122,6 +1213,7 @@
             gdl[...] += -rate * jnp.sum(dt * glog, axis=0, keepdims=True)
 
         loop(0, seqs, bc_tile)
+        convs.m_done(convs.chunks - 2)
         wave(2 * i + 1)
         partial(cols)
         pconv[:, CONVW : CONVW + HALF] = mm(nt[...], gz_s[:, CONVW : CONVW + HALF]).astype(bf16)
@@ -1129,11 +1221,13 @@
         rows = [gcw[k : k + 1, j * HALF : (j + 1) * HALF] for k in range(KCONV) for j in range(CONVW // HALF)]
         rows += [gcb[:, j * HALF : (j + 1) * HALF] for j in range(CONVW // HALF)]
         rows += [gdb[...], gdl[...]]
-        rows += [gskip[:, j * HALF : (j + 1) * HALF] for j in range(PAIRS)]
+        rows += [gather_heads(rows_of(gskip[...]), sel[:HALF])[0:1]]
         rows += [gggain[:, j * HALF : (j + 1) * HALF] for j in range(PAIRS)]
+        little.held[0, SMALL_ROWS - 8 :] = jnp.zeros((8, HALF), f32)
         for r, row in enumerate(rows):
             little.held[0, r : r + 1, :] = row
         little.start(0)
+        load_w.wait()
         edges = mm_nt(gzh_s[...], wfull[:, DIN:ZXW])
         for q in range(seqs):
             rim_out[q] = back(rhalo[q], edges[q * RIM : (q + 1) * RIM]).astype(bf16)
@@ -1151,9 +1245,15 @@
     @pl.when(i > bc_step)
     def _():
         s = i - bc_step - 1
-        grad = mm_nt(gz_s[span(s), :], wfull[:, DIN:]) + mm_nt(ggate[0], wfull[:, :DIN])
+        grad = mm_nt(gz_s[span(s), :CONVW], wfull[:, DIN:]) + mm_nt(ggate[0], wfull[:, :DIN])
+        grad = grad + mm_nt(gz_s[span(s), CONVW:], wd[...])
+
+        @pl.when(s == 0)
+        def _():
+            convs.m_done(convs.chunks - 1)
+
         wave(2 * i + 1)
-        live = (lax.broadcasted_iota(jnp.int32, (SPAN, 1), 0) < rel[s]).astype(f32)
+        live = live_rows(lengths, s)
         out = live * cot[0].astype(f32) + back(tok[0], grad)
         gtok[0, : SPAN - RIM] = out[: SPAN - RIM].astype(bf16)
         pl.when(me < count - 1)(lambda: rim_copy(s).wait_recv())
@@ -1169,15 +1269,37 @@
         small_out[...] = little.held[2]
         least.done(0)
         least.start(1)
-        loop(2 * (bc_step + seqs) + 2, 2 * bc_step + 1 + convs.chunks + 4 * STAGE_LAG, wave)
+        loop(2 * (bc_step + seqs) + 2, last_conv + 4 * STAGE_LAG + 1, wave)
         for r in (gates, outs, convs):
-            loop(0, r.chunks, r.drain)
+            loop(0, r.chunks, r.drain_ctx)
+        loop(0, convs.chunks, convs.drain_group)
         little.drain()
         for q in range(seqs):
             pl.when(me > 0)(lambda q=q: rim_copy(q).wait_send())
         least.done(1)
         ggain_out[...] = least.held[2]
         least.drain()
+
+
+def done_kernel(rzx, rout, small, gain_sum, g_gain, g_zx, g_delta, g_out, g_cw, g_cb, g_db, g_dl, g_skip, g_gated):
+    g_zx[...] = rzx[:, :ZXW].astype(f32)
+    g_delta[...] = rzx[:, ZXW : ZXW + HEADS].astype(f32)
+    g_out[...] = rout[...].astype(f32)
+    tiles = CONVW // HALF
+    for k in range(KCONV):
+        for j in range(tiles):
+            g_cw[k : k + 1, j * HALF : (j + 1) * HALF] = small[k * tiles + j : k * tiles + j + 1, :]
+    at = KCONV * tiles
+    for j in range(tiles):
+        g_cb[j * HALF : (j + 1) * HALF] = small[at + j, :]
+    at += tiles
+    for ref in (g_db, g_dl, g_skip):
+        ref[...] = small[at, :][:HEADS]
+        at += 1
+    for j in range(PAIRS):
+        g_gated[j * HALF : (j + 1) * HALF] = small[at + j, :]
+    for j in range(D // HALF):
+        g_gain[j * HALF : (j + 1) * HALF] = gain_sum[j, :]
 
 
 def whole(shape):
@@ -1224,10 +1346,6 @@
     )
 
 
-def lanes_of(v):
-    return jnp.pad(v[None, :], ((0, 0), (0, HALF - v.shape[0])))
-
-
 def local(
     tokens_in, seq_lengths, norm_gain, w_zx, w_delta, w_out, conv_weight, conv_bias,
     delta_bias, decay_log, skip_gain, gated_gain, cotangent,
@@ -1236,14 +1354,7 @@
     count = lax.axis_size("ctx")
     group = lax.axis_size("group")
     chips = max(group // 2, 1)
-    rel = seq_lengths - lax.axis_index("ctx") * SPAN
-    gain = norm_gain[None, :]
-    cb = conv_bias[None, :]
-    db = lanes_of(delta_bias)
-    dl = lanes_of(decay_log)
-    skip = jnp.repeat(skip_gain, HEADDIM)[None, :]
-    ggain = gated_gain[None, :]
-    wcat = jnp.concatenate([w_zx, jnp.pad(w_delta, ((0, 0), (0, HALF - HEADS)))], axis=1)
+    w_delta = jnp.pad(w_delta, ((0, 0), (0, HALF - HEADS)))
     dma = pltpu.SemaphoreType.DMA
     at0 = lambda *shape: staged(seqs, 0, *shape)
     at1 = lambda *shape: staged(seqs, 1, *shape)
@@ -1257,11 +1368,10 @@
         return pl.BlockSpec((seqs, rows, TILE), index)
 
     state = (seqs, NSTATE, DIN)
-    nt, nth, rhalo, cin, xb, spb, vraw, cum, st0, loc, ylocal, gate, decs, wfull, wofull, state_in = call(
+    nt, nth, rhalo, cin, xb, spb, vraw, cum, st0, loc, ylocal, gate, decs, wfull, wdfull, wofull, state_in = call(
         front_kernel,
         PIECES,
-        [whole((seqs, SPAN, D)), ANY, ANY, ANY, whole((1, D)), whole((KCONV, CONVW)), whole((1, CONVW)), whole((1, HALF)),
-         whole((1, HALF))],
+        [whole((seqs, SPAN, D)), ANY, ANY, ANY, ANY, whole((D,)), whole((KCONV, CONVW)), whole((CONVW,)), SMEM, SMEM],
         [
             (summed((D, seqs * SPAN)), (D, seqs * SPAN), bf16),
             (summed((D, seqs * RIM)), (D, seqs * RIM), bf16),
@@ -1276,29 +1386,32 @@
             (tiled(SPAN, TILES + 1), (seqs, SPAN, DIN), bf16),
             (tiled(SPAN, TILES + 1), (seqs, SPAN, DIN), bf16),
             (summed((seqs, count * 8, HALF)), (seqs, count * 8, HALF), f32),
-            (ANY, (D, ZXW + HALF), bf16),
+            (ANY, (D, ZXW), bf16),
+            (ANY, (D, HALF), bf16),
             (ANY, (DIN, D), bf16),
             (ANY, state, bf16),
         ],
-        [((2 * HALF, DIN), bf16), ((seqs, RIM, D), bf16), ((seqs * RIM, D), f32), ((seqs, RIM + SPAN, D), bf16), ((D, ZXW + HALF), bf16),
+        [((2 * HALF, DIN), bf16), ((seqs, RIM, D), bf16), ((seqs * RIM, D), f32), ((seqs, RIM + SPAN, D), bf16), ((D, ZXW), bf16),
+         ((D, HALF), bf16), ((1, CONVW), f32),
          ((seqs, RIM + SPAN, TILE), f32), ((seqs, SPAN, DIN), bf16), ((seqs, NSTATE, SPAN), bf16),
          ((seqs, 2, HALF, HALF), f32), ((seqs, SPAN, 2 * HALF), bf16), ((seqs, SPAN, 2 * HALF), bf16),
          ((seqs, 2, HALF, HALF), f32), ((seqs, 8, DIN), f32), ((seqs, count * 8, HALF), f32)]
-        + [dma((2,))] + [dma((PIECES + 1, chips))] * 4 + [dma((2,)), dma((1,)), dma((count,)), dma((count,))]
+        + [dma((2,))] + [dma((PIECES + 2, chips))] * 4 + [dma((3,)), dma((2,)), dma((count,)), dma((count,))]
         + Exchange.scratch(TILES, seqs, TILE, count),
         "front",
         0,
-    )(tokens_in, tokens_in, wcat, w_out, gain, conv_weight, cb, db, dl)
-
-    mixed_out, mlow, dy, ggate, wred, dir1, gskip, gggain, dxs, dbc, later = call(
+    )(tokens_in, tokens_in, w_zx, w_delta, w_out, norm_gain, conv_weight, conv_bias, delta_bias, decay_log)
+
+    x_gate_shape = (DIN // GATE_CHUNK, D // group, GATE_CHUNK)
+    x_out_shape = (D // OUT_CHUNK, DIN // group, OUT_CHUNK)
+    mixed_out, dy, ggate, wred, dir1, gskip, gggain, dxs, dbc, x_gate, x_out, later = call(
         middle_kernel,
         2 * seqs,
-        [SMEM, at1(SPAN, D), at0(SPAN, D), at0(SPAN, DIN), at0(SPAN, DIN), at01(SPAN, CONVW), at01(SPAN, HALF),
+        [SMEM, SMEM, at1(SPAN, D), at0(SPAN, D), at0(SPAN, DIN), at0(SPAN, DIN), at01(SPAN, CONVW), at01(SPAN, HALF),
          at01(SPAN, HALF), at0(NSTATE, DIN), at0(NSTATE, DIN), whole((seqs, count * 8, HALF)), whole((DIN, D)),
-         whole((1, DIN)), whole((1, DIN))],
+         whole((DIN,)), whole((D, seqs * SPAN))],
         [
             (at1(SPAN, D), (seqs, SPAN, D), bf16),
-            (at0(SPAN, DIN), (seqs, SPAN, DIN), bf16),
             (at0(SPAN, DIN), (seqs, SPAN, DIN), bf16),
             (at0(SPAN, DIN), (seqs, SPAN, DIN), bf16),
             (at0(SPAN, HALF), (seqs, SPAN, HALF), f32),
@@ -1307,21 +1420,20 @@
             (summed((1, DIN)), (1, DIN), f32),
             (at1(SPAN, DIN), (seqs, SPAN, DIN), bf16),
             (at1(SPAN, 2 * NSTATE), (seqs, SPAN, 2 * NSTATE), f32),
+            (summed(x_gate_shape), x_gate_shape, bf16),
+            (summed(x_out_shape), x_out_shape, bf16),
             (ANY, (seqs, NSTATE, DIN), bf16),
         ],
-        [((2 * HALF, DIN), bf16), ((2, HALF, HALF), f32), ((SPAN, DIN), f32), ((SPAN, DIN), f32), ((SPAN, DIN), f32),
+        [((2 * HALF, DIN), bf16), ((1, DIN), f32), ((1, DIN), f32), ((2, HALF, HALF), f32), ((SPAN, DIN), f32), ((SPAN, DIN), f32), ((SPAN, DIN), f32),
          ((SPAN, DIN), f32), ((2, NSTATE, DIN), bf16), ((seqs, SPAN, HALF), f32), ((seqs, SPAN, DIN), bf16),
-         ((seqs, SPAN, DIN), bf16), ((2, HALF, HALF), f32), ((2, HALF, HALF), f32)]
-        + Exchange.scratch(seqs, 1, DIN, count),
+         ((seqs * SPAN, DIN), bf16), ((seqs * SPAN, DIN), bf16), ((seqs * SPAN, D), bf16), ((D, DIN), bf16), ((DIN, D), bf16),
+         ((2, HALF, HALF), f32), ((2, HALF, HALF), f32)]
+        + Exchange.scratch(seqs, 1, DIN, count)
+        + Reducer.group_scratch(*x_gate_shape, group)
+        + Reducer.group_scratch(*x_out_shape, group),
         "middle",
         1,
-    )(rel, tokens_in, cotangent, ylocal, gate, xb, vraw, cum, st0, state_in, decs, wofull, skip, ggain)
-
-    live = (jnp.arange(SPAN, dtype=jnp.int32)[None, :] < rel[:, None]).astype(f32)[:, :, None]
-    drive = (live * cotangent.astype(f32)).astype(bf16)
-    flat = lambda v: v.reshape(-1, v.shape[-1])
-    p_out = mm_tn(flat(mlow), flat(drive)).astype(bf16)
-    p_gate = mm(nt, flat(ggate)).astype(bf16)
+    )(seq_lengths, skip_gain, tokens_in, cotangent, ylocal, gate, xb, vraw, cum, st0, state_in, decs, wofull, gated_gain, nt)
 
     def tile_in(rows, tiles):
         return pl.BlockSpec((seqs, rows, TILE), lambda i: (0, 0, jnp.minimum(i, tiles - 1)))
@@ -1331,52 +1443,50 @@
         return pl.BlockSpec((1,) + shape, lambda i: (jnp.clip(i - TILES - 1, 0, seqs - 1),) + zeros)
 
     bc_spec = pl.BlockSpec((seqs, SPAN, TILE), lambda i: (0, 0, TILES), pipeline_mode=pl.Buffered(1))
-    sizes = (KCONV * CONVW, CONVW, HALF, HALF, DIN, DIN)
-    height = sum(sizes) // HALF
-    gtok, r_gate, r_out, r_conv, small, g_gain = call(
+    height = SMALL_ROWS
+    x_conv_shape = (GZW // CONV_CHUNK, D // group, CONV_CHUNK)
+    gtok, r_zx, r_out, small, gain_sum = call(
         back_kernel,
         TILES + 1 + seqs,
-        [SMEM, late(SPAN, D), late(SPAN, D), whole((seqs, RIM, D)), whole((1, D)), late(SPAN, DIN), whole((D, ZXW + HALF)),
+        [SMEM, SMEM, SMEM, late(SPAN, D), late(SPAN, D), whole((seqs, RIM, D)), whole((D,)), late(SPAN, DIN), ANY, whole((D, HALF)),
          tile_in(RIM + SPAN, TILES + 1), tile_in(SPAN, TILES + 1), tile_in(SPAN, TILES + 1), bc_spec, tile_in(SPAN, TILES),
          tile_in(SPAN, TILES), tile_in(NSTATE, TILES), tile_in(NSTATE, TILES), tile_in(NSTATE, TILES), tile_in(NSTATE, TILES),
          whole((seqs, SPAN, HALF)), whole((seqs, SPAN, HALF)), whole((seqs, SPAN, HALF)), whole((seqs, SPAN, 2 * NSTATE)),
-         whole((KCONV, CONVW)), whole((1, HALF)), whole((1, DIN)), whole((D, seqs * SPAN)), whole((D, seqs * RIM)),
-         whole((D, DIN)), whole((DIN, D)), whole((1, DIN)), whole((1, DIN))],
+         whole((KCONV, CONVW)), whole((D, seqs * SPAN)), whole((D, seqs * RIM)),
+         whole(x_gate_shape), whole(x_out_shape), whole((1, DIN)), whole((1, DIN))],
         [
             (late(SPAN, D), (seqs, SPAN, D), bf16),
-            (summed((D // group, DIN)), (D // group, DIN), bf16),
+            (summed((D // group, DIN + GZW)), (D // group, DIN + GZW), bf16),
             (summed((DIN // group, D)), (DIN // group, D), bf16),
-            (summed((D // group, GZW)), (D // group, GZW), bf16),
             (summed((height, HALF)), (height, HALF), f32),
             (summed((8, HALF)), (8, HALF), f32),
         ],
-        [((2 * HALF, DIN), bf16), ((seqs, SPAN, 2 * HALF), bf16), ((seqs, SPAN, 2 * HALF), bf16), ((seqs, 16, DIN), f32),
+        [((2 * HALF, DIN), bf16), ((1, DIN), f32), ((D, ZXW), bf16), dma((1,)), ((seqs, SPAN, 2 * HALF), bf16),
+         ((seqs, SPAN, 2 * HALF), bf16), ((seqs, 16, DIN), f32),
          ((seqs, SPAN, NSTATE), f32), ((seqs, SPAN, HALF), f32), ((seqs, 8, HALF), f32), ((RIM + SPAN + 8, TILE), f32),
          ((seqs * SPAN, CONVW + HALF), bf16), ((seqs * RIM, CONVW), bf16), ((D, GZW), bf16), ((KCONV, CONVW), f32),
          ((1, CONVW), f32), ((1, HALF), f32), ((1, HALF), f32), ((1, D), f32), ((seqs, RIM, D), bf16), ((seqs, RIM, D), bf16),
          dma((seqs,)), dma((seqs,))]
-        + Reducer.scratch(DIN // GATE_CHUNK, D // group, GATE_CHUNK, False, group, count)
-        + Reducer.scratch(D // OUT_CHUNK, DIN // group, OUT_CHUNK, True, group, count)
-        + Reducer.scratch(GZW // CONV_CHUNK, D // group, CONV_CHUNK, False, group, count)
+        + Reducer.ctx_scratch(*x_gate_shape, False, count)
+        + Reducer.ctx_scratch(*x_out_shape, True, count)
+        + Reducer.group_scratch(*x_conv_shape, group)
+        + [(x_conv_shape, bf16)]
+        + Reducer.ctx_scratch(*x_conv_shape, False, count)
         + Small.scratch(height, group, count)
         + Small.scratch(8, group, count),
         "back",
         2,
-    )(rel, tokens_in, cotangent, rhalo, gain, ggate, wfull, cin, xb, spb, xb, dy, dxs, dir1, later, state_in, loc,
-      vraw, cum, wred, dbc, conv_weight, dl, skip, nt, nth, p_gate, p_out, gskip, gggain)
-
-    g_zx = jnp.concatenate([r_gate, r_conv[:, :CONVW]], axis=1).astype(f32)
-    g_delta = r_conv[:, CONVW : CONVW + HEADS].astype(f32)
-    small = small.reshape(-1)
-    at = 0
-    pieces = []
-    for size in sizes:
-        pieces.append(small[at : at + size])
-        at += size
-    return (
-        mixed_out, gtok, g_gain.reshape(-1)[:D], g_zx, g_delta, r_out.astype(f32), pieces[0].reshape(KCONV, CONVW), pieces[1],
-        pieces[2][:HEADS], pieces[3][:HEADS], pieces[4].reshape(HEADS, HEADDIM).sum(1), pieces[5],
-    )
+    )(seq_lengths, decay_log, skip_gain, tokens_in, cotangent, rhalo, norm_gain, ggate, wfull, wdfull, cin, xb, spb, xb, dy, dxs, dir1, later, state_in, loc,
+      vraw, cum, wred, dbc, conv_weight, nt, nth, x_gate, x_out, gskip, gggain)
+
+    shapes = [(D,), (D // group, ZXW), (D // group, HEADS), (DIN // group, D), (KCONV, CONVW), (CONVW,), (HEADS,), (HEADS,),
+              (HEADS,), (DIN,)]
+    grads = pl.pallas_call(
+        done_kernel,
+        out_shape=[jax.ShapeDtypeStruct(shape, f32) for shape in shapes],
+        name="done",
+    )(r_zx, r_out, small, gain_sum)
+    return (mixed_out, gtok, *grads)
 
 
 def solution(mesh):

time: 296 us -> 263 us (0.89)
  matrix products: 10.3 us -> 0 us
  other arithmetic: 8.4 us -> 0 us
  Pallas kernels: 264 us -> 256 us
  local copies, waits for them, and re-layouts: 13 us -> 6.16 us
    dot_general x2 -> x0, matrix products: 10.3 us -> none  [the longest x1 6.03 us: mm(): return jnp.dot(a, b, preferred_element_type=f32)]
    pallas_call x3 -> x4, Pallas kernels: 264 us -> 256 us  [the longest x1 86.8 us: local(): call(back_kernel, TILES + 1 + seqs, [SMEM, SMEM, SMEM, late(SPAN, D), lat...]
    convert_element_type x4 -> x0, other arithmetic: 4.78 us -> none  [the longest x1 2.82 us: local(): g_zx = jnp.concatenate([r_gate, r_conv[:, :CONVW]], axis=1).astype(f32)]
    slice x6 -> x0, local copies, waits for them, and re-layouts: 3.52 us -> none  [the longest x1 1.21 us: local(): g_zx = jnp.concatenate([r_gate, r_conv[:, :CONVW]], axis=1).astype(f32)]
where the time goes in v7:
time: 263 us
  Pallas kernels  256 us (97%)
  local copies, waits for them, and re-layouts  6.16 us (2%)
    pallas_call x1, Pallas kernels, local(): call(back_kernel, TILES + 1 + seqs, [SMEM, SMEM, SMEM, late(SPAN, D), lat...  86.8 us
    pallas_call x1, Pallas kernels, local(): call(middle_kernel, 2 * seqs, [SMEM, SMEM, at1(SPAN, D), at0(SPAN, D), at...  84 us
    pallas_call x1, Pallas kernels, local(): call(front_kernel, PIECES, [whole((seqs, SPAN, D)), ANY, ANY, ANY, ANY, w...  81.3 us
    unnamed x8, local copies, waits for them, and re-layouts  5.52 us

profile of v7, /device:TPU:0, one launch (start us, length us, event | category | flops | bytes accessed | tf_op | source)
XLA Modules:
  0.0 262.7 jit_solution(16337036999716909608)
XLA Ops:
  0.6 0.8 copy.25
  1.5 0.6 pad.4.wdl
  2.1 81.3 %front.1 = (bf16[768,1024]{1,0:T(8,128)(2,1)}, bf16[768,64]{1,0:T(8,128)(2,1)}, bf16[4,16,768]{2,1,0:T(8,128)(2,1)}, bf16[4,272,1792]{2,1,0:T(8,128)(2,1)}, bf16...) custom-call(bf16[4,256,768]{2,1,0:T(8,128)(2,1)} %tok.5, ...), custom_call_target="tpu_custom_call" | custom-call | tf_op jit(solution)/shard_map/front/pallas_call | solution.py:1371
  83.4 84.0 %middle.1 = (bf16[4,256,768]{2,1,0:T(8,128)(2,1)}, bf16[4,256,1536]{2,1,0:T(8,128)(2,1)}, bf16[4,256,1536]{2,1,0:T(8,128)(2,1)}, f32[4,256,128]{2,1,0:T(8,128)},...) custom-call(s32[4]{0:T(128)} %lengths.3, ...), custom_call_target="tpu_custom_call" | custom-call | tf_op jit(solution)/shard_map/middle/pallas_call | solution.py:1407
  167.4 86.8 %back.1 = (bf16[4,256,768]{2,1,0:T(8,128)(2,1)}, bf16[192,3584]{1,0:T(8,128)(2,1)}, bf16[384,768]{1,0:T(8,128)(2,1)}, f32[88,128]{1,0:T(8,128)}, f32[8,128]{1,0:T(8,128)}) custom-call(s32[4]{0:T(128)} %lengths.3, f32[24]{0:T(128)} %dl.3, f32[24]{0:T(128)} %skip_in.3, bf16[4,256,768]{2,1,0:T(8,128)(2,1)} %tok.5, bf16[4,256,768]{2,1,0:T(8,128)(2,1)} %cot.3, ...), custom_call_target="tpu_custom_call" | custom-call | tf_op jit(solution)/shard_map/back/pallas_call | solution.py:1448
  254.3 0.0 copy-start
  254.3 3.7 %done.1 = (f32[768]{0:T(1024)}, f32[192,3328]{1,0:T(8,128)}, f32[192,24]{1,0:T(8,128)}, f32[384,768]{1,0:T(8,128)}, f32[4,1792]{1,0:T(4,128)}, /*index=5*/f32[17...) custom-call(bf16[192,3584]{1,0:T(8,128)(2,1)} %get-tuple-element.86.rzx, ...), custom_call_target="tpu_custom_call" | custom-call | tf_op jit(solution)/shard_map/done/pallas_call | solution.py:1484
  258.0 1.6 copy.26
  259.6 0.0 copy-done
  259.6 0.0 copy-start.1
  259.6 1.1 copy.29
  260.7 0.8 copy-done.1
  261.5 1.1 copy.30
Async XLA Ops:
  254.3 5.3 %copy-start = (bf16[4,256,768]{2,1,0:T(8,128)(2,1)S(1)}, bf16[4,256,768]{2,1,0:T(8,128)(2,1)}, u32[]{:S(2)}) copy-start(bf16[4,256,768]{2,1,0:T(8,128)(2,1)} %get-tuple-element.124) | copy-start | bytes 4718596
  259.6 2.0 copy-start.1

commit v8 on v7

--- a/solution.py
+++ b/solution.py
@@ -28,8 +28,9 @@
 GATE_CHUNK = 512
 OUT_CHUNK = 256
 CONV_CHUNK = 512
-BACK_LAGS = (5, 7, 9)
+BACK_LAGS = (4, 7, 9)
 STAGE_LAG = 4
+CONV_LAG = 3
 MIDDLE_LAG = 2
 SCAN_LAG = 4
 HOPS = ("group", "ctx")
@@ -77,8 +78,14 @@
     return jnp.where(keep, 1.0, 0.0).astype(f32)
 
 
-def exact_mm(a, b):
-    return jnp.dot(a, b, precision=lax.Precision.HIGHEST, preferred_element_type=f32)
+def running_sum(v, lower):
+    rest, terms = v, []
+    for _ in range(3):
+        high = rest.astype(bf16)
+        rest = rest - high.astype(f32)
+        terms.append(high)
+    tri = triangle(v.shape[0], lower).astype(bf16)
+    return mm(tri, terms[0]) + (mm(tri, terms[1]) + mm(tri, terms[2]))
 
 
 def softplus(v):
@@ -144,21 +151,27 @@
     lax.fori_loop(start, stop, step, 0)
 
 
-def meet(axes):
+def greet(axes):
     barrier = pltpu.get_barrier_semaphore()
-    total = 0
     for axis in axes:
         size = lax.axis_size(axis)
         me = lax.axis_index(axis)
 
-        def greet(d):
+        def signal(d, axis=axis, size=size, me=me):
             pl.semaphore_signal(
                 barrier, inc=1, device_id={axis: lax.rem(me + d, size)}, device_id_type=pl.DeviceIdType.MESH
             )
 
-        loop(1, size, greet)
-        total += size - 1
-    pl.semaphore_wait(barrier, total)
+        loop(1, size, signal)
+
+
+def settle(axes):
+    pl.semaphore_wait(pltpu.get_barrier_semaphore(), sum(lax.axis_size(axis) - 1 for axis in axes))
+
+
+def meet(axes):
+    greet(axes)
+    settle(axes)
 
 
 class Exchange:
@@ -542,9 +555,9 @@
         self.if_owner(lambda: self.other_lines(lambda line: self.b_copy(k, line, self.mine).wait_send()))
         self.f_copy(k, self.inner).wait_send()
 
-    def wave(self, t, acts, chunk_at):
+    def wave(self, t, acts, chunk_at, lag=STAGE_LAG):
         for order, act in reversed(list(enumerate(acts))):
-            k, is_due = chunk_at(t - order * STAGE_LAG)
+            k, is_due = chunk_at(t - order * lag)
             pl.when(is_due)(lambda k=k, act=act: act(k))
 
     def each(self, t):
@@ -626,6 +639,7 @@
 TILES = DIN // TILE
 PIECES = 2 * TILES + 1
 DT0 = DIN + CONVW - 2 * NSTATE
+AHEAD = 5
 
 
 def front_kernel(
@@ -689,8 +703,8 @@
         de.start_chip(2)
         zx.start_chip(0)
         cb[...] = row_of(cb_in)
-        zx.start(1, piece(1))
-        zx.start(2, piece(2))
+        for p in range(1, AHEAD):
+            zx.start(p, piece(p))
         wo.start_chip(1)
         sel[...] = head_map()
 
@@ -726,11 +740,11 @@
     def _():
         zx.forward(i + 1, piece(i + 1))
 
-    @pl.when(i + 3 < PIECES)
-    def _():
-        zx.start(i + 3, piece(i + 3))
-
-    @pl.when(i + 3 == PIECES)
+    @pl.when(i + AHEAD < PIECES)
+    def _():
+        zx.start(i + AHEAD, piece(i + AHEAD))
+
+    @pl.when(i + AHEAD == PIECES)
     def _():
         wo.start(last, slice(None))
 
@@ -749,7 +763,7 @@
             v = mm(ext[s, RIM:], wd[...]) + shift
             vout[s] = v
             dt = softplus(v)
-            cum = exact_mm(triangle(SPAN, True), -rate * dt)
+            cum = running_sum(-rate * dt, True)
             cumout[s] = cum
             for q in range(2):
                 cum_t[s, q] = jnp.transpose(cum[both(q)])
@@ -894,12 +908,20 @@
 
     @pl.when(i == 0)
     def _():
-        meet(("ctx", "group"))
+        greet(("ctx", "group"))
         sel[...] = head_map()
         skip[...] = spread(rows_of(lane_row(skip_in)), sel)[0:1]
         ggain[...] = row_of(ggain_in)
         gskip[...] = jnp.zeros_like(gskip)
         gggain[...] = jnp.zeros_like(gggain)
+
+    @pl.when(i == 1)
+    def _():
+        settle(("ctx", "group"))
+
+    @pl.when(jnp.logical_and(i >= 1, i <= seqs))
+    def _():
+        ex.start(i - 1)
 
     wave(2 * i)
 
@@ -979,7 +1001,6 @@
         wred[0] = acc
         for q in range(2):
             dcs[s, both(q)] = dc[q]
-        ex.start(s)
 
     @pl.when(i >= seqs)
     def _():
@@ -1023,7 +1044,11 @@
         def _():
             loop(0, outs.chunks, outs.m_done)
 
-        loop(0, PAIRS // 2, pair_step)
+        def two_pairs(pp):
+            for h in range(2):
+                pair_step(2 * pp + h)
+
+        loop(0, PAIRS // 4, two_pairs)
         wave(2 * i + 1)
 
         @pl.when(s == 0)
@@ -1037,7 +1062,7 @@
             loop(0, DIN // TILE, out_rows)
             loop(0, outs.chunks, outs.m_start)
 
-        loop(PAIRS // 2, PAIRS, pair_step)
+        loop(PAIRS // 4, PAIRS // 2, two_pairs)
         for q in range(2):
             rows = both(q)
             dg = dg_s[q].astype(bf16)
@@ -1087,7 +1112,7 @@
     def wave(t):
         for r, at in ((gates, 2), (outs, 2 + gates.chunks)):
             r.wave(t - at, [r.y_done, r.z_done, r.b_done, r.f_done], r.each)
-        convs.wave(t, [convs.x_done, convs.y_done, convs.z_done, convs.b_done, convs.f_done], conv_at)
+        convs.wave(t, [convs.x_done, convs.y_done, convs.z_done, convs.b_done, convs.f_done], conv_at, CONV_LAG)
 
     def rim_copy(q):
         return remote(rim_out.at[q], rim_in.at[q], rim_send.at[q], rim_recv.at[q], ctx=lax.rem(me + count - 1, count))
@@ -1204,7 +1229,7 @@
             q = qacc[s]
             at_end = lax.broadcasted_iota(jnp.int32, (SPAN, 1), 0) == SPAN - 1
             dcum = wred[s] - dt * q + jnp.where(at_end, ends[s][0:1], 0.0)
-            glog = exact_mm(triangle(SPAN, False), dcum)
+            glog = running_sum(dcum, False)
             gpd = (q - rate * glog) * sigmoid(v)
             lanes = lax.broadcasted_iota(jnp.int32, (SPAN, HALF), 1) < HEADS
             gpd = jnp.where(lanes, gpd, 0.0)
@@ -1267,9 +1292,12 @@
         least.start(0)
         little.done(1)
         small_out[...] = little.held[2]
+        ends_at = max(last_conv + 4 * CONV_LAG, 1 + gates.chunks + outs.chunks + 3 * STAGE_LAG) + 1
+        here = 2 * (bc_step + seqs) + 2
+        loop(here, min(here + 2, ends_at), wave)
         least.done(0)
         least.start(1)
-        loop(2 * (bc_step + seqs) + 2, last_conv + 4 * STAGE_LAG + 1, wave)
+        loop(here + 2, ends_at, wave)
         for r in (gates, outs, convs):
             loop(0, r.chunks, r.drain_ctx)
         loop(0, convs.chunks, convs.drain_group)

time: 263 us -> 253 us (0.962)
  Pallas kernels: 256 us -> 246 us
    pallas_call x1, Pallas kernels: 84 us -> 76.7 us  [local(): call(middle_kernel, 2 * seqs, [SMEM, SMEM, at1(SPAN, D), at0(SPAN, D), at...]
where the time goes in v8:
time: 253 us
  Pallas kernels  246 us (97%)
  local copies, waits for them, and re-layouts  6.16 us (2%)
    pallas_call x1, Pallas kernels, local(): call(back_kernel, TILES + 1 + seqs, [SMEM, SMEM, SMEM, late(SPAN, D), lat...  86.5 us
    pallas_call x1, Pallas kernels, local(): call(front_kernel, PIECES, [whole((seqs, SPAN, D)), ANY, ANY, ANY, ANY, w...  78.8 us
    pallas_call x1, Pallas kernels, local(): call(middle_kernel, 2 * seqs, [SMEM, SMEM, at1(SPAN, D), at0(SPAN, D), at...  76.7 us
    unnamed x8, local copies, waits for them, and re-layouts  5.52 us

profile of v8, /device:TPU:0, one launch (start us, length us, event | category | flops | bytes accessed | tf_op | source)
XLA Modules:
  0.0 252.5 jit_solution(4210574314669635014)
XLA Ops:
  0.6 0.8 copy.25
  1.5 0.6 pad.4.wdl
  2.1 78.8 %front.1 = (bf16[768,1024]{1,0:T(8,128)(2,1)}, bf16[768,64]{1,0:T(8,128)(2,1)}, bf16[4,16,768]{2,1,0:T(8,128)(2,1)}, bf16[4,272,1792]{2,1,0:T(8,128)(2,1)}, bf16...) custom-call(bf16[4,256,768]{2,1,0:T(8,128)(2,1)} %tok.5, ...), custom_call_target="tpu_custom_call" | custom-call | tf_op jit(solution)/shard_map/front/pallas_call | solution.py:1399
  80.9 76.7 %middle.1 = (bf16[4,256,768]{2,1,0:T(8,128)(2,1)}, bf16[4,256,1536]{2,1,0:T(8,128)(2,1)}, bf16[4,256,1536]{2,1,0:T(8,128)(2,1)}, f32[4,256,128]{2,1,0:T(8,128)},...) custom-call(s32[4]{0:T(128)} %lengths.3, ...), custom_call_target="tpu_custom_call" | custom-call | tf_op jit(solution)/shard_map/middle/pallas_call | solution.py:1435
  157.6 86.5 %back.1 = (bf16[4,256,768]{2,1,0:T(8,128)(2,1)}, bf16[192,3584]{1,0:T(8,128)(2,1)}, bf16[384,768]{1,0:T(8,128)(2,1)}, f32[88,128]{1,0:T(8,128)}, f32[8,128]{1,0:T(8,128)}) custom-call(s32[4]{0:T(128)} %lengths.3, f32[24]{0:T(128)} %dl.3, f32[24]{0:T(128)} %skip_in.3, bf16[4,256,768]{2,1,0:T(8,128)(2,1)} %tok.5, bf16[4,256,768]{2,1,0:T(8,128)(2,1)} %cot.3, ...), custom_call_target="tpu_custom_call" | custom-call | tf_op jit(solution)/shard_map/back/pallas_call | solution.py:1476
  244.1 0.0 copy-start
  244.1 3.7 %done.1 = (f32[768]{0:T(1024)}, f32[192,3328]{1,0:T(8,128)}, f32[192,24]{1,0:T(8,128)}, f32[384,768]{1,0:T(8,128)}, f32[4,1792]{1,0:T(4,128)}, /*index=5*/f32[17...) custom-call(bf16[192,3584]{1,0:T(8,128)(2,1)} %get-tuple-element.86.rzx, ...), custom_call_target="tpu_custom_call" | custom-call | tf_op jit(solution)/shard_map/done/pallas_call | solution.py:1512
  247.8 1.6 copy.26
  249.4 0.0 copy-done
  249.4 0.0 copy-start.1
  249.4 1.1 copy.29
  250.6 0.8 copy-done.1
  251.4 1.1 copy.30
Async XLA Ops:
  244.1 5.3 %copy-start = (bf16[4,256,768]{2,1,0:T(8,128)(2,1)S(1)}, bf16[4,256,768]{2,1,0:T(8,128)(2,1)}, u32[]{:S(2)}) copy-start(bf16[4,256,768]{2,1,0:T(8,128)(2,1)} %get-tuple-element.124) | copy-start | bytes 4718596
  249.4 2.0 copy-start.1

commit v9 on v8

--- a/solution.py
+++ b/solution.py
@@ -1140,8 +1140,9 @@
         skip[...] = spread(rows_of(lane_row(skip_in)), sel)[0:1]
         for acc in (db_s, qacc, ends, gcw, gcb, gdb, gdl, ggain):
             acc[...] = jnp.zeros_like(acc)
-        gp[0:RIM] = jnp.zeros((RIM, TILE), f32)
-        gp[RIM + SPAN :] = jnp.zeros((8, TILE), f32)
+        for slot in range(2):
+            gp[slot, 0:RIM] = jnp.zeros((RIM, TILE), f32)
+            gp[slot, RIM + SPAN :] = jnp.zeros((8, TILE), f32)
         pconv[:, CONVW + HALF :] = jnp.zeros((D, GZW - CONVW - HALF), bf16)
 
         def setup(s):
@@ -1154,9 +1155,9 @@
 
         loop(0, seqs, setup)
 
-    def conv_back(s, dact, cols):
+    def conv_back(s, dact, cols, slot=0):
         gco = dact * spb[s].astype(f32)
-        gp[RIM : RIM + SPAN] = gco
+        gp[slot, RIM : RIM + SPAN] = gco
         gcb[:, cols] += jnp.sum(gco, axis=0, keepdims=True)
         own = cin[s, RIM:].astype(f32)
         before = cin[s, :RIM].astype(f32)
@@ -1164,8 +1165,8 @@
         rim = jnp.zeros((RIM, TILE), f32)
         for k in range(KCONV):
             ahead = KCONV - 1 - k
-            moved = gco if ahead == 0 else gp[RIM + ahead : RIM + ahead + SPAN]
-            early = gp[ahead : ahead + RIM]
+            moved = gco if ahead == 0 else gp[slot, RIM + ahead : RIM + ahead + SPAN]
+            early = gp[slot, ahead : ahead + RIM]
             main = main + cw[k : k + 1, cols] * moved
             rim = rim + cw[k : k + 1, cols] * early
             gcw[k : k + 1, cols] += jnp.sum(own * moved, axis=0, keepdims=True) + jnp.sum(
@@ -1183,7 +1184,7 @@
     def _():
         cols = pl.ds(pl.multiple_of(i * TILE, TILE), TILE)
 
-        def x_tile(s):
+        def x_tile(s, slot):
             dte = mm(dt_cat[s], sel[:, cols])
             eo = mm(eo_cat[s], sel[:, cols])
             near = later[s]
@@ -1201,16 +1202,20 @@
                 db_s[s, both(q)] += mm_nt(xw[both(q)], reach[q])
             held = near32 * (tot[8:9] * sin[s].astype(f32) + loc[s].astype(f32))
             ends[s] += gather_heads(rows_of(jnp.sum(held, axis=0, keepdims=True)), sel[:HALF, cols])
-            conv_back(s, dte * dx_s + skip[:, cols] * dy[s].astype(f32), cols)
-
-        loop(0, seqs // 2, x_tile)
+            conv_back(s, dte * dx_s + skip[:, cols] * dy[s].astype(f32), cols, slot)
+
+        def two_seqs(h):
+            for slot in range(2):
+                x_tile(2 * h + slot, slot)
+
+        loop(0, seqs // 4, two_seqs)
 
         @pl.when(jnp.logical_and(lax.rem(i, 2) == 0, i >= 2))
         def _():
             convs.m_done(lax.div(i, 2) - 1)
 
         wave(2 * i + 1)
-        loop(seqs // 2, seqs, x_tile)
+        loop(seqs // 4, seqs // 2, two_seqs)
         partial(cols)
 
         @pl.when(lax.rem(i, 2) == 1)
@@ -1309,25 +1314,31 @@
         least.drain()
 
 
-def done_kernel(rzx, rout, small, gain_sum, g_gain, g_zx, g_delta, g_out, g_cw, g_cb, g_db, g_dl, g_skip, g_gated):
+def done_kernel(
+    rzx, rdelta, rout, small, gain_sum,
+    g_gain, g_zx, g_delta, g_out, g_cw, g_cb, g_db, g_dl, g_skip, g_gated,
+):
+    @pl.when(pl.program_id(0) == 0)
+    def _():
+        tiles = CONVW // HALF
+        for k in range(KCONV):
+            for j in range(tiles):
+                g_cw[k : k + 1, j * HALF : (j + 1) * HALF] = small[k * tiles + j : k * tiles + j + 1, :]
+        at = KCONV * tiles
+        for j in range(tiles):
+            g_cb[j * HALF : (j + 1) * HALF] = small[at + j, :]
+        at += tiles
+        for ref in (g_db, g_dl, g_skip):
+            ref[...] = small[at, :][:HEADS]
+            at += 1
+        for j in range(PAIRS):
+            g_gated[j * HALF : (j + 1) * HALF] = small[at + j, :]
+        for j in range(D // HALF):
+            g_gain[j * HALF : (j + 1) * HALF] = gain_sum[j, :]
+        g_delta[...] = jnp.transpose(rdelta[...].astype(f32))[:HEADS]
+
     g_zx[...] = rzx[:, :ZXW].astype(f32)
-    g_delta[...] = rzx[:, ZXW : ZXW + HEADS].astype(f32)
     g_out[...] = rout[...].astype(f32)
-    tiles = CONVW // HALF
-    for k in range(KCONV):
-        for j in range(tiles):
-            g_cw[k : k + 1, j * HALF : (j + 1) * HALF] = small[k * tiles + j : k * tiles + j + 1, :]
-    at = KCONV * tiles
-    for j in range(tiles):
-        g_cb[j * HALF : (j + 1) * HALF] = small[at + j, :]
-    at += tiles
-    for ref in (g_db, g_dl, g_skip):
-        ref[...] = small[at, :][:HEADS]
-        at += 1
-    for j in range(PAIRS):
-        g_gated[j * HALF : (j + 1) * HALF] = small[at + j, :]
-    for j in range(D // HALF):
-        g_gain[j * HALF : (j + 1) * HALF] = gain_sum[j, :]
 
 
 def whole(shape):
@@ -1491,7 +1502,7 @@
         ],
         [((2 * HALF, DIN), bf16), ((1, DIN), f32), ((D, ZXW), bf16), dma((1,)), ((seqs, SPAN, 2 * HALF), bf16),
          ((seqs, SPAN, 2 * HALF), bf16), ((seqs, 16, DIN), f32),
-         ((seqs, SPAN, NSTATE), f32), ((seqs, SPAN, HALF), f32), ((seqs, 8, HALF), f32), ((RIM + SPAN + 8, TILE), f32),
+         ((seqs, SPAN, NSTATE), f32), ((seqs, SPAN, HALF), f32), ((seqs, 8, HALF), f32), ((2, RIM + SPAN + 8, TILE), f32),
          ((seqs * SPAN, CONVW + HALF), bf16), ((seqs * RIM, CONVW), bf16), ((D, GZW), bf16), ((KCONV, CONVW), f32),
          ((1, CONVW), f32), ((1, HALF), f32), ((1, HALF), f32), ((1, D), f32), ((seqs, RIM, D), bf16), ((seqs, RIM, D), bf16),
          dma((seqs,)), dma((seqs,))]
@@ -1507,14 +1518,25 @@
     )(seq_lengths, decay_log, skip_gain, tokens_in, cotangent, rhalo, norm_gain, ggate, wfull, wdfull, cin, xb, spb, xb, dy, dxs, dir1, later, state_in, loc,
       vraw, cum, wred, dbc, conv_weight, nt, nth, x_gate, x_out, gskip, gggain)
 
-    shapes = [(D,), (D // group, ZXW), (D // group, HEADS), (DIN // group, D), (KCONV, CONVW), (CONVW,), (HEADS,), (HEADS,),
-              (HEADS,), (DIN,)]
-    grads = pl.pallas_call(
+    zx_rows, out_rows = D // group, DIN // group
+    turns = 2
+    halved = lambda rows, cols: pl.BlockSpec((rows // turns, cols), lambda i: (i, 0))
+    grad = lambda *shape: (summed(shape), jax.ShapeDtypeStruct(shape, f32))
+    specs, shapes = zip(
+        grad(D), (halved(zx_rows, ZXW), jax.ShapeDtypeStruct((zx_rows, ZXW), f32)),
+        grad(HEADS, zx_rows), (halved(out_rows, D), jax.ShapeDtypeStruct((out_rows, D), f32)), grad(KCONV, CONVW), grad(CONVW),
+        grad(HEADS), grad(HEADS), grad(HEADS), grad(DIN),
+    )
+    results = pl.pallas_call(
         done_kernel,
-        out_shape=[jax.ShapeDtypeStruct(shape, f32) for shape in shapes],
+        grid=(turns,),
+        in_specs=[halved(zx_rows, DIN + GZW), pl.BlockSpec((zx_rows, HALF), lambda i: (0, ZXW // HALF)), halved(out_rows, D),
+                  whole((SMALL_ROWS, HALF)), whole((8, HALF))],
+        out_specs=specs,
+        out_shape=shapes,
         name="done",
-    )(r_zx, r_out, small, gain_sum)
-    return (mixed_out, gtok, *grads)
+    )(r_zx, r_zx, r_out, small, gain_sum)
+    return (mixed_out, gtok, *results[:2], results[2].T, *results[3:])
 
 
 def solution(mesh):

time: 253 us -> 249 us (0.984)
    unnamed x8 -> x7, local copies, waits for them, and re-layouts: 5.52 us -> 3.94 us
where the time goes in v9:
time: 249 us
  Pallas kernels  244 us (98%)
  local copies, waits for them, and re-layouts  4.58 us (2%)
    pallas_call x1, Pallas kernels, local(): call(back_kernel, TILES + 1 + seqs, [SMEM, SMEM, SMEM, late(SPAN, D), lat...  85.1 us
    pallas_call x1, Pallas kernels, local(): call(front_kernel, PIECES, [whole((seqs, SPAN, D)), ANY, ANY, ANY, ANY, w...  78.8 us
    pallas_call x1, Pallas kernels, local(): call(middle_kernel, 2 * seqs, [SMEM, SMEM, at1(SPAN, D), at0(SPAN, D), at...  76.7 us

profile of v9, /device:TPU:0, one launch (start us, length us, event | category | flops | bytes accessed | tf_op | source)
XLA Modules:
  0.0 249.3 jit_solution(10652804545961208022)
XLA Ops:
  0.6 0.8 copy.25
  1.5 0.6 pad.4.wdl
  2.1 78.8 %front.1 = (bf16[768,1024]{1,0:T(8,128)(2,1)}, bf16[768,64]{1,0:T(8,128)(2,1)}, bf16[4,16,768]{2,1,0:T(8,128)(2,1)}, bf16[4,272,1792]{2,1,0:T(8,128)(2,1)}, bf16...) custom-call(bf16[4,256,768]{2,1,0:T(8,128)(2,1)} %tok.5, ...), custom_call_target="tpu_custom_call" | custom-call | tf_op jit(solution)/shard_map/front/pallas_call | solution.py:1410
  80.9 76.7 %middle.1 = (bf16[4,256,768]{2,1,0:T(8,128)(2,1)}, bf16[4,256,1536]{2,1,0:T(8,128)(2,1)}, bf16[4,256,1536]{2,1,0:T(8,128)(2,1)}, f32[4,256,128]{2,1,0:T(8,128)},...) custom-call(s32[4]{0:T(128)} %lengths.3, ...), custom_call_target="tpu_custom_call" | custom-call | tf_op jit(solution)/shard_map/middle/pallas_call | solution.py:1446
  157.6 85.1 %back.1 = (bf16[4,256,768]{2,1,0:T(8,128)(2,1)}, bf16[192,3584]{1,0:T(8,128)(2,1)}, bf16[384,768]{1,0:T(8,128)(2,1)}, f32[88,128]{1,0:T(8,128)}, f32[8,128]{1,0:T(8,128)}) custom-call(s32[4]{0:T(128)} %lengths.3, f32[24]{0:T(128)} %dl.3, f32[24]{0:T(128)} %skip_in.3, bf16[4,256,768]{2,1,0:T(8,128)(2,1)} %tok.5, bf16[4,256,768]{2,1,0:T(8,128)(2,1)} %cot.3, ...), custom_call_target="tpu_custom_call" | custom-call | tf_op jit(solution)/shard_map/back/pallas_call | solution.py:1487
  242.7 0.0 copy-start
  242.7 3.4 %done.1 = (f32[768]{0:T(1024)}, f32[192,3328]{1,0:T(8,128)}, f32[24,192]{1,0:T(8,128)}, f32[384,768]{1,0:T(8,128)}, f32[4,1792]{1,0:T(4,128)}, /*index=5*/f32[17...) custom-call(bf16[192,3584]{1,0:T(8,128)(2,1)} %get-tuple-element.86.rzx.rdelta, ...), custom_call_target="tpu_custom_call" | custom-call | tf_op jit(solution)/shard_map/done/pallas_call | solution.py:1530
  246.1 0.0 copy-done
  246.1 0.0 copy-start.1
  246.2 1.1 copy.28
  247.3 0.8 copy-done.1
  248.1 1.1 copy.29
Async XLA Ops:
  242.7 3.4 %copy-start = (bf16[4,256,768]{2,1,0:T(8,128)(2,1)S(1)}, bf16[4,256,768]{2,1,0:T(8,128)(2,1)}, u32[]{:S(2)}) copy-start(bf16[4,256,768]{2,1,0:T(8,128)(2,1)} %get-tuple-element.112) | copy-start | bytes 4718596
  246.1 2.0 copy-start.1

commit v10 on v9

--- a/solution.py
+++ b/solution.py
@@ -846,7 +846,11 @@
                     ylocal[s, rows, lanes] = mm(m, x.astype(bf16)).astype(bf16)
             gate[s] = mm(ext[s, RIM:], w[:, piece(i)]).astype(bf16)
 
-        loop(0, seqs, intra)
+        def two_intra(h):
+            for b in range(2):
+                intra(2 * h + b)
+
+        loop(0, seqs // 2, two_intra)
 
     @pl.when(i == PIECES - 1)
     def _():

time: 249 us -> 247 us (level)
  no operation moved by 1% of the time
where the time goes in v10:
time: 247 us
  Pallas kernels  242 us (98%)
  local copies, waits for them, and re-layouts  4.58 us (2%)
    pallas_call x1, Pallas kernels, local(): call(back_kernel, TILES + 1 + seqs, [SMEM, SMEM, SMEM, late(SPAN, D), lat...  84 us
    pallas_call x1, Pallas kernels, local(): call(front_kernel, PIECES, [whole((seqs, SPAN, D)), ANY, ANY, ANY, ANY, w...  78.1 us
    pallas_call x1, Pallas kernels, local(): call(middle_kernel, 2 * seqs, [SMEM, SMEM, at1(SPAN, D), at0(SPAN, D), at...  76.4 us

profile of v10, /device:TPU:0, one launch (start us, length us, event | category | flops | bytes accessed | tf_op | source)
XLA Modules:
  0.0 247.1 jit_solution(9902376008542803589)
XLA Ops:
  0.6 0.8 copy.25
  1.5 0.6 pad.4.wdl
  2.1 78.1 %front.1 = (bf16[768,1024]{1,0:T(8,128)(2,1)}, bf16[768,64]{1,0:T(8,128)(2,1)}, bf16[4,16,768]{2,1,0:T(8,128)(2,1)}, bf16[4,272,1792]{2,1,0:T(8,128)(2,1)}, bf16...) custom-call(bf16[4,256,768]{2,1,0:T(8,128)(2,1)} %tok.5, ...), custom_call_target="tpu_custom_call" | custom-call | tf_op jit(solution)/shard_map/front/pallas_call | solution.py:1414
  80.2 76.4 %middle.1 = (bf16[4,256,768]{2,1,0:T(8,128)(2,1)}, bf16[4,256,1536]{2,1,0:T(8,128)(2,1)}, bf16[4,256,1536]{2,1,0:T(8,128)(2,1)}, f32[4,256,128]{2,1,0:T(8,128)},...) custom-call(s32[4]{0:T(128)} %lengths.3, ...), custom_call_target="tpu_custom_call" | custom-call | tf_op jit(solution)/shard_map/middle/pallas_call | solution.py:1450
  156.6 84.0 %back.1 = (bf16[4,256,768]{2,1,0:T(8,128)(2,1)}, bf16[192,3584]{1,0:T(8,128)(2,1)}, bf16[384,768]{1,0:T(8,128)(2,1)}, f32[88,128]{1,0:T(8,128)}, f32[8,128]{1,0:T(8,128)}) custom-call(s32[4]{0:T(128)} %lengths.3, f32[24]{0:T(128)} %dl.3, f32[24]{0:T(128)} %skip_in.3, bf16[4,256,768]{2,1,0:T(8,128)(2,1)} %tok.5, bf16[4,256,768]{2,1,0:T(8,128)(2,1)} %cot.3, ...), custom_call_target="tpu_custom_call" | custom-call | tf_op jit(solution)/shard_map/back/pallas_call | solution.py:1491
  240.6 0.0 copy-start
  240.6 3.4 %done.1 = (f32[768]{0:T(1024)}, f32[192,3328]{1,0:T(8,128)}, f32[24,192]{1,0:T(8,128)}, f32[384,768]{1,0:T(8,128)}, f32[4,1792]{1,0:T(4,128)}, /*index=5*/f32[17...) custom-call(bf16[192,3584]{1,0:T(8,128)(2,1)} %get-tuple-element.86.rzx.rdelta, ...), custom_call_target="tpu_custom_call" | custom-call | tf_op jit(solution)/shard_map/done/pallas_call | solution.py:1534
  244.0 0.0 copy-done
  244.0 0.0 copy-start.1
  244.0 1.1 copy.28
  245.2 0.8 copy-done.1
  246.0 1.1 copy.29
Async XLA Ops:
  240.6 3.4 %copy-start = (bf16[4,256,768]{2,1,0:T(8,128)(2,1)S(1)}, bf16[4,256,768]{2,1,0:T(8,128)(2,1)}, u32[]{:S(2)}) copy-start(bf16[4,256,768]{2,1,0:T(8,128)(2,1)} %get-tuple-element.112) | copy-start | bytes 4718596
  244.0 2.0 copy-start.1

commit v11 on v10

--- a/solution.py
+++ b/solution.py
@@ -1231,8 +1231,8 @@
         cols = slice(DIN, CONVW)
         rate = jnp.exp(lane_row(dl))
 
-        def bc_tile(s):
-            conv_back(s, jnp.concatenate([dbc[s, :, :NSTATE] + db_s[s], dbc[s, :, NSTATE:]], axis=1), cols)
+        def bc_tile(s, slot):
+            conv_back(s, jnp.concatenate([dbc[s, :, :NSTATE] + db_s[s], dbc[s, :, NSTATE:]], axis=1), cols, slot)
             v = vin[s]
             dt = softplus(v)
             q = qacc[s]
@@ -1246,7 +1246,11 @@
             gdb[...] += jnp.sum(gpd, axis=0, keepdims=True)
             gdl[...] += -rate * jnp.sum(dt * glog, axis=0, keepdims=True)
 
-        loop(0, seqs, bc_tile)
+        def two_bc(h):
+            for slot in range(2):
+                bc_tile(2 * h + slot, slot)
+
+        loop(0, seqs // 2, two_bc)
         convs.m_done(convs.chunks - 2)
         wave(2 * i + 1)
         partial(cols)

time: 247 us -> 247 us (level)
  no operation moved by 1% of the time
where the time goes in v11:
time: 247 us
  Pallas kernels  242 us (98%)
  local copies, waits for them, and re-layouts  4.58 us (2%)
    pallas_call x1, Pallas kernels, local(): call(back_kernel, TILES + 1 + seqs, [SMEM, SMEM, SMEM, late(SPAN, D), lat...  83.8 us
    pallas_call x1, Pallas kernels, local(): call(front_kernel, PIECES, [whole((seqs, SPAN, D)), ANY, ANY, ANY, ANY, w...  78.1 us
    pallas_call x1, Pallas kernels, local(): call(middle_kernel, 2 * seqs, [SMEM, SMEM, at1(SPAN, D), at0(SPAN, D), at...  76.4 us

profile of v11, /device:TPU:0, one launch (start us, length us, event | category | flops | bytes accessed | tf_op | source)
XLA Modules:
  0.0 246.9 jit_solution(13773948009431000088)
XLA Ops:
  0.6 0.8 copy.25
  1.5 0.6 pad.4.wdl
  2.1 78.1 %front.1 = (bf16[768,1024]{1,0:T(8,128)(2,1)}, bf16[768,64]{1,0:T(8,128)(2,1)}, bf16[4,16,768]{2,1,0:T(8,128)(2,1)}, bf16[4,272,1792]{2,1,0:T(8,128)(2,1)}, bf16...) custom-call(bf16[4,256,768]{2,1,0:T(8,128)(2,1)} %tok.5, ...), custom_call_target="tpu_custom_call" | custom-call | tf_op jit(solution)/shard_map/front/pallas_call | solution.py:1418
  80.2 76.4 %middle.1 = (bf16[4,256,768]{2,1,0:T(8,128)(2,1)}, bf16[4,256,1536]{2,1,0:T(8,128)(2,1)}, bf16[4,256,1536]{2,1,0:T(8,128)(2,1)}, f32[4,256,128]{2,1,0:T(8,128)},...) custom-call(s32[4]{0:T(128)} %lengths.3, ...), custom_call_target="tpu_custom_call" | custom-call | tf_op jit(solution)/shard_map/middle/pallas_call | solution.py:1454
  156.6 83.8 %back.1 = (bf16[4,256,768]{2,1,0:T(8,128)(2,1)}, bf16[192,3584]{1,0:T(8,128)(2,1)}, bf16[384,768]{1,0:T(8,128)(2,1)}, f32[88,128]{1,0:T(8,128)}, f32[8,128]{1,0:T(8,128)}) custom-call(s32[4]{0:T(128)} %lengths.3, f32[24]{0:T(128)} %dl.3, f32[24]{0:T(128)} %skip_in.3, bf16[4,256,768]{2,1,0:T(8,128)(2,1)} %tok.5, bf16[4,256,768]{2,1,0:T(8,128)(2,1)} %cot.3, ...), custom_call_target="tpu_custom_call" | custom-call | tf_op jit(solution)/shard_map/back/pallas_call | solution.py:1495
  240.4 0.0 copy-start
  240.4 3.4 %done.1 = (f32[768]{0:T(1024)}, f32[192,3328]{1,0:T(8,128)}, f32[24,192]{1,0:T(8,128)}, f32[384,768]{1,0:T(8,128)}, f32[4,1792]{1,0:T(4,128)}, /*index=5*/f32[17...) custom-call(bf16[192,3584]{1,0:T(8,128)(2,1)} %get-tuple-element.86.rzx.rdelta, ...), custom_call_target="tpu_custom_call" | custom-call | tf_op jit(solution)/shard_map/done/pallas_call | solution.py:1538
  243.8 0.0 copy-done
  243.8 0.0 copy-start.1
  243.8 1.1 copy.28
  245.0 0.8 copy-done.1
  245.8 1.1 copy.29
Async XLA Ops:
  240.4 3.4 %copy-start = (bf16[4,256,768]{2,1,0:T(8,128)(2,1)S(1)}, bf16[4,256,768]{2,1,0:T(8,128)(2,1)}, u32[]{:S(2)}) copy-start(bf16[4,256,768]{2,1,0:T(8,128)(2,1)} %get-tuple-element.112) | copy-start | bytes 4718596
  243.8 2.0 copy-start.1
